TPU v7x, 256 devices: a whole 4x4x8 slice. The times are simulated.
256 devices in a mesh: slab: 8 (over x, core), patch: 32 (over z, y).
Axes of the slice: x: 4, y: 4, z: 8, core: 2. Of those that a mesh axis runs over, the one named last changes fastest.
Arguments:
- right_side: float32 [8, 32, 256, 768], P('slab', 'patch'), may hold values from -6 to 6
- inverse_factor: bfloat16 [8, 32, 768, 768], P('slab', 'patch'), may hold values from -0.12990381 to 1.5, as said below
- forward_trace: bfloat16 [8, 32, 128, 768], P('slab', 'patch'), may hold values from -0.375 to 0.375
- backward_trace: bfloat16 [8, 32, 128, 768], P('slab', 'patch'), may hold values from -0.375 to 0.375
- margin: int32 [8, 32], P('slab', 'patch'), may hold values from 1 to 256, as said below
Outputs:
- correction: float32 [8, 32, 256, 768], P('slab', 'patch')
Inputs may be any that keep to these rules, and one draw needn't show every extreme that they name: `inverse_factor`: lower triangular: zero above the diagonal, positive on it. margin[s, q] counts the last unknowns of patch q that are the first unknowns of patch q + 1 (of patch 0 for q = 31). In every slab some pair shares exactly 256.
All inputs are finite; a program needn't handle non-finite values.
Results may differ from a plain program's by a relative error of at most 0.035.
Values may be sent and summed in bfloat16 or wider, within the bound.
No kernel may reach another device: no remote copies, remote signals or barrier semaphores. Data moves between devices by JAX's collectives and lax.ppermute only.
A program may use at most 64 MiB of HBM per device.

v0:
```python
import jax
import jax.numpy as jnp
from jax import lax
from jax.sharding import PartitionSpec as P

M = 768
KMAX = 256
FACE = 128


def from_behind(value, axis, steps):
    count = lax.axis_size(axis)
    pairs = [(source, (source + steps) % count) for source in range(count)]
    return lax.ppermute(value, axis, pairs)


def from_behind_2(array, axis, by):
    count = lax.axis_size(axis)
    pairs = [(i, i + by) for i in range(count) if 0 <= i + by < count]
    return lax.ppermute(array, axis, pairs)


def placement(counts):
    source_index = jnp.arange(KMAX, dtype=jnp.int32)[None, :, None]
    target_index = jnp.arange(KMAX, dtype=jnp.int32)[None, None, :]
    limit = counts[:, None, None]
    hit = (source_index == KMAX - limit + target_index) & (target_index < limit)
    return jnp.where(hit, 1.0, 0.0).astype(jnp.bfloat16)


def solve(values, factor):
    halfway = jnp.einsum(
        "pck,pik->pci", values.astype(jnp.bfloat16), factor, preferred_element_type=jnp.float32
    )
    return jnp.einsum(
        "pci,pik->pck", halfway.astype(jnp.bfloat16), factor, preferred_element_type=jnp.float32
    )


def slab_step(residual, factor, placing):
    initial = solve(residual, factor).astype(jnp.bfloat16)
    tail_rows = initial[:, :, M - KMAX :]
    head_rows = initial[:, :, :KMAX]
    placed = jnp.einsum(
        "pcs,psd->pcd", tail_rows, placing, preferred_element_type=jnp.float32
    ).astype(jnp.bfloat16)
    incoming = from_behind(placed, "patch", 1)
    from_left = jnp.concatenate([incoming, placed[:-1]], axis=0)
    beyond = from_behind(head_rows, "patch", -1)
    neighbours = jnp.concatenate([head_rows[1:], beyond], axis=0)
    from_right = jnp.einsum("pci,pti->pct", neighbours, placing, preferred_element_type=jnp.float32)
    middle = jnp.zeros((residual.shape[0], residual.shape[1], M - 2 * KMAX), jnp.float32)
    shared = jnp.concatenate([from_left.astype(jnp.float32), middle, from_right], axis=2)
    return solve(residual - 0.5 * shared, factor)


def face_map(matrix, corrected):
    return jnp.einsum(
        "pck,ptk->pct", corrected.astype(jnp.bfloat16), matrix, preferred_element_type=jnp.float32
    ).astype(jnp.bfloat16)


def face_terms(down_face, up_face):
    middle = jnp.zeros((down_face.shape[0], down_face.shape[1], M - 2 * FACE), jnp.float32)
    return jnp.concatenate(
        [down_face.astype(jnp.float32), middle, up_face.astype(jnp.float32)], axis=2
    )


def keep(store, fresh, active):
    return jnp.where(active, fresh, store)


def on_device(right_side, inverse_factor, forward_trace, backward_trace, margin):
    slab_index = lax.axis_index("slab")
    slab_count = lax.axis_size("slab")
    source = right_side[0]
    factor = inverse_factor[0]
    down_matrix = forward_trace[0]
    up_matrix = backward_trace[0]
    placing = placement(margin[0])
    patches = source.shape[0]
    columns = source.shape[1]
    blocks = columns // columns
    is_last = slab_index == slab_count - 1
    zero_face = jnp.zeros((patches, columns, FACE), jnp.bfloat16)

    def forward_section(section_index, carry):
        arriving, down_store, last_store, up_store = carry
        batch_index = section_index - slab_index
        active = (batch_index >= 0) & (batch_index < blocks)
        corrected = slab_step(source - face_terms(arriving, zero_face), factor, placing)
        down_store = keep(down_store, arriving, active)
        last_store = keep(last_store, corrected, active)
        up_store = keep(up_store, face_map(up_matrix, corrected), active)
        sending = face_map(down_matrix, corrected)
        arriving = from_behind_2(sending, "slab", 1)
        return (arriving, down_store, last_store, up_store)

    last_init = jnp.zeros((patches, columns, M), jnp.float32)
    up_init = jnp.zeros((patches, columns, FACE), jnp.bfloat16)
    down_init = jnp.zeros((patches, columns, FACE), jnp.bfloat16)
    carry = lax.fori_loop(
        0, slab_count + blocks - 1, forward_section, (zero_face, down_init, last_init, up_init)
    )
    down_store, last_store, up_store = (carry[1], carry[2], carry[3])
    lead = slab_count - 2
    sections = slab_count + blocks - 2
    pending_init = jnp.where(is_last, up_store, zero_face)

    def reverse_section(section_index, carry):
        pending, out_store = carry
        arriving = from_behind_2(pending, "slab", -1)
        batch_index = section_index - (lead - slab_index)
        active = (batch_index >= 0) & (batch_index < blocks)
        corrected = slab_step(source - face_terms(down_store, arriving), factor, placing)
        out_store = keep(out_store, corrected, active)
        pending = face_map(up_matrix, corrected)
        pending = jnp.where(is_last, up_store, pending)
        return (pending, out_store)

    out_init = jnp.zeros((patches, columns, M), jnp.float32)
    out_store = lax.fori_loop(0, sections, reverse_section, (pending_init, out_init))[1]
    out_store = jnp.where(is_last, last_store, out_store)
    return out_store[None]


def solution(mesh):
    placed = (
        P("slab", "patch", None, None),
        P("slab", "patch", None, None),
        P("slab", "patch", None, None),
        P("slab", "patch", None, None),
        P("slab", "patch"),
    )
    return jax.shard_map(
        on_device,
        mesh=mesh,
        in_specs=placed,
        out_specs=P("slab", "patch", None, None),
        check_vma=False,
    )
```

profile of v0, /device:TPU:1, one launch (start us, length us, event | category | flops | bytes accessed | tf_op | source)
XLA Modules:
  0.0 310.1 jit_solution(14764007084108764631)
XLA Ops:
  0.7 172.6 %while.38 = (s32[]{:T(128)}, bf16[1,256,128]{2,1,0:T(8,128)(2,1)S(1)}, bf16[1,256,128]{2,1,0:T(8,128)(2,1)S(1)}, f32[1,256,768]{2,1,0:T(8,128)S(1)}, bf16[1,256,...) while((s32[]{:T(128)}, ...), condition=%wide.region_1.2_spmd.clone, body=%wide.region_0.1_spmd.clone.sunk | while | flops 1380155392 | bytes 13527177 | solution.py:103
  3.7 8.9 %collective-permute-start = (bf16[1,256,256]{2,1,0:T(8,128)(2,1)S(1)}, bf16[1,256,256]{2,1,0:T(8,128)(2,1)S(1)}, u32[]{:S(2)}, u32[]{:S(2)}) collective-permute-start(bf16[1,256,256]{2,1,0:T(8,128)(2,1)S(1)} %slice.49), channel_id=1, source_target_pairs={{0,31},{1,0},{2,1},{3,2},{4,3},{5,4},{6,5},{7,6},{8,7},{9,8},{10,9... | collective-permute-start | bytes 393224 | tf_op jit(solution)/shard_map/while/body/eval_jaxpr/ppermute | solution.py:14
  15.0 5.0 %collective-permute-done.1 = bf16[1,256,256]{2,1,0:T(8,128)(2,1)S(1)} collective-permute-done((bf16[1,256,256]{2,1,0:T(8,128)(2,1)S(1)}, bf16[1,256,256]{2,1,0:T(8,128)(2,1)S(1)}, u32[]{:S(2)}, u32[]{:S(2)}) %collective-permute-start.1) | collective-permute-done | bytes 131104 | tf_op jit(solution)/shard_map/while/body/eval_jaxpr/ppermute | solution.py:14
  20.1 3.0 bitcast_select_fusion.4
  23.4 5.1 %collective-permute-start.2 = (bf16[1,256,128]{2,1,0:T(8,128)(2,1)S(1)}, bf16[1,256,128]{2,1,0:T(8,128)(2,1)S(1)}, u32[]{:S(2)}, u32[]{:S(2)}) collective-permute-start(bf16[1,256,128]{2,1,0:T(8,128)(2,1)S(1)} %fusion.155), channel_id=1, source_target_pairs={{0,32},{32,64},{64,96},{96,128},{128,160},{160,192},{192,224},{1,3... | collective-permute-start | bytes 196616 | tf_op jit(solution)/shard_map/while/body/eval_jaxpr/ppermute | solution.py:20
  36.8 3.4 %collective-permute-done.1 = bf16[1,256,256]{2,1,0:T(8,128)(2,1)S(1)} collective-permute-done((bf16[1,256,256]{2,1,0:T(8,128)(2,1)S(1)}, bf16[1,256,256]{2,1,0:T(8,128)(2,1)S(1)}, u32[]{:S(2)}, u32[]{:S(2)}) %collective-permute-start.1) | collective-permute-done | bytes 131104 | tf_op jit(solution)/shard_map/while/body/eval_jaxpr/ppermute | solution.py:14
  40.3 3.0 bitcast_select_fusion.4
  43.5 5.6 %collective-permute-start.2 = (bf16[1,256,128]{2,1,0:T(8,128)(2,1)S(1)}, bf16[1,256,128]{2,1,0:T(8,128)(2,1)S(1)}, u32[]{:S(2)}, u32[]{:S(2)}) collective-permute-start(bf16[1,256,128]{2,1,0:T(8,128)(2,1)S(1)} %fusion.155), channel_id=1, source_target_pairs={{0,32},{32,64},{64,96},{96,128},{128,160},{160,192},{192,224},{1,3... | collective-permute-start | bytes 196616 | tf_op jit(solution)/shard_map/while/body/eval_jaxpr/ppermute | solution.py:20
  57.8 3.1 collective-permute-done.1
  61.0 3.0 bitcast_select_fusion.4
  64.2 5.4 %collective-permute-start.2 = (bf16[1,256,128]{2,1,0:T(8,128)(2,1)S(1)}, bf16[1,256,128]{2,1,0:T(8,128)(2,1)S(1)}, u32[]{:S(2)}, u32[]{:S(2)}) collective-permute-start(bf16[1,256,128]{2,1,0:T(8,128)(2,1)S(1)} %fusion.155), channel_id=1, source_target_pairs={{0,32},{32,64},{64,96},{96,128},{128,160},{160,192},{192,224},{1,3... | collective-permute-start | bytes 196616 | tf_op jit(solution)/shard_map/while/body/eval_jaxpr/ppermute | solution.py:20
  78.3 3.1 collective-permute-done.1
  81.4 3.0 bitcast_select_fusion.4
  84.7 5.4 %collective-permute-start.2 = (bf16[1,256,128]{2,1,0:T(8,128)(2,1)S(1)}, bf16[1,256,128]{2,1,0:T(8,128)(2,1)S(1)}, u32[]{:S(2)}, u32[]{:S(2)}) collective-permute-start(bf16[1,256,128]{2,1,0:T(8,128)(2,1)S(1)} %fusion.155), channel_id=1, source_target_pairs={{0,32},{32,64},{64,96},{96,128},{128,160},{160,192},{192,224},{1,3... | collective-permute-start | bytes 196616 | tf_op jit(solution)/shard_map/while/body/eval_jaxpr/ppermute | solution.py:20
  98.7 3.1 collective-permute-done.1
  101.9 3.0 bitcast_select_fusion.4
  105.2 5.4 %collective-permute-start.2 = (bf16[1,256,128]{2,1,0:T(8,128)(2,1)S(1)}, bf16[1,256,128]{2,1,0:T(8,128)(2,1)S(1)}, u32[]{:S(2)}, u32[]{:S(2)}) collective-permute-start(bf16[1,256,128]{2,1,0:T(8,128)(2,1)S(1)} %fusion.155), channel_id=1, source_target_pairs={{0,32},{32,64},{64,96},{96,128},{128,160},{160,192},{192,224},{1,3... | collective-permute-start | bytes 196616 | tf_op jit(solution)/shard_map/while/body/eval_jaxpr/ppermute | solution.py:20
  119.2 3.1 collective-permute-done.1
  122.4 3.0 bitcast_select_fusion.4
  125.7 5.4 %collective-permute-start.2 = (bf16[1,256,128]{2,1,0:T(8,128)(2,1)S(1)}, bf16[1,256,128]{2,1,0:T(8,128)(2,1)S(1)}, u32[]{:S(2)}, u32[]{:S(2)}) collective-permute-start(bf16[1,256,128]{2,1,0:T(8,128)(2,1)S(1)} %fusion.155), channel_id=1, source_target_pairs={{0,32},{32,64},{64,96},{96,128},{128,160},{160,192},{192,224},{1,3... | collective-permute-start | bytes 196616 | tf_op jit(solution)/shard_map/while/body/eval_jaxpr/ppermute | solution.py:20
  139.7 3.1 collective-permute-done.1
  142.9 3.0 bitcast_select_fusion.4
  146.1 5.4 %collective-permute-start.2 = (bf16[1,256,128]{2,1,0:T(8,128)(2,1)S(1)}, bf16[1,256,128]{2,1,0:T(8,128)(2,1)S(1)}, u32[]{:S(2)}, u32[]{:S(2)}) collective-permute-start(bf16[1,256,128]{2,1,0:T(8,128)(2,1)S(1)} %fusion.155), channel_id=1, source_target_pairs={{0,32},{32,64},{64,96},{96,128},{128,160},{160,192},{192,224},{1,3... | collective-permute-start | bytes 196616 | tf_op jit(solution)/shard_map/while/body/eval_jaxpr/ppermute | solution.py:20
  160.2 3.1 collective-permute-done.1
  163.4 3.0 bitcast_select_fusion.4
  166.6 5.4 %collective-permute-start.2 = (bf16[1,256,128]{2,1,0:T(8,128)(2,1)S(1)}, bf16[1,256,128]{2,1,0:T(8,128)(2,1)S(1)}, u32[]{:S(2)}, u32[]{:S(2)}) collective-permute-start(bf16[1,256,128]{2,1,0:T(8,128)(2,1)S(1)} %fusion.155), channel_id=1, source_target_pairs={{0,32},{32,64},{64,96},{96,128},{128,160},{160,192},{192,224},{1,3... | collective-permute-start | bytes 196616 | tf_op jit(solution)/shard_map/while/body/eval_jaxpr/ppermute | solution.py:20
  173.4 135.7 %while.39 = (s32[]{:T(128)}, bf16[1,256,128]{2,1,0:T(8,128)(2,1)S(1)}, f32[1,256,768]{2,1,0:T(8,128)S(1)}, pred[]{:T(512)}, bf16[1,256,128]{2,1,0:T(8,128)(2,1)S...) while((s32[]{:T(128)}, ...), condition=%wide.region_3.4_spmd.clone, body=%wide.region_2.3_spmd.clone.sunk | while | flops 1329725440 | bytes 12402794 | solution.py:123
  175.4 4.2 %collective-permute-done.3 = bf16[1,256,128]{2,1,0:T(8,128)(2,1)S(1)} collective-permute-done((bf16[1,256,128]{2,1,0:T(8,128)(2,1)S(1)}, bf16[1,256,128]{2,1,0:T(8,128)(2,1)S(1)}, u32[]{:S(2)}, u32[]{:S(2)}) %collective-permute-start.3) | collective-permute-done | bytes 65568 | tf_op jit(solution)/shard_map/while/body/eval_jaxpr/ppermute | solution.py:20
  186.9 3.1 collective-permute-done.5
  190.0 3.0 bitcast_select_fusion.5
  195.3 3.8 %collective-permute-done.3 = bf16[1,256,128]{2,1,0:T(8,128)(2,1)S(1)} collective-permute-done((bf16[1,256,128]{2,1,0:T(8,128)(2,1)S(1)}, bf16[1,256,128]{2,1,0:T(8,128)(2,1)S(1)}, u32[]{:S(2)}, u32[]{:S(2)}) %collective-permute-start.3) | collective-permute-done | bytes 65568 | tf_op jit(solution)/shard_map/while/body/eval_jaxpr/ppermute | solution.py:20
  206.0 3.4 %collective-permute-done.5 = bf16[1,256,256]{2,1,0:T(8,128)(2,1)S(1)} collective-permute-done((bf16[1,256,256]{2,1,0:T(8,128)(2,1)S(1)}, bf16[1,256,256]{2,1,0:T(8,128)(2,1)S(1)}, u32[]{:S(2)}, u32[]{:S(2)}) %collective-permute-start.5) | collective-permute-done | bytes 131104 | tf_op jit(solution)/shard_map/while/body/eval_jaxpr/ppermute | solution.py:14
  209.4 3.0 bitcast_select_fusion.5
  214.7 3.6 %collective-permute-done.3 = bf16[1,256,128]{2,1,0:T(8,128)(2,1)S(1)} collective-permute-done((bf16[1,256,128]{2,1,0:T(8,128)(2,1)S(1)}, bf16[1,256,128]{2,1,0:T(8,128)(2,1)S(1)}, u32[]{:S(2)}, u32[]{:S(2)}) %collective-permute-start.3) | collective-permute-done | bytes 65568 | tf_op jit(solution)/shard_map/while/body/eval_jaxpr/ppermute | solution.py:20
  225.3 3.4 %collective-permute-done.5 = bf16[1,256,256]{2,1,0:T(8,128)(2,1)S(1)} collective-permute-done((bf16[1,256,256]{2,1,0:T(8,128)(2,1)S(1)}, bf16[1,256,256]{2,1,0:T(8,128)(2,1)S(1)}, u32[]{:S(2)}, u32[]{:S(2)}) %collective-permute-start.5) | collective-permute-done | bytes 131104 | tf_op jit(solution)/shard_map/while/body/eval_jaxpr/ppermute | solution.py:14
  228.7 3.0 bitcast_select_fusion.5
  234.0 3.6 %collective-permute-done.3 = bf16[1,256,128]{2,1,0:T(8,128)(2,1)S(1)} collective-permute-done((bf16[1,256,128]{2,1,0:T(8,128)(2,1)S(1)}, bf16[1,256,128]{2,1,0:T(8,128)(2,1)S(1)}, u32[]{:S(2)}, u32[]{:S(2)}) %collective-permute-start.3) | collective-permute-done | bytes 65568 | tf_op jit(solution)/shard_map/while/body/eval_jaxpr/ppermute | solution.py:20
  244.6 3.4 %collective-permute-done.5 = bf16[1,256,256]{2,1,0:T(8,128)(2,1)S(1)} collective-permute-done((bf16[1,256,256]{2,1,0:T(8,128)(2,1)S(1)}, bf16[1,256,256]{2,1,0:T(8,128)(2,1)S(1)}, u32[]{:S(2)}, u32[]{:S(2)}) %collective-permute-start.5) | collective-permute-done | bytes 131104 | tf_op jit(solution)/shard_map/while/body/eval_jaxpr/ppermute | solution.py:14
  248.0 3.0 bitcast_select_fusion.5
  253.2 3.6 %collective-permute-done.3 = bf16[1,256,128]{2,1,0:T(8,128)(2,1)S(1)} collective-permute-done((bf16[1,256,128]{2,1,0:T(8,128)(2,1)S(1)}, bf16[1,256,128]{2,1,0:T(8,128)(2,1)S(1)}, u32[]{:S(2)}, u32[]{:S(2)}) %collective-permute-start.3) | collective-permute-done | bytes 65568 | tf_op jit(solution)/shard_map/while/body/eval_jaxpr/ppermute | solution.py:20
  263.8 3.4 %collective-permute-done.5 = bf16[1,256,256]{2,1,0:T(8,128)(2,1)S(1)} collective-permute-done((bf16[1,256,256]{2,1,0:T(8,128)(2,1)S(1)}, bf16[1,256,256]{2,1,0:T(8,128)(2,1)S(1)}, u32[]{:S(2)}, u32[]{:S(2)}) %collective-permute-start.5) | collective-permute-done | bytes 131104 | tf_op jit(solution)/shard_map/while/body/eval_jaxpr/ppermute | solution.py:14
  267.3 3.0 bitcast_select_fusion.5
  272.5 3.6 %collective-permute-done.3 = bf16[1,256,128]{2,1,0:T(8,128)(2,1)S(1)} collective-permute-done((bf16[1,256,128]{2,1,0:T(8,128)(2,1)S(1)}, bf16[1,256,128]{2,1,0:T(8,128)(2,1)S(1)}, u32[]{:S(2)}, u32[]{:S(2)}) %collective-permute-start.3) | collective-permute-done | bytes 65568 | tf_op jit(solution)/shard_map/while/body/eval_jaxpr/ppermute | solution.py:20
  283.1 3.4 %collective-permute-done.5 = bf16[1,256,256]{2,1,0:T(8,128)(2,1)S(1)} collective-permute-done((bf16[1,256,256]{2,1,0:T(8,128)(2,1)S(1)}, bf16[1,256,256]{2,1,0:T(8,128)(2,1)S(1)}, u32[]{:S(2)}, u32[]{:S(2)}) %collective-permute-start.5) | collective-permute-done | bytes 131104 | tf_op jit(solution)/shard_map/while/body/eval_jaxpr/ppermute | solution.py:14
  286.6 3.0 bitcast_select_fusion.5
  291.8 3.6 %collective-permute-done.3 = bf16[1,256,128]{2,1,0:T(8,128)(2,1)S(1)} collective-permute-done((bf16[1,256,128]{2,1,0:T(8,128)(2,1)S(1)}, bf16[1,256,128]{2,1,0:T(8,128)(2,1)S(1)}, u32[]{:S(2)}, u32[]{:S(2)}) %collective-permute-start.3) | collective-permute-done | bytes 65568 | tf_op jit(solution)/shard_map/while/body/eval_jaxpr/ppermute | solution.py:20
  302.4 3.4 %collective-permute-done.5 = bf16[1,256,256]{2,1,0:T(8,128)(2,1)S(1)} collective-permute-done((bf16[1,256,256]{2,1,0:T(8,128)(2,1)S(1)}, bf16[1,256,256]{2,1,0:T(8,128)(2,1)S(1)}, u32[]{:S(2)}, u32[]{:S(2)}) %collective-permute-start.5) | collective-permute-done | bytes 131104 | tf_op jit(solution)/shard_map/while/body/eval_jaxpr/ppermute | solution.py:14
  305.8 3.0 bitcast_select_fusion.5
  (295 shorter events, 134.0 us)
Async XLA Ops:
  3.7 11.1 %collective-permute-start = (bf16[1,256,256]{2,1,0:T(8,128)(2,1)S(1)}, bf16[1,256,256]{2,1,0:T(8,128)(2,1)S(1)}, u32[]{:S(2)}, u32[]{:S(2)}) collective-permute-start(bf16[1,256,256]{2,1,0:T(8,128)(2,1)S(1)} %slice.49), channel_id=1, source_target_pairs={{0,31},{1,0},{2,1},{3,2},{4,3},{5,4},{6,5},{7,6},{8,7},{9,8},{10,9... | collective-permute-start | bytes 393224 | tf_op jit(solution)/shard_map/while/body/eval_jaxpr/ppermute | solution.py:14
  12.8 7.2 %collective-permute-start.1 = (bf16[1,256,256]{2,1,0:T(8,128)(2,1)S(1)}, bf16[1,256,256]{2,1,0:T(8,128)(2,1)S(1)}, u32[]{:S(2)}, u32[]{:S(2)}) collective-permute-start(bf16[1,256,256]{2,1,0:T(8,128)(2,1)S(1)} %fusion.154), channel_id=1, source_target_pairs={{0,1},{1,2},{2,3},{3,4},{4,5},{5,6},{6,7},{7,8},{8,9},{9,10},{10,1... | collective-permute-start | bytes 393224 | tf_op jit(solution)/shard_map/while/body/eval_jaxpr/ppermute | solution.py:14
  23.4 6.4 %collective-permute-start.2 = (bf16[1,256,128]{2,1,0:T(8,128)(2,1)S(1)}, bf16[1,256,128]{2,1,0:T(8,128)(2,1)S(1)}, u32[]{:S(2)}, u32[]{:S(2)}) collective-permute-start(bf16[1,256,128]{2,1,0:T(8,128)(2,1)S(1)} %fusion.155), channel_id=1, source_target_pairs={{0,32},{32,64},{64,96},{96,128},{128,160},{160,192},{192,224},{1,3... | collective-permute-start | bytes 196616 | tf_op jit(solution)/shard_map/while/body/eval_jaxpr/ppermute | solution.py:20
  32.7 3.9 %collective-permute-start = (bf16[1,256,256]{2,1,0:T(8,128)(2,1)S(1)}, bf16[1,256,256]{2,1,0:T(8,128)(2,1)S(1)}, u32[]{:S(2)}, u32[]{:S(2)}) collective-permute-start(bf16[1,256,256]{2,1,0:T(8,128)(2,1)S(1)} %slice.49), channel_id=1, source_target_pairs={{0,31},{1,0},{2,1},{3,2},{4,3},{5,4},{6,5},{7,6},{8,7},{9,8},{10,9... | collective-permute-start | bytes 393224 | tf_op jit(solution)/shard_map/while/body/eval_jaxpr/ppermute | solution.py:14
  33.0 7.2 %collective-permute-start.1 = (bf16[1,256,256]{2,1,0:T(8,128)(2,1)S(1)}, bf16[1,256,256]{2,1,0:T(8,128)(2,1)S(1)}, u32[]{:S(2)}, u32[]{:S(2)}) collective-permute-start(bf16[1,256,256]{2,1,0:T(8,128)(2,1)S(1)} %fusion.154), channel_id=1, source_target_pairs={{0,1},{1,2},{2,3},{3,4},{4,5},{5,6},{6,7},{7,8},{8,9},{9,10},{10,1... | collective-permute-start | bytes 393224 | tf_op jit(solution)/shard_map/while/body/eval_jaxpr/ppermute | solution.py:14
  40.2 8.9 %copy-start = (bf16[1,128,768]{2,1,0:T(8,128)(2,1)S(1)}, bf16[1,128,768]{2,1,0:T(8,128)(2,1)}, u32[]{:S(2)}) copy-start(bf16[1,128,768]{2,1,0:T(8,128)(2,1)} %get-tuple-element.792) | copy-start | bytes 589828 | tf_op jit(solution)/shard_map/while
  43.5 7.0 %collective-permute-start.2 = (bf16[1,256,128]{2,1,0:T(8,128)(2,1)S(1)}, bf16[1,256,128]{2,1,0:T(8,128)(2,1)S(1)}, u32[]{:S(2)}, u32[]{:S(2)}) collective-permute-start(bf16[1,256,128]{2,1,0:T(8,128)(2,1)S(1)} %fusion.155), channel_id=1, source_target_pairs={{0,32},{32,64},{64,96},{96,128},{128,160},{160,192},{192,224},{1,3... | collective-permute-start | bytes 196616 | tf_op jit(solution)/shard_map/while/body/eval_jaxpr/ppermute | solution.py:20
  53.4 4.2 %collective-permute-start = (bf16[1,256,256]{2,1,0:T(8,128)(2,1)S(1)}, bf16[1,256,256]{2,1,0:T(8,128)(2,1)S(1)}, u32[]{:S(2)}, u32[]{:S(2)}) collective-permute-start(bf16[1,256,256]{2,1,0:T(8,128)(2,1)S(1)} %slice.49), channel_id=1, source_target_pairs={{0,31},{1,0},{2,1},{3,2},{4,3},{5,4},{6,5},{7,6},{8,7},{9,8},{10,9... | collective-permute-start | bytes 393224 | tf_op jit(solution)/shard_map/while/body/eval_jaxpr/ppermute | solution.py:14
  53.7 7.2 %collective-permute-start.1 = (bf16[1,256,256]{2,1,0:T(8,128)(2,1)S(1)}, bf16[1,256,256]{2,1,0:T(8,128)(2,1)S(1)}, u32[]{:S(2)}, u32[]{:S(2)}) collective-permute-start(bf16[1,256,256]{2,1,0:T(8,128)(2,1)S(1)} %fusion.154), channel_id=1, source_target_pairs={{0,1},{1,2},{2,3},{3,4},{4,5},{5,6},{6,7},{7,8},{8,9},{9,10},{10,1... | collective-permute-start | bytes 393224 | tf_op jit(solution)/shard_map/while/body/eval_jaxpr/ppermute | solution.py:14
  64.2 6.7 %collective-permute-start.2 = (bf16[1,256,128]{2,1,0:T(8,128)(2,1)S(1)}, bf16[1,256,128]{2,1,0:T(8,128)(2,1)S(1)}, u32[]{:S(2)}, u32[]{:S(2)}) collective-permute-start(bf16[1,256,128]{2,1,0:T(8,128)(2,1)S(1)} %fusion.155), channel_id=1, source_target_pairs={{0,32},{32,64},{64,96},{96,128},{128,160},{160,192},{192,224},{1,3... | collective-permute-start | bytes 196616 | tf_op jit(solution)/shard_map/while/body/eval_jaxpr/ppermute | solution.py:20
  73.8 4.2 %collective-permute-start = (bf16[1,256,256]{2,1,0:T(8,128)(2,1)S(1)}, bf16[1,256,256]{2,1,0:T(8,128)(2,1)S(1)}, u32[]{:S(2)}, u32[]{:S(2)}) collective-permute-start(bf16[1,256,256]{2,1,0:T(8,128)(2,1)S(1)} %slice.49), channel_id=1, source_target_pairs={{0,31},{1,0},{2,1},{3,2},{4,3},{5,4},{6,5},{7,6},{8,7},{9,8},{10,9... | collective-permute-start | bytes 393224 | tf_op jit(solution)/shard_map/while/body/eval_jaxpr/ppermute | solution.py:14
  74.1 7.2 %collective-permute-start.1 = (bf16[1,256,256]{2,1,0:T(8,128)(2,1)S(1)}, bf16[1,256,256]{2,1,0:T(8,128)(2,1)S(1)}, u32[]{:S(2)}, u32[]{:S(2)}) collective-permute-start(bf16[1,256,256]{2,1,0:T(8,128)(2,1)S(1)} %fusion.154), channel_id=1, source_target_pairs={{0,1},{1,2},{2,3},{3,4},{4,5},{5,6},{6,7},{7,8},{8,9},{9,10},{10,1... | collective-permute-start | bytes 393224 | tf_op jit(solution)/shard_map/while/body/eval_jaxpr/ppermute | solution.py:14
  81.4 8.7 %copy-start = (bf16[1,128,768]{2,1,0:T(8,128)(2,1)S(1)}, bf16[1,128,768]{2,1,0:T(8,128)(2,1)}, u32[]{:S(2)}) copy-start(bf16[1,128,768]{2,1,0:T(8,128)(2,1)} %get-tuple-element.792) | copy-start | bytes 589828 | tf_op jit(solution)/shard_map/while
  84.7 6.7 %collective-permute-start.2 = (bf16[1,256,128]{2,1,0:T(8,128)(2,1)S(1)}, bf16[1,256,128]{2,1,0:T(8,128)(2,1)S(1)}, u32[]{:S(2)}, u32[]{:S(2)}) collective-permute-start(bf16[1,256,128]{2,1,0:T(8,128)(2,1)S(1)} %fusion.155), channel_id=1, source_target_pairs={{0,32},{32,64},{64,96},{96,128},{128,160},{160,192},{192,224},{1,3... | collective-permute-start | bytes 196616 | tf_op jit(solution)/shard_map/while/body/eval_jaxpr/ppermute | solution.py:20
  94.3 4.2 %collective-permute-start = (bf16[1,256,256]{2,1,0:T(8,128)(2,1)S(1)}, bf16[1,256,256]{2,1,0:T(8,128)(2,1)S(1)}, u32[]{:S(2)}, u32[]{:S(2)}) collective-permute-start(bf16[1,256,256]{2,1,0:T(8,128)(2,1)S(1)} %slice.49), channel_id=1, source_target_pairs={{0,31},{1,0},{2,1},{3,2},{4,3},{5,4},{6,5},{7,6},{8,7},{9,8},{10,9... | collective-permute-start | bytes 393224 | tf_op jit(solution)/shard_map/while/body/eval_jaxpr/ppermute | solution.py:14
  94.6 7.2 %collective-permute-start.1 = (bf16[1,256,256]{2,1,0:T(8,128)(2,1)S(1)}, bf16[1,256,256]{2,1,0:T(8,128)(2,1)S(1)}, u32[]{:S(2)}, u32[]{:S(2)}) collective-permute-start(bf16[1,256,256]{2,1,0:T(8,128)(2,1)S(1)} %fusion.154), channel_id=1, source_target_pairs={{0,1},{1,2},{2,3},{3,4},{4,5},{5,6},{6,7},{7,8},{8,9},{9,10},{10,1... | collective-permute-start | bytes 393224 | tf_op jit(solution)/shard_map/while/body/eval_jaxpr/ppermute | solution.py:14
  105.2 6.7 %collective-permute-start.2 = (bf16[1,256,128]{2,1,0:T(8,128)(2,1)S(1)}, bf16[1,256,128]{2,1,0:T(8,128)(2,1)S(1)}, u32[]{:S(2)}, u32[]{:S(2)}) collective-permute-start(bf16[1,256,128]{2,1,0:T(8,128)(2,1)S(1)} %fusion.155), channel_id=1, source_target_pairs={{0,32},{32,64},{64,96},{96,128},{128,160},{160,192},{192,224},{1,3... | collective-permute-start | bytes 196616 | tf_op jit(solution)/shard_map/while/body/eval_jaxpr/ppermute | solution.py:20
  114.8 4.2 %collective-permute-start = (bf16[1,256,256]{2,1,0:T(8,128)(2,1)S(1)}, bf16[1,256,256]{2,1,0:T(8,128)(2,1)S(1)}, u32[]{:S(2)}, u32[]{:S(2)}) collective-permute-start(bf16[1,256,256]{2,1,0:T(8,128)(2,1)S(1)} %slice.49), channel_id=1, source_target_pairs={{0,31},{1,0},{2,1},{3,2},{4,3},{5,4},{6,5},{7,6},{8,7},{9,8},{10,9... | collective-permute-start | bytes 393224 | tf_op jit(solution)/shard_map/while/body/eval_jaxpr/ppermute | solution.py:14
  115.1 7.2 %collective-permute-start.1 = (bf16[1,256,256]{2,1,0:T(8,128)(2,1)S(1)}, bf16[1,256,256]{2,1,0:T(8,128)(2,1)S(1)}, u32[]{:S(2)}, u32[]{:S(2)}) collective-permute-start(bf16[1,256,256]{2,1,0:T(8,128)(2,1)S(1)} %fusion.154), channel_id=1, source_target_pairs={{0,1},{1,2},{2,3},{3,4},{4,5},{5,6},{6,7},{7,8},{8,9},{9,10},{10,1... | collective-permute-start | bytes 393224 | tf_op jit(solution)/shard_map/while/body/eval_jaxpr/ppermute | solution.py:14
  125.7 6.7 %collective-permute-start.2 = (bf16[1,256,128]{2,1,0:T(8,128)(2,1)S(1)}, bf16[1,256,128]{2,1,0:T(8,128)(2,1)S(1)}, u32[]{:S(2)}, u32[]{:S(2)}) collective-permute-start(bf16[1,256,128]{2,1,0:T(8,128)(2,1)S(1)} %fusion.155), channel_id=1, source_target_pairs={{0,32},{32,64},{64,96},{96,128},{128,160},{160,192},{192,224},{1,3... | collective-permute-start | bytes 196616 | tf_op jit(solution)/shard_map/while/body/eval_jaxpr/ppermute | solution.py:20
  135.3 4.2 %collective-permute-start = (bf16[1,256,256]{2,1,0:T(8,128)(2,1)S(1)}, bf16[1,256,256]{2,1,0:T(8,128)(2,1)S(1)}, u32[]{:S(2)}, u32[]{:S(2)}) collective-permute-start(bf16[1,256,256]{2,1,0:T(8,128)(2,1)S(1)} %slice.49), channel_id=1, source_target_pairs={{0,31},{1,0},{2,1},{3,2},{4,3},{5,4},{6,5},{7,6},{8,7},{9,8},{10,9... | collective-permute-start | bytes 393224 | tf_op jit(solution)/shard_map/while/body/eval_jaxpr/ppermute | solution.py:14
  135.6 7.2 %collective-permute-start.1 = (bf16[1,256,256]{2,1,0:T(8,128)(2,1)S(1)}, bf16[1,256,256]{2,1,0:T(8,128)(2,1)S(1)}, u32[]{:S(2)}, u32[]{:S(2)}) collective-permute-start(bf16[1,256,256]{2,1,0:T(8,128)(2,1)S(1)} %fusion.154), channel_id=1, source_target_pairs={{0,1},{1,2},{2,3},{3,4},{4,5},{5,6},{6,7},{7,8},{8,9},{9,10},{10,1... | collective-permute-start | bytes 393224 | tf_op jit(solution)/shard_map/while/body/eval_jaxpr/ppermute | solution.py:14
  142.9 8.7 %copy-start = (bf16[1,128,768]{2,1,0:T(8,128)(2,1)S(1)}, bf16[1,128,768]{2,1,0:T(8,128)(2,1)}, u32[]{:S(2)}) copy-start(bf16[1,128,768]{2,1,0:T(8,128)(2,1)} %get-tuple-element.792) | copy-start | bytes 589828 | tf_op jit(solution)/shard_map/while
  146.1 6.7 %collective-permute-start.2 = (bf16[1,256,128]{2,1,0:T(8,128)(2,1)S(1)}, bf16[1,256,128]{2,1,0:T(8,128)(2,1)S(1)}, u32[]{:S(2)}, u32[]{:S(2)}) collective-permute-start(bf16[1,256,128]{2,1,0:T(8,128)(2,1)S(1)} %fusion.155), channel_id=1, source_target_pairs={{0,32},{32,64},{64,96},{96,128},{128,160},{160,192},{192,224},{1,3... | collective-permute-start | bytes 196616 | tf_op jit(solution)/shard_map/while/body/eval_jaxpr/ppermute | solution.py:20
  155.8 4.2 %collective-permute-start = (bf16[1,256,256]{2,1,0:T(8,128)(2,1)S(1)}, bf16[1,256,256]{2,1,0:T(8,128)(2,1)S(1)}, u32[]{:S(2)}, u32[]{:S(2)}) collective-permute-start(bf16[1,256,256]{2,1,0:T(8,128)(2,1)S(1)} %slice.49), channel_id=1, source_target_pairs={{0,31},{1,0},{2,1},{3,2},{4,3},{5,4},{6,5},{7,6},{8,7},{9,8},{10,9... | collective-permute-start | bytes 393224 | tf_op jit(solution)/shard_map/while/body/eval_jaxpr/ppermute | solution.py:14
  156.1 7.2 %collective-permute-start.1 = (bf16[1,256,256]{2,1,0:T(8,128)(2,1)S(1)}, bf16[1,256,256]{2,1,0:T(8,128)(2,1)S(1)}, u32[]{:S(2)}, u32[]{:S(2)}) collective-permute-start(bf16[1,256,256]{2,1,0:T(8,128)(2,1)S(1)} %fusion.154), channel_id=1, source_target_pairs={{0,1},{1,2},{2,3},{3,4},{4,5},{5,6},{6,7},{7,8},{8,9},{9,10},{10,1... | collective-permute-start | bytes 393224 | tf_op jit(solution)/shard_map/while/body/eval_jaxpr/ppermute | solution.py:14
  166.6 6.7 %collective-permute-start.2 = (bf16[1,256,128]{2,1,0:T(8,128)(2,1)S(1)}, bf16[1,256,128]{2,1,0:T(8,128)(2,1)S(1)}, u32[]{:S(2)}, u32[]{:S(2)}) collective-permute-start(bf16[1,256,128]{2,1,0:T(8,128)(2,1)S(1)} %fusion.155), channel_id=1, source_target_pairs={{0,32},{32,64},{64,96},{96,128},{128,160},{160,192},{192,224},{1,3... | collective-permute-start | bytes 196616 | tf_op jit(solution)/shard_map/while/body/eval_jaxpr/ppermute | solution.py:20
  173.4 6.2 %collective-permute-start.3 = (bf16[1,256,128]{2,1,0:T(8,128)(2,1)S(1)}, bf16[1,256,128]{2,1,0:T(8,128)(2,1)S(1)}, u32[]{:S(2)}, u32[]{:S(2)}) collective-permute-start(bf16[1,256,128]{2,1,0:T(8,128)(2,1)S(1)} %get-tuple-element.816), channel_id=1, source_target_pairs={{32,0},{64,32},{96,64},{128,96},{160,128},{192,160},{224,192},{33,... | collective-permute-start | bytes 196616 | tf_op jit(solution)/shard_map/while/body/eval_jaxpr/ppermute | solution.py:20
  182.4 4.2 %collective-permute-start.4 = (bf16[1,256,256]{2,1,0:T(8,128)(2,1)S(1)}, bf16[1,256,256]{2,1,0:T(8,128)(2,1)S(1)}, u32[]{:S(2)}, u32[]{:S(2)}) collective-permute-start(bf16[1,256,256]{2,1,0:T(8,128)(2,1)S(1)} %slice.51), channel_id=1, source_target_pairs={{0,31},{1,0},{2,1},{3,2},{4,3},{5,4},{6,5},{7,6},{8,7},{9,8},{10,9... | collective-permute-start | bytes 393224 | tf_op jit(solution)/shard_map/while/body/eval_jaxpr/ppermute | solution.py:14
  182.7 7.2 %collective-permute-start.5 = (bf16[1,256,256]{2,1,0:T(8,128)(2,1)S(1)}, bf16[1,256,256]{2,1,0:T(8,128)(2,1)S(1)}, u32[]{:S(2)}, u32[]{:S(2)}) collective-permute-start(bf16[1,256,256]{2,1,0:T(8,128)(2,1)S(1)} %fusion.168), channel_id=1, source_target_pairs={{0,1},{1,2},{2,3},{3,4},{4,5},{5,6},{6,7},{7,8},{8,9},{9,10},{10,1... | collective-permute-start | bytes 393224 | tf_op jit(solution)/shard_map/while/body/eval_jaxpr/ppermute | solution.py:14
  193.3 5.7 %collective-permute-start.3 = (bf16[1,256,128]{2,1,0:T(8,128)(2,1)S(1)}, bf16[1,256,128]{2,1,0:T(8,128)(2,1)S(1)}, u32[]{:S(2)}, u32[]{:S(2)}) collective-permute-start(bf16[1,256,128]{2,1,0:T(8,128)(2,1)S(1)} %get-tuple-element.816), channel_id=1, source_target_pairs={{32,0},{64,32},{96,64},{128,96},{160,128},{192,160},{224,192},{33,... | collective-permute-start | bytes 196616 | tf_op jit(solution)/shard_map/while/body/eval_jaxpr/ppermute | solution.py:20
  201.9 3.9 %collective-permute-start.4 = (bf16[1,256,256]{2,1,0:T(8,128)(2,1)S(1)}, bf16[1,256,256]{2,1,0:T(8,128)(2,1)S(1)}, u32[]{:S(2)}, u32[]{:S(2)}) collective-permute-start(bf16[1,256,256]{2,1,0:T(8,128)(2,1)S(1)} %slice.51), channel_id=1, source_target_pairs={{0,31},{1,0},{2,1},{3,2},{4,3},{5,4},{6,5},{7,6},{8,7},{9,8},{10,9... | collective-permute-start | bytes 393224 | tf_op jit(solution)/shard_map/while/body/eval_jaxpr/ppermute | solution.py:14
  202.2 7.2 %collective-permute-start.5 = (bf16[1,256,256]{2,1,0:T(8,128)(2,1)S(1)}, bf16[1,256,256]{2,1,0:T(8,128)(2,1)S(1)}, u32[]{:S(2)}, u32[]{:S(2)}) collective-permute-start(bf16[1,256,256]{2,1,0:T(8,128)(2,1)S(1)} %fusion.168), channel_id=1, source_target_pairs={{0,1},{1,2},{2,3},{3,4},{4,5},{5,6},{6,7},{7,8},{8,9},{9,10},{10,1... | collective-permute-start | bytes 393224 | tf_op jit(solution)/shard_map/while/body/eval_jaxpr/ppermute | solution.py:14
  212.7 5.6 %collective-permute-start.3 = (bf16[1,256,128]{2,1,0:T(8,128)(2,1)S(1)}, bf16[1,256,128]{2,1,0:T(8,128)(2,1)S(1)}, u32[]{:S(2)}, u32[]{:S(2)}) collective-permute-start(bf16[1,256,128]{2,1,0:T(8,128)(2,1)S(1)} %get-tuple-element.816), channel_id=1, source_target_pairs={{32,0},{64,32},{96,64},{128,96},{160,128},{192,160},{224,192},{33,... | collective-permute-start | bytes 196616 | tf_op jit(solution)/shard_map/while/body/eval_jaxpr/ppermute | solution.py:20
  221.1 3.9 %collective-permute-start.4 = (bf16[1,256,256]{2,1,0:T(8,128)(2,1)S(1)}, bf16[1,256,256]{2,1,0:T(8,128)(2,1)S(1)}, u32[]{:S(2)}, u32[]{:S(2)}) collective-permute-start(bf16[1,256,256]{2,1,0:T(8,128)(2,1)S(1)} %slice.51), channel_id=1, source_target_pairs={{0,31},{1,0},{2,1},{3,2},{4,3},{5,4},{6,5},{7,6},{8,7},{9,8},{10,9... | collective-permute-start | bytes 393224 | tf_op jit(solution)/shard_map/while/body/eval_jaxpr/ppermute | solution.py:14
  221.4 7.2 %collective-permute-start.5 = (bf16[1,256,256]{2,1,0:T(8,128)(2,1)S(1)}, bf16[1,256,256]{2,1,0:T(8,128)(2,1)S(1)}, u32[]{:S(2)}, u32[]{:S(2)}) collective-permute-start(bf16[1,256,256]{2,1,0:T(8,128)(2,1)S(1)} %fusion.168), channel_id=1, source_target_pairs={{0,1},{1,2},{2,3},{3,4},{4,5},{5,6},{6,7},{7,8},{8,9},{9,10},{10,1... | collective-permute-start | bytes 393224 | tf_op jit(solution)/shard_map/while/body/eval_jaxpr/ppermute | solution.py:14
  232.0 5.6 %collective-permute-start.3 = (bf16[1,256,128]{2,1,0:T(8,128)(2,1)S(1)}, bf16[1,256,128]{2,1,0:T(8,128)(2,1)S(1)}, u32[]{:S(2)}, u32[]{:S(2)}) collective-permute-start(bf16[1,256,128]{2,1,0:T(8,128)(2,1)S(1)} %get-tuple-element.816), channel_id=1, source_target_pairs={{32,0},{64,32},{96,64},{128,96},{160,128},{192,160},{224,192},{33,... | collective-permute-start | bytes 196616 | tf_op jit(solution)/shard_map/while/body/eval_jaxpr/ppermute | solution.py:20
  240.4 3.9 %collective-permute-start.4 = (bf16[1,256,256]{2,1,0:T(8,128)(2,1)S(1)}, bf16[1,256,256]{2,1,0:T(8,128)(2,1)S(1)}, u32[]{:S(2)}, u32[]{:S(2)}) collective-permute-start(bf16[1,256,256]{2,1,0:T(8,128)(2,1)S(1)} %slice.51), channel_id=1, source_target_pairs={{0,31},{1,0},{2,1},{3,2},{4,3},{5,4},{6,5},{7,6},{8,7},{9,8},{10,9... | collective-permute-start | bytes 393224 | tf_op jit(solution)/shard_map/while/body/eval_jaxpr/ppermute | solution.py:14
  240.7 7.2 %collective-permute-start.5 = (bf16[1,256,256]{2,1,0:T(8,128)(2,1)S(1)}, bf16[1,256,256]{2,1,0:T(8,128)(2,1)S(1)}, u32[]{:S(2)}, u32[]{:S(2)}) collective-permute-start(bf16[1,256,256]{2,1,0:T(8,128)(2,1)S(1)} %fusion.168), channel_id=1, source_target_pairs={{0,1},{1,2},{2,3},{3,4},{4,5},{5,6},{6,7},{7,8},{8,9},{9,10},{10,1... | collective-permute-start | bytes 393224 | tf_op jit(solution)/shard_map/while/body/eval_jaxpr/ppermute | solution.py:14
  251.3 5.6 %collective-permute-start.3 = (bf16[1,256,128]{2,1,0:T(8,128)(2,1)S(1)}, bf16[1,256,128]{2,1,0:T(8,128)(2,1)S(1)}, u32[]{:S(2)}, u32[]{:S(2)}) collective-permute-start(bf16[1,256,128]{2,1,0:T(8,128)(2,1)S(1)} %get-tuple-element.816), channel_id=1, source_target_pairs={{32,0},{64,32},{96,64},{128,96},{160,128},{192,160},{224,192},{33,... | collective-permute-start | bytes 196616 | tf_op jit(solution)/shard_map/while/body/eval_jaxpr/ppermute | solution.py:20
  259.7 3.9 %collective-permute-start.4 = (bf16[1,256,256]{2,1,0:T(8,128)(2,1)S(1)}, bf16[1,256,256]{2,1,0:T(8,128)(2,1)S(1)}, u32[]{:S(2)}, u32[]{:S(2)}) collective-permute-start(bf16[1,256,256]{2,1,0:T(8,128)(2,1)S(1)} %slice.51), channel_id=1, source_target_pairs={{0,31},{1,0},{2,1},{3,2},{4,3},{5,4},{6,5},{7,6},{8,7},{9,8},{10,9... | collective-permute-start | bytes 393224 | tf_op jit(solution)/shard_map/while/body/eval_jaxpr/ppermute | solution.py:14
  260.0 7.2 %collective-permute-start.5 = (bf16[1,256,256]{2,1,0:T(8,128)(2,1)S(1)}, bf16[1,256,256]{2,1,0:T(8,128)(2,1)S(1)}, u32[]{:S(2)}, u32[]{:S(2)}) collective-permute-start(bf16[1,256,256]{2,1,0:T(8,128)(2,1)S(1)} %fusion.168), channel_id=1, source_target_pairs={{0,1},{1,2},{2,3},{3,4},{4,5},{5,6},{6,7},{7,8},{8,9},{9,10},{10,1... | collective-permute-start | bytes 393224 | tf_op jit(solution)/shard_map/while/body/eval_jaxpr/ppermute | solution.py:14
  270.6 5.6 %collective-permute-start.3 = (bf16[1,256,128]{2,1,0:T(8,128)(2,1)S(1)}, bf16[1,256,128]{2,1,0:T(8,128)(2,1)S(1)}, u32[]{:S(2)}, u32[]{:S(2)}) collective-permute-start(bf16[1,256,128]{2,1,0:T(8,128)(2,1)S(1)} %get-tuple-element.816), channel_id=1, source_target_pairs={{32,0},{64,32},{96,64},{128,96},{160,128},{192,160},{224,192},{33,... | collective-permute-start | bytes 196616 | tf_op jit(solution)/shard_map/while/body/eval_jaxpr/ppermute | solution.py:20
  279.0 3.9 %collective-permute-start.4 = (bf16[1,256,256]{2,1,0:T(8,128)(2,1)S(1)}, bf16[1,256,256]{2,1,0:T(8,128)(2,1)S(1)}, u32[]{:S(2)}, u32[]{:S(2)}) collective-permute-start(bf16[1,256,256]{2,1,0:T(8,128)(2,1)S(1)} %slice.51), channel_id=1, source_target_pairs={{0,31},{1,0},{2,1},{3,2},{4,3},{5,4},{6,5},{7,6},{8,7},{9,8},{10,9... | collective-permute-start | bytes 393224 | tf_op jit(solution)/shard_map/while/body/eval_jaxpr/ppermute | solution.py:14
  279.3 7.2 %collective-permute-start.5 = (bf16[1,256,256]{2,1,0:T(8,128)(2,1)S(1)}, bf16[1,256,256]{2,1,0:T(8,128)(2,1)S(1)}, u32[]{:S(2)}, u32[]{:S(2)}) collective-permute-start(bf16[1,256,256]{2,1,0:T(8,128)(2,1)S(1)} %fusion.168), channel_id=1, source_target_pairs={{0,1},{1,2},{2,3},{3,4},{4,5},{5,6},{6,7},{7,8},{8,9},{9,10},{10,1... | collective-permute-start | bytes 393224 | tf_op jit(solution)/shard_map/while/body/eval_jaxpr/ppermute | solution.py:14
  289.8 5.6 %collective-permute-start.3 = (bf16[1,256,128]{2,1,0:T(8,128)(2,1)S(1)}, bf16[1,256,128]{2,1,0:T(8,128)(2,1)S(1)}, u32[]{:S(2)}, u32[]{:S(2)}) collective-permute-start(bf16[1,256,128]{2,1,0:T(8,128)(2,1)S(1)} %get-tuple-element.816), channel_id=1, source_target_pairs={{32,0},{64,32},{96,64},{128,96},{160,128},{192,160},{224,192},{33,... | collective-permute-start | bytes 196616 | tf_op jit(solution)/shard_map/while/body/eval_jaxpr/ppermute | solution.py:20
  298.3 3.9 %collective-permute-start.4 = (bf16[1,256,256]{2,1,0:T(8,128)(2,1)S(1)}, bf16[1,256,256]{2,1,0:T(8,128)(2,1)S(1)}, u32[]{:S(2)}, u32[]{:S(2)}) collective-permute-start(bf16[1,256,256]{2,1,0:T(8,128)(2,1)S(1)} %slice.51), channel_id=1, source_target_pairs={{0,31},{1,0},{2,1},{3,2},{4,3},{5,4},{6,5},{7,6},{8,7},{9,8},{10,9... | collective-permute-start | bytes 393224 | tf_op jit(solution)/shard_map/while/body/eval_jaxpr/ppermute | solution.py:14
  298.6 7.2 %collective-permute-start.5 = (bf16[1,256,256]{2,1,0:T(8,128)(2,1)S(1)}, bf16[1,256,256]{2,1,0:T(8,128)(2,1)S(1)}, u32[]{:S(2)}, u32[]{:S(2)}) collective-permute-start(bf16[1,256,256]{2,1,0:T(8,128)(2,1)S(1)} %fusion.168), channel_id=1, source_target_pairs={{0,1},{1,2},{2,3},{3,4},{4,5},{5,6},{6,7},{7,8},{8,9},{9,10},{10,1... | collective-permute-start | bytes 393224 | tf_op jit(solution)/shard_map/while/body/eval_jaxpr/ppermute | solution.py:14
  (20 other events, 88.4 us)
where the time goes:
time: 312 us; the launch traced here: 310 us
  waiting for transfers between devices  117 us (38%)
  matrix products  99.2 us (32%)
  starting transfers between devices  88.3 us (28%)
    dot_general x30, matrix products, solve(): jnp.einsum('pci,pik->pck', halfway.astype(jnp.bfloat16), factor, preferre...  86.7 us
    ppermute x30, waiting for transfers between devices, from_behind(): return lax.ppermute(value, axis, pairs)  83.4 us
    ppermute x15, starting transfers between devices, from_behind_2(): return lax.ppermute(array, axis, pairs)  56.7 us
    ppermute x15, waiting for transfers between devices, from_behind_2(): return lax.ppermute(array, axis, pairs)  34.1 us
    ppermute x30, starting transfers between devices, from_behind(): return lax.ppermute(value, axis, pairs)  31.6 us
  transfers between devices with their start and end apart: 45, of which 45 were waited for; matrix products, arithmetic and copies ran while one was open for 3% of the time, Pallas kernels for 0%

commit v1 on v0

v1 whole, which is shorter than its diff:
```python
import jax
import jax.numpy as jnp
from jax import lax
from jax.sharding import PartitionSpec as P

M = 768
KMAX = 256
FACE = 128
BF = jnp.bfloat16
F32 = jnp.float32
AXES = ("slab", "patch")


def dot(a, b):
    return lax.dot_general(a, b, (((1,), (0,)), ((), ())), preferred_element_type=F32)


def dot_t(a, b):
    return lax.dot_general(a, b, (((1,), (1,)), ((), ())), preferred_element_type=F32)


def t_dot(a, b):
    return lax.dot_general(a, b, (((0,), (0,)), ((), ())), preferred_element_type=F32)


def placement(limit):
    source = lax.broadcasted_iota(jnp.int32, (KMAX, KMAX), 0)
    target = lax.broadcasted_iota(jnp.int32, (KMAX, KMAX), 1)
    hit = (source == KMAX - limit + target) & (target < limit)
    return jnp.where(hit, 1.0, 0.0).astype(BF)


def prepare(residual, factor, down_map, up_map, limit):
    rows = jnp.concatenate([residual.astype(BF), down_map, up_map], axis=0)
    solved = dot(dot_t(rows, factor).astype(BF), factor).astype(BF)
    low = t_dot(factor[:, :FACE], factor)
    high = t_dot(factor[M - FACE :, M - FACE :], factor[M - FACE :])
    basis = jnp.concatenate([low, high], axis=0).astype(BF)
    columns = residual.shape[0]
    both = jnp.concatenate([solved[:columns], basis], axis=0)
    tail = dot(both[:, M - KMAX :], placement(limit)).astype(BF)
    return tail, both[:, :KMAX], solved[columns:]


def local_operators(residual, left, right, maps, limit):
    columns = residual.shape[0]
    right = dot_t(right, placement(limit)).astype(BF)
    middle = jnp.zeros((columns, M - 2 * KMAX), F32)
    shared = jnp.concatenate([left[:columns].astype(F32), middle, right[:columns].astype(F32)], axis=1)
    adjusted = residual - 0.5 * shared
    terms = dot_t(adjusted.astype(BF), maps)
    from_left = (0.5 * dot_t(left[columns:], maps[:, :KMAX])).astype(BF)
    from_right = (0.5 * dot_t(right[columns:], maps[:, M - KMAX :])).astype(BF)

    def stack(inputs, outputs, own):
        return jnp.concatenate([from_left[inputs, outputs], -own.T, from_right[inputs, outputs]], axis=0)

    down, up = slice(0, FACE), slice(FACE, 2 * FACE)
    down_down = stack(down, down, maps[:FACE, :FACE])
    down_up = stack(down, up, maps[FACE:, :FACE])
    up_up = stack(up, up, maps[FACE:, M - FACE :])
    return adjusted, right, terms[:, :FACE], terms[:, FACE:], down_down, down_up, up_up


def finish(adjusted, left, right, down, up, factor):
    columns = adjusted.shape[0]

    def side(at, basis):
        part = slice(at * FACE, (at + 1) * FACE)
        return 0.5 * dot(jnp.concatenate([down[:, part], up[:, part]], axis=1), basis)

    own = slice(FACE, 2 * FACE)
    low = side(0, left[columns:])
    high = side(2, right[columns:])
    low = low - jnp.pad(down[:, own].astype(F32), ((0, 0), (0, KMAX - FACE)))
    high = high - jnp.pad(up[:, own].astype(F32), ((0, 0), (KMAX - FACE, 0)))
    middle = jnp.zeros((columns, M - 2 * KMAX), F32)
    adjusted = adjusted + jnp.concatenate([low, middle, high], axis=1)
    return dot(dot_t(adjusted.astype(BF), factor).astype(BF), factor)


def on_device(right_side, inverse_factor, forward_trace, backward_trace, margin):
    slabs = lax.axis_size("slab")
    patches = lax.axis_size("patch")
    chips = slabs // 2

    def place(slab, patch):
        return slab * patches + patch % patches

    everywhere = [(slab, patch) for slab in range(slabs) for patch in range(patches)]

    def send(value, pairs):
        return lax.ppermute(value, AXES, pairs)

    def swap(value):
        return send(value, [(place(s, q), place(s ^ 1, q)) for s, q in everywhere])

    def neighbours(to_next, to_previous):
        left = send(to_next, [(place(s, q), place(s, q + 1)) for s, q in everywhere])
        right = send(to_previous, [(place(s, q), place(s, q - 1)) for s, q in everywhere])
        return left, right

    def hop(value, chip, step):
        even, odd, shift = 2 * chip, 2 * chip + 1, 2 * step
        found = []
        for by in (2, 1):
            pairs = [(place(even, q), place(even + shift, q + by)) for q in range(patches)]
            pairs += [(place(odd, q), place(odd + shift, q - by)) for q in range(patches)]
            found.append(send(value, pairs))
        found.append(send(value, [(place(even, q), place(even + shift, q)) for q in range(patches)]))
        return jnp.concatenate(found, axis=1)

    first = lax.axis_index("slab") % 2 == 0

    def pick(on_first, on_second):
        return jnp.where(first, on_first, on_second)

    residual = right_side[0, 0]
    factor = inverse_factor[0, 0]
    limit = margin[0, 0]
    columns = residual.shape[0]

    def block(array, at):
        return array[at * FACE : (at + 1) * FACE]

    tail, head, maps = prepare(residual, factor, forward_trace[0, 0], backward_trace[0, 0], limit)
    left, right = neighbours(tail, head)
    adjusted, right, down0, up0, down_down, down_up, up_up = local_operators(
        residual, left, right, maps, limit
    )
    down0_half = down0.astype(BF)
    inner = pick(down_down, up_up)
    outer = pick(up_up, down_down)
    message = jnp.concatenate([down0_half, inner], axis=0)
    got_left, got_right = neighbours(message, message)
    swapped = swap(jnp.concatenate([down0_half, outer], axis=0))
    outer = swapped[columns:]
    inner3 = [got_left[columns:], inner, got_right[columns:]]
    down3 = jnp.concatenate([got_left[:columns], down0_half, got_right[:columns]], axis=1)
    products = [dot(inner3[m], block(outer, m)) for m in range(3)]
    pair = [sum(block(products[m], at - m) for m in range(3) if 0 <= at - m < 3) for at in range(5)]
    start = swapped[:columns].astype(F32) + dot(down3, outer)
    low_blocks = jnp.concatenate([pair[0], pair[1], pair[2]], axis=0).astype(BF)
    high_blocks = jnp.concatenate([pair[4], pair[3], pair[2]], axis=0).astype(BF)
    kept = pick(low_blocks, high_blocks)
    got = swap(pick(high_blocks, low_blocks))
    forward_pair = pick(kept, got)
    backward_pair = pick(got, kept)

    def sweep(base, operator, order, step):
        arrived = jnp.zeros((columns, 3 * FACE), BF)
        for position, chip in enumerate(order):
            part = base if position == 0 else base + dot(arrived, operator)
            total = (part + swap(part)).astype(BF)
            arrived = arrived + hop(total, chip, step)
        other = swap(arrived)
        low, high = pick(arrived, other), pick(other, arrived)
        return jnp.concatenate([low, high[:, FACE : 2 * FACE], high[:, :FACE]], axis=1)

    def between(base3, faces5):
        found = []
        for m in range(3):
            part = slice(m * FACE, (m + 1) * FACE)
            reach = slice(m * FACE, (m + 3) * FACE)
            found.append(base3[:, part].astype(F32) + dot(faces5[:, reach], inner3[m]))
        return jnp.concatenate(found, axis=1).astype(BF)

    middle3 = slice(FACE, 4 * FACE)
    base = pick(start, jnp.zeros_like(start))
    down5 = sweep(base, forward_pair, range(chips - 1), 1)
    down = pick(down5[:, middle3], swap(between(down3, down5)))
    up0 = up0 + dot(down, down_up)
    up0_half = up0.astype(BF)
    up_left, up_right = neighbours(up0_half, up0_half)
    up3 = jnp.concatenate([up_left, up0_half, up_right], axis=1)
    base = pick(up0, dot(up3, outer))
    up5 = sweep(base, backward_pair, range(chips - 1, 0, -1), -1)
    up = pick(swap(between(up3, up5)), up5[:, middle3])
    return finish(adjusted, left, right, down, up, factor)[None, None]


def solution(mesh):
    placed = (
        P("slab", "patch", None, None),
        P("slab", "patch", None, None),
        P("slab", "patch", None, None),
        P("slab", "patch", None, None),
        P("slab", "patch"),
    )
    return jax.shard_map(
        on_device,
        mesh=mesh,
        in_specs=placed,
        out_specs=P("slab", "patch", None, None),
        check_vma=False,
    )
```

time: 312 us -> 132 us (0.42)
  matrix products: 99.2 us -> 13.8 us
  waiting for transfers between devices: 117 us -> 64.4 us
  starting transfers between devices: 88.3 us -> 46.7 us
    dot_general x83 -> x27, matrix products: 99.2 us -> 13.8 us  [the longest x21 8.85 us: dot(): lax.dot_general(a, b, (((1,), (0,)), ((), ())), preferred_element_type=F32)]
    ppermute x45 -> x36, waiting for transfers between devices: 117 us -> 64.4 us  [send(): return lax.ppermute(value, AXES, pairs)]
    ppermute x45 -> x36, starting transfers between devices: 88.3 us -> 46.7 us  [send(): return lax.ppermute(value, AXES, pairs)]
  transfers between devices with their start and end apart: 45 -> 36, of which waited for: 45 -> 19; matrix products, arithmetic and copies ran while one was open for 3% -> 2% of each run, Pallas kernels for 0% -> 0%
where the time goes in v1:
time: 132 us; the launch traced here: 131 us
  waiting for transfers between devices  64.4 us (49%)
  starting transfers between devices  46.7 us (35%)
  matrix products  13.8 us (10%)
  local copies, waits for them, and re-layouts  2.77 us (2%)
  other arithmetic  2.16 us (2%)
  between operations  1.43 us (1%)
    ppermute x36, waiting for transfers between devices, send(): return lax.ppermute(value, AXES, pairs)  64.4 us
    ppermute x36, starting transfers between devices, send(): return lax.ppermute(value, AXES, pairs)  46.7 us
    dot_general x21, matrix products, dot(): lax.dot_general(a, b, (((1,), (0,)), ((), ())), preferred_element_type=F32)  8.85 us
    dot_general x2, matrix products, t_dot(): lax.dot_general(a, b, (((0,), (0,)), ((), ())), preferred_element_type=F32)  3 us
  transfers between devices with their start and end apart: 36, of which 19 were waited for; matrix products, arithmetic and copies ran while one was open for 2% of the time, Pallas kernels for 0%

profile of v1, /device:TPU:1, one launch (start us, length us, event | category | flops | bytes accessed | tf_op | source)
XLA Modules:
  0.0 131.2 jit_solution(9649836038028548316)
XLA Ops:
  0.0 1.3 convolution_convert_fusion.5
  1.3 1.7 %convolution_convert_fusion.6 = bf16[128,768]{1,0:T(8,128)(2,1)S(1)} fusion(bf16[768,768]{1,0:T(8,128)(2,1)} %bitcast.50), kind=kOutput, calls=%fused_computation.7 | convolution fusion | flops 151093248 | bytes 1572864 | tf_op jit(solution)/shard_map/dot_general | solution.py:23
  4.0 0.8 copy.8
  4.8 0.8 copy.7
  5.6 2.5 %convolution_convert_fusion = bf16[512,768]{1,0:T(8,128)(2,1)S(1)} fusion(bf16[128,768]{0,1:T(8,128)(2,1)} %bitcast.51, bf16[128,768]{0,1:T(8,128)(2,1)} %bitcast.52, bf16[256,768]{0,1:T(8,128)(2,1)S(1)} %bitcast_convert_fusion, bf16[1,1,768,768]{3,2,1,0:T(8,128)(2,1)S(1)} %copy-done), kind=kOutput, calls=%fused_computation | convolution fusion | flops 1211105280 | bytes 2752512 | tf_op jit(solution)/shard_map/dot_general | solution.py:15
  8.2 0.7 pad_maximum_fusion
  9.0 8.9 %collective-permute-start.1 = (bf16[512,256]{1,0:T(8,128)(2,1)}, bf16[512,256]{1,0:T(8,128)(2,1)}, u32[]{:S(2)}, u32[]{:S(2)}) collective-permute-start(bf16[512,256]{1,0:T(8,128)(2,1)} %pad_maximum_fusion), channel_id=1, source_target_pairs={{0,31},{1,0},{2,1},{3,2},{4,3},{5,4},{6,5},{7,6},{8,7},{9,8},{10,9... | collective-permute-start | bytes 786440 | tf_op jit(solution)/shard_map/ppermute | solution.py:93
  18.5 1.0 convolution_convert_fusion.4
  19.5 3.6 %collective-permute-done.1 = bf16[512,256]{1,0:T(8,128)(2,1)} collective-permute-done((bf16[512,256]{1,0:T(8,128)(2,1)}, bf16[512,256]{1,0:T(8,128)(2,1)}, u32[]{:S(2)}, u32[]{:S(2)}) %collective-permute-start.1) | collective-permute-done | bytes 262176 | tf_op jit(solution)/shard_map/ppermute | solution.py:93
  23.1 1.3 %convolution_convert_fusion.3 = bf16[512,256]{0,1:T(8,128)(2,1)S(1)} fusion(bf16[512,256]{1,0:T(8,128)(2,1)} %collective-permute-done.1, s32[256]{0:T(256)S(1)} %iota_add_fusion, pred[256]{0:T(512)(128)(4,1)S(1)} %iota_compare_fusion.1), kind=kOutput, calls=%fused_computation.4 | convolution fusion | flops 67502080 | bytes 525568 | tf_op jit(solution)/shard_map/dot_general | solution.py:19
  24.7 5.2 %collective-permute-done = bf16[512,256]{0,1:T(8,128)(2,1)S(1)} collective-permute-done((bf16[512,256]{0,1:T(8,128)(2,1)}, bf16[512,256]{0,1:T(8,128)(2,1)S(1)}, u32[]{:S(2)}, u32[]{:S(2)}) %collective-permute-start) | collective-permute-done | bytes 262176 | tf_op jit(solution)/shard_map/ppermute | solution.py:93
  29.9 0.7 slice_convert_fusion.2
  31.4 1.9 %collective-permute-start.2 = (bf16[640,128]{0,1:T(8,128)(2,1)S(1)}, bf16[640,128]{0,1:T(8,128)(2,1)S(1)}, u32[]{:S(2)}, u32[]{:S(2)}) collective-permute-start(bf16[640,128]{0,1:T(8,128)(2,1)S(1)} %get-tuple-element.37), channel_id=1, source_target_pairs={{0,32},{1,33},{2,34},{3,35},{4,36},{5,37},{6,38},{7,39},{8,40},{9,... | collective-permute-start | bytes 491528 | tf_op jit(solution)/shard_map/ppermute | solution.py:93
  33.3 5.0 %collective-permute-start.4 = (bf16[640,128]{0,1:T(8,128)(2,1)S(1)}, bf16[640,128]{0,1:T(8,128)(2,1)S(1)}, u32[]{:S(2)}, u32[]{:S(2)}) collective-permute-start(bf16[640,128]{0,1:T(8,128)(2,1)S(1)} %get-tuple-element.38), channel_id=1, source_target_pairs={{0,31},{1,0},{2,1},{3,2},{4,3},{5,4},{6,5},{7,6},{8,7},{9,8},{10,9... | collective-permute-start | bytes 491528 | tf_op jit(solution)/shard_map/ppermute | solution.py:93
  39.0 2.9 %collective-permute-done.4 = bf16[640,128]{0,1:T(8,128)(2,1)S(1)} collective-permute-done((bf16[640,128]{0,1:T(8,128)(2,1)S(1)}, bf16[640,128]{0,1:T(8,128)(2,1)S(1)}, u32[]{:S(2)}, u32[]{:S(2)}) %collective-permute-start.4) | collective-permute-done | bytes 163872 | tf_op jit(solution)/shard_map/ppermute | solution.py:93
  42.3 0.9 collective-permute-start.5
  43.4 0.8 collective-permute-done.5
  44.2 4.8 %collective-permute-start.6 = (bf16[256,128]{0,1:T(8,128)(2,1)S(1)}, bf16[256,128]{0,1:T(8,128)(2,1)S(1)}, u32[]{:S(2)}, u32[]{:S(2)}) collective-permute-start(bf16[256,128]{0,1:T(8,128)(2,1)S(1)} %add_convert_fusion.10), channel_id=1, source_target_pairs={{0,66},{1,67},{2,68},{3,69},{4,70},{5,71},{6,72},{7,73},{8,74},{9,... | collective-permute-start | bytes 196616 | tf_op jit(solution)/shard_map/ppermute | solution.py:93
  49.1 5.2 %collective-permute-start.7 = (bf16[256,128]{0,1:T(8,128)(2,1)S(1)}, bf16[256,128]{0,1:T(8,128)(2,1)S(1)}, u32[]{:S(2)}, u32[]{:S(2)}) collective-permute-start(bf16[256,128]{0,1:T(8,128)(2,1)S(1)} %add_convert_fusion.10), channel_id=1, source_target_pairs={{0,65},{1,66},{2,67},{3,68},{4,69},{5,70},{6,71},{7,72},{8,73},{9,... | collective-permute-start | bytes 196616 | tf_op jit(solution)/shard_map/ppermute | solution.py:93
  56.0 1.3 %collective-permute-done.10 = f32[256,128]{0,1:T(8,128)S(1)} collective-permute-done((f32[256,128]{0,1:T(8,128)S(1)}, f32[256,128]{0,1:T(8,128)S(1)}, u32[]{:S(2)}, u32[]{:S(2)}) %collective-permute-start.10) | collective-permute-done | bytes 131104 | tf_op jit(solution)/shard_map/ppermute | solution.py:93
  57.3 0.7 collective-permute-start.13
  58.0 0.7 collective-permute-start.12
  59.8 1.2 collective-permute-done.14
  61.0 0.7 collective-permute-start.17
  61.7 0.7 collective-permute-start.16
  62.4 0.7 collective-permute-start.15
  63.4 1.3 collective-permute-done.18
  65.6 1.3 collective-permute-done.19
  67.2 2.5 %collective-permute-start.21 = (bf16[256,128]{0,1:T(8,128)(2,1)S(1)}, bf16[256,128]{0,1:T(8,128)(2,1)S(1)}, u32[]{:S(2)}, u32[]{:S(2)}) collective-permute-start(bf16[256,128]{0,1:T(8,128)(2,1)S(1)} %get-tuple-element.39), channel_id=1, source_target_pairs={{0,31},{1,0},{2,1},{3,2},{4,3},{5,4},{6,5},{7,6},{8,7},{9,8},{10,9... | collective-permute-start | bytes 196616 | tf_op jit(solution)/shard_map/ppermute | solution.py:93
  69.7 2.1 %collective-permute-done.21 = bf16[256,128]{0,1:T(8,128)(2,1)S(1)} collective-permute-done((bf16[256,128]{0,1:T(8,128)(2,1)S(1)}, bf16[256,128]{0,1:T(8,128)(2,1)S(1)}, u32[]{:S(2)}, u32[]{:S(2)}) %collective-permute-start.21) | collective-permute-done | bytes 65568 | tf_op jit(solution)/shard_map/ppermute | solution.py:93
  71.8 4.2 %collective-permute-done.20 = bf16[256,128]{0,1:T(8,128)(2,1)S(1)} collective-permute-done((bf16[256,128]{0,1:T(8,128)(2,1)S(1)}, bf16[256,128]{0,1:T(8,128)(2,1)S(1)}, u32[]{:S(2)}, u32[]{:S(2)}) %collective-permute-start.20) | collective-permute-done | bytes 65568 | tf_op jit(solution)/shard_map/ppermute | solution.py:93
  76.2 1.9 %collective-permute-start.22 = (f32[256,128]{0,1:T(8,128)S(1)}, f32[256,128]{0,1:T(8,128)S(1)}, u32[]{:S(2)}, u32[]{:S(2)}) collective-permute-start(f32[256,128]{0,1:T(8,128)S(1)} %convolution_select_fusion), channel_id=1, source_target_pairs={{0,32},{1,33},{2,34},{3,35},{4,36},{5,37},{6,38},{7,39},{8,40},{9,... | collective-permute-start | bytes 393224 | tf_op jit(solution)/shard_map/ppermute | solution.py:93
  78.1 1.0 collective-permute-done.22
  79.1 0.7 collective-permute-start.23
  79.8 0.7 collective-permute-start.24
  80.5 0.7 collective-permute-start.25
  81.9 1.0 collective-permute-done.26
  82.9 0.7 collective-permute-start.29
  84.2 0.7 collective-permute-start.27
  85.6 1.0 collective-permute-done.30
  87.3 1.3 collective-permute-start.32
  88.6 1.3 collective-permute-start.31
  89.9 32.0 %collective-permute-done.32 = bf16[256,128]{0,1:T(8,128)(2,1)S(1)} collective-permute-done((bf16[256,128]{0,1:T(8,128)(2,1)S(1)}, bf16[256,128]{0,1:T(8,128)(2,1)S(1)}, u32[]{:S(2)}, u32[]{:S(2)}) %collective-permute-start.32) | collective-permute-done | bytes 65568 | tf_op jit(solution)/shard_map/ppermute | solution.py:93
  121.9 2.2 %collective-permute-done.31 = bf16[256,128]{0,1:T(8,128)(2,1)S(1)} collective-permute-done((bf16[256,128]{0,1:T(8,128)(2,1)S(1)}, bf16[256,128]{0,1:T(8,128)(2,1)S(1)}, u32[]{:S(2)}, u32[]{:S(2)}) %collective-permute-start.31) | collective-permute-done | bytes 65568 | tf_op jit(solution)/shard_map/ppermute | solution.py:93
  124.1 1.4 %collective-permute-start.34 = (bf16[256,384]{0,1:T(8,128)(2,1)S(1)}, bf16[256,384]{0,1:T(8,128)(2,1)S(1)}, u32[]{:S(2)}, u32[]{:S(2)}) collective-permute-start(bf16[256,384]{0,1:T(8,128)(2,1)S(1)} %maximum_add_fusion.3), channel_id=1, source_target_pairs={{0,32},{1,33},{2,34},{3,35},{4,36},{5,37},{6,38},{7,39},{8,40},{9,... | collective-permute-start | bytes 589832 | tf_op jit(solution)/shard_map/ppermute | solution.py:93
  125.5 1.1 collective-permute-done.34
  127.7 1.0 collective-permute-done.35
  129.2 1.9 %convolution_bitcast_fusion = f32[1,1,256,768]{3,2,1,0:T(8,128)} fusion(f32[1,1,256,768]{2,3,1,0:T(8,128)S(1)} %copy.10, f32[1,1,256,256]{2,3,1,0:T(8,128)S(1)} %get-tuple-element.18, f32[1,1,256,256]{2,3,1,0:T(8,128)S(1)} %copy-done.2, f32[1,1,256,256]{2,3,1,0:T(8,128)S(1)} %fusion.1, f32[1,1,256,256]{2,3,1,0:T(8,128)S(1)} %fusion.3, ...), kind=kOutput, calls=%fused_computation.2 | convolution fusion | flops 605749248 | bytes 3804160 | tf_op jit(solution)/shard_map/dot_general | solution.py:15
  (110 shorter events, 12.2 us)
Async XLA Ops:
  0.0 3.0 %copy-start.1 = (f32[1,1,256,768]{3,2,1,0:T(8,128)S(1)}, f32[1,1,256,768]{3,2,1,0:T(8,128)}, u32[]{:S(2)}) copy-start(f32[1,1,256,768]{3,2,1,0:T(8,128)} %param.5) | copy-start | bytes 2359300
  3.0 0.9 copy-start.3
  3.0 1.7 %copy-start.4 = (bf16[1,1,128,768]{3,2,1,0:T(8,128)(2,1)S(1)}, bf16[1,1,128,768]{3,2,1,0:T(8,128)(2,1)}, u32[]{:S(2)}) copy-start(bf16[1,1,128,768]{3,2,1,0:T(8,128)(2,1)} %param.7) | copy-start | bytes 589828
  4.0 1.7 %copy-start = (bf16[1,1,768,768]{3,2,1,0:T(8,128)(2,1)S(1)}, bf16[1,1,768,768]{3,2,1,0:T(8,128)(2,1)}, u32[]{:S(2)}) copy-start(bf16[1,1,768,768]{3,2,1,0:T(8,128)(2,1)} %param.6) | copy-start | bytes 3538948
  9.0 14.1 %collective-permute-start.1 = (bf16[512,256]{1,0:T(8,128)(2,1)}, bf16[512,256]{1,0:T(8,128)(2,1)}, u32[]{:S(2)}, u32[]{:S(2)}) collective-permute-start(bf16[512,256]{1,0:T(8,128)(2,1)} %pad_maximum_fusion), channel_id=1, source_target_pairs={{0,31},{1,0},{2,1},{3,2},{4,3},{5,4},{6,5},{7,6},{8,7},{9,8},{10,9... | collective-permute-start | bytes 786440 | tf_op jit(solution)/shard_map/ppermute | solution.py:93
  19.5 10.4 %collective-permute-start = (bf16[512,256]{0,1:T(8,128)(2,1)}, bf16[512,256]{0,1:T(8,128)(2,1)S(1)}, u32[]{:S(2)}, u32[]{:S(2)}) collective-permute-start(bf16[512,256]{0,1:T(8,128)(2,1)} %convolution_convert_fusion.4), channel_id=1, source_target_pairs={{0,1},{1,2},{2,3},{3,4},{4,5},{5,6},{6,7},{7,8},{8,9},{9,10},{10,1... | collective-permute-start | bytes 786440 | tf_op jit(solution)/shard_map/ppermute | solution.py:93
  31.3 7.6 %collective-permute-start.3 = (bf16[640,128]{0,1:T(8,128)(2,1)S(1)}, bf16[640,128]{0,1:T(8,128)(2,1)S(1)}, u32[]{:S(2)}, u32[]{:S(2)}) collective-permute-start(bf16[640,128]{0,1:T(8,128)(2,1)S(1)} %get-tuple-element.38), channel_id=1, source_target_pairs={{0,1},{1,2},{2,3},{3,4},{4,5},{5,6},{6,7},{7,8},{8,9},{9,10},{10,1... | collective-permute-start | bytes 491528 | tf_op jit(solution)/shard_map/ppermute | solution.py:93
  31.4 7.5 %collective-permute-start.2 = (bf16[640,128]{0,1:T(8,128)(2,1)S(1)}, bf16[640,128]{0,1:T(8,128)(2,1)S(1)}, u32[]{:S(2)}, u32[]{:S(2)}) collective-permute-start(bf16[640,128]{0,1:T(8,128)(2,1)S(1)} %get-tuple-element.37), channel_id=1, source_target_pairs={{0,32},{1,33},{2,34},{3,35},{4,36},{5,37},{6,38},{7,39},{8,40},{9,... | collective-permute-start | bytes 491528 | tf_op jit(solution)/shard_map/ppermute | solution.py:93
  33.3 8.6 %collective-permute-start.4 = (bf16[640,128]{0,1:T(8,128)(2,1)S(1)}, bf16[640,128]{0,1:T(8,128)(2,1)S(1)}, u32[]{:S(2)}, u32[]{:S(2)}) collective-permute-start(bf16[640,128]{0,1:T(8,128)(2,1)S(1)} %get-tuple-element.38), channel_id=1, source_target_pairs={{0,31},{1,0},{2,1},{3,2},{4,3},{5,4},{6,5},{7,6},{8,7},{9,8},{10,9... | collective-permute-start | bytes 491528 | tf_op jit(solution)/shard_map/ppermute | solution.py:93
  42.3 1.9 %collective-permute-start.5 = (f32[256,128]{0,1:T(8,128)S(1)}, f32[256,128]{0,1:T(8,128)S(1)}, u32[]{:S(2)}, u32[]{:S(2)}) collective-permute-start(f32[256,128]{0,1:T(8,128)S(1)} %add_select_fusion), channel_id=1, source_target_pairs={{0,32},{1,33},{2,34},{3,35},{4,36},{5,37},{6,38},{7,39},{8,40},{9,... | collective-permute-start | bytes 393224 | tf_op jit(solution)/shard_map/ppermute | solution.py:93
  44.2 10.8 %collective-permute-start.6 = (bf16[256,128]{0,1:T(8,128)(2,1)S(1)}, bf16[256,128]{0,1:T(8,128)(2,1)S(1)}, u32[]{:S(2)}, u32[]{:S(2)}) collective-permute-start(bf16[256,128]{0,1:T(8,128)(2,1)S(1)} %add_convert_fusion.10), channel_id=1, source_target_pairs={{0,66},{1,67},{2,68},{3,69},{4,70},{5,71},{6,72},{7,73},{8,74},{9,... | collective-permute-start | bytes 196616 | tf_op jit(solution)/shard_map/ppermute | solution.py:93
  49.0 6.7 %collective-permute-start.9 = (bf16[384,128]{0,1:T(8,128)(2,1)S(1)}, bf16[384,128]{0,1:T(8,128)(2,1)S(1)}, u32[]{:S(2)}, u32[]{:S(2)}) collective-permute-start(bf16[384,128]{0,1:T(8,128)(2,1)S(1)} %broadcast_select_fusion.8), channel_id=1, source_target_pairs={{0,32},{1,33},{2,34},{3,35},{4,36},{5,37},{6,38},{7,39},{8,40},{9,... | collective-permute-start | bytes 294920 | tf_op jit(solution)/shard_map/ppermute | solution.py:93
  49.1 6.5 %collective-permute-start.7 = (bf16[256,128]{0,1:T(8,128)(2,1)S(1)}, bf16[256,128]{0,1:T(8,128)(2,1)S(1)}, u32[]{:S(2)}, u32[]{:S(2)}) collective-permute-start(bf16[256,128]{0,1:T(8,128)(2,1)S(1)} %add_convert_fusion.10), channel_id=1, source_target_pairs={{0,65},{1,66},{2,67},{3,68},{4,69},{5,70},{6,71},{7,72},{8,73},{9,... | collective-permute-start | bytes 196616 | tf_op jit(solution)/shard_map/ppermute | solution.py:93
  54.3 1.3 %collective-permute-start.8 = (bf16[256,128]{0,1:T(8,128)(2,1)S(1)}, bf16[256,128]{0,1:T(8,128)(2,1)S(1)}, u32[]{:S(2)}, u32[]{:S(2)}) collective-permute-start(bf16[256,128]{0,1:T(8,128)(2,1)S(1)} %add_convert_fusion.10), channel_id=1, source_target_pairs={{0,64},{1,65},{2,66},{3,67},{4,68},{5,69},{6,70},{7,71},{8,72},{9,... | collective-permute-start | bytes 196616 | tf_op jit(solution)/shard_map/ppermute | solution.py:93
  55.9 1.4 %collective-permute-start.10 = (f32[256,128]{0,1:T(8,128)S(1)}, f32[256,128]{0,1:T(8,128)S(1)}, u32[]{:S(2)}, u32[]{:S(2)}) collective-permute-start(f32[256,128]{0,1:T(8,128)S(1)} %convolution_add_fusion.5), channel_id=1, source_target_pairs={{0,32},{1,33},{2,34},{3,35},{4,36},{5,37},{6,38},{7,39},{8,40},{9,... | collective-permute-start | bytes 393224 | tf_op jit(solution)/shard_map/ppermute | solution.py:93
  57.3 2.0 %collective-permute-start.13 = (bf16[256,128]{0,1:T(8,128)(2,1)S(1)}, bf16[256,128]{0,1:T(8,128)(2,1)S(1)}, u32[]{:S(2)}, u32[]{:S(2)}) collective-permute-start(bf16[256,128]{0,1:T(8,128)(2,1)S(1)} %add_convert_fusion.9), channel_id=1, source_target_pairs={{64,128},{65,129},{66,130},{67,131},{68,132},{69,133},{70,134},{71... | collective-permute-start | bytes 196616 | tf_op jit(solution)/shard_map/ppermute | solution.py:93
  58.0 1.4 %collective-permute-start.12 = (bf16[256,128]{0,1:T(8,128)(2,1)S(1)}, bf16[256,128]{0,1:T(8,128)(2,1)S(1)}, u32[]{:S(2)}, u32[]{:S(2)}) collective-permute-start(bf16[256,128]{0,1:T(8,128)(2,1)S(1)} %add_convert_fusion.9), channel_id=1, source_target_pairs={{64,129},{65,130},{66,131},{67,132},{68,133},{69,134},{70,135},{71... | collective-permute-start | bytes 196616 | tf_op jit(solution)/shard_map/ppermute | solution.py:93
  58.7 0.7 collective-permute-start.11
  59.6 1.4 %collective-permute-start.14 = (f32[256,128]{0,1:T(8,128)S(1)}, f32[256,128]{0,1:T(8,128)S(1)}, u32[]{:S(2)}, u32[]{:S(2)}) collective-permute-start(f32[256,128]{0,1:T(8,128)S(1)} %convolution_add_fusion.4), channel_id=1, source_target_pairs={{0,32},{1,33},{2,34},{3,35},{4,36},{5,37},{6,38},{7,39},{8,40},{9,... | collective-permute-start | bytes 393224 | tf_op jit(solution)/shard_map/ppermute | solution.py:93
  61.0 2.0 %collective-permute-start.17 = (bf16[256,128]{0,1:T(8,128)(2,1)S(1)}, bf16[256,128]{0,1:T(8,128)(2,1)S(1)}, u32[]{:S(2)}, u32[]{:S(2)}) collective-permute-start(bf16[256,128]{0,1:T(8,128)(2,1)S(1)} %add_convert_fusion.8), channel_id=1, source_target_pairs={{128,192},{129,193},{130,194},{131,195},{132,196},{133,197},{134,1... | collective-permute-start | bytes 196616 | tf_op jit(solution)/shard_map/ppermute | solution.py:93
  61.7 1.4 %collective-permute-start.16 = (bf16[256,128]{0,1:T(8,128)(2,1)S(1)}, bf16[256,128]{0,1:T(8,128)(2,1)S(1)}, u32[]{:S(2)}, u32[]{:S(2)}) collective-permute-start(bf16[256,128]{0,1:T(8,128)(2,1)S(1)} %add_convert_fusion.8), channel_id=1, source_target_pairs={{128,193},{129,194},{130,195},{131,196},{132,197},{133,198},{134,1... | collective-permute-start | bytes 196616 | tf_op jit(solution)/shard_map/ppermute | solution.py:93
  62.4 0.7 collective-permute-start.15
  63.2 1.5 %collective-permute-start.18 = (bf16[256,384]{0,1:T(8,128)(2,1)S(1)}, bf16[256,384]{0,1:T(8,128)(2,1)S(1)}, u32[]{:S(2)}, u32[]{:S(2)}) collective-permute-start(bf16[256,384]{0,1:T(8,128)(2,1)S(1)} %maximum_add_fusion.1), channel_id=1, source_target_pairs={{0,32},{1,33},{2,34},{3,35},{4,36},{5,37},{6,38},{7,39},{8,40},{9,... | collective-permute-start | bytes 589832 | tf_op jit(solution)/shard_map/ppermute | solution.py:93
  65.4 1.5 %collective-permute-start.19 = (bf16[256,384]{0,1:T(8,128)(2,1)S(1)}, bf16[256,384]{0,1:T(8,128)(2,1)S(1)}, u32[]{:S(2)}, u32[]{:S(2)}) collective-permute-start(bf16[256,384]{0,1:T(8,128)(2,1)S(1)} %pad_maximum_fusion.12), channel_id=1, source_target_pairs={{0,32},{1,33},{2,34},{3,35},{4,36},{5,37},{6,38},{7,39},{8,40},{9,... | collective-permute-start | bytes 589832 | tf_op jit(solution)/shard_map/ppermute | solution.py:93
  67.2 4.6 %collective-permute-start.21 = (bf16[256,128]{0,1:T(8,128)(2,1)S(1)}, bf16[256,128]{0,1:T(8,128)(2,1)S(1)}, u32[]{:S(2)}, u32[]{:S(2)}) collective-permute-start(bf16[256,128]{0,1:T(8,128)(2,1)S(1)} %get-tuple-element.39), channel_id=1, source_target_pairs={{0,31},{1,0},{2,1},{3,2},{4,3},{5,4},{6,5},{7,6},{8,7},{9,8},{10,9... | collective-permute-start | bytes 196616 | tf_op jit(solution)/shard_map/ppermute | solution.py:93
  69.6 6.4 %collective-permute-start.20 = (bf16[256,128]{0,1:T(8,128)(2,1)S(1)}, bf16[256,128]{0,1:T(8,128)(2,1)S(1)}, u32[]{:S(2)}, u32[]{:S(2)}) collective-permute-start(bf16[256,128]{0,1:T(8,128)(2,1)S(1)} %get-tuple-element.39), channel_id=1, source_target_pairs={{0,1},{1,2},{2,3},{3,4},{4,5},{5,6},{6,7},{7,8},{8,9},{9,10},{10,1... | collective-permute-start | bytes 196616 | tf_op jit(solution)/shard_map/ppermute | solution.py:93
  76.2 2.9 %collective-permute-start.22 = (f32[256,128]{0,1:T(8,128)S(1)}, f32[256,128]{0,1:T(8,128)S(1)}, u32[]{:S(2)}, u32[]{:S(2)}) collective-permute-start(f32[256,128]{0,1:T(8,128)S(1)} %convolution_select_fusion), channel_id=1, source_target_pairs={{0,32},{1,33},{2,34},{3,35},{4,36},{5,37},{6,38},{7,39},{8,40},{9,... | collective-permute-start | bytes 393224 | tf_op jit(solution)/shard_map/ppermute | solution.py:93
  79.1 2.0 %collective-permute-start.23 = (bf16[256,128]{0,1:T(8,128)(2,1)S(1)}, bf16[256,128]{0,1:T(8,128)(2,1)S(1)}, u32[]{:S(2)}, u32[]{:S(2)}) collective-permute-start(bf16[256,128]{0,1:T(8,128)(2,1)S(1)} %add_convert_fusion.5), channel_id=1, source_target_pairs={{192,130},{193,131},{194,132},{195,133},{196,134},{197,135},{198,1... | collective-permute-start | bytes 196616 | tf_op jit(solution)/shard_map/ppermute | solution.py:93
  79.8 1.4 %collective-permute-start.24 = (bf16[256,128]{0,1:T(8,128)(2,1)S(1)}, bf16[256,128]{0,1:T(8,128)(2,1)S(1)}, u32[]{:S(2)}, u32[]{:S(2)}) collective-permute-start(bf16[256,128]{0,1:T(8,128)(2,1)S(1)} %add_convert_fusion.5), channel_id=1, source_target_pairs={{192,129},{193,130},{194,131},{195,132},{196,133},{197,134},{198,1... | collective-permute-start | bytes 196616 | tf_op jit(solution)/shard_map/ppermute | solution.py:93
  80.5 0.7 collective-permute-start.25
  81.4 1.4 %collective-permute-start.26 = (f32[256,128]{0,1:T(8,128)S(1)}, f32[256,128]{0,1:T(8,128)S(1)}, u32[]{:S(2)}, u32[]{:S(2)}) collective-permute-start(f32[256,128]{0,1:T(8,128)S(1)} %convolution_add_fusion.1), channel_id=1, source_target_pairs={{0,32},{1,33},{2,34},{3,35},{4,36},{5,37},{6,38},{7,39},{8,40},{9,... | collective-permute-start | bytes 393224 | tf_op jit(solution)/shard_map/ppermute | solution.py:93
  82.9 2.0 %collective-permute-start.29 = (bf16[256,128]{0,1:T(8,128)(2,1)S(1)}, bf16[256,128]{0,1:T(8,128)(2,1)S(1)}, u32[]{:S(2)}, u32[]{:S(2)}) collective-permute-start(bf16[256,128]{0,1:T(8,128)(2,1)S(1)} %add_convert_fusion.4), channel_id=1, source_target_pairs={{128,64},{129,65},{130,66},{131,67},{132,68},{133,69},{134,70},{13... | collective-permute-start | bytes 196616 | tf_op jit(solution)/shard_map/ppermute | solution.py:93
  83.5 1.4 %collective-permute-start.28 = (bf16[256,128]{0,1:T(8,128)(2,1)S(1)}, bf16[256,128]{0,1:T(8,128)(2,1)S(1)}, u32[]{:S(2)}, u32[]{:S(2)}) collective-permute-start(bf16[256,128]{0,1:T(8,128)(2,1)S(1)} %add_convert_fusion.4), channel_id=1, source_target_pairs={{128,65},{129,66},{130,67},{131,68},{132,69},{133,70},{134,71},{13... | collective-permute-start | bytes 196616 | tf_op jit(solution)/shard_map/ppermute | solution.py:93
  84.2 0.7 collective-permute-start.27
  85.1 1.4 %collective-permute-start.30 = (f32[256,128]{0,1:T(8,128)S(1)}, f32[256,128]{0,1:T(8,128)S(1)}, u32[]{:S(2)}, u32[]{:S(2)}) collective-permute-start(f32[256,128]{0,1:T(8,128)S(1)} %convolution_add_fusion), channel_id=1, source_target_pairs={{0,32},{1,33},{2,34},{3,35},{4,36},{5,37},{6,38},{7,39},{8,40},{9,... | collective-permute-start | bytes 393224 | tf_op jit(solution)/shard_map/ppermute | solution.py:93
  86.6 3.3 %collective-permute-start.33 = (bf16[256,128]{0,1:T(8,128)(2,1)S(1)}, bf16[256,128]{0,1:T(8,128)(2,1)S(1)}, u32[]{:S(2)}, u32[]{:S(2)}) collective-permute-start(bf16[256,128]{0,1:T(8,128)(2,1)S(1)} %add_convert_fusion.3), channel_id=1, source_target_pairs={{64,0},{65,1},{66,2},{67,3},{68,4},{69,5},{70,6},{71,7},{72,8},{73... | collective-permute-start | bytes 196616 | tf_op jit(solution)/shard_map/ppermute | solution.py:93
  87.3 34.6 %collective-permute-start.32 = (bf16[256,128]{0,1:T(8,128)(2,1)S(1)}, bf16[256,128]{0,1:T(8,128)(2,1)S(1)}, u32[]{:S(2)}, u32[]{:S(2)}) collective-permute-start(bf16[256,128]{0,1:T(8,128)(2,1)S(1)} %add_convert_fusion.3), channel_id=1, source_target_pairs={{64,1},{65,2},{66,3},{67,4},{68,5},{69,6},{70,7},{71,8},{72,9},{73... | collective-permute-start | bytes 196616 | tf_op jit(solution)/shard_map/ppermute | solution.py:93
  88.6 35.5 %collective-permute-start.31 = (bf16[256,128]{0,1:T(8,128)(2,1)S(1)}, bf16[256,128]{0,1:T(8,128)(2,1)S(1)}, u32[]{:S(2)}, u32[]{:S(2)}) collective-permute-start(bf16[256,128]{0,1:T(8,128)(2,1)S(1)} %add_convert_fusion.3), channel_id=1, source_target_pairs={{64,2},{65,3},{66,4},{67,5},{68,6},{69,7},{70,8},{71,9},{72,10},{7... | collective-permute-start | bytes 196616 | tf_op jit(solution)/shard_map/ppermute | solution.py:93
  124.1 2.4 %collective-permute-start.34 = (bf16[256,384]{0,1:T(8,128)(2,1)S(1)}, bf16[256,384]{0,1:T(8,128)(2,1)S(1)}, u32[]{:S(2)}, u32[]{:S(2)}) collective-permute-start(bf16[256,384]{0,1:T(8,128)(2,1)S(1)} %maximum_add_fusion.3), channel_id=1, source_target_pairs={{0,32},{1,33},{2,34},{3,35},{4,36},{5,37},{6,38},{7,39},{8,40},{9,... | collective-permute-start | bytes 589832 | tf_op jit(solution)/shard_map/ppermute | solution.py:93
  127.2 1.5 %collective-permute-start.35 = (bf16[256,384]{0,1:T(8,128)(2,1)S(1)}, bf16[256,384]{0,1:T(8,128)(2,1)S(1)}, u32[]{:S(2)}, u32[]{:S(2)}) collective-permute-start(bf16[256,384]{0,1:T(8,128)(2,1)S(1)} %pad_maximum_fusion.13), channel_id=1, source_target_pairs={{0,32},{1,33},{2,34},{3,35},{4,36},{5,37},{6,38},{7,39},{8,40},{9,... | collective-permute-start | bytes 589832 | tf_op jit(solution)/shard_map/ppermute | solution.py:93
  127.7 1.5 %copy-start.2 = (f32[1,1,256,256]{2,3,1,0:T(8,128)S(1)}, f32[1,1,256,256]{2,3,1,0:T(8,128)}, u32[]{:S(2)}) copy-start(f32[1,1,256,256]{2,3,1,0:T(8,128)} %get-tuple-element.16) | copy-start | bytes 786436

commit v2 on v1

v2 whole, which is shorter than its diff:
```python
import jax
import jax.numpy as jnp
from jax import lax
from jax.experimental import pallas as pl
from jax.experimental.pallas import tpu as pltpu
from jax.sharding import PartitionSpec as P

M = 768
KMAX = 256
FACE = 128
BF = jnp.bfloat16
F32 = jnp.float32
AXES = ("slab", "patch")
VMEM = pl.BlockSpec(memory_space=pltpu.VMEM)
SMEM = pl.BlockSpec(memory_space=pltpu.SMEM)


def dot(a, b):
    return lax.dot_general(a, b, (((1,), (0,)), ((), ())), preferred_element_type=F32)


def dot_t(a, b):
    return lax.dot_general(a, b, (((1,), (1,)), ((), ())), preferred_element_type=F32)


def placement(limit):
    source = lax.broadcasted_iota(jnp.int32, (KMAX, KMAX), 0)
    target = lax.broadcasted_iota(jnp.int32, (KMAX, KMAX), 1)
    hit = (source == KMAX - limit + target) & (target < limit)
    return jnp.where(hit, 1.0, 0.0).astype(BF)


def halves(rows, factor):
    found = []
    for at in range(0, M, KMAX):
        end = at + KMAX
        found.append(dot_t(rows[:, :end], factor[at:end, :end]).astype(BF))
    return jnp.concatenate(found, axis=1)


def call(kernel, shapes, scalars, arrays, cost):
    return pl.pallas_call(
        kernel,
        out_shape=[jax.ShapeDtypeStruct(shape, kind) for shape, kind in shapes],
        in_specs=[SMEM] + [VMEM] * len(arrays),
        out_specs=[VMEM] * len(shapes),
        cost_estimate=pl.CostEstimate(flops=cost[0], bytes_accessed=cost[1], transcendentals=0),
        compiler_params=pltpu.CompilerParams(vmem_limit_bytes=40 << 20),
    )(scalars, *arrays)


def prepare_kernel(scalars, residual, factor_ref, down_map, up_map, tail, head, maps):
    factor = factor_ref[...]
    columns = residual.shape[0]
    rows = jnp.concatenate([residual[...].astype(BF), down_map[...], up_map[...]], axis=0)
    half = halves(rows, factor)
    last = M - KMAX
    first_block = dot(half, factor[:, :KMAX]).astype(BF)
    last_block = dot(half[:, last:], factor[last:, last:]).astype(BF)
    middle_block = dot(half[columns:, KMAX:], factor[KMAX:, KMAX:last]).astype(BF)
    low = factor[:, :FACE].T
    high = factor[M - FACE :, M - FACE :].T
    head[:columns] = first_block[:columns]
    head[columns : columns + FACE] = dot(low, factor[:, :KMAX]).astype(BF)
    head[columns + FACE :] = dot(high, factor[M - FACE :, :KMAX]).astype(BF)
    ends = jnp.concatenate(
        [
            last_block[:columns],
            dot(low[:, last:], factor[last:, last:]).astype(BF),
            dot(high, factor[M - FACE :, last:]).astype(BF),
        ],
        axis=0,
    )
    tail[...] = dot(ends, placement(scalars[1])).astype(BF)
    maps[:, :KMAX] = first_block[columns:]
    maps[:, KMAX:last] = middle_block
    maps[:, last:] = last_block[columns:]


def prepare(scalars, residual, factor, down_map, up_map):
    columns = residual.shape[0]
    reach = columns + 2 * FACE
    shapes = [((reach, KMAX), BF), ((reach, KMAX), BF), ((2 * FACE, M), BF)]
    return call(prepare_kernel, shapes, scalars, [residual, factor, down_map, up_map], (1 << 30, 3 << 20))


def operators_kernel(
    scalars, residual, left, right, maps_ref, adjusted, right_basis, message, outer, extra, up_out
):
    columns = residual.shape[0]
    maps = maps_ref[...]
    first = scalars[0] == 0
    placed = dot_t(right[...], placement(scalars[1])).astype(BF)
    right_basis[...] = placed[columns:]
    adjusted[...] = residual[...]
    adjusted[:, :KMAX] = residual[:, :KMAX] - 0.5 * left[:columns].astype(F32)
    adjusted[:, M - KMAX :] = residual[:, M - KMAX :] - 0.5 * placed[:columns].astype(F32)
    terms = dot_t(adjusted[...].astype(BF), maps)
    from_left = (0.5 * dot_t(left[columns:], maps[:, :KMAX])).astype(BF)
    from_right = (0.5 * dot_t(placed[columns:], maps[:, M - KMAX :])).astype(BF)

    def stack(inputs, outputs, own):
        turned = (-own.astype(F32)).T.astype(BF)
        return jnp.concatenate([from_left[inputs, outputs], turned, from_right[inputs, outputs]], axis=0)

    down, up = slice(0, FACE), slice(FACE, 2 * FACE)
    down_down = stack(down, down, maps[:FACE, :FACE])
    down_up = stack(down, up, maps[FACE:, :FACE])
    up_up = stack(up, up, maps[FACE:, M - FACE :])
    down0 = terms[:, :FACE].astype(BF)
    message[:columns] = down0
    message[columns:] = jnp.where(first, down_down, up_up)
    outer[:columns] = down0
    outer[columns:] = jnp.where(first, up_up, down_down)
    extra[:columns] = terms[:, FACE:].astype(BF)
    extra[columns:] = down_up
    up_out[...] = terms[:, FACE:]


def local_operators(scalars, residual, left, right, maps):
    columns = residual.shape[0]
    pack = ((columns + 3 * FACE, FACE), BF)
    shapes = [((columns, M), F32), ((2 * FACE, KMAX), BF), pack, pack, pack, ((columns, FACE), F32)]
    return call(operators_kernel, shapes, scalars, [residual, left, right, maps], (1 << 28, 3 << 20))


def five(first, mine, other):
    low, high = jnp.where(first, mine, other), jnp.where(first, other, mine)
    return jnp.concatenate([low, high[:, FACE : 2 * FACE], high[:, :FACE]], axis=1)


def between(base3, faces5, rows3):
    found = []
    for m in range(3):
        part = slice(m * FACE, (m + 1) * FACE)
        reach = slice(m * FACE, (m + 3) * FACE)
        found.append((base3[:, part].astype(F32) + dot(faces5[:, reach], rows3[m])).astype(BF))
    return jnp.concatenate(found, axis=1)


def finish_kernel(
    scalars, adjusted, left_basis, right_basis, down, mine, other, up3, rows_l, rows_o, rows_r, factor_ref, out
):
    first = scalars[0] == 0
    factor = factor_ref[...]
    faces5 = five(first, mine[...], other[...])
    inside = between(up3[...], faces5, [rows_l[...], rows_o[...], rows_r[...]])
    up = jnp.where(first, inside, faces5[:, FACE : 4 * FACE])

    def side(at, basis):
        part = slice(at * FACE, (at + 1) * FACE)
        return 0.5 * dot(jnp.concatenate([down[:, part], up[:, part]], axis=1), basis)

    own = slice(FACE, 2 * FACE)
    low = adjusted[:, :KMAX] + side(0, left_basis[...])
    high = adjusted[:, M - KMAX :] + side(2, right_basis[...])
    rows = jnp.concatenate(
        [
            (low[:, :FACE] - down[:, own].astype(F32)).astype(BF),
            low[:, FACE:].astype(BF),
            adjusted[:, KMAX : M - KMAX].astype(BF),
            high[:, : KMAX - FACE].astype(BF),
            (high[:, KMAX - FACE :] - up[:, own].astype(F32)).astype(BF),
        ],
        axis=1,
    )
    half = halves(rows, factor)
    for at in range(0, M, KMAX):
        out[:, at : at + KMAX] = dot(half[:, at:], factor[at:, at : at + KMAX])


def on_device(right_side, inverse_factor, forward_trace, backward_trace, margin):
    slabs = lax.axis_size("slab")
    patches = lax.axis_size("patch")
    chips = slabs // 2

    def place(slab, patch):
        return slab * patches + patch % patches

    everywhere = [(slab, patch) for slab in range(slabs) for patch in range(patches)]

    def send(value, pairs):
        return lax.ppermute(value, AXES, pairs)

    def swap(value):
        return send(value, [(place(s, q), place(s ^ 1, q)) for s, q in everywhere])

    def neighbours(to_next, to_previous):
        left = send(to_next, [(place(s, q), place(s, q + 1)) for s, q in everywhere])
        right = send(to_previous, [(place(s, q), place(s, q - 1)) for s, q in everywhere])
        return left, right

    def outward(value):
        return send(value, [(place(s, q), place(s, q + (1 if s % 2 == 0 else -1))) for s, q in everywhere])

    def hop(value, chip, step):
        even, odd, shift = 2 * chip, 2 * chip + 1, 2 * step
        found = []
        for by in (2, 1):
            pairs = [(place(even, q), place(even + shift, q + by)) for q in range(patches)]
            pairs += [(place(odd, q), place(odd + shift, q - by)) for q in range(patches)]
            found.append(send(value, pairs))
        found.append(send(value, [(place(even, q), place(even + shift, q)) for q in range(patches)]))
        return jnp.concatenate(found, axis=1)

    core = lax.axis_index("slab") % 2
    first = core == 0

    def pick(on_first, on_second):
        return jnp.where(first, on_first, on_second)

    residual = right_side[0, 0]
    factor = inverse_factor[0, 0]
    columns = residual.shape[0]
    scalars = jnp.stack([core.astype(jnp.int32), margin[0, 0]])

    def block(array, at):
        return array[at * FACE : (at + 1) * FACE]

    tail, head, maps = prepare(scalars, residual, factor, forward_trace[0, 0], backward_trace[0, 0])
    left, right = neighbours(tail, head)
    adjusted, right_basis, message, outer, extra, up0 = local_operators(scalars, residual, left, right, maps)
    from_left, from_right = neighbours(message, message)
    swapped = swap(outer)

    down3 = jnp.concatenate([from_left[:columns], message[:columns], from_right[:columns]], axis=1)
    start = swapped[:columns].astype(F32) + dot(down3, swapped[columns:])
    base = pick(start, jnp.zeros_like(start))
    total = (base + swap(base)).astype(BF)
    total, packs = lax.optimization_barrier((total, (from_left, message, from_right, extra)))

    arrived = hop(total, 0, 1)
    others = [swap(pack) for pack in packs]
    even3 = [pick(mine, other) for mine, other in zip(packs[:3], others[:3])]
    odd3 = [pick(other, mine) for mine, other in zip(packs[:3], others[:3])]
    odd_extra = pick(others[3], packs[3])
    down3 = jnp.concatenate([pack[:columns] for pack in even3], axis=1)
    down_rows = [pack[columns:] for pack in even3]
    up_rows = [pack[columns:] for pack in odd3]
    odd_down = pick(swapped[columns:], outer[columns:])
    even_up = pick(outer[columns:], swapped[columns:])

    def compose(rows3, last):
        products = [dot(rows3[m], block(last, m)) for m in range(3)]
        pair = [sum(block(products[m], at - m) for m in range(3) if 0 <= at - m < 3) for at in range(5)]
        return jnp.concatenate([pick(pair[0], pair[4]), pick(pair[1], pair[3]), pair[2]], axis=0).astype(BF)

    forward_pair = compose(down_rows, odd_down)
    backward_pair = compose(up_rows, even_up)

    def sweep(base, arrived, operator, order, step):
        for chip in order:
            part = base if arrived is None else base + dot(arrived, operator)
            total = (part + swap(part)).astype(BF)
            new = hop(total, chip, step)
            arrived = new if arrived is None else arrived + new
        return arrived

    arrived = sweep(base, arrived, forward_pair, range(1, chips - 1), 1)
    down5 = five(first, arrived, swap(arrived))
    inside = between(down3, down5, down_rows)
    outside = down5[:, FACE : 4 * FACE]
    down = pick(outside, inside)
    odd_up0 = (odd_extra[:columns].astype(F32) + dot(inside, odd_extra[columns:])).astype(BF)
    even_up0 = up0 + dot(outside, extra[columns:])
    beside = outward(odd_up0)
    pair = jnp.concatenate([beside, pick(odd_up0, jnp.zeros_like(odd_up0))], axis=1)
    turn = jnp.concatenate([pick(block(even_up, 0), block(even_up, 2)), block(even_up, 1)], axis=0)
    base = pick(even_up0, jnp.zeros_like(even_up0)) + dot(pair, turn)
    arrived = sweep(base, None, backward_pair, range(chips - 1, 0, -1), -1)
    beside_other = swap(beside)
    up3 = jnp.concatenate([pick(beside, beside_other), odd_up0, pick(beside_other, beside)], axis=1)
    out = call(
        finish_kernel,
        [((columns, M), F32)],
        scalars,
        [adjusted, left[columns:], right_basis, down, arrived, swap(arrived), up3, *up_rows, factor],
        (1 << 29, 4 << 20),
    )[0]
    return out[None, None]


def solution(mesh):
    placed = (
        P("slab", "patch", None, None),
        P("slab", "patch", None, None),
        P("slab", "patch", None, None),
        P("slab", "patch", None, None),
        P("slab", "patch"),
    )
    return jax.shard_map(
        on_device,
        mesh=mesh,
        in_specs=placed,
        out_specs=P("slab", "patch", None, None),
        check_vma=False,
    )
```

time: 132 us -> 119 us (0.902)
  matrix products: 13.8 us -> 3.06 us
  waiting for transfers between devices: 64.4 us -> 54.7 us
  Pallas kernels: 0 us -> 5.13 us
  starting transfers between devices: 46.7 us -> 49.6 us
  local copies, waits for them, and re-layouts: 2.77 us -> 4.4 us
  other arithmetic: 2.16 us -> 0.76 us
    ppermute x36 -> x37, waiting for transfers between devices: 64.4 us -> 54.7 us  [send(): return lax.ppermute(value, AXES, pairs)]
    dot_general x21 -> x17, matrix products: 8.85 us -> 3.06 us  [dot(): lax.dot_general(a, b, (((1,), (0,)), ((), ())), preferred_element_type=F32)]
    pallas_call x0 -> x3, Pallas kernels: none -> 5.13 us  [call(): pl.pallas_call(kernel, out_shape=[jax.ShapeDtypeStruct(shape, kind) for s...]
    dot_general x6 -> x0, matrix products: 4.97 us -> none  [the longest x2 3 us: t_dot(): lax.dot_general(a, b, (((0,), (0,)), ((), ())), preferred_element_type=F32)]
    ppermute x36 -> x37, starting transfers between devices: 46.7 us -> 49.6 us  [send(): return lax.ppermute(value, AXES, pairs)]
    unnamed x17 -> x14, local copies, waits for them, and re-layouts: 2.57 us -> 4.32 us
  transfers between devices with their start and end apart: 36 -> 37, of which waited for: 19 -> 15; matrix products, arithmetic and copies ran while one was open for 2% -> 2% of each run, Pallas kernels for 0% -> 0%
where the time goes in v2:
time: 119 us
  waiting for transfers between devices  54.7 us (46%)
  starting transfers between devices  49.6 us (42%)
  Pallas kernels  5.13 us (4%)
  local copies, waits for them, and re-layouts  4.4 us (4%)
  matrix products  3.06 us (3%)
  between operations  1.25 us (1%)
    ppermute x37, waiting for transfers between devices, send(): return lax.ppermute(value, AXES, pairs)  54.7 us
    ppermute x37, starting transfers between devices, send(): return lax.ppermute(value, AXES, pairs)  49.6 us
    pallas_call x3, Pallas kernels, call(): pl.pallas_call(kernel, out_shape=[jax.ShapeDtypeStruct(shape, kind) for s...  5.13 us
    unnamed x14, local copies, waits for them, and re-layouts  4.32 us
    dot_general x17, matrix products, dot(): lax.dot_general(a, b, (((1,), (0,)), ((), ())), preferred_element_type=F32)  3.06 us
  transfers between devices with their start and end apart: 37, of which 15 were waited for; matrix products, arithmetic and copies ran while one was open for 2% of the time, Pallas kernels for 0%

profile of v2, /device:TPU:1, one launch (start us, length us, event | category | flops | bytes accessed | tf_op | source)
XLA Modules:
  0.0 118.9 jit_solution(16841988598454727659)
XLA Ops:
  0.7 1.3 %copy-done = bf16[1,1,768,768]{3,2,1,0:T(8,128)(2,1)S(1)} copy-done((bf16[1,1,768,768]{3,2,1,0:T(8,128)(2,1)S(1)}, bf16[1,1,768,768]{3,2,1,0:T(8,128)(2,1)}, u32[]{:S(2)}) %copy-start) | copy-done | bytes 1179672
  2.0 1.1 copy-done.2
  3.1 0.9 copy-done.3
  4.1 0.9 copy-done.4
  5.0 1.8 %shard_map.55 = (bf16[512,256]{1,0:T(8,128)(2,1)S(1)}, bf16[512,256]{1,0:T(8,128)(2,1)S(1)}, bf16[256,768]{1,0:T(8,128)(2,1)S(1)}) custom-call(s32[2]{0:T(128)S(1)} %pad_add_fusion.scalars, f32[256,768]{1,0:T(8,128)S(1)} %bitcast.16, bf16[768,768]{1,0:T(8,128)(2,1)S(1)} %bitcast.14, bf16[128,768]{1,0:T(8,128)(2,1)S(1)} %bitcast.18, bf16[128,768]{1,0:T(8,128)(2,1)S(1)} %bitcast.19), custom_call_target="tpu_custom_call" | custom-call | flops 1073741824 | bytes 3145728 | tf_op jit(solution)/shard_map/pallas_call | solution.py:42
  6.8 2.2 %collective-permute-start = (bf16[512,256]{1,0:T(8,128)(2,1)S(1)}, bf16[512,256]{1,0:T(8,128)(2,1)S(1)}, u32[]{:S(2)}, u32[]{:S(2)}) collective-permute-start(bf16[512,256]{1,0:T(8,128)(2,1)S(1)} %get-tuple-element.19), channel_id=1, source_target_pairs={{0,1},{1,2},{2,3},{3,4},{4,5},{5,6},{6,7},{7,8},{8,9},{9,10},{10,1... | collective-permute-start | bytes 786440 | tf_op jit(solution)/shard_map/ppermute | solution.py:183
  9.0 6.8 %collective-permute-start.1 = (bf16[512,256]{1,0:T(8,128)(2,1)S(1)}, bf16[512,256]{1,0:T(8,128)(2,1)S(1)}, u32[]{:S(2)}, u32[]{:S(2)}) collective-permute-start(bf16[512,256]{1,0:T(8,128)(2,1)S(1)} %get-tuple-element.20), channel_id=1, source_target_pairs={{0,31},{1,0},{2,1},{3,2},{4,3},{5,4},{6,5},{7,6},{8,7},{9,8},{10,9... | collective-permute-start | bytes 786440 | tf_op jit(solution)/shard_map/ppermute | solution.py:183
  15.8 5.9 %collective-permute-done.left = bf16[512,256]{1,0:T(8,128)(2,1)S(1)} collective-permute-done((bf16[512,256]{1,0:T(8,128)(2,1)S(1)}, bf16[512,256]{1,0:T(8,128)(2,1)S(1)}, u32[]{:S(2)}, u32[]{:S(2)}) %collective-permute-start) | collective-permute-done | bytes 262176 | tf_op jit(solution)/shard_map/ppermute | solution.py:183
  21.7 1.0 shard_map.56
  22.8 4.6 %collective-permute-start.4 = (bf16[640,128]{1,0:T(8,128)(2,1)S(1)}, bf16[640,128]{1,0:T(8,128)(2,1)S(1)}, u32[]{:S(2)}, u32[]{:S(2)}) collective-permute-start(bf16[640,128]{1,0:T(8,128)(2,1)S(1)} %get-tuple-element.30), channel_id=1, source_target_pairs={{0,31},{1,0},{2,1},{3,2},{4,3},{5,4},{6,5},{7,6},{8,7},{9,8},{10,9... | collective-permute-start | bytes 491528 | tf_op jit(solution)/shard_map/ppermute | solution.py:183
  27.4 1.8 %collective-permute-start.2 = (bf16[640,128]{1,0:T(8,128)(2,1)S(1)}, bf16[640,128]{1,0:T(8,128)(2,1)S(1)}, u32[]{:S(2)}, u32[]{:S(2)}) collective-permute-start(bf16[640,128]{1,0:T(8,128)(2,1)S(1)} %get-tuple-element.24), channel_id=1, source_target_pairs={{0,32},{1,33},{2,34},{3,35},{4,36},{5,37},{6,38},{7,39},{8,40},{9,... | collective-permute-start | bytes 491528 | tf_op jit(solution)/shard_map/ppermute | solution.py:183
  29.7 5.2 %collective-permute-done.3 = bf16[640,128]{1,0:T(8,128)(2,1)S(1)} collective-permute-done((bf16[640,128]{1,0:T(8,128)(2,1)S(1)}, bf16[640,128]{1,0:T(8,128)(2,1)S(1)}, u32[]{:S(2)}, u32[]{:S(2)}) %collective-permute-start.3) | collective-permute-done | bytes 163872 | tf_op jit(solution)/shard_map/ppermute | solution.py:183
  35.1 3.1 %collective-permute-start.5 = (f32[256,128]{1,0:T(8,128)S(1)}, f32[256,128]{1,0:T(8,128)S(1)}, u32[]{:S(2)}, u32[]{:S(2)}) collective-permute-start(f32[256,128]{1,0:T(8,128)S(1)} %add_select_fusion), channel_id=1, source_target_pairs={{0,32},{1,33},{2,34},{3,35},{4,36},{5,37},{6,38},{7,39},{8,40},{9,... | collective-permute-start | bytes 393224 | tf_op jit(solution)/shard_map/ppermute | solution.py:183
  38.2 1.0 collective-permute-done.5
  39.2 1.3 %collective-permute-start.6 = (bf16[256,128]{1,0:T(8,128)(2,1)S(1)}, bf16[256,128]{1,0:T(8,128)(2,1)S(1)}, u32[]{:S(2)}, u32[]{:S(2)}) collective-permute-start(bf16[256,128]{1,0:T(8,128)(2,1)S(1)} %add_convert_fusion.9), channel_id=1, source_target_pairs={{0,66},{1,67},{2,68},{3,69},{4,70},{5,71},{6,72},{7,73},{8,74},{9,... | collective-permute-start | bytes 196616 | tf_op jit(solution)/shard_map/ppermute | solution.py:183
  40.5 0.7 collective-permute-start.8
  41.2 2.6 %collective-permute-start.7 = (bf16[256,128]{1,0:T(8,128)(2,1)S(1)}, bf16[256,128]{1,0:T(8,128)(2,1)S(1)}, u32[]{:S(2)}, u32[]{:S(2)}) collective-permute-start(bf16[256,128]{1,0:T(8,128)(2,1)S(1)} %add_convert_fusion.9), channel_id=1, source_target_pairs={{0,65},{1,66},{2,67},{3,68},{4,69},{5,70},{6,71},{7,72},{8,73},{9,... | collective-permute-start | bytes 196616 | tf_op jit(solution)/shard_map/ppermute | solution.py:183
  43.7 1.9 %collective-permute-start.21 = (bf16[640,128]{1,0:T(8,128)(2,1)S(1)}, bf16[640,128]{1,0:T(8,128)(2,1)S(1)}, u32[]{:S(2)}, u32[]{:S(2)}) collective-permute-start(bf16[640,128]{1,0:T(8,128)(2,1)S(1)} %get-tuple-element.32), channel_id=1, source_target_pairs={{0,32},{1,33},{2,34},{3,35},{4,36},{5,37},{6,38},{7,39},{8,40},{9,... | collective-permute-start | bytes 491528 | tf_op jit(solution)/shard_map/ppermute | solution.py:183
  46.2 1.3 %collective-permute-start.11 = (bf16[640,128]{1,0:T(8,128)(2,1)S(1)}, bf16[640,128]{1,0:T(8,128)(2,1)S(1)}, u32[]{:S(2)}, u32[]{:S(2)}) collective-permute-start(bf16[640,128]{1,0:T(8,128)(2,1)S(1)} %get-tuple-element.30), channel_id=1, source_target_pairs={{0,32},{1,33},{2,34},{3,35},{4,36},{5,37},{6,38},{7,39},{8,40},{9,... | collective-permute-start | bytes 491528 | tf_op jit(solution)/shard_map/ppermute | solution.py:183
  49.6 0.8 collective-permute-done.12
  50.4 0.7 collective-permute-start.15
  51.0 0.7 collective-permute-start.14
  51.7 0.7 collective-permute-start.13
  53.3 0.8 collective-permute-done.16
  54.1 0.7 collective-permute-start.19
  54.8 0.7 collective-permute-start.18
  55.5 0.7 collective-permute-start.17
  56.9 0.9 collective-permute-done.20
  58.7 4.8 %collective-permute-start.22 = (bf16[256,128]{1,0:T(8,128)(2,1)S(1)}, bf16[256,128]{1,0:T(8,128)(2,1)S(1)}, u32[]{:S(2)}, u32[]{:S(2)}) collective-permute-start(bf16[256,128]{1,0:T(8,128)(2,1)S(1)} %get-tuple-element.48), channel_id=1, source_target_pairs={{0,1},{1,2},{2,3},{3,4},{4,5},{5,6},{6,7},{7,8},{8,9},{9,10},{10,1... | collective-permute-start | bytes 196616 | tf_op jit(solution)/shard_map/ppermute | solution.py:183
  63.7 1.1 collective-permute-done.22
  65.0 2.2 %collective-permute-start.23 = (f32[256,128]{1,0:T(8,128)S(1)}, f32[256,128]{1,0:T(8,128)S(1)}, u32[]{:S(2)}, u32[]{:S(2)}) collective-permute-start(f32[256,128]{1,0:T(8,128)S(1)} %select_add_fusion), channel_id=1, source_target_pairs={{0,32},{1,33},{2,34},{3,35},{4,36},{5,37},{6,38},{7,39},{8,40},{9,... | collective-permute-start | bytes 393224 | tf_op jit(solution)/shard_map/ppermute | solution.py:183
  67.2 1.0 collective-permute-done.23
  68.2 0.7 collective-permute-start.24
  68.9 0.7 collective-permute-start.26
  69.5 0.7 collective-permute-start.25
  71.0 1.0 collective-permute-done.27
  72.7 0.7 collective-permute-start.29
  73.3 0.7 collective-permute-start.28
  74.7 1.0 collective-permute-done.31
  75.7 0.7 collective-permute-start.34
  76.4 1.3 %collective-permute-start.33 = (bf16[256,128]{1,0:T(8,128)(2,1)S(1)}, bf16[256,128]{1,0:T(8,128)(2,1)S(1)}, u32[]{:S(2)}, u32[]{:S(2)}) collective-permute-start(bf16[256,128]{1,0:T(8,128)(2,1)S(1)} %add_convert_fusion), channel_id=1, source_target_pairs={{64,1},{65,2},{66,3},{67,4},{68,5},{69,6},{70,7},{71,8},{72,9},{73... | collective-permute-start | bytes 196616 | tf_op jit(solution)/shard_map/ppermute | solution.py:183
  77.7 1.3 %collective-permute-start.32 = (bf16[256,128]{1,0:T(8,128)(2,1)S(1)}, bf16[256,128]{1,0:T(8,128)(2,1)S(1)}, u32[]{:S(2)}, u32[]{:S(2)}) collective-permute-start(bf16[256,128]{1,0:T(8,128)(2,1)S(1)} %add_convert_fusion), channel_id=1, source_target_pairs={{64,2},{65,3},{66,4},{67,5},{68,6},{69,7},{70,8},{71,9},{72,10},{7... | collective-permute-start | bytes 196616 | tf_op jit(solution)/shard_map/ppermute | solution.py:183
  79.0 1.1 collective-permute-start.36
  80.1 32.5 %collective-permute-done.33 = bf16[256,128]{1,0:T(8,128)(2,1)S(1)} collective-permute-done((bf16[256,128]{1,0:T(8,128)(2,1)S(1)}, bf16[256,128]{1,0:T(8,128)(2,1)S(1)}, u32[]{:S(2)}, u32[]{:S(2)}) %collective-permute-start.33) | collective-permute-done | bytes 65568 | tf_op jit(solution)/shard_map/ppermute | solution.py:183
  112.6 1.4 %collective-permute-done.32 = bf16[256,128]{1,0:T(8,128)(2,1)S(1)} collective-permute-done((bf16[256,128]{1,0:T(8,128)(2,1)S(1)}, bf16[256,128]{1,0:T(8,128)(2,1)S(1)}, u32[]{:S(2)}, u32[]{:S(2)}) %collective-permute-start.32) | collective-permute-done | bytes 65568 | tf_op jit(solution)/shard_map/ppermute | solution.py:183
  114.1 1.4 %collective-permute-start.35 = (bf16[256,384]{1,0:T(8,128)(2,1)S(1)}, bf16[256,384]{1,0:T(8,128)(2,1)S(1)}, u32[]{:S(2)}, u32[]{:S(2)}) collective-permute-start(bf16[256,384]{1,0:T(8,128)(2,1)S(1)} %maximum_add_fusion.3.mine), channel_id=1, source_target_pairs={{0,32},{1,33},{2,34},{3,35},{4,36},{5,37},{6,38},{7,39},{8,40},{9,... | collective-permute-start | bytes 589832 | tf_op jit(solution)/shard_map/ppermute | solution.py:183
  115.6 1.0 collective-permute-done.35.other
  116.6 2.3 %shard_map.57 = f32[256,768]{1,0:T(8,128)} custom-call(s32[2]{0:T(128)S(1)} %pad_add_fusion.scalars, f32[256,768]{1,0:T(8,128)S(1)} %get-tuple-element.22.adjusted, bf16[256,256]{1,0:T(8,128)(2,1)S(1)} %slice.196.left_basis, bf16[256,256]{1,0:T(8,128)(2,1)S(1)} %get-tuple-element.23.right_basis, bf16[256,384]{1,0:T(8,128)(2,1)S(1)} %broadcast_select_fusion.down, ...), custom_call_target="tpu_custom_call" | custom-call | flops 536870912 | bytes 4194304 | tf_op jit(solution)/shard_map/pallas_call | solution.py:42
  (93 shorter events, 8.5 us)
Async XLA Ops:
  0.7 1.3 %copy-start = (bf16[1,1,768,768]{3,2,1,0:T(8,128)(2,1)S(1)}, bf16[1,1,768,768]{3,2,1,0:T(8,128)(2,1)}, u32[]{:S(2)}) copy-start(bf16[1,1,768,768]{3,2,1,0:T(8,128)(2,1)} %param.6) | copy-start | bytes 3538948
  2.0 1.1 copy-start.2
  3.1 0.9 copy-start.3
  4.1 0.9 copy-start.4
  6.8 15.0 %collective-permute-start = (bf16[512,256]{1,0:T(8,128)(2,1)S(1)}, bf16[512,256]{1,0:T(8,128)(2,1)S(1)}, u32[]{:S(2)}, u32[]{:S(2)}) collective-permute-start(bf16[512,256]{1,0:T(8,128)(2,1)S(1)} %get-tuple-element.19), channel_id=1, source_target_pairs={{0,1},{1,2},{2,3},{3,4},{4,5},{5,6},{6,7},{7,8},{8,9},{9,10},{10,1... | collective-permute-start | bytes 786440 | tf_op jit(solution)/shard_map/ppermute | solution.py:183
  9.0 12.8 %collective-permute-start.1 = (bf16[512,256]{1,0:T(8,128)(2,1)S(1)}, bf16[512,256]{1,0:T(8,128)(2,1)S(1)}, u32[]{:S(2)}, u32[]{:S(2)}) collective-permute-start(bf16[512,256]{1,0:T(8,128)(2,1)S(1)} %get-tuple-element.20), channel_id=1, source_target_pairs={{0,31},{1,0},{2,1},{3,2},{4,3},{5,4},{6,5},{7,6},{8,7},{9,8},{10,9... | collective-permute-start | bytes 786440 | tf_op jit(solution)/shard_map/ppermute | solution.py:183
  22.8 6.9 %collective-permute-start.4 = (bf16[640,128]{1,0:T(8,128)(2,1)S(1)}, bf16[640,128]{1,0:T(8,128)(2,1)S(1)}, u32[]{:S(2)}, u32[]{:S(2)}) collective-permute-start(bf16[640,128]{1,0:T(8,128)(2,1)S(1)} %get-tuple-element.30), channel_id=1, source_target_pairs={{0,31},{1,0},{2,1},{3,2},{4,3},{5,4},{6,5},{7,6},{8,7},{9,8},{10,9... | collective-permute-start | bytes 491528 | tf_op jit(solution)/shard_map/ppermute | solution.py:183
  27.4 7.5 %collective-permute-start.3 = (bf16[640,128]{1,0:T(8,128)(2,1)S(1)}, bf16[640,128]{1,0:T(8,128)(2,1)S(1)}, u32[]{:S(2)}, u32[]{:S(2)}) collective-permute-start(bf16[640,128]{1,0:T(8,128)(2,1)S(1)} %get-tuple-element.30), channel_id=1, source_target_pairs={{0,1},{1,2},{2,3},{3,4},{4,5},{5,6},{6,7},{7,8},{8,9},{9,10},{10,1... | collective-permute-start | bytes 491528 | tf_op jit(solution)/shard_map/ppermute | solution.py:183
  27.4 7.5 %collective-permute-start.2 = (bf16[640,128]{1,0:T(8,128)(2,1)S(1)}, bf16[640,128]{1,0:T(8,128)(2,1)S(1)}, u32[]{:S(2)}, u32[]{:S(2)}) collective-permute-start(bf16[640,128]{1,0:T(8,128)(2,1)S(1)} %get-tuple-element.24), channel_id=1, source_target_pairs={{0,32},{1,33},{2,34},{3,35},{4,36},{5,37},{6,38},{7,39},{8,40},{9,... | collective-permute-start | bytes 491528 | tf_op jit(solution)/shard_map/ppermute | solution.py:183
  35.1 4.1 %collective-permute-start.5 = (f32[256,128]{1,0:T(8,128)S(1)}, f32[256,128]{1,0:T(8,128)S(1)}, u32[]{:S(2)}, u32[]{:S(2)}) collective-permute-start(f32[256,128]{1,0:T(8,128)S(1)} %add_select_fusion), channel_id=1, source_target_pairs={{0,32},{1,33},{2,34},{3,35},{4,36},{5,37},{6,38},{7,39},{8,40},{9,... | collective-permute-start | bytes 393224 | tf_op jit(solution)/shard_map/ppermute | solution.py:183
  39.2 6.6 %collective-permute-start.6 = (bf16[256,128]{1,0:T(8,128)(2,1)S(1)}, bf16[256,128]{1,0:T(8,128)(2,1)S(1)}, u32[]{:S(2)}, u32[]{:S(2)}) collective-permute-start(bf16[256,128]{1,0:T(8,128)(2,1)S(1)} %add_convert_fusion.9), channel_id=1, source_target_pairs={{0,66},{1,67},{2,68},{3,69},{4,70},{5,71},{6,72},{7,73},{8,74},{9,... | collective-permute-start | bytes 196616 | tf_op jit(solution)/shard_map/ppermute | solution.py:183
  40.5 7.0 %collective-permute-start.8 = (bf16[256,128]{1,0:T(8,128)(2,1)S(1)}, bf16[256,128]{1,0:T(8,128)(2,1)S(1)}, u32[]{:S(2)}, u32[]{:S(2)}) collective-permute-start(bf16[256,128]{1,0:T(8,128)(2,1)S(1)} %add_convert_fusion.9), channel_id=1, source_target_pairs={{0,64},{1,65},{2,66},{3,67},{4,68},{5,69},{6,70},{7,71},{8,72},{9,... | collective-permute-start | bytes 196616 | tf_op jit(solution)/shard_map/ppermute | solution.py:183
  41.2 5.0 %collective-permute-start.7 = (bf16[256,128]{1,0:T(8,128)(2,1)S(1)}, bf16[256,128]{1,0:T(8,128)(2,1)S(1)}, u32[]{:S(2)}, u32[]{:S(2)}) collective-permute-start(bf16[256,128]{1,0:T(8,128)(2,1)S(1)} %add_convert_fusion.9), channel_id=1, source_target_pairs={{0,65},{1,66},{2,67},{3,68},{4,69},{5,70},{6,71},{7,72},{8,73},{9,... | collective-permute-start | bytes 196616 | tf_op jit(solution)/shard_map/ppermute | solution.py:183
  43.7 5.6 %collective-permute-start.21 = (bf16[640,128]{1,0:T(8,128)(2,1)S(1)}, bf16[640,128]{1,0:T(8,128)(2,1)S(1)}, u32[]{:S(2)}, u32[]{:S(2)}) collective-permute-start(bf16[640,128]{1,0:T(8,128)(2,1)S(1)} %get-tuple-element.32), channel_id=1, source_target_pairs={{0,32},{1,33},{2,34},{3,35},{4,36},{5,37},{6,38},{7,39},{8,40},{9,... | collective-permute-start | bytes 491528 | tf_op jit(solution)/shard_map/ppermute | solution.py:183
  45.6 2.1 %collective-permute-start.9 = (bf16[640,128]{1,0:T(8,128)(2,1)S(1)}, bf16[640,128]{1,0:T(8,128)(2,1)S(1)}, u32[]{:S(2)}, u32[]{:S(2)}) collective-permute-start(bf16[640,128]{1,0:T(8,128)(2,1)S(1)} %collective-permute-done.3), channel_id=1, source_target_pairs={{0,32},{1,33},{2,34},{3,35},{4,36},{5,37},{6,38},{7,39},{8,40},{9,... | collective-permute-start | bytes 491528 | tf_op jit(solution)/shard_map/ppermute | solution.py:183
  45.7 1.8 %collective-permute-start.10 = (bf16[640,128]{1,0:T(8,128)(2,1)S(1)}, bf16[640,128]{1,0:T(8,128)(2,1)S(1)}, u32[]{:S(2)}, u32[]{:S(2)}) collective-permute-start(bf16[640,128]{1,0:T(8,128)(2,1)S(1)} %collective-permute-done.4), channel_id=1, source_target_pairs={{0,32},{1,33},{2,34},{3,35},{4,36},{5,37},{6,38},{7,39},{8,40},{9,... | collective-permute-start | bytes 491528 | tf_op jit(solution)/shard_map/ppermute | solution.py:183
  46.2 2.3 %collective-permute-start.11 = (bf16[640,128]{1,0:T(8,128)(2,1)S(1)}, bf16[640,128]{1,0:T(8,128)(2,1)S(1)}, u32[]{:S(2)}, u32[]{:S(2)}) collective-permute-start(bf16[640,128]{1,0:T(8,128)(2,1)S(1)} %get-tuple-element.30), channel_id=1, source_target_pairs={{0,32},{1,33},{2,34},{3,35},{4,36},{5,37},{6,38},{7,39},{8,40},{9,... | collective-permute-start | bytes 491528 | tf_op jit(solution)/shard_map/ppermute | solution.py:183
  48.9 1.4 %collective-permute-start.12 = (f32[256,128]{1,0:T(8,128)S(1)}, f32[256,128]{1,0:T(8,128)S(1)}, u32[]{:S(2)}, u32[]{:S(2)}) collective-permute-start(f32[256,128]{1,0:T(8,128)S(1)} %convolution_add_fusion.3), channel_id=1, source_target_pairs={{0,32},{1,33},{2,34},{3,35},{4,36},{5,37},{6,38},{7,39},{8,40},{9,... | collective-permute-start | bytes 393224 | tf_op jit(solution)/shard_map/ppermute | solution.py:183
  50.4 2.0 %collective-permute-start.15 = (bf16[256,128]{1,0:T(8,128)(2,1)S(1)}, bf16[256,128]{1,0:T(8,128)(2,1)S(1)}, u32[]{:S(2)}, u32[]{:S(2)}) collective-permute-start(bf16[256,128]{1,0:T(8,128)(2,1)S(1)} %add_convert_fusion.8), channel_id=1, source_target_pairs={{64,128},{65,129},{66,130},{67,131},{68,132},{69,133},{70,134},{71... | collective-permute-start | bytes 196616 | tf_op jit(solution)/shard_map/ppermute | solution.py:183
  51.0 1.4 %collective-permute-start.14 = (bf16[256,128]{1,0:T(8,128)(2,1)S(1)}, bf16[256,128]{1,0:T(8,128)(2,1)S(1)}, u32[]{:S(2)}, u32[]{:S(2)}) collective-permute-start(bf16[256,128]{1,0:T(8,128)(2,1)S(1)} %add_convert_fusion.8), channel_id=1, source_target_pairs={{64,129},{65,130},{66,131},{67,132},{68,133},{69,134},{70,135},{71... | collective-permute-start | bytes 196616 | tf_op jit(solution)/shard_map/ppermute | solution.py:183
  51.7 0.7 collective-permute-start.13
  52.7 1.4 %collective-permute-start.16 = (f32[256,128]{1,0:T(8,128)S(1)}, f32[256,128]{1,0:T(8,128)S(1)}, u32[]{:S(2)}, u32[]{:S(2)}) collective-permute-start(f32[256,128]{1,0:T(8,128)S(1)} %convolution_add_fusion.2), channel_id=1, source_target_pairs={{0,32},{1,33},{2,34},{3,35},{4,36},{5,37},{6,38},{7,39},{8,40},{9,... | collective-permute-start | bytes 393224 | tf_op jit(solution)/shard_map/ppermute | solution.py:183
  54.1 2.0 %collective-permute-start.19 = (bf16[256,128]{1,0:T(8,128)(2,1)S(1)}, bf16[256,128]{1,0:T(8,128)(2,1)S(1)}, u32[]{:S(2)}, u32[]{:S(2)}) collective-permute-start(bf16[256,128]{1,0:T(8,128)(2,1)S(1)} %add_convert_fusion.7), channel_id=1, source_target_pairs={{128,192},{129,193},{130,194},{131,195},{132,196},{133,197},{134,1... | collective-permute-start | bytes 196616 | tf_op jit(solution)/shard_map/ppermute | solution.py:183
  54.8 1.4 %collective-permute-start.18 = (bf16[256,128]{1,0:T(8,128)(2,1)S(1)}, bf16[256,128]{1,0:T(8,128)(2,1)S(1)}, u32[]{:S(2)}, u32[]{:S(2)}) collective-permute-start(bf16[256,128]{1,0:T(8,128)(2,1)S(1)} %add_convert_fusion.7), channel_id=1, source_target_pairs={{128,193},{129,194},{130,195},{131,196},{132,197},{133,198},{134,1... | collective-permute-start | bytes 196616 | tf_op jit(solution)/shard_map/ppermute | solution.py:183
  55.5 0.7 collective-permute-start.17
  56.3 1.5 %collective-permute-start.20 = (bf16[256,384]{1,0:T(8,128)(2,1)S(1)}, bf16[256,384]{1,0:T(8,128)(2,1)S(1)}, u32[]{:S(2)}, u32[]{:S(2)}) collective-permute-start(bf16[256,384]{1,0:T(8,128)(2,1)S(1)} %maximum_add_fusion.1), channel_id=1, source_target_pairs={{0,32},{1,33},{2,34},{3,35},{4,36},{5,37},{6,38},{7,39},{8,40},{9,... | collective-permute-start | bytes 589832 | tf_op jit(solution)/shard_map/ppermute | solution.py:183
  58.7 6.1 %collective-permute-start.22 = (bf16[256,128]{1,0:T(8,128)(2,1)S(1)}, bf16[256,128]{1,0:T(8,128)(2,1)S(1)}, u32[]{:S(2)}, u32[]{:S(2)}) collective-permute-start(bf16[256,128]{1,0:T(8,128)(2,1)S(1)} %get-tuple-element.48), channel_id=1, source_target_pairs={{0,1},{1,2},{2,3},{3,4},{4,5},{5,6},{6,7},{7,8},{8,9},{9,10},{10,1... | collective-permute-start | bytes 196616 | tf_op jit(solution)/shard_map/ppermute | solution.py:183
  65.0 3.2 %collective-permute-start.23 = (f32[256,128]{1,0:T(8,128)S(1)}, f32[256,128]{1,0:T(8,128)S(1)}, u32[]{:S(2)}, u32[]{:S(2)}) collective-permute-start(f32[256,128]{1,0:T(8,128)S(1)} %select_add_fusion), channel_id=1, source_target_pairs={{0,32},{1,33},{2,34},{3,35},{4,36},{5,37},{6,38},{7,39},{8,40},{9,... | collective-permute-start | bytes 393224 | tf_op jit(solution)/shard_map/ppermute | solution.py:183
  68.2 2.0 %collective-permute-start.24 = (bf16[256,128]{1,0:T(8,128)(2,1)S(1)}, bf16[256,128]{1,0:T(8,128)(2,1)S(1)}, u32[]{:S(2)}, u32[]{:S(2)}) collective-permute-start(bf16[256,128]{1,0:T(8,128)(2,1)S(1)} %add_convert_fusion.2), channel_id=1, source_target_pairs={{192,130},{193,131},{194,132},{195,133},{196,134},{197,135},{198,1... | collective-permute-start | bytes 196616 | tf_op jit(solution)/shard_map/ppermute | solution.py:183
  68.9 1.4 %collective-permute-start.26 = (bf16[256,128]{1,0:T(8,128)(2,1)S(1)}, bf16[256,128]{1,0:T(8,128)(2,1)S(1)}, u32[]{:S(2)}, u32[]{:S(2)}) collective-permute-start(bf16[256,128]{1,0:T(8,128)(2,1)S(1)} %add_convert_fusion.2), channel_id=1, source_target_pairs={{192,128},{193,129},{194,130},{195,131},{196,132},{197,133},{198,1... | collective-permute-start | bytes 196616 | tf_op jit(solution)/shard_map/ppermute | solution.py:183
  69.5 0.7 collective-permute-start.25
  70.5 1.4 %collective-permute-start.27 = (f32[256,128]{1,0:T(8,128)S(1)}, f32[256,128]{1,0:T(8,128)S(1)}, u32[]{:S(2)}, u32[]{:S(2)}) collective-permute-start(f32[256,128]{1,0:T(8,128)S(1)} %convolution_add_fusion.1), channel_id=1, source_target_pairs={{0,32},{1,33},{2,34},{3,35},{4,36},{5,37},{6,38},{7,39},{8,40},{9,... | collective-permute-start | bytes 393224 | tf_op jit(solution)/shard_map/ppermute | solution.py:183
  72.0 2.0 %collective-permute-start.30 = (bf16[256,128]{1,0:T(8,128)(2,1)S(1)}, bf16[256,128]{1,0:T(8,128)(2,1)S(1)}, u32[]{:S(2)}, u32[]{:S(2)}) collective-permute-start(bf16[256,128]{1,0:T(8,128)(2,1)S(1)} %add_convert_fusion.1), channel_id=1, source_target_pairs={{128,64},{129,65},{130,66},{131,67},{132,68},{133,69},{134,70},{13... | collective-permute-start | bytes 196616 | tf_op jit(solution)/shard_map/ppermute | solution.py:183
  72.7 1.4 %collective-permute-start.29 = (bf16[256,128]{1,0:T(8,128)(2,1)S(1)}, bf16[256,128]{1,0:T(8,128)(2,1)S(1)}, u32[]{:S(2)}, u32[]{:S(2)}) collective-permute-start(bf16[256,128]{1,0:T(8,128)(2,1)S(1)} %add_convert_fusion.1), channel_id=1, source_target_pairs={{128,65},{129,66},{130,67},{131,68},{132,69},{133,70},{134,71},{13... | collective-permute-start | bytes 196616 | tf_op jit(solution)/shard_map/ppermute | solution.py:183
  73.3 0.7 collective-permute-start.28
  74.2 1.4 %collective-permute-start.31 = (f32[256,128]{1,0:T(8,128)S(1)}, f32[256,128]{1,0:T(8,128)S(1)}, u32[]{:S(2)}, u32[]{:S(2)}) collective-permute-start(f32[256,128]{1,0:T(8,128)S(1)} %convolution_add_fusion), channel_id=1, source_target_pairs={{0,32},{1,33},{2,34},{3,35},{4,36},{5,37},{6,38},{7,39},{8,40},{9,... | collective-permute-start | bytes 393224 | tf_op jit(solution)/shard_map/ppermute | solution.py:183
  74.7 41.9 %copy-start.1 = (bf16[1,1,768,768]{3,2,1,0:T(8,128)(2,1)S(1)}, bf16[1,1,768,768]{3,2,1,0:T(8,128)(2,1)}, u32[]{:S(2)}) copy-start(bf16[1,1,768,768]{3,2,1,0:T(8,128)(2,1)} %param.6) | copy-start | bytes 3538948
  75.7 4.4 %collective-permute-start.34 = (bf16[256,128]{1,0:T(8,128)(2,1)S(1)}, bf16[256,128]{1,0:T(8,128)(2,1)S(1)}, u32[]{:S(2)}, u32[]{:S(2)}) collective-permute-start(bf16[256,128]{1,0:T(8,128)(2,1)S(1)} %add_convert_fusion), channel_id=1, source_target_pairs={{64,0},{65,1},{66,2},{67,3},{68,4},{69,5},{70,6},{71,7},{72,8},{73... | collective-permute-start | bytes 196616 | tf_op jit(solution)/shard_map/ppermute | solution.py:183
  76.4 36.2 %collective-permute-start.33 = (bf16[256,128]{1,0:T(8,128)(2,1)S(1)}, bf16[256,128]{1,0:T(8,128)(2,1)S(1)}, u32[]{:S(2)}, u32[]{:S(2)}) collective-permute-start(bf16[256,128]{1,0:T(8,128)(2,1)S(1)} %add_convert_fusion), channel_id=1, source_target_pairs={{64,1},{65,2},{66,3},{67,4},{68,5},{69,6},{70,7},{71,8},{72,9},{73... | collective-permute-start | bytes 196616 | tf_op jit(solution)/shard_map/ppermute | solution.py:183
  77.7 36.4 %collective-permute-start.32 = (bf16[256,128]{1,0:T(8,128)(2,1)S(1)}, bf16[256,128]{1,0:T(8,128)(2,1)S(1)}, u32[]{:S(2)}, u32[]{:S(2)}) collective-permute-start(bf16[256,128]{1,0:T(8,128)(2,1)S(1)} %add_convert_fusion), channel_id=1, source_target_pairs={{64,2},{65,3},{66,4},{67,5},{68,6},{69,7},{70,8},{71,9},{72,10},{7... | collective-permute-start | bytes 196616 | tf_op jit(solution)/shard_map/ppermute | solution.py:183
  79.0 36.5 %collective-permute-start.36 = (bf16[256,128]{1,0:T(8,128)(2,1)S(1)}, bf16[256,128]{1,0:T(8,128)(2,1)S(1)}, u32[]{:S(2)}, u32[]{:S(2)}) collective-permute-start(bf16[256,128]{1,0:T(8,128)(2,1)S(1)} %collective-permute-done.22), channel_id=1, source_target_pairs={{0,32},{1,33},{2,34},{3,35},{4,36},{5,37},{6,38},{7,39},{8,40},{9,... | collective-permute-start | bytes 196616 | tf_op jit(solution)/shard_map/ppermute | solution.py:183
  114.1 2.4 %collective-permute-start.35 = (bf16[256,384]{1,0:T(8,128)(2,1)S(1)}, bf16[256,384]{1,0:T(8,128)(2,1)S(1)}, u32[]{:S(2)}, u32[]{:S(2)}) collective-permute-start(bf16[256,384]{1,0:T(8,128)(2,1)S(1)} %maximum_add_fusion.3.mine), channel_id=1, source_target_pairs={{0,32},{1,33},{2,34},{3,35},{4,36},{5,37},{6,38},{7,39},{8,40},{9,... | collective-permute-start | bytes 589832 | tf_op jit(solution)/shard_map/ppermute | solution.py:183

commit v3 on v2

v3 whole, which is shorter than its diff:
```python
import functools

import jax
import jax.numpy as jnp
from jax import lax
from jax.experimental import pallas as pl
from jax.experimental.pallas import tpu as pltpu
from jax.sharding import PartitionSpec as P

M = 768
KMAX = 256
FACE = 128
BF = jnp.bfloat16
F32 = jnp.float32
AXES = ("slab", "patch")
VMEM = pl.BlockSpec(memory_space=pltpu.VMEM)
SMEM = pl.BlockSpec(memory_space=pltpu.SMEM)


def dot(a, b):
    return lax.dot_general(a, b, (((1,), (0,)), ((), ())), preferred_element_type=F32)


def dot_t(a, b):
    return lax.dot_general(a, b, (((1,), (1,)), ((), ())), preferred_element_type=F32)


def placement(limit):
    source = lax.broadcasted_iota(jnp.int32, (KMAX, KMAX), 0)
    target = lax.broadcasted_iota(jnp.int32, (KMAX, KMAX), 1)
    hit = (source == KMAX - limit + target) & (target < limit)
    return jnp.where(hit, 1.0, 0.0).astype(BF)


def halves(rows, factor):
    found = []
    for at in range(0, M, KMAX):
        end = at + KMAX
        found.append(dot_t(rows[:, :end], factor[at:end, :end]).astype(BF))
    return jnp.concatenate(found, axis=1)


def call(kernel, shapes, scalars, arrays, cost, spaces=None, scratch=()):
    return pl.pallas_call(
        kernel,
        out_shape=[jax.ShapeDtypeStruct(shape, kind) for shape, kind in shapes],
        in_specs=[SMEM] + (spaces or [VMEM] * len(arrays)),
        out_specs=[VMEM] * len(shapes),
        scratch_shapes=list(scratch),
        cost_estimate=pl.CostEstimate(flops=cost[0], bytes_accessed=cost[1], transcendentals=0),
        compiler_params=pltpu.CompilerParams(vmem_limit_bytes=40 << 20),
    )(scalars, *arrays)


def prepare_kernel(
    scalars, residual_in, factor_in, down_in, up_in, near, far, maps, residual, factor, down_map, up_map, sems
):
    last = M - KMAX
    copies = [
        pltpu.make_async_copy(source, target, sems.at[at])
        for at, (source, target) in enumerate(
            [
                (residual_in, residual),
                (down_in, down_map),
                (up_in, up_map),
                (factor_in.at[:KMAX], factor.at[:KMAX]),
                (factor_in.at[KMAX:last], factor.at[KMAX:last]),
                (factor_in.at[last:], factor.at[last:]),
            ]
        )
    ]
    for copy in copies:
        copy.start()
    columns = residual.shape[0]
    first = scalars[0] == 0
    for copy in copies[:4]:
        copy.wait()
    rows = jnp.concatenate([residual[...].astype(BF), down_map[...], up_map[...]], axis=0)
    half0 = dot_t(rows[:, :KMAX], factor[:KMAX, :KMAX]).astype(BF)
    copies[4].wait()
    half1 = dot_t(rows[:, :last], factor[KMAX:last, :last]).astype(BF)
    copies[5].wait()
    half2 = dot_t(rows, factor[last:, :]).astype(BF)
    half = jnp.concatenate([half0, half1, half2], axis=1)
    first_block = dot(half, factor[:, :KMAX]).astype(BF)
    last_block = dot(half2, factor[last:, last:]).astype(BF)
    middle_block = dot(half[columns:, KMAX:], factor[KMAX:, KMAX:last]).astype(BF)
    low = factor[:, :FACE].T
    high = factor[M - FACE :, M - FACE :].T
    head = jnp.concatenate(
        [
            first_block[:columns],
            dot(low, factor[:, :KMAX]).astype(BF),
            dot(high, factor[M - FACE :, :KMAX]).astype(BF),
        ],
        axis=0,
    )
    ends = jnp.concatenate(
        [
            last_block[:columns],
            dot(low[:, last:], factor[last:, last:]).astype(BF),
            dot(high, factor[M - FACE :, last:]).astype(BF),
        ],
        axis=0,
    )
    tail = dot(ends, placement(scalars[1])).astype(BF)
    near[...] = jnp.where(first, tail, head)
    far[...] = jnp.where(first, head, tail)
    maps[:, :KMAX] = first_block[columns:]
    maps[:, KMAX:last] = middle_block
    maps[:, last:] = last_block[columns:]


def prepare(scalars, residual, factor, down_map, up_map):
    columns = residual.shape[0]
    reach = columns + 2 * FACE
    shapes = [((reach, KMAX), BF), ((reach, KMAX), BF), ((2 * FACE, M), BF)]
    arrays = [residual, factor, down_map, up_map]
    scratch = [pltpu.VMEM(array.shape, array.dtype) for array in arrays] + [pltpu.SemaphoreType.DMA((6,))]
    spaces = [pl.BlockSpec(memory_space=pltpu.HBM)] * 4
    arrays = [pltpu.with_memory_space_constraint(array, pltpu.HBM) for array in arrays]
    return call(prepare_kernel, shapes, scalars, arrays, (1 << 30, 3 << 20), spaces, scratch)


def operators_kernel(
    scalars, residual, near, far, maps_ref, adjusted, near_basis, far_basis, message, outer, extra, up_out
):
    columns = residual.shape[0]
    maps = maps_ref[...]
    first = scalars[0] == 0
    left = jnp.where(first, near[...], far[...])
    right = jnp.where(first, far[...], near[...])
    right = dot_t(right, placement(scalars[1])).astype(BF)
    near_basis[...] = jnp.where(first, left[columns:], right[columns:])
    far_basis[...] = jnp.where(first, right[columns:], left[columns:])
    adjusted[...] = residual[...]
    adjusted[:, :KMAX] = residual[:, :KMAX] - 0.5 * left[:columns].astype(F32)
    adjusted[:, M - KMAX :] = residual[:, M - KMAX :] - 0.5 * right[:columns].astype(F32)
    terms = dot_t(adjusted[...].astype(BF), maps)
    from_left = (0.5 * dot_t(left[columns:], maps[:, :KMAX])).astype(BF)
    from_right = (0.5 * dot_t(right[columns:], maps[:, M - KMAX :])).astype(BF)
    from_near = jnp.where(first, from_left, from_right)
    from_far = jnp.where(first, from_right, from_left)

    def stack(inputs, outputs, own):
        turned = (-own.astype(F32)).T.astype(BF)
        return jnp.concatenate([from_near[inputs, outputs], turned, from_far[inputs, outputs]], axis=0)

    down, up = slice(0, FACE), slice(FACE, 2 * FACE)
    down_down = stack(down, down, maps[:FACE, :FACE])
    down_up = stack(down, up, maps[FACE:, :FACE])
    up_up = stack(up, up, maps[FACE:, M - FACE :])
    down0 = terms[:, :FACE].astype(BF)
    message[:columns] = down0
    message[columns:] = jnp.where(first, down_down, up_up)
    outer[:columns] = down0
    outer[columns:] = jnp.where(first, up_up, down_down)
    extra[:columns] = terms[:, FACE:].astype(BF)
    extra[columns:] = down_up
    up_out[...] = terms[:, FACE:]


def local_operators(scalars, residual, near, far, maps):
    columns = residual.shape[0]
    pack, basis = ((columns + 3 * FACE, FACE), BF), ((2 * FACE, KMAX), BF)
    shapes = [((columns, M), F32), basis, basis, pack, pack, pack, ((columns, FACE), F32)]
    return call(operators_kernel, shapes, scalars, [residual, near, far, maps], (1 << 28, 3 << 20))


def block(array, at):
    return array[at * FACE : (at + 1) * FACE]


def turned(rows):
    return jnp.concatenate([block(rows, 2), block(rows, 1), block(rows, 0)], axis=0)


def compose(rows3, last, width):
    products = [dot(rows3[m], block(last, m)) for m in range(3)]
    return [sum(block(products[m], at - m) for m in range(3) if 0 <= at - m < width) for at in range(width + 2)]


def share_kernel(
    scalars, near, own, far, far_o, own_o, near_o, outer, outer_o, extra, extra_o, up0,
    forward, backward, reach, reach_start, even_rows, odd_rows, even_down, turn, even_start,
):
    columns = own.shape[0] - 3 * FACE
    first = scalars[0] == 0

    def split(mine, other):
        a, b = mine[columns:], turned(other[columns:])
        return jnp.where(first, a, b), jnp.where(first, b, a)

    pairs = [split(near, far_o), split(own, own_o), split(far, near_o)]
    even3, odd3 = [pair[0] for pair in pairs], [pair[1] for pair in pairs]
    even_up, odd_down = split(outer, outer_o)
    even_mixed, odd_mixed = split(extra, extra_o)
    down3 = [
        jnp.where(first, mine[:columns], other[:columns])
        for mine, other in ((near, far_o), (own, own_o), (far, near_o))
    ]
    down3 = jnp.concatenate(down3, axis=1)
    even_down[...] = down3
    for at in range(3):
        even_rows[at * 3 * FACE : (at + 1) * 3 * FACE] = even3[at]
        odd_rows[at * 3 * FACE : (at + 1) * 3 * FACE] = odd3[at]
    forward[...] = jnp.concatenate(compose(even3, odd_down, 3), axis=0).astype(BF)
    backward[...] = jnp.concatenate(compose(odd3, even_up, 3), axis=0).astype(BF)
    up_other = extra_o[:columns].astype(F32)
    odd_start = jnp.where(first, up_other, up0[...]) + dot(down3, odd_mixed)
    reach_start[...] = odd_start
    reach[:columns] = odd_start.astype(BF)
    reach[columns:] = jnp.concatenate(compose(even3, odd_mixed, 3), axis=0).astype(BF)
    turn[: 3 * FACE] = even_mixed
    turn[3 * FACE :] = even_up
    even_start[...] = jnp.where(first, up0[...], up_other)


def turn_kernel(scalars, near, own, far, turn, even_start, operator, start):
    columns = even_start.shape[0]
    last = turn[3 * FACE :]
    far_rows = jnp.concatenate([block(far[columns:], at) for at in range(4, -1, -1)], axis=0)
    wide = compose([near[columns:], own[columns:], far_rows], last, 5)
    mixed = [block(turn, at).astype(F32) for at in range(3)]
    wide = [wide[at] + mixed[at - 2] if 2 <= at < 5 else wide[at] for at in range(7)]
    operator[...] = jnp.concatenate(wide, axis=0).astype(BF)
    rows = jnp.concatenate([near[:columns], own[:columns], far[:columns]], axis=1)
    start[...] = jnp.where(scalars[0] == 0, even_start[...] + dot(rows, last), 0.0)


def five(mine, other):
    own = mine[:, 2 * FACE :] + other[:, 2 * FACE :]
    return jnp.concatenate([mine[:, : 2 * FACE], own, other[:, FACE : 2 * FACE], other[:, :FACE]], axis=1)


def step_kernel(width, scalars, base, operator, reach, seen, reached, *refs):
    pieces, (part, seen_out, reached_out) = refs[:width], refs[-3:]
    start = reach.shape[0] - 5 * FACE
    total = base[...]
    between_total = reached[...]
    for at in range(width):
        piece = pieces[at][...]
        total += dot(piece, block(operator, at))
        here = at - (width - 3)
        if here >= 0:
            where = slice(here * FACE, (here + 1) * FACE)
            seen_out[:, where] = seen[:, where] + piece
            between_total += dot(piece, reach[start + here * FACE : start + (here + 1) * FACE])
    part[...] = total
    reached_out[...] = between_total


def close_kernel(scalars, seen, near, own, turn, even_start, base):
    total = dot(seen[:, FACE : 2 * FACE], block(turn, 0)) + dot(seen[:, 2 * FACE :], block(turn, 1))
    total += dot(near[...], block(turn, 3))
    base[...] = total + jnp.where(scalars[0] == 0, even_start[...] + dot(own[...], block(turn, 4)), 0.0)


def between(base3, faces5, rows):
    found = []
    for m in range(3):
        part = slice(m * FACE, (m + 1) * FACE)
        reach = slice(m * FACE, (m + 3) * FACE)
        inside = rows[m * 3 * FACE : (m + 1) * 3 * FACE]
        found.append((base3[:, part].astype(F32) + dot(faces5[:, reach], inside)).astype(BF))
    return jnp.concatenate(found, axis=1)


def faces_kernel(scalars, mine, other, even_down, even_rows, down):
    faces = five(mine, other)
    inside = between(even_down[...], faces, even_rows[...])
    down[...] = jnp.where(scalars[0] == 0, faces[:, FACE : 4 * FACE], inside)


def finish_kernel(
    scalars, adjusted, near_basis, far_basis, down, mine, other, near, own, far, near_l, own_l, far_l,
    odd_rows, factor_ref, out,
):
    first = scalars[0] == 0
    factor = factor_ref[...]
    faces = five(mine, other)
    last = scalars[2] == 1
    up3 = [jnp.where(last, late[...], early[...]) for early, late in ((near, near_l), (own, own_l), (far, far_l))]
    inside = between(jnp.concatenate(up3, axis=1), faces, odd_rows[...])
    up = jnp.where(first, inside, faces[:, FACE : 4 * FACE])

    def side(at, basis):
        part = slice(at * FACE, (at + 1) * FACE)
        return 0.5 * dot(jnp.concatenate([down[:, part], up[:, part]], axis=1), basis[...])

    own = slice(FACE, 2 * FACE)
    near, far = side(0, near_basis), side(2, far_basis)
    low = adjusted[:, :KMAX] + jnp.where(first, near, far)
    high = adjusted[:, M - KMAX :] + jnp.where(first, far, near)
    rows = jnp.concatenate(
        [
            (low[:, :FACE] - down[:, own].astype(F32)).astype(BF),
            low[:, FACE:].astype(BF),
            adjusted[:, KMAX : M - KMAX].astype(BF),
            high[:, : KMAX - FACE].astype(BF),
            (high[:, KMAX - FACE :] - up[:, own].astype(F32)).astype(BF),
        ],
        axis=1,
    )
    half = halves(rows, factor)
    for at in range(0, M, KMAX):
        out[:, at : at + KMAX] = dot(half[:, at:], factor[at:, at : at + KMAX])


def on_device(right_side, inverse_factor, forward_trace, backward_trace, margin):
    slabs = lax.axis_size("slab")
    patches = lax.axis_size("patch")
    chips = slabs // 2

    def place(slab, patch):
        return slab * patches + patch % patches

    everywhere = [(slab, patch) for slab in range(slabs) for patch in range(patches)]

    def send(value, pairs):
        return lax.ppermute(value, AXES, pairs)

    def swap(value):
        return send(value, [(place(s, q), place(s ^ 1, q)) for s, q in everywhere])

    def from_near(value):
        return send(value, [(place(s, q), place(s, q + (-1) ** s)) for s, q in everywhere])

    def from_far(value):
        return send(value, [(place(s, q), place(s, q - (-1) ** s)) for s, q in everywhere])

    def hop(value, chip, step, width):
        shift = 2 * step
        arrived = []
        for by in range(width, -1, -1):
            pairs = []
            for slab in (2 * chip, 2 * chip + 1)[: 2 if by else 1]:
                pairs += [(place(slab, q), place(slab + shift, q + by * (-1) ** slab)) for q in range(patches)]
            arrived.append(send(value, pairs))
        return arrived

    core = lax.axis_index("slab") % 2
    first = core == 0
    last_chip = lax.axis_index("slab") // 2 == chips - 1
    residual = right_side[0, 0]
    factor = inverse_factor[0, 0]
    columns = residual.shape[0]
    scalars = jnp.stack([core.astype(jnp.int32), margin[0, 0], last_chip.astype(jnp.int32)])
    face = (columns, FACE)
    three, five_, seven = 3 * FACE, 5 * FACE, 7 * FACE

    to_near, to_far, maps = prepare(scalars, residual, factor, forward_trace[0, 0], backward_trace[0, 0])
    near, far = from_near(to_near), from_far(to_far)
    adjusted, near_basis, far_basis, message, outer, extra, up0 = local_operators(
        scalars, residual, near, far, maps
    )
    near, far = from_near(message), from_far(message)
    outer_other = swap(outer)

    def joined(part):
        return (part + swap(part)).astype(BF)

    nothing = jnp.zeros(face, F32)
    down3 = jnp.concatenate([near[:columns], message[:columns], far[:columns]], axis=1)
    start = outer_other[:columns].astype(F32) + dot(down3, turned(outer_other[columns:]))
    base = jnp.where(first, start, nothing)
    total = joined(base)
    pieces = hop(total, 0, 1, 2)

    near_other, own_other, far_other, extra_other = [swap(pack) for pack in (near, message, far, extra)]
    rows = ((3 * three, FACE), BF)
    band = ((five_, FACE), BF)
    forward, backward, reach, reach_start, even_rows, odd_rows, even_down, turn, even_start = call(
        share_kernel,
        [band, band, ((columns + five_, FACE), BF), (face, F32), rows, rows, ((columns, three), BF),
         ((2 * three, FACE), BF), (face, F32)],
        scalars,
        [near, message, far, far_other, own_other, near_other, outer, outer_other, extra, extra_other, up0],
        (1 << 28, 4 << 20),
    )

    def step(pieces, base, operator, seen, reached, later=()):
        width = len(pieces)
        arrays = [base, operator, reach, seen, reached, *pieces, *later]
        spaces = [VMEM] * (5 + width) + [pl.BlockSpec(memory_space=pl.ANY)] * len(later)
        shapes = [(face, F32), ((columns, three), BF), (face, F32)]
        return call(functools.partial(step_kernel, width), shapes, scalars, arrays, (1 << 26, 1 << 19), spaces)

    unseen = jnp.zeros((columns, three), BF)
    part, seen, reached = step(pieces, base, forward, unseen, nothing)
    pieces = hop(joined(part), 1, 1, 2)
    reach_near = from_near(reach)
    part, seen, reached = step(pieces, base, forward, seen, reached, [reach_near])
    pieces = hop(joined(part), 2, 1, 3)

    operator, even_turn = call(
        turn_kernel,
        [((seven, FACE), BF), (face, F32)],
        scalars,
        [reach_near, reach, swap(reach_near), turn, even_start],
        (1 << 28, 2 << 20),
    )
    reached_other = swap(reached)
    part, seen_all, reached_last = step(pieces, even_turn, operator, seen, nothing, [reached_other])
    pieces = hop(joined(part), 3, -1, 2)

    own = (reach_start + reached + reached_other).astype(BF)
    near = from_near(own)
    base = call(close_kernel, [(face, F32)], scalars, [seen, near, own, turn, even_start], (1 << 27, 1 << 20))[0]
    reached_other = swap(reached_last)
    seen_other = swap(seen_all)
    part, seen, _ = step(pieces, base, backward, unseen, nothing, [reached_other, seen_other])
    pieces = hop(joined(part), 2, -1, 2)

    own_last = (reach_start + reached_last + reached_other).astype(BF)
    near_last = from_near(own_last)
    far = swap(near)
    down = call(
        faces_kernel, [((columns, three), BF)], scalars, [seen_all, seen_other, even_down, even_rows], (1 << 27, 1 << 20)
    )[0]
    part, seen, _ = step(pieces, base, backward, seen, nothing, [near_last, far, down])
    pieces = hop(joined(part), 1, -1, 2)
    far_last = swap(near_last)
    seen = seen + jnp.concatenate(pieces, axis=1)
    out = call(
        finish_kernel,
        [((columns, M), F32)],
        scalars,
        [
            adjusted, near_basis, far_basis, down, seen, swap(seen), near, own, far,
            near_last, own_last, far_last, odd_rows, factor,
        ],
        (1 << 29, 4 << 20),
    )[0]
    return out[None, None]


def solution(mesh):
    placed = (
        P("slab", "patch", None, None),
        P("slab", "patch", None, None),
        P("slab", "patch", None, None),
        P("slab", "patch", None, None),
        P("slab", "patch"),
    )
    return jax.shard_map(
        on_device,
        mesh=mesh,
        in_specs=placed,
        out_specs=P("slab", "patch", None, None),
        check_vma=False,
    )
```

time: 119 us -> 113 us (0.950)
  waiting for transfers between devices: 54.7 us -> 34.4 us
  Pallas kernels: 5.13 us -> 16.1 us
  starting transfers between devices: 49.6 us -> 60.4 us
  local copies, waits for them, and re-layouts: 4.4 us -> 0.07 us
  matrix products: 3.06 us -> 0.2 us
    ppermute x37 -> x44, waiting for transfers between devices: 54.7 us -> 34.4 us  [send(): return lax.ppermute(value, AXES, pairs)]
    pallas_call x3 -> x12, Pallas kernels: 5.13 us -> 16.1 us  [call(): pl.pallas_call(kernel, out_shape=[jax.ShapeDtypeStruct(shape, kind) for s...]
    ppermute x37 -> x44, starting transfers between devices: 49.6 us -> 60.4 us  [send(): return lax.ppermute(value, AXES, pairs)]
    unnamed x14 -> x4, local copies, waits for them, and re-layouts: 4.32 us -> 0.01 us
    dot_general x17 -> x1, matrix products: 3.06 us -> 0.2 us  [dot(): lax.dot_general(a, b, (((1,), (0,)), ((), ())), preferred_element_type=F32)]
  transfers between devices with their start and end apart: 37 -> 44, of which waited for: 15 -> 11; matrix products, arithmetic and copies ran while one was open for 2% -> 0% of each run, Pallas kernels for 0% -> 3%
where the time goes in v3:
time: 113 us
  starting transfers between devices  60.4 us (53%)
  waiting for transfers between devices  34.4 us (30%)
  Pallas kernels  16.1 us (14%)
  between operations  1.18 us (1%)
    ppermute x44, starting transfers between devices, send(): return lax.ppermute(value, AXES, pairs)  60.4 us
    ppermute x44, waiting for transfers between devices, send(): return lax.ppermute(value, AXES, pairs)  34.4 us
    pallas_call x12, Pallas kernels, call(): pl.pallas_call(kernel, out_shape=[jax.ShapeDtypeStruct(shape, kind) for s...  16.1 us
  transfers between devices with their start and end apart: 44, of which 11 were waited for; matrix products, arithmetic and copies ran while one was open for 0% of the time, Pallas kernels for 3%

profile of v3, /device:TPU:1, one launch (start us, length us, event | category | flops | bytes accessed | tf_op | source)
XLA Modules:
  0.0 112.6 jit_solution(7359523158949754631)
XLA Ops:
  0.7 3.8 %shard_map.55 = (bf16[512,256]{1,0:T(8,128)(2,1)S(1)}, bf16[512,256]{1,0:T(8,128)(2,1)S(1)}, bf16[256,768]{1,0:T(8,128)(2,1)S(1)}) custom-call(s32[3]{0:T(128)S(1)} %pad_add_fusion.scalars, f32[256,768]{1,0:T(8,128)} %bitcast.11, bf16[768,768]{1,0:T(8,128)(2,1)} %bitcast.9, bf16[128,768]{1,0:T(8,128)(2,1)} %bitcast.13, bf16[128,768]{1,0:T(8,128)(2,1)} %bitcast.14), custom_call_target="tpu_custom_call" | custom-call | flops 1073741824 | bytes 3145728 | tf_op jit(solution)/shard_map/pallas_call | solution.py:44
  4.5 8.9 %collective-permute-start = (bf16[512,256]{1,0:T(8,128)(2,1)S(1)}, bf16[512,256]{1,0:T(8,128)(2,1)S(1)}, u32[]{:S(2)}, u32[]{:S(2)}) collective-permute-start(bf16[512,256]{1,0:T(8,128)(2,1)S(1)} %get-tuple-element.39), channel_id=1, source_target_pairs={{0,1},{1,2},{2,3},{3,4},{4,5},{5,6},{6,7},{7,8},{8,9},{9,10},{10,1... | collective-permute-start | bytes 786440 | tf_op jit(solution)/shard_map/ppermute | solution.py:321
  13.4 4.9 %collective-permute-done.near = bf16[512,256]{1,0:T(8,128)(2,1)S(1)} collective-permute-done((bf16[512,256]{1,0:T(8,128)(2,1)S(1)}, bf16[512,256]{1,0:T(8,128)(2,1)S(1)}, u32[]{:S(2)}, u32[]{:S(2)}) %collective-permute-start) | collective-permute-done | bytes 262176 | tf_op jit(solution)/shard_map/ppermute | solution.py:321
  18.3 3.7 %collective-permute-done.1.far = bf16[512,256]{1,0:T(8,128)(2,1)S(1)} collective-permute-done((bf16[512,256]{1,0:T(8,128)(2,1)S(1)}, bf16[512,256]{1,0:T(8,128)(2,1)S(1)}, u32[]{:S(2)}, u32[]{:S(2)}) %collective-permute-start.1) | collective-permute-done | bytes 262176 | tf_op jit(solution)/shard_map/ppermute | solution.py:321
  22.0 1.0 shard_map.56
  23.1 4.8 %collective-permute-start.2 = (bf16[640,128]{1,0:T(8,128)(2,1)S(1)}, bf16[640,128]{1,0:T(8,128)(2,1)S(1)}, u32[]{:S(2)}, u32[]{:S(2)}) collective-permute-start(bf16[640,128]{1,0:T(8,128)(2,1)S(1)} %get-tuple-element.45.own), channel_id=1, source_target_pairs={{0,1},{1,2},{2,3},{3,4},{4,5},{5,6},{6,7},{7,8},{8,9},{9,10},{10,1... | collective-permute-start | bytes 491528 | tf_op jit(solution)/shard_map/ppermute | solution.py:321
  27.9 2.7 %collective-permute-done.3.far = bf16[640,128]{1,0:T(8,128)(2,1)S(1)} collective-permute-done((bf16[640,128]{1,0:T(8,128)(2,1)S(1)}, bf16[640,128]{1,0:T(8,128)(2,1)S(1)}, u32[]{:S(2)}, u32[]{:S(2)}) %collective-permute-start.3) | collective-permute-done | bytes 163872 | tf_op jit(solution)/shard_map/ppermute | solution.py:321
  31.3 4.5 %collective-permute-start.11 = (f32[256,128]{1,0:T(8,128)S(1)}, f32[256,128]{1,0:T(8,128)S(1)}, u32[]{:S(2)}, u32[]{:S(2)}) collective-permute-start(f32[256,128]{1,0:T(8,128)S(1)} %add_select_fusion.base), channel_id=1, source_target_pairs={{0,32},{1,33},{2,34},{3,35},{4,36},{5,37},{6,38},{7,39},{8,40},{9,... | collective-permute-start | bytes 393224 | tf_op jit(solution)/shard_map/ppermute | solution.py:321
  36.9 1.3 %collective-permute-start.12 = (bf16[256,128]{1,0:T(8,128)(2,1)S(1)}, bf16[256,128]{1,0:T(8,128)(2,1)S(1)}, u32[]{:S(2)}, u32[]{:S(2)}) collective-permute-start(bf16[256,128]{1,0:T(8,128)(2,1)S(1)} %add_convert_fusion.7), channel_id=1, source_target_pairs={{0,66},{1,67},{2,68},{3,69},{4,70},{5,71},{6,72},{7,73},{8,74},{9,... | collective-permute-start | bytes 196616 | tf_op jit(solution)/shard_map/ppermute | solution.py:321
  38.2 4.0 %collective-permute-start.13 = (bf16[256,128]{1,0:T(8,128)(2,1)S(1)}, bf16[256,128]{1,0:T(8,128)(2,1)S(1)}, u32[]{:S(2)}, u32[]{:S(2)}) collective-permute-start(bf16[256,128]{1,0:T(8,128)(2,1)S(1)} %add_convert_fusion.7), channel_id=1, source_target_pairs={{0,65},{1,66},{2,67},{3,68},{4,69},{5,70},{6,71},{7,72},{8,73},{9,... | collective-permute-start | bytes 196616 | tf_op jit(solution)/shard_map/ppermute | solution.py:321
  42.1 0.7 collective-permute-start.14
  42.8 1.1 shard_map.57
  44.0 0.8 shard_map.59
  44.8 1.2 %collective-permute-start.15 = (f32[256,128]{1,0:T(8,128)S(1)}, f32[256,128]{1,0:T(8,128)S(1)}, u32[]{:S(2)}, u32[]{:S(2)}) collective-permute-start(f32[256,128]{1,0:T(8,128)S(1)} %get-tuple-element.57), channel_id=1, source_target_pairs={{0,32},{1,33},{2,34},{3,35},{4,36},{5,37},{6,38},{7,39},{8,40},{9,... | collective-permute-start | bytes 393224 | tf_op jit(solution)/shard_map/ppermute | solution.py:321
  46.0 4.5 %collective-permute-start.9 = (bf16[896,128]{1,0:T(8,128)(2,1)S(1)}, bf16[896,128]{1,0:T(8,128)(2,1)S(1)}, u32[]{:S(2)}, u32[]{:S(2)}) collective-permute-start(bf16[896,128]{1,0:T(8,128)(2,1)S(1)} %get-tuple-element.49.own.reach), channel_id=1, source_target_pairs={{0,1},{1,2},{2,3},{3,4},{4,5},{5,6},{6,7},{7,8},{8,9},{9,10},{10,1... | collective-permute-start | bytes 688136 | tf_op jit(solution)/shard_map/ppermute | solution.py:321
  50.6 0.7 collective-permute-start.16
  51.9 0.7 collective-permute-start.18
  52.6 0.9 collective-permute-done.9.near.refs_3_
  53.5 0.8 shard_map.60
  54.3 2.1 %collective-permute-start.19 = (f32[256,128]{1,0:T(8,128)S(1)}, f32[256,128]{1,0:T(8,128)S(1)}, u32[]{:S(2)}, u32[]{:S(2)}) collective-permute-start(f32[256,128]{1,0:T(8,128)S(1)} %get-tuple-element.59), channel_id=1, source_target_pairs={{0,32},{1,33},{2,34},{3,35},{4,36},{5,37},{6,38},{7,39},{8,40},{9,... | collective-permute-start | bytes 393224 | tf_op jit(solution)/shard_map/ppermute | solution.py:321
  57.4 0.7 collective-permute-start.20
  58.1 0.7 collective-permute-start.21
  58.7 0.7 collective-permute-start.22
  59.4 0.7 collective-permute-start.23
  60.1 0.9 shard_map.58
  61.0 0.8 shard_map.61
  63.3 3.7 %collective-permute-start.26 = (bf16[256,128]{1,0:T(8,128)(2,1)S(1)}, bf16[256,128]{1,0:T(8,128)(2,1)S(1)}, u32[]{:S(2)}, u32[]{:S(2)}) collective-permute-start(bf16[256,128]{1,0:T(8,128)(2,1)S(1)} %get-tuple-element.77.own), channel_id=1, source_target_pairs={{0,1},{1,2},{2,3},{3,4},{4,5},{5,6},{6,7},{7,8},{8,9},{9,10},{10,1... | collective-permute-start | bytes 196616 | tf_op jit(solution)/shard_map/ppermute | solution.py:321
  67.0 0.7 collective-permute-start.28
  67.7 0.7 collective-permute-start.29
  68.4 0.7 collective-permute-start.30
  69.1 0.8 shard_map.63.base
  69.9 1.5 %shard_map.64 = (f32[256,128]{1,0:T(8,128)S(1)}, bf16[256,384]{1,0:T(8,128)(2,1)S(1)}, f32[256,128]{1,0:T(8,128)}) custom-call(s32[3]{0:T(128)S(1)} %pad_add_fusion.scalars, f32[256,128]{1,0:T(8,128)S(1)} %shard_map.63.base, bf16[640,128]{1,0:T(8,128)(2,1)S(1)} %get-tuple-element.65.operator, bf16[896,128]{1,0:T(8,128)(2,1)S(1)} %get-tuple-element.49.own.reach, ...), custom_call_target="tpu_custom_call" | custom-call | flops 67108864 | bytes 524288 | tf_op jit(solution)/shard_map/pallas_call | solution.py:44
  71.3 2.3 %collective-permute-start.32 = (f32[256,128]{1,0:T(8,128)S(1)}, f32[256,128]{1,0:T(8,128)S(1)}, u32[]{:S(2)}, u32[]{:S(2)}) collective-permute-start(f32[256,128]{1,0:T(8,128)S(1)} %get-tuple-element.69), channel_id=1, source_target_pairs={{0,32},{1,33},{2,34},{3,35},{4,36},{5,37},{6,38},{7,39},{8,40},{9,... | collective-permute-start | bytes 393224 | tf_op jit(solution)/shard_map/ppermute | solution.py:321
  73.6 2.1 %collective-permute-start.36 = (bf16[256,128]{1,0:T(8,128)(2,1)S(1)}, bf16[256,128]{1,0:T(8,128)(2,1)S(1)}, u32[]{:S(2)}, u32[]{:S(2)}) collective-permute-start(bf16[256,128]{1,0:T(8,128)(2,1)S(1)} %get-tuple-element.76.own_l), channel_id=1, source_target_pairs={{0,1},{1,2},{2,3},{3,4},{4,5},{5,6},{6,7},{7,8},{8,9},{9,10},{10,1... | collective-permute-start | bytes 196616 | tf_op jit(solution)/shard_map/ppermute | solution.py:321
  75.7 0.7 collective-permute-start.33
  76.4 0.7 collective-permute-start.34
  77.1 0.7 collective-permute-start.35
  77.8 0.9 shard_map.62.refs_5_.down
  78.7 1.5 %shard_map.65 = (f32[256,128]{1,0:T(8,128)S(1)}, bf16[256,384]{1,0:T(8,128)(2,1)S(1)}, f32[256,128]{1,0:T(8,128)}) custom-call(s32[3]{0:T(128)S(1)} %pad_add_fusion.scalars, f32[256,128]{1,0:T(8,128)S(1)} %shard_map.63.base, bf16[640,128]{1,0:T(8,128)(2,1)S(1)} %get-tuple-element.65.operator, bf16[896,128]{1,0:T(8,128)(2,1)S(1)} %get-tuple-element.49.own.reach, ...), custom_call_target="tpu_custom_call" | custom-call | flops 67108864 | bytes 524288 | tf_op jit(solution)/shard_map/pallas_call | solution.py:44
  80.1 2.5 %collective-permute-start.38 = (f32[256,128]{1,0:T(8,128)S(1)}, f32[256,128]{1,0:T(8,128)S(1)}, u32[]{:S(2)}, u32[]{:S(2)}) collective-permute-start(f32[256,128]{1,0:T(8,128)S(1)} %get-tuple-element.71), channel_id=1, source_target_pairs={{0,32},{1,33},{2,34},{3,35},{4,36},{5,37},{6,38},{7,39},{8,40},{9,... | collective-permute-start | bytes 393224 | tf_op jit(solution)/shard_map/ppermute | solution.py:321
  82.7 1.0 collective-permute-done.38
  84.3 1.3 %collective-permute-start.40 = (bf16[256,128]{1,0:T(8,128)(2,1)S(1)}, bf16[256,128]{1,0:T(8,128)(2,1)S(1)}, u32[]{:S(2)}, u32[]{:S(2)}) collective-permute-start(bf16[256,128]{1,0:T(8,128)(2,1)S(1)} %add_convert_fusion), channel_id=1, source_target_pairs={{64,1},{65,2},{66,3},{67,4},{68,5},{69,6},{70,7},{71,8},{72,9},{73... | collective-permute-start | bytes 196616 | tf_op jit(solution)/shard_map/ppermute | solution.py:321
  85.6 1.3 %collective-permute-start.39 = (bf16[256,128]{1,0:T(8,128)(2,1)S(1)}, bf16[256,128]{1,0:T(8,128)(2,1)S(1)}, u32[]{:S(2)}, u32[]{:S(2)}) collective-permute-start(bf16[256,128]{1,0:T(8,128)(2,1)S(1)} %add_convert_fusion), channel_id=1, source_target_pairs={{64,2},{65,3},{66,4},{67,5},{68,6},{69,7},{70,8},{71,9},{72,10},{7... | collective-permute-start | bytes 196616 | tf_op jit(solution)/shard_map/ppermute | solution.py:321
  87.0 17.0 %collective-permute-done.40 = bf16[256,128]{1,0:T(8,128)(2,1)S(1)} collective-permute-done((bf16[256,128]{1,0:T(8,128)(2,1)S(1)}, bf16[256,128]{1,0:T(8,128)(2,1)S(1)}, u32[]{:S(2)}, u32[]{:S(2)}) %collective-permute-start.40) | collective-permute-done | bytes 65568 | tf_op jit(solution)/shard_map/ppermute | solution.py:321
  104.0 1.5 %collective-permute-done.39 = bf16[256,128]{1,0:T(8,128)(2,1)S(1)} collective-permute-done((bf16[256,128]{1,0:T(8,128)(2,1)S(1)}, bf16[256,128]{1,0:T(8,128)(2,1)S(1)}, u32[]{:S(2)}, u32[]{:S(2)}) %collective-permute-start.39) | collective-permute-done | bytes 65568 | tf_op jit(solution)/shard_map/ppermute | solution.py:321
  105.6 3.3 %collective-permute-start.42 = (bf16[256,384]{1,0:T(8,128)(2,1)S(1)}, bf16[256,384]{1,0:T(8,128)(2,1)S(1)}, u32[]{:S(2)}, u32[]{:S(2)}) collective-permute-start(bf16[256,384]{1,0:T(8,128)(2,1)S(1)} %maximum_add_fusion.mine), channel_id=1, source_target_pairs={{0,32},{1,33},{2,34},{3,35},{4,36},{5,37},{6,38},{7,39},{8,40},{9,... | collective-permute-start | bytes 589832 | tf_op jit(solution)/shard_map/ppermute | solution.py:321
  109.0 1.2 %collective-permute-done.43.far_l = bf16[256,128]{1,0:T(8,128)(2,1)S(1)} collective-permute-done((bf16[256,128]{1,0:T(8,128)(2,1)S(1)}, bf16[256,128]{1,0:T(8,128)(2,1)S(1)}, u32[]{:S(2)}, u32[]{:S(2)}) %collective-permute-start.43) | collective-permute-done | bytes 65568 | tf_op jit(solution)/shard_map/ppermute | solution.py:321
  110.1 2.5 %shard_map.66 = f32[256,768]{1,0:T(8,128)} custom-call(s32[3]{0:T(128)S(1)} %pad_add_fusion.scalars, f32[256,768]{1,0:T(8,128)S(1)} %get-tuple-element.42.adjusted, bf16[256,256]{1,0:T(8,128)(2,1)S(1)} %get-tuple-element.43.near_basis, bf16[256,256]{1,0:T(8,128)(2,1)S(1)} %get-tuple-element.44.far_basis, bf16[256,384]{1,0:T(8,128)(2,1)S(1)} %shard_map.62.refs_5_.down, ...), custom_call_target="tpu_custom_call" | custom-call | flops 536870912 | bytes 4194304 | tf_op jit(solution)/shard_map/pallas_call | solution.py:44
  (72 shorter events, 6.1 us)
Async XLA Ops:
  0.7 21.2 %copy-start.1 = (f32[1,1,256,768]{3,2,1,0:T(8,128)S(1)}, f32[1,1,256,768]{3,2,1,0:T(8,128)}, u32[]{:S(2)}) copy-start(f32[1,1,256,768]{3,2,1,0:T(8,128)} %param.5) | copy-start | bytes 2359300
  4.5 13.8 %collective-permute-start = (bf16[512,256]{1,0:T(8,128)(2,1)S(1)}, bf16[512,256]{1,0:T(8,128)(2,1)S(1)}, u32[]{:S(2)}, u32[]{:S(2)}) collective-permute-start(bf16[512,256]{1,0:T(8,128)(2,1)S(1)} %get-tuple-element.39), channel_id=1, source_target_pairs={{0,1},{1,2},{2,3},{3,4},{4,5},{5,6},{6,7},{7,8},{8,9},{9,10},{10,1... | collective-permute-start | bytes 786440 | tf_op jit(solution)/shard_map/ppermute | solution.py:321
  13.4 8.5 %collective-permute-start.1 = (bf16[512,256]{1,0:T(8,128)(2,1)S(1)}, bf16[512,256]{1,0:T(8,128)(2,1)S(1)}, u32[]{:S(2)}, u32[]{:S(2)}) collective-permute-start(bf16[512,256]{1,0:T(8,128)(2,1)S(1)} %get-tuple-element.40), channel_id=1, source_target_pairs={{0,31},{1,0},{2,1},{3,2},{4,3},{5,4},{6,5},{7,6},{8,7},{9,8},{10,9... | collective-permute-start | bytes 786440 | tf_op jit(solution)/shard_map/ppermute | solution.py:321
  23.0 7.6 %collective-permute-start.3 = (bf16[640,128]{1,0:T(8,128)(2,1)S(1)}, bf16[640,128]{1,0:T(8,128)(2,1)S(1)}, u32[]{:S(2)}, u32[]{:S(2)}) collective-permute-start(bf16[640,128]{1,0:T(8,128)(2,1)S(1)} %get-tuple-element.45.own), channel_id=1, source_target_pairs={{0,31},{1,0},{2,1},{3,2},{4,3},{5,4},{6,5},{7,6},{8,7},{9,8},{10,9... | collective-permute-start | bytes 491528 | tf_op jit(solution)/shard_map/ppermute | solution.py:321
  23.1 8.0 %collective-permute-start.2 = (bf16[640,128]{1,0:T(8,128)(2,1)S(1)}, bf16[640,128]{1,0:T(8,128)(2,1)S(1)}, u32[]{:S(2)}, u32[]{:S(2)}) collective-permute-start(bf16[640,128]{1,0:T(8,128)(2,1)S(1)} %get-tuple-element.45.own), channel_id=1, source_target_pairs={{0,1},{1,2},{2,3},{3,4},{4,5},{5,6},{6,7},{7,8},{8,9},{9,10},{10,1... | collective-permute-start | bytes 491528 | tf_op jit(solution)/shard_map/ppermute | solution.py:321
  27.9 3.2 %collective-permute-start.7 = (bf16[640,128]{1,0:T(8,128)(2,1)S(1)}, bf16[640,128]{1,0:T(8,128)(2,1)S(1)}, u32[]{:S(2)}, u32[]{:S(2)}) collective-permute-start(bf16[640,128]{1,0:T(8,128)(2,1)S(1)} %get-tuple-element.46.outer), channel_id=1, source_target_pairs={{0,32},{1,33},{2,34},{3,35},{4,36},{5,37},{6,38},{7,39},{8,40},{9,... | collective-permute-start | bytes 491528 | tf_op jit(solution)/shard_map/ppermute | solution.py:321
  31.3 5.6 %collective-permute-start.11 = (f32[256,128]{1,0:T(8,128)S(1)}, f32[256,128]{1,0:T(8,128)S(1)}, u32[]{:S(2)}, u32[]{:S(2)}) collective-permute-start(f32[256,128]{1,0:T(8,128)S(1)} %add_select_fusion.base), channel_id=1, source_target_pairs={{0,32},{1,33},{2,34},{3,35},{4,36},{5,37},{6,38},{7,39},{8,40},{9,... | collective-permute-start | bytes 393224 | tf_op jit(solution)/shard_map/ppermute | solution.py:321
  35.8 2.3 %collective-permute-start.5 = (bf16[640,128]{1,0:T(8,128)(2,1)S(1)}, bf16[640,128]{1,0:T(8,128)(2,1)S(1)}, u32[]{:S(2)}, u32[]{:S(2)}) collective-permute-start(bf16[640,128]{1,0:T(8,128)(2,1)S(1)} %get-tuple-element.45.own), channel_id=1, source_target_pairs={{0,32},{1,33},{2,34},{3,35},{4,36},{5,37},{6,38},{7,39},{8,40},{9,... | collective-permute-start | bytes 491528 | tf_op jit(solution)/shard_map/ppermute | solution.py:321
  35.9 6.2 %collective-permute-start.8 = (bf16[640,128]{1,0:T(8,128)(2,1)S(1)}, bf16[640,128]{1,0:T(8,128)(2,1)S(1)}, u32[]{:S(2)}, u32[]{:S(2)}) collective-permute-start(bf16[640,128]{1,0:T(8,128)(2,1)S(1)} %get-tuple-element.47.extra), channel_id=1, source_target_pairs={{0,32},{1,33},{2,34},{3,35},{4,36},{5,37},{6,38},{7,39},{8,40},{9,... | collective-permute-start | bytes 491528 | tf_op jit(solution)/shard_map/ppermute | solution.py:321
  36.3 6.5 %collective-permute-start.4 = (bf16[640,128]{1,0:T(8,128)(2,1)S(1)}, bf16[640,128]{1,0:T(8,128)(2,1)S(1)}, u32[]{:S(2)}, u32[]{:S(2)}) collective-permute-start(bf16[640,128]{1,0:T(8,128)(2,1)S(1)} %collective-permute-done.3.far), channel_id=1, source_target_pairs={{0,32},{1,33},{2,34},{3,35},{4,36},{5,37},{6,38},{7,39},{8,40},{9,... | collective-permute-start | bytes 491528 | tf_op jit(solution)/shard_map/ppermute | solution.py:321
  36.4 6.4 %collective-permute-start.6 = (bf16[640,128]{1,0:T(8,128)(2,1)S(1)}, bf16[640,128]{1,0:T(8,128)(2,1)S(1)}, u32[]{:S(2)}, u32[]{:S(2)}) collective-permute-start(bf16[640,128]{1,0:T(8,128)(2,1)S(1)} %collective-permute-done.2.near), channel_id=1, source_target_pairs={{0,32},{1,33},{2,34},{3,35},{4,36},{5,37},{6,38},{7,39},{8,40},{9,... | collective-permute-start | bytes 491528 | tf_op jit(solution)/shard_map/ppermute | solution.py:321
  36.9 7.1 %collective-permute-start.12 = (bf16[256,128]{1,0:T(8,128)(2,1)S(1)}, bf16[256,128]{1,0:T(8,128)(2,1)S(1)}, u32[]{:S(2)}, u32[]{:S(2)}) collective-permute-start(bf16[256,128]{1,0:T(8,128)(2,1)S(1)} %add_convert_fusion.7), channel_id=1, source_target_pairs={{0,66},{1,67},{2,68},{3,69},{4,70},{5,71},{6,72},{7,73},{8,74},{9,... | collective-permute-start | bytes 196616 | tf_op jit(solution)/shard_map/ppermute | solution.py:321
  38.2 5.8 %collective-permute-start.13 = (bf16[256,128]{1,0:T(8,128)(2,1)S(1)}, bf16[256,128]{1,0:T(8,128)(2,1)S(1)}, u32[]{:S(2)}, u32[]{:S(2)}) collective-permute-start(bf16[256,128]{1,0:T(8,128)(2,1)S(1)} %add_convert_fusion.7), channel_id=1, source_target_pairs={{0,65},{1,66},{2,67},{3,68},{4,69},{5,70},{6,71},{7,72},{8,73},{9,... | collective-permute-start | bytes 196616 | tf_op jit(solution)/shard_map/ppermute | solution.py:321
  42.1 1.8 %collective-permute-start.14 = (bf16[256,128]{1,0:T(8,128)(2,1)S(1)}, bf16[256,128]{1,0:T(8,128)(2,1)S(1)}, u32[]{:S(2)}, u32[]{:S(2)}) collective-permute-start(bf16[256,128]{1,0:T(8,128)(2,1)S(1)} %add_convert_fusion.7), channel_id=1, source_target_pairs={{0,64},{1,65},{2,66},{3,67},{4,68},{5,69},{6,70},{7,71},{8,72},{9,... | collective-permute-start | bytes 196616 | tf_op jit(solution)/shard_map/ppermute | solution.py:321
  44.8 5.7 %collective-permute-start.15 = (f32[256,128]{1,0:T(8,128)S(1)}, f32[256,128]{1,0:T(8,128)S(1)}, u32[]{:S(2)}, u32[]{:S(2)}) collective-permute-start(f32[256,128]{1,0:T(8,128)S(1)} %get-tuple-element.57), channel_id=1, source_target_pairs={{0,32},{1,33},{2,34},{3,35},{4,36},{5,37},{6,38},{7,39},{8,40},{9,... | collective-permute-start | bytes 393224 | tf_op jit(solution)/shard_map/ppermute | solution.py:321
  46.0 7.5 %collective-permute-start.9 = (bf16[896,128]{1,0:T(8,128)(2,1)S(1)}, bf16[896,128]{1,0:T(8,128)(2,1)S(1)}, u32[]{:S(2)}, u32[]{:S(2)}) collective-permute-start(bf16[896,128]{1,0:T(8,128)(2,1)S(1)} %get-tuple-element.49.own.reach), channel_id=1, source_target_pairs={{0,1},{1,2},{2,3},{3,4},{4,5},{5,6},{6,7},{7,8},{8,9},{9,10},{10,1... | collective-permute-start | bytes 688136 | tf_op jit(solution)/shard_map/ppermute | solution.py:321
  50.6 2.9 %collective-permute-start.16 = (bf16[256,128]{1,0:T(8,128)(2,1)S(1)}, bf16[256,128]{1,0:T(8,128)(2,1)S(1)}, u32[]{:S(2)}, u32[]{:S(2)}) collective-permute-start(bf16[256,128]{1,0:T(8,128)(2,1)S(1)} %add_convert_fusion.6), channel_id=1, source_target_pairs={{64,130},{65,131},{66,132},{67,133},{68,134},{69,135},{70,136},{71... | collective-permute-start | bytes 196616 | tf_op jit(solution)/shard_map/ppermute | solution.py:321
  51.2 2.3 %collective-permute-start.17 = (bf16[256,128]{1,0:T(8,128)(2,1)S(1)}, bf16[256,128]{1,0:T(8,128)(2,1)S(1)}, u32[]{:S(2)}, u32[]{:S(2)}) collective-permute-start(bf16[256,128]{1,0:T(8,128)(2,1)S(1)} %add_convert_fusion.6), channel_id=1, source_target_pairs={{64,129},{65,130},{66,131},{67,132},{68,133},{69,134},{70,135},{71... | collective-permute-start | bytes 196616 | tf_op jit(solution)/shard_map/ppermute | solution.py:321
  51.9 1.6 %collective-permute-start.18 = (bf16[256,128]{1,0:T(8,128)(2,1)S(1)}, bf16[256,128]{1,0:T(8,128)(2,1)S(1)}, u32[]{:S(2)}, u32[]{:S(2)}) collective-permute-start(bf16[256,128]{1,0:T(8,128)(2,1)S(1)} %add_convert_fusion.6), channel_id=1, source_target_pairs={{64,128},{65,129},{66,130},{67,131},{68,132},{69,133},{70,134},{71... | collective-permute-start | bytes 196616 | tf_op jit(solution)/shard_map/ppermute | solution.py:321
  54.3 3.0 %collective-permute-start.19 = (f32[256,128]{1,0:T(8,128)S(1)}, f32[256,128]{1,0:T(8,128)S(1)}, u32[]{:S(2)}, u32[]{:S(2)}) collective-permute-start(f32[256,128]{1,0:T(8,128)S(1)} %get-tuple-element.59), channel_id=1, source_target_pairs={{0,32},{1,33},{2,34},{3,35},{4,36},{5,37},{6,38},{7,39},{8,40},{9,... | collective-permute-start | bytes 393224 | tf_op jit(solution)/shard_map/ppermute | solution.py:321
  56.4 4.6 %collective-permute-start.24 = (f32[256,128]{1,0:T(8,128)S(1)}, f32[256,128]{1,0:T(8,128)S(1)}, u32[]{:S(2)}, u32[]{:S(2)}) collective-permute-start(f32[256,128]{1,0:T(8,128)S(1)} %get-tuple-element.60), channel_id=1, source_target_pairs={{0,32},{1,33},{2,34},{3,35},{4,36},{5,37},{6,38},{7,39},{8,40},{9,... | collective-permute-start | bytes 393224 | tf_op jit(solution)/shard_map/ppermute | solution.py:321
  56.5 2.9 %collective-permute-start.10 = (bf16[896,128]{1,0:T(8,128)(2,1)S(1)}, bf16[896,128]{1,0:T(8,128)(2,1)S(1)}, u32[]{:S(2)}, u32[]{:S(2)}) collective-permute-start(bf16[896,128]{1,0:T(8,128)(2,1)S(1)} %collective-permute-done.9.near.refs_3_), channel_id=1, source_target_pairs={{0,32},{1,33},{2,34},{3,35},{4,36},{5,37},{6,38},{7,39},{8,40},{9,... | collective-permute-start | bytes 688136 | tf_op jit(solution)/shard_map/ppermute | solution.py:321
  57.4 3.6 %collective-permute-start.20 = (bf16[256,128]{1,0:T(8,128)(2,1)S(1)}, bf16[256,128]{1,0:T(8,128)(2,1)S(1)}, u32[]{:S(2)}, u32[]{:S(2)}) collective-permute-start(bf16[256,128]{1,0:T(8,128)(2,1)S(1)} %add_convert_fusion.5), channel_id=1, source_target_pairs={{128,195},{129,196},{130,197},{131,198},{132,199},{133,200},{134,2... | collective-permute-start | bytes 196616 | tf_op jit(solution)/shard_map/ppermute | solution.py:321
  58.1 2.9 %collective-permute-start.21 = (bf16[256,128]{1,0:T(8,128)(2,1)S(1)}, bf16[256,128]{1,0:T(8,128)(2,1)S(1)}, u32[]{:S(2)}, u32[]{:S(2)}) collective-permute-start(bf16[256,128]{1,0:T(8,128)(2,1)S(1)} %add_convert_fusion.5), channel_id=1, source_target_pairs={{128,194},{129,195},{130,196},{131,197},{132,198},{133,199},{134,2... | collective-permute-start | bytes 196616 | tf_op jit(solution)/shard_map/ppermute | solution.py:321
  58.7 2.3 %collective-permute-start.22 = (bf16[256,128]{1,0:T(8,128)(2,1)S(1)}, bf16[256,128]{1,0:T(8,128)(2,1)S(1)}, u32[]{:S(2)}, u32[]{:S(2)}) collective-permute-start(bf16[256,128]{1,0:T(8,128)(2,1)S(1)} %add_convert_fusion.5), channel_id=1, source_target_pairs={{128,193},{129,194},{130,195},{131,196},{132,197},{133,198},{134,1... | collective-permute-start | bytes 196616 | tf_op jit(solution)/shard_map/ppermute | solution.py:321
  59.4 1.6 %collective-permute-start.23 = (bf16[256,128]{1,0:T(8,128)(2,1)S(1)}, bf16[256,128]{1,0:T(8,128)(2,1)S(1)}, u32[]{:S(2)}, u32[]{:S(2)}) collective-permute-start(bf16[256,128]{1,0:T(8,128)(2,1)S(1)} %add_convert_fusion.5), channel_id=1, source_target_pairs={{128,192},{129,193},{130,194},{131,195},{132,196},{133,197},{134,1... | collective-permute-start | bytes 196616 | tf_op jit(solution)/shard_map/ppermute | solution.py:321
  61.8 1.4 %collective-permute-start.31 = (f32[256,128]{1,0:T(8,128)S(1)}, f32[256,128]{1,0:T(8,128)S(1)}, u32[]{:S(2)}, u32[]{:S(2)}) collective-permute-start(f32[256,128]{1,0:T(8,128)S(1)} %get-tuple-element.67), channel_id=1, source_target_pairs={{0,32},{1,33},{2,34},{3,35},{4,36},{5,37},{6,38},{7,39},{8,40},{9,... | collective-permute-start | bytes 393224 | tf_op jit(solution)/shard_map/ppermute | solution.py:321
  62.3 7.5 %collective-permute-start.25 = (bf16[256,384]{1,0:T(8,128)(2,1)S(1)}, bf16[256,384]{1,0:T(8,128)(2,1)S(1)}, u32[]{:S(2)}, u32[]{:S(2)}) collective-permute-start(bf16[256,384]{1,0:T(8,128)(2,1)S(1)} %get-tuple-element.61.mine), channel_id=1, source_target_pairs={{0,32},{1,33},{2,34},{3,35},{4,36},{5,37},{6,38},{7,39},{8,40},{9,... | collective-permute-start | bytes 589832 | tf_op jit(solution)/shard_map/ppermute | solution.py:321
  62.4 4.6 %collective-permute-start.27 = (f32[256,128]{1,0:T(8,128)S(1)}, f32[256,128]{1,0:T(8,128)S(1)}, u32[]{:S(2)}, u32[]{:S(2)}) collective-permute-start(f32[256,128]{1,0:T(8,128)S(1)} %get-tuple-element.66), channel_id=1, source_target_pairs={{0,32},{1,33},{2,34},{3,35},{4,36},{5,37},{6,38},{7,39},{8,40},{9,... | collective-permute-start | bytes 393224 | tf_op jit(solution)/shard_map/ppermute | solution.py:321
  63.3 5.7 %collective-permute-start.26 = (bf16[256,128]{1,0:T(8,128)(2,1)S(1)}, bf16[256,128]{1,0:T(8,128)(2,1)S(1)}, u32[]{:S(2)}, u32[]{:S(2)}) collective-permute-start(bf16[256,128]{1,0:T(8,128)(2,1)S(1)} %get-tuple-element.77.own), channel_id=1, source_target_pairs={{0,1},{1,2},{2,3},{3,4},{4,5},{5,6},{6,7},{7,8},{8,9},{9,10},{10,1... | collective-permute-start | bytes 196616 | tf_op jit(solution)/shard_map/ppermute | solution.py:321
  67.0 2.8 %collective-permute-start.28 = (bf16[256,128]{1,0:T(8,128)(2,1)S(1)}, bf16[256,128]{1,0:T(8,128)(2,1)S(1)}, u32[]{:S(2)}, u32[]{:S(2)}) collective-permute-start(bf16[256,128]{1,0:T(8,128)(2,1)S(1)} %add_convert_fusion.3), channel_id=1, source_target_pairs={{192,130},{193,131},{194,132},{195,133},{196,134},{197,135},{198,1... | collective-permute-start | bytes 196616 | tf_op jit(solution)/shard_map/ppermute | solution.py:321
  67.7 2.1 %collective-permute-start.29 = (bf16[256,128]{1,0:T(8,128)(2,1)S(1)}, bf16[256,128]{1,0:T(8,128)(2,1)S(1)}, u32[]{:S(2)}, u32[]{:S(2)}) collective-permute-start(bf16[256,128]{1,0:T(8,128)(2,1)S(1)} %add_convert_fusion.3), channel_id=1, source_target_pairs={{192,129},{193,130},{194,131},{195,132},{196,133},{197,134},{198,1... | collective-permute-start | bytes 196616 | tf_op jit(solution)/shard_map/ppermute | solution.py:321
  68.4 1.5 %collective-permute-start.30 = (bf16[256,128]{1,0:T(8,128)(2,1)S(1)}, bf16[256,128]{1,0:T(8,128)(2,1)S(1)}, u32[]{:S(2)}, u32[]{:S(2)}) collective-permute-start(bf16[256,128]{1,0:T(8,128)(2,1)S(1)} %add_convert_fusion.3), channel_id=1, source_target_pairs={{192,128},{193,129},{194,130},{195,131},{196,132},{197,133},{198,1... | collective-permute-start | bytes 196616 | tf_op jit(solution)/shard_map/ppermute | solution.py:321
  71.3 4.4 %collective-permute-start.32 = (f32[256,128]{1,0:T(8,128)S(1)}, f32[256,128]{1,0:T(8,128)S(1)}, u32[]{:S(2)}, u32[]{:S(2)}) collective-permute-start(f32[256,128]{1,0:T(8,128)S(1)} %get-tuple-element.69), channel_id=1, source_target_pairs={{0,32},{1,33},{2,34},{3,35},{4,36},{5,37},{6,38},{7,39},{8,40},{9,... | collective-permute-start | bytes 393224 | tf_op jit(solution)/shard_map/ppermute | solution.py:321
  73.6 5.0 %collective-permute-start.36 = (bf16[256,128]{1,0:T(8,128)(2,1)S(1)}, bf16[256,128]{1,0:T(8,128)(2,1)S(1)}, u32[]{:S(2)}, u32[]{:S(2)}) collective-permute-start(bf16[256,128]{1,0:T(8,128)(2,1)S(1)} %get-tuple-element.76.own_l), channel_id=1, source_target_pairs={{0,1},{1,2},{2,3},{3,4},{4,5},{5,6},{6,7},{7,8},{8,9},{9,10},{10,1... | collective-permute-start | bytes 196616 | tf_op jit(solution)/shard_map/ppermute | solution.py:321
  75.7 2.9 %collective-permute-start.37 = (bf16[256,128]{1,0:T(8,128)(2,1)S(1)}, bf16[256,128]{1,0:T(8,128)(2,1)S(1)}, u32[]{:S(2)}, u32[]{:S(2)}) collective-permute-start(bf16[256,128]{1,0:T(8,128)(2,1)S(1)} %collective-permute-done.26.near), channel_id=1, source_target_pairs={{0,32},{1,33},{2,34},{3,35},{4,36},{5,37},{6,38},{7,39},{8,40},{9,... | collective-permute-start | bytes 196616 | tf_op jit(solution)/shard_map/ppermute | solution.py:321
  75.7 2.9 %collective-permute-start.33 = (bf16[256,128]{1,0:T(8,128)(2,1)S(1)}, bf16[256,128]{1,0:T(8,128)(2,1)S(1)}, u32[]{:S(2)}, u32[]{:S(2)}) collective-permute-start(bf16[256,128]{1,0:T(8,128)(2,1)S(1)} %add_convert_fusion.2), channel_id=1, source_target_pairs={{128,66},{129,67},{130,68},{131,69},{132,70},{133,71},{134,72},{13... | collective-permute-start | bytes 196616 | tf_op jit(solution)/shard_map/ppermute | solution.py:321
  76.4 2.3 %collective-permute-start.34 = (bf16[256,128]{1,0:T(8,128)(2,1)S(1)}, bf16[256,128]{1,0:T(8,128)(2,1)S(1)}, u32[]{:S(2)}, u32[]{:S(2)}) collective-permute-start(bf16[256,128]{1,0:T(8,128)(2,1)S(1)} %add_convert_fusion.2), channel_id=1, source_target_pairs={{128,65},{129,66},{130,67},{131,68},{132,69},{133,70},{134,71},{13... | collective-permute-start | bytes 196616 | tf_op jit(solution)/shard_map/ppermute | solution.py:321
  77.1 1.6 %collective-permute-start.35 = (bf16[256,128]{1,0:T(8,128)(2,1)S(1)}, bf16[256,128]{1,0:T(8,128)(2,1)S(1)}, u32[]{:S(2)}, u32[]{:S(2)}) collective-permute-start(bf16[256,128]{1,0:T(8,128)(2,1)S(1)} %add_convert_fusion.2), channel_id=1, source_target_pairs={{128,64},{129,65},{130,66},{131,67},{132,68},{133,69},{134,70},{13... | collective-permute-start | bytes 196616 | tf_op jit(solution)/shard_map/ppermute | solution.py:321
  78.6 31.5 %copy-start = (bf16[1,1,768,768]{3,2,1,0:T(8,128)(2,1)S(1)}, bf16[1,1,768,768]{3,2,1,0:T(8,128)(2,1)}, u32[]{:S(2)}) copy-start(bf16[1,1,768,768]{3,2,1,0:T(8,128)(2,1)} %param.6) | copy-start | bytes 3538948
  80.1 3.5 %collective-permute-start.38 = (f32[256,128]{1,0:T(8,128)S(1)}, f32[256,128]{1,0:T(8,128)S(1)}, u32[]{:S(2)}, u32[]{:S(2)}) collective-permute-start(f32[256,128]{1,0:T(8,128)S(1)} %get-tuple-element.71), channel_id=1, source_target_pairs={{0,32},{1,33},{2,34},{3,35},{4,36},{5,37},{6,38},{7,39},{8,40},{9,... | collective-permute-start | bytes 393224 | tf_op jit(solution)/shard_map/ppermute | solution.py:321
  83.7 3.3 %collective-permute-start.41 = (bf16[256,128]{1,0:T(8,128)(2,1)S(1)}, bf16[256,128]{1,0:T(8,128)(2,1)S(1)}, u32[]{:S(2)}, u32[]{:S(2)}) collective-permute-start(bf16[256,128]{1,0:T(8,128)(2,1)S(1)} %add_convert_fusion), channel_id=1, source_target_pairs={{64,0},{65,1},{66,2},{67,3},{68,4},{69,5},{70,6},{71,7},{72,8},{73... | collective-permute-start | bytes 196616 | tf_op jit(solution)/shard_map/ppermute | solution.py:321
  84.3 19.6 %collective-permute-start.40 = (bf16[256,128]{1,0:T(8,128)(2,1)S(1)}, bf16[256,128]{1,0:T(8,128)(2,1)S(1)}, u32[]{:S(2)}, u32[]{:S(2)}) collective-permute-start(bf16[256,128]{1,0:T(8,128)(2,1)S(1)} %add_convert_fusion), channel_id=1, source_target_pairs={{64,1},{65,2},{66,3},{67,4},{68,5},{69,6},{70,7},{71,8},{72,9},{73... | collective-permute-start | bytes 196616 | tf_op jit(solution)/shard_map/ppermute | solution.py:321
  85.6 19.9 %collective-permute-start.39 = (bf16[256,128]{1,0:T(8,128)(2,1)S(1)}, bf16[256,128]{1,0:T(8,128)(2,1)S(1)}, u32[]{:S(2)}, u32[]{:S(2)}) collective-permute-start(bf16[256,128]{1,0:T(8,128)(2,1)S(1)} %add_convert_fusion), channel_id=1, source_target_pairs={{64,2},{65,3},{66,4},{67,5},{68,6},{69,7},{70,8},{71,9},{72,10},{7... | collective-permute-start | bytes 196616 | tf_op jit(solution)/shard_map/ppermute | solution.py:321
  105.6 4.5 %collective-permute-start.42 = (bf16[256,384]{1,0:T(8,128)(2,1)S(1)}, bf16[256,384]{1,0:T(8,128)(2,1)S(1)}, u32[]{:S(2)}, u32[]{:S(2)}) collective-permute-start(bf16[256,384]{1,0:T(8,128)(2,1)S(1)} %maximum_add_fusion.mine), channel_id=1, source_target_pairs={{0,32},{1,33},{2,34},{3,35},{4,36},{5,37},{6,38},{7,39},{8,40},{9,... | collective-permute-start | bytes 589832 | tf_op jit(solution)/shard_map/ppermute | solution.py:321
  108.9 1.3 %collective-permute-start.43 = (bf16[256,128]{1,0:T(8,128)(2,1)S(1)}, bf16[256,128]{1,0:T(8,128)(2,1)S(1)}, u32[]{:S(2)}, u32[]{:S(2)}) collective-permute-start(bf16[256,128]{1,0:T(8,128)(2,1)S(1)} %collective-permute-done.36.refs_3_.near_l), channel_id=1, source_target_pairs={{0,32},{1,33},{2,34},{3,35},{4,36},{5,37},{6,38},{7,39},{8,40},{9,... | collective-permute-start | bytes 196616 | tf_op jit(solution)/shard_map/ppermute | solution.py:321

commit v4 on v3

--- a/solution.py
+++ b/solution.py
@@ -1,5 +1,3 @@
-import functools
-
 import jax
 import jax.numpy as jnp
 from jax import lax
@@ -63,8 +61,8 @@
                 (residual_in, residual),
                 (down_in, down_map),
                 (up_in, up_map),
-                (factor_in.at[:KMAX], factor.at[:KMAX]),
-                (factor_in.at[KMAX:last], factor.at[KMAX:last]),
+                (factor_in.at[:KMAX, :KMAX], factor.at[:KMAX, :KMAX]),
+                (factor_in.at[KMAX:last, :last], factor.at[KMAX:last, :last]),
                 (factor_in.at[last:], factor.at[last:]),
             ]
         )
@@ -181,25 +179,22 @@
 
 
 def share_kernel(
-    scalars, near, own, far, far_o, own_o, near_o, outer, outer_o, extra, extra_o, up0,
+    scalars, near, own, far, outer, outer_o, extra, extra_o, up0,
     forward, backward, reach, reach_start, even_rows, odd_rows, even_down, turn, even_start,
 ):
-    columns = own.shape[0] - 3 * FACE
+    columns = up0.shape[0]
+    end = columns + 3 * FACE
     first = scalars[0] == 0
 
     def split(mine, other):
         a, b = mine[columns:], turned(other[columns:])
         return jnp.where(first, a, b), jnp.where(first, b, a)
 
-    pairs = [split(near, far_o), split(own, own_o), split(far, near_o)]
-    even3, odd3 = [pair[0] for pair in pairs], [pair[1] for pair in pairs]
+    even3 = [near[columns:end], own[columns:end], turned(far[columns:end])]
+    odd3 = [near[end:], own[end:], turned(far[end:])]
     even_up, odd_down = split(outer, outer_o)
     even_mixed, odd_mixed = split(extra, extra_o)
-    down3 = [
-        jnp.where(first, mine[:columns], other[:columns])
-        for mine, other in ((near, far_o), (own, own_o), (far, near_o))
-    ]
-    down3 = jnp.concatenate(down3, axis=1)
+    down3 = jnp.concatenate([near[:columns], own[:columns], far[:columns]], axis=1)
     even_down[...] = down3
     for at in range(3):
         even_rows[at * 3 * FACE : (at + 1) * 3 * FACE] = even3[at]
@@ -233,29 +228,6 @@
     return jnp.concatenate([mine[:, : 2 * FACE], own, other[:, FACE : 2 * FACE], other[:, :FACE]], axis=1)
 
 
-def step_kernel(width, scalars, base, operator, reach, seen, reached, *refs):
-    pieces, (part, seen_out, reached_out) = refs[:width], refs[-3:]
-    start = reach.shape[0] - 5 * FACE
-    total = base[...]
-    between_total = reached[...]
-    for at in range(width):
-        piece = pieces[at][...]
-        total += dot(piece, block(operator, at))
-        here = at - (width - 3)
-        if here >= 0:
-            where = slice(here * FACE, (here + 1) * FACE)
-            seen_out[:, where] = seen[:, where] + piece
-            between_total += dot(piece, reach[start + here * FACE : start + (here + 1) * FACE])
-    part[...] = total
-    reached_out[...] = between_total
-
-
-def close_kernel(scalars, seen, near, own, turn, even_start, base):
-    total = dot(seen[:, FACE : 2 * FACE], block(turn, 0)) + dot(seen[:, 2 * FACE :], block(turn, 1))
-    total += dot(near[...], block(turn, 3))
-    base[...] = total + jnp.where(scalars[0] == 0, even_start[...] + dot(own[...], block(turn, 4)), 0.0)
-
-
 def between(base3, faces5, rows):
     found = []
     for m in range(3):
@@ -273,15 +245,13 @@
 
 
 def finish_kernel(
-    scalars, adjusted, near_basis, far_basis, down, mine, other, near, own, far, near_l, own_l, far_l,
-    odd_rows, factor_ref, out,
+    scalars, adjusted, near_basis, far_basis, down, mine, other, near, own, far, odd_rows, factor_ref, out
 ):
     first = scalars[0] == 0
     factor = factor_ref[...]
     faces = five(mine, other)
-    last = scalars[2] == 1
-    up3 = [jnp.where(last, late[...], early[...]) for early, late in ((near, near_l), (own, own_l), (far, far_l))]
-    inside = between(jnp.concatenate(up3, axis=1), faces, odd_rows[...])
+    up3 = jnp.concatenate([near[...], own[...], far[...]], axis=1)
+    inside = between(up3, faces, odd_rows[...])
     up = jnp.where(first, inside, faces[:, FACE : 4 * FACE])
 
     def side(at, basis):
@@ -341,6 +311,9 @@
 
     core = lax.axis_index("slab") % 2
     first = core == 0
+    def pick(on_first, on_second):
+        return jnp.where(first, on_first, on_second)
+
     last_chip = lax.axis_index("slab") // 2 == chips - 1
     residual = right_side[0, 0]
     factor = inverse_factor[0, 0]
@@ -354,20 +327,26 @@
     adjusted, near_basis, far_basis, message, outer, extra, up0 = local_operators(
         scalars, residual, near, far, maps
     )
-    near, far = from_near(message), from_far(message)
+
+    message_other = swap(message)
     outer_other = swap(outer)
+    mine, other = message[columns:], turned(message_other[columns:])
+    pack = jnp.concatenate(
+        [pick(message[:columns], message_other[:columns]), pick(mine, other), pick(other, mine)], axis=0
+    )
+    near = from_near(pack)
 
     def joined(part):
         return (part + swap(part)).astype(BF)
 
     nothing = jnp.zeros(face, F32)
-    down3 = jnp.concatenate([near[:columns], message[:columns], far[:columns]], axis=1)
-    start = outer_other[:columns].astype(F32) + dot(down3, turned(outer_other[columns:]))
-    base = jnp.where(first, start, nothing)
-    total = joined(base)
-    pieces = hop(total, 0, 1, 2)
-
-    near_other, own_other, far_other, extra_other = [swap(pack) for pack in (near, message, far, extra)]
+    odd_down = pick(turned(outer_other[columns:]), outer[columns:])
+    own_down = pick(pack[:columns], jnp.zeros(face, BF))
+    base = dot(jnp.concatenate([near[:columns], own_down], axis=1), odd_down[: 2 * FACE])
+    base = base + pick(outer_other[:columns].astype(F32), nothing)
+    pieces = hop(joined(base), 0, 1, 2)
+
+    far, extra_other = swap(near), swap(extra)
     rows = ((3 * three, FACE), BF)
     band = ((five_, FACE), BF)
     forward, backward, reach, reach_start, even_rows, odd_rows, even_down, turn, even_start = call(
@@ -375,60 +354,73 @@
         [band, band, ((columns + five_, FACE), BF), (face, F32), rows, rows, ((columns, three), BF),
          ((2 * three, FACE), BF), (face, F32)],
         scalars,
-        [near, message, far, far_other, own_other, near_other, outer, outer_other, extra, extra_other, up0],
-        (1 << 28, 4 << 20),
-    )
-
-    def step(pieces, base, operator, seen, reached, later=()):
-        width = len(pieces)
-        arrays = [base, operator, reach, seen, reached, *pieces, *later]
-        spaces = [VMEM] * (5 + width) + [pl.BlockSpec(memory_space=pl.ANY)] * len(later)
-        shapes = [(face, F32), ((columns, three), BF), (face, F32)]
-        return call(functools.partial(step_kernel, width), shapes, scalars, arrays, (1 << 26, 1 << 19), spaces)
-
-    unseen = jnp.zeros((columns, three), BF)
-    part, seen, reached = step(pieces, base, forward, unseen, nothing)
-    pieces = hop(joined(part), 1, 1, 2)
+        [near, pack, far, outer, outer_other, extra, extra_other, up0],
+        (1 << 10, 1 << 10),
+    )
+
+    def step(pieces, base, operator, *later, beside=()):
+        pieces, base, operator, later, beside = barrier((pieces, base, operator, later, list(beside)))
+        rows = jnp.concatenate([*pieces, *beside], axis=1)
+        part = base + dot(rows, operator[: rows.shape[1]])
+        part, pieces, beside = barrier((part, pieces, beside))
+        return joined(part), jnp.concatenate(pieces[-3:], axis=1), *later, *beside
+
+    def inward(seen):
+        return dot(seen, reach[columns : columns + three])
+
+    barrier = lax.optimization_barrier
+    total, seen = step(pieces, base, forward)
+    pieces = hop(total, 1, 1, 2)
     reach_near = from_near(reach)
-    part, seen, reached = step(pieces, base, forward, seen, reached, [reach_near])
-    pieces = hop(joined(part), 2, 1, 3)
+    total, new, reach_near, seen = step(pieces, base, forward, reach_near, seen)
+    pieces = hop(total, 2, 1, 3)
+    seen = seen + new
+    reached = inward(seen)
 
     operator, even_turn = call(
         turn_kernel,
         [((seven, FACE), BF), (face, F32)],
         scalars,
         [reach_near, reach, swap(reach_near), turn, even_start],
-        (1 << 28, 2 << 20),
+        (1 << 10, 1 << 10),
     )
     reached_other = swap(reached)
-    part, seen_all, reached_last = step(pieces, even_turn, operator, seen, nothing, [reached_other])
-    pieces = hop(joined(part), 3, -1, 2)
-
+    total, new, reached_other, operator = step(pieces, even_turn, operator, reached_other, operator)
+    pieces = hop(total, 3, -1, 2)
+
+    seen_all = seen + new
+    reached_last = inward(new)
+    last_other = swap(reached_last)
+    reached_other, last_other = barrier((reached_other, last_other))
     own = (reach_start + reached + reached_other).astype(BF)
     near = from_near(own)
-    base = call(close_kernel, [(face, F32)], scalars, [seen, near, own, turn, even_start], (1 << 27, 1 << 20))[0]
-    reached_other = swap(reached_last)
+    own_part = jnp.concatenate([seen[:, FACE:], pick(own, jnp.zeros(face, BF))], axis=1)
+    own_turn = jnp.concatenate([turn[: 2 * FACE], turn[4 * FACE : 5 * FACE]], axis=0)
+    near_turn = turn[3 * FACE : 4 * FACE]
+    base = pick(even_start, nothing) + dot(own_part, own_turn)
+    turned_back = jnp.concatenate([backward[:three], near_turn], axis=0)
+    total, seen, last_other, near = step(pieces, base, turned_back, last_other, beside=[near])
+    pieces = hop(total, 2, -1, 2)
+    base = base + dot(near, near_turn)
+
+    own_last = (reach_start + reached_last + last_other).astype(BF)
+    near_last = from_near(own_last)
     seen_other = swap(seen_all)
-    part, seen, _ = step(pieces, base, backward, unseen, nothing, [reached_other, seen_other])
-    pieces = hop(joined(part), 2, -1, 2)
-
-    own_last = (reach_start + reached_last + reached_other).astype(BF)
-    near_last = from_near(own_last)
-    far = swap(near)
     down = call(
-        faces_kernel, [((columns, three), BF)], scalars, [seen_all, seen_other, even_down, even_rows], (1 << 27, 1 << 20)
+        faces_kernel, [((columns, three), BF)], scalars, [seen_all, seen_other, even_down, even_rows], (1 << 10, 1 << 10)
     )[0]
-    part, seen, _ = step(pieces, base, backward, seen, nothing, [near_last, far, down])
-    pieces = hop(joined(part), 1, -1, 2)
-    far_last = swap(near_last)
+    total, new, near_last, down = step(pieces, base, backward, near_last, down)
+    pieces = hop(total, 1, -1, 2)
+    seen = seen + new
+    near, own = jnp.where(last_chip, near_last, near), jnp.where(last_chip, own_last, own)
+    pieces, seen, far = barrier((pieces, seen, swap(near)))
     seen = seen + jnp.concatenate(pieces, axis=1)
     out = call(
         finish_kernel,
         [((columns, M), F32)],
         scalars,
         [
-            adjusted, near_basis, far_basis, down, seen, swap(seen), near, own, far,
-            near_last, own_last, far_last, odd_rows, factor,
+            adjusted, near_basis, far_basis, down, seen, swap(seen), near, own, far, odd_rows, factor,
         ],
         (1 << 29, 4 << 20),
     )[0]

time: 113 us -> 107 us (0.947)
  Pallas kernels: 16.1 us -> 9.94 us
  matrix products: 0.2 us -> 1.92 us
    pallas_call x12 -> x6, Pallas kernels: 16.1 us -> 9.94 us  [call(): pl.pallas_call(kernel, out_shape=[jax.ShapeDtypeStruct(shape, kind) for s...]
    dot_general x1 -> x10, matrix products: 0.2 us -> 1.92 us  [dot(): lax.dot_general(a, b, (((1,), (0,)), ((), ())), preferred_element_type=F32)]
    ppermute x44 -> x41, starting transfers between devices: 60.4 us -> 59.3 us  [send(): return lax.ppermute(value, AXES, pairs)]
    ppermute x44 -> x41, waiting for transfers between devices: 34.4 us -> 33.3 us  [send(): return lax.ppermute(value, AXES, pairs)]
  transfers between devices with their start and end apart: 44 -> 41, of which waited for: 11 -> 13; matrix products, arithmetic and copies ran while one was open for 0% -> 1% of each run, Pallas kernels for 3% -> 3%
where the time goes in v4:
time: 107 us
  starting transfers between devices  59.3 us (55%)
  waiting for transfers between devices  33.3 us (31%)
  Pallas kernels  9.94 us (9%)
  matrix products  1.92 us (2%)
  between operations  1.32 us (1%)
    ppermute x41, starting transfers between devices, send(): return lax.ppermute(value, AXES, pairs)  59.3 us
    ppermute x41, waiting for transfers between devices, send(): return lax.ppermute(value, AXES, pairs)  33.3 us
    pallas_call x6, Pallas kernels, call(): pl.pallas_call(kernel, out_shape=[jax.ShapeDtypeStruct(shape, kind) for s...  9.94 us
  transfers between devices with their start and end apart: 41, of which 13 were waited for; matrix products, arithmetic and copies ran while one was open for 1% of the time, Pallas kernels for 3%

profile of v4, /device:TPU:1, one launch (start us, length us, event | category | flops | bytes accessed | tf_op | source)
XLA Modules:
  0.0 106.7 jit_solution(11783758387919364173)
XLA Ops:
  0.7 3.7 %shard_map.55 = (bf16[512,256]{1,0:T(8,128)(2,1)S(1)}, bf16[512,256]{1,0:T(8,128)(2,1)S(1)}, bf16[256,768]{1,0:T(8,128)(2,1)S(1)}) custom-call(s32[3]{0:T(128)S(1)} %pad_add_fusion.scalars, f32[256,768]{1,0:T(8,128)} %bitcast.15, bf16[768,768]{1,0:T(8,128)(2,1)} %bitcast.13, bf16[128,768]{1,0:T(8,128)(2,1)} %bitcast.17, bf16[128,768]{1,0:T(8,128)(2,1)} %bitcast.18), custom_call_target="tpu_custom_call" | custom-call | flops 1073741824 | bytes 3145728 | tf_op jit(solution)/shard_map/pallas_call | solution.py:42
  4.4 8.9 %collective-permute-start = (bf16[512,256]{1,0:T(8,128)(2,1)S(1)}, bf16[512,256]{1,0:T(8,128)(2,1)S(1)}, u32[]{:S(2)}, u32[]{:S(2)}) collective-permute-start(bf16[512,256]{1,0:T(8,128)(2,1)S(1)} %get-tuple-element.87), channel_id=1, source_target_pairs={{0,1},{1,2},{2,3},{3,4},{4,5},{5,6},{6,7},{7,8},{8,9},{9,10},{10,1... | collective-permute-start | bytes 786440 | tf_op jit(solution)/shard_map/ppermute | solution.py:291
  13.3 4.9 %collective-permute-done.near = bf16[512,256]{1,0:T(8,128)(2,1)S(1)} collective-permute-done((bf16[512,256]{1,0:T(8,128)(2,1)S(1)}, bf16[512,256]{1,0:T(8,128)(2,1)S(1)}, u32[]{:S(2)}, u32[]{:S(2)}) %collective-permute-start) | collective-permute-done | bytes 262176 | tf_op jit(solution)/shard_map/ppermute | solution.py:291
  18.2 3.7 %collective-permute-done.1.far = bf16[512,256]{1,0:T(8,128)(2,1)S(1)} collective-permute-done((bf16[512,256]{1,0:T(8,128)(2,1)S(1)}, bf16[512,256]{1,0:T(8,128)(2,1)S(1)}, u32[]{:S(2)}, u32[]{:S(2)}) %collective-permute-start.1) | collective-permute-done | bytes 262176 | tf_op jit(solution)/shard_map/ppermute | solution.py:291
  21.9 1.0 shard_map.56
  23.0 0.5 collective-permute-start.4
  23.5 0.9 collective-permute-done.2
  24.5 3.2 %collective-permute-start.3 = (bf16[1024,128]{1,0:T(8,128)(2,1)S(1)}, bf16[1024,128]{1,0:T(8,128)(2,1)S(1)}, u32[]{:S(2)}, u32[]{:S(2)}) collective-permute-start(bf16[1024,128]{1,0:T(8,128)(2,1)S(1)} %pad_maximum_fusion.own), channel_id=1, source_target_pairs={{0,1},{1,2},{2,3},{3,4},{4,5},{5,6},{6,7},{7,8},{8,9},{9,10},{10,1... | collective-permute-start | bytes 786440 | tf_op jit(solution)/shard_map/ppermute | solution.py:291
  27.7 3.3 %collective-permute-done.3.near = bf16[1024,128]{1,0:T(8,128)(2,1)S(1)} collective-permute-done((bf16[1024,128]{1,0:T(8,128)(2,1)S(1)}, bf16[1024,128]{1,0:T(8,128)(2,1)S(1)}, u32[]{:S(2)}, u32[]{:S(2)}) %collective-permute-start.3) | collective-permute-done | bytes 262176 | tf_op jit(solution)/shard_map/ppermute | solution.py:291
  31.2 3.5 %collective-permute-start.5 = (f32[256,128]{1,0:T(8,128)S(1)}, f32[256,128]{1,0:T(8,128)S(1)}, u32[]{:S(2)}, u32[]{:S(2)}) collective-permute-start(f32[256,128]{1,0:T(8,128)S(1)} %convolution_add_fusion), channel_id=1, source_target_pairs={{0,32},{1,33},{2,34},{3,35},{4,36},{5,37},{6,38},{7,39},{8,40},{9,... | collective-permute-start | bytes 393224 | tf_op jit(solution)/shard_map/ppermute | solution.py:291
  35.7 1.9 %collective-permute-start.6 = (bf16[256,128]{1,0:T(8,128)(2,1)S(1)}, bf16[256,128]{1,0:T(8,128)(2,1)S(1)}, u32[]{:S(2)}, u32[]{:S(2)}) collective-permute-start(bf16[256,128]{1,0:T(8,128)(2,1)S(1)} %add_convert_fusion.7), channel_id=1, source_target_pairs={{0,66},{1,67},{2,68},{3,69},{4,70},{5,71},{6,72},{7,73},{8,74},{9,... | collective-permute-start | bytes 196616 | tf_op jit(solution)/shard_map/ppermute | solution.py:291
  37.6 4.5 %collective-permute-start.7 = (bf16[256,128]{1,0:T(8,128)(2,1)S(1)}, bf16[256,128]{1,0:T(8,128)(2,1)S(1)}, u32[]{:S(2)}, u32[]{:S(2)}) collective-permute-start(bf16[256,128]{1,0:T(8,128)(2,1)S(1)} %add_convert_fusion.7), channel_id=1, source_target_pairs={{0,65},{1,66},{2,67},{3,68},{4,69},{5,70},{6,71},{7,72},{8,73},{9,... | collective-permute-start | bytes 196616 | tf_op jit(solution)/shard_map/ppermute | solution.py:291
  42.0 0.7 collective-permute-start.8
  42.7 1.1 shard_map.57
  44.3 4.5 %collective-permute-start.15 = (bf16[896,128]{1,0:T(8,128)(2,1)S(1)}, bf16[896,128]{1,0:T(8,128)(2,1)S(1)}, u32[]{:S(2)}, u32[]{:S(2)}) collective-permute-start(bf16[896,128]{1,0:T(8,128)(2,1)S(1)} %get-tuple-element.104.own), channel_id=1, source_target_pairs={{0,1},{1,2},{2,3},{3,4},{4,5},{5,6},{6,7},{7,8},{8,9},{9,10},{10,1... | collective-permute-start | bytes 688136 | tf_op jit(solution)/shard_map/ppermute | solution.py:291
  48.8 0.7 collective-permute-start.12
  49.5 0.7 collective-permute-start.13
  50.2 0.7 collective-permute-start.14
  50.9 0.8 collective-permute-done.15.near
  52.0 2.4 %collective-permute-start.16 = (f32[256,128]{1,0:T(8,128)S(1)}, f32[256,128]{1,0:T(8,128)S(1)}, u32[]{:S(2)}, u32[]{:S(2)}) collective-permute-start(f32[256,128]{1,0:T(8,128)S(1)} %add.76), channel_id=1, source_target_pairs={{0,32},{1,33},{2,34},{3,35},{4,36},{5,37},{6,38},{7,39},{8,40},{9,... | collective-permute-start | bytes 393224 | tf_op jit(solution)/shard_map/ppermute | solution.py:291
  54.7 0.5 collective-permute-start.21
  55.3 0.7 collective-permute-start.17
  56.0 0.7 collective-permute-start.18
  56.7 0.7 collective-permute-start.19
  57.3 0.8 collective-permute-start.20
  58.2 0.9 shard_map.58
  60.8 0.6 collective-permute-done.23
  61.4 0.7 collective-permute-start.24
  62.0 0.7 collective-permute-start.25
  62.7 0.7 collective-permute-start.26
  63.4 3.3 %collective-permute-start.28 = (bf16[256,128]{1,0:T(8,128)(2,1)S(1)}, bf16[256,128]{1,0:T(8,128)(2,1)S(1)}, u32[]{:S(2)}, u32[]{:S(2)}) collective-permute-start(bf16[256,128]{1,0:T(8,128)(2,1)S(1)} %get-tuple-element.172), channel_id=1, source_target_pairs={{0,1},{1,2},{2,3},{3,4},{4,5},{5,6},{6,7},{7,8},{8,9},{9,10},{10,1... | collective-permute-start | bytes 196616 | tf_op jit(solution)/shard_map/ppermute | solution.py:291
  67.0 1.1 %collective-permute-done.28 = bf16[256,128]{1,0:T(8,128)(2,1)S(1)} collective-permute-done((bf16[256,128]{1,0:T(8,128)(2,1)S(1)}, bf16[256,128]{1,0:T(8,128)(2,1)S(1)}, u32[]{:S(2)}, u32[]{:S(2)}) %collective-permute-start.28) | collective-permute-done | bytes 65568 | tf_op jit(solution)/shard_map/ppermute | solution.py:291
  68.3 3.4 %collective-permute-start.29 = (f32[256,128]{1,0:T(8,128)S(1)}, f32[256,128]{1,0:T(8,128)S(1)}, u32[]{:S(2)}, u32[]{:S(2)}) collective-permute-start(f32[256,128]{1,0:T(8,128)S(1)} %add.84), channel_id=1, source_target_pairs={{0,32},{1,33},{2,34},{3,35},{4,36},{5,37},{6,38},{7,39},{8,40},{9,... | collective-permute-start | bytes 393224 | tf_op jit(solution)/shard_map/ppermute | solution.py:291
  71.8 1.9 %collective-permute-start.33 = (bf16[256,128]{1,0:T(8,128)(2,1)S(1)}, bf16[256,128]{1,0:T(8,128)(2,1)S(1)}, u32[]{:S(2)}, u32[]{:S(2)}) collective-permute-start(bf16[256,128]{1,0:T(8,128)(2,1)S(1)} %get-tuple-element.170), channel_id=1, source_target_pairs={{0,1},{1,2},{2,3},{3,4},{4,5},{5,6},{6,7},{7,8},{8,9},{9,10},{10,1... | collective-permute-start | bytes 196616 | tf_op jit(solution)/shard_map/ppermute | solution.py:291
  73.7 0.7 collective-permute-start.30
  74.4 0.7 collective-permute-start.31
  75.0 0.7 collective-permute-start.32
  75.9 0.9 shard_map.59.down
  77.0 2.8 %collective-permute-start.35 = (f32[256,128]{1,0:T(8,128)S(1)}, f32[256,128]{1,0:T(8,128)S(1)}, u32[]{:S(2)}, u32[]{:S(2)}) collective-permute-start(f32[256,128]{1,0:T(8,128)S(1)} %add.90), channel_id=1, source_target_pairs={{0,32},{1,33},{2,34},{3,35},{4,36},{5,37},{6,38},{7,39},{8,40},{9,... | collective-permute-start | bytes 393224 | tf_op jit(solution)/shard_map/ppermute | solution.py:291
  79.9 0.9 collective-permute-done.35
  80.8 1.3 %collective-permute-start.36 = (bf16[256,128]{1,0:T(8,128)(2,1)S(1)}, bf16[256,128]{1,0:T(8,128)(2,1)S(1)}, u32[]{:S(2)}, u32[]{:S(2)}) collective-permute-start(bf16[256,128]{1,0:T(8,128)(2,1)S(1)} %add_convert_fusion), channel_id=1, source_target_pairs={{64,2},{65,3},{66,4},{67,5},{68,6},{69,7},{70,8},{71,9},{72,10},{7... | collective-permute-start | bytes 196616 | tf_op jit(solution)/shard_map/ppermute | solution.py:291
  82.1 1.3 %collective-permute-start.37 = (bf16[256,128]{1,0:T(8,128)(2,1)S(1)}, bf16[256,128]{1,0:T(8,128)(2,1)S(1)}, u32[]{:S(2)}, u32[]{:S(2)}) collective-permute-start(bf16[256,128]{1,0:T(8,128)(2,1)S(1)} %add_convert_fusion), channel_id=1, source_target_pairs={{64,1},{65,2},{66,3},{67,4},{68,5},{69,6},{70,7},{71,8},{72,9},{73... | collective-permute-start | bytes 196616 | tf_op jit(solution)/shard_map/ppermute | solution.py:291
  83.4 0.7 collective-permute-start.38
  84.1 12.6 %collective-permute-done.36 = bf16[256,128]{1,0:T(8,128)(2,1)S(1)} collective-permute-done((bf16[256,128]{1,0:T(8,128)(2,1)S(1)}, bf16[256,128]{1,0:T(8,128)(2,1)S(1)}, u32[]{:S(2)}, u32[]{:S(2)}) %collective-permute-start.36) | collective-permute-done | bytes 65568 | tf_op jit(solution)/shard_map/ppermute | solution.py:291
  96.7 3.0 %collective-permute-done.37 = bf16[256,128]{1,0:T(8,128)(2,1)S(1)} collective-permute-done((bf16[256,128]{1,0:T(8,128)(2,1)S(1)}, bf16[256,128]{1,0:T(8,128)(2,1)S(1)}, u32[]{:S(2)}, u32[]{:S(2)}) %collective-permute-start.37) | collective-permute-done | bytes 65568 | tf_op jit(solution)/shard_map/ppermute | solution.py:291
  99.8 3.4 %collective-permute-start.40 = (bf16[256,384]{1,0:T(8,128)(2,1)S(1)}, bf16[256,384]{1,0:T(8,128)(2,1)S(1)}, u32[]{:S(2)}, u32[]{:S(2)}) collective-permute-start(bf16[256,384]{1,0:T(8,128)(2,1)S(1)} %maximum_add_fusion.2.mine), channel_id=1, source_target_pairs={{0,32},{1,33},{2,34},{3,35},{4,36},{5,37},{6,38},{7,39},{8,40},{9,... | collective-permute-start | bytes 589832 | tf_op jit(solution)/shard_map/ppermute | solution.py:291
  103.2 1.1 %collective-permute-done.40.other = bf16[256,384]{1,0:T(8,128)(2,1)S(1)} collective-permute-done((bf16[256,384]{1,0:T(8,128)(2,1)S(1)}, bf16[256,384]{1,0:T(8,128)(2,1)S(1)}, u32[]{:S(2)}, u32[]{:S(2)}) %collective-permute-start.40) | collective-permute-done | bytes 196640 | tf_op jit(solution)/shard_map/ppermute | solution.py:291
  104.2 2.5 %shard_map.60 = f32[256,768]{1,0:T(8,128)} custom-call(s32[3]{0:T(128)S(1)} %pad_add_fusion.scalars, f32[256,768]{1,0:T(8,128)S(1)} %get-tuple-element.90.adjusted, bf16[256,256]{1,0:T(8,128)(2,1)S(1)} %get-tuple-element.91.near_basis, bf16[256,256]{1,0:T(8,128)(2,1)S(1)} %get-tuple-element.92.far_basis, bf16[256,384]{1,0:T(8,128)(2,1)S(1)} %shard_map.59.down, ...), custom_call_target="tpu_custom_call" | custom-call | flops 536870912 | bytes 4194304 | tf_op jit(solution)/shard_map/pallas_call | solution.py:42
  (92 shorter events, 5.5 us)
Async XLA Ops:
  0.7 21.2 %copy-start.1 = (f32[1,1,256,768]{3,2,1,0:T(8,128)S(1)}, f32[1,1,256,768]{3,2,1,0:T(8,128)}, u32[]{:S(2)}) copy-start(f32[1,1,256,768]{3,2,1,0:T(8,128)} %param.5) | copy-start | bytes 2359300
  4.4 13.8 %collective-permute-start = (bf16[512,256]{1,0:T(8,128)(2,1)S(1)}, bf16[512,256]{1,0:T(8,128)(2,1)S(1)}, u32[]{:S(2)}, u32[]{:S(2)}) collective-permute-start(bf16[512,256]{1,0:T(8,128)(2,1)S(1)} %get-tuple-element.87), channel_id=1, source_target_pairs={{0,1},{1,2},{2,3},{3,4},{4,5},{5,6},{6,7},{7,8},{8,9},{9,10},{10,1... | collective-permute-start | bytes 786440 | tf_op jit(solution)/shard_map/ppermute | solution.py:291
  13.3 8.5 %collective-permute-start.1 = (bf16[512,256]{1,0:T(8,128)(2,1)S(1)}, bf16[512,256]{1,0:T(8,128)(2,1)S(1)}, u32[]{:S(2)}, u32[]{:S(2)}) collective-permute-start(bf16[512,256]{1,0:T(8,128)(2,1)S(1)} %get-tuple-element.88), channel_id=1, source_target_pairs={{0,31},{1,0},{2,1},{3,2},{4,3},{5,4},{6,5},{7,6},{8,7},{9,8},{10,9... | collective-permute-start | bytes 786440 | tf_op jit(solution)/shard_map/ppermute | solution.py:291
  22.9 1.5 %collective-permute-start.2 = (bf16[640,128]{1,0:T(8,128)(2,1)S(1)}, bf16[640,128]{1,0:T(8,128)(2,1)S(1)}, u32[]{:S(2)}, u32[]{:S(2)}) collective-permute-start(bf16[640,128]{1,0:T(8,128)(2,1)S(1)} %get-tuple-element.93), channel_id=1, source_target_pairs={{0,32},{1,33},{2,34},{3,35},{4,36},{5,37},{6,38},{7,39},{8,40},{9,... | collective-permute-start | bytes 491528 | tf_op jit(solution)/shard_map/ppermute | solution.py:291
  23.0 4.7 %collective-permute-start.4 = (bf16[640,128]{1,0:T(8,128)(2,1)S(1)}, bf16[640,128]{1,0:T(8,128)(2,1)S(1)}, u32[]{:S(2)}, u32[]{:S(2)}) collective-permute-start(bf16[640,128]{1,0:T(8,128)(2,1)S(1)} %get-tuple-element.94.outer), channel_id=1, source_target_pairs={{0,32},{1,33},{2,34},{3,35},{4,36},{5,37},{6,38},{7,39},{8,40},{9,... | collective-permute-start | bytes 491528 | tf_op jit(solution)/shard_map/ppermute | solution.py:291
  24.5 6.5 %collective-permute-start.3 = (bf16[1024,128]{1,0:T(8,128)(2,1)S(1)}, bf16[1024,128]{1,0:T(8,128)(2,1)S(1)}, u32[]{:S(2)}, u32[]{:S(2)}) collective-permute-start(bf16[1024,128]{1,0:T(8,128)(2,1)S(1)} %pad_maximum_fusion.own), channel_id=1, source_target_pairs={{0,1},{1,2},{2,3},{3,4},{4,5},{5,6},{6,7},{7,8},{8,9},{9,10},{10,1... | collective-permute-start | bytes 786440 | tf_op jit(solution)/shard_map/ppermute | solution.py:291
  31.2 4.5 %collective-permute-start.5 = (f32[256,128]{1,0:T(8,128)S(1)}, f32[256,128]{1,0:T(8,128)S(1)}, u32[]{:S(2)}, u32[]{:S(2)}) collective-permute-start(f32[256,128]{1,0:T(8,128)S(1)} %convolution_add_fusion), channel_id=1, source_target_pairs={{0,32},{1,33},{2,34},{3,35},{4,36},{5,37},{6,38},{7,39},{8,40},{9,... | collective-permute-start | bytes 393224 | tf_op jit(solution)/shard_map/ppermute | solution.py:291
  34.7 8.0 %collective-permute-start.10 = (bf16[640,128]{1,0:T(8,128)(2,1)S(1)}, bf16[640,128]{1,0:T(8,128)(2,1)S(1)}, u32[]{:S(2)}, u32[]{:S(2)}) collective-permute-start(bf16[640,128]{1,0:T(8,128)(2,1)S(1)} %get-tuple-element.95.extra), channel_id=1, source_target_pairs={{0,32},{1,33},{2,34},{3,35},{4,36},{5,37},{6,38},{7,39},{8,40},{9,... | collective-permute-start | bytes 491528 | tf_op jit(solution)/shard_map/ppermute | solution.py:291
  34.8 7.9 %collective-permute-start.9 = (bf16[1024,128]{1,0:T(8,128)(2,1)S(1)}, bf16[1024,128]{1,0:T(8,128)(2,1)S(1)}, u32[]{:S(2)}, u32[]{:S(2)}) collective-permute-start(bf16[1024,128]{1,0:T(8,128)(2,1)S(1)} %collective-permute-done.3.near), channel_id=1, source_target_pairs={{0,32},{1,33},{2,34},{3,35},{4,36},{5,37},{6,38},{7,39},{8,40},{9,... | collective-permute-start | bytes 786440 | tf_op jit(solution)/shard_map/ppermute | solution.py:291
  35.7 8.1 %collective-permute-start.6 = (bf16[256,128]{1,0:T(8,128)(2,1)S(1)}, bf16[256,128]{1,0:T(8,128)(2,1)S(1)}, u32[]{:S(2)}, u32[]{:S(2)}) collective-permute-start(bf16[256,128]{1,0:T(8,128)(2,1)S(1)} %add_convert_fusion.7), channel_id=1, source_target_pairs={{0,66},{1,67},{2,68},{3,69},{4,70},{5,71},{6,72},{7,73},{8,74},{9,... | collective-permute-start | bytes 196616 | tf_op jit(solution)/shard_map/ppermute | solution.py:291
  37.6 6.3 %collective-permute-start.7 = (bf16[256,128]{1,0:T(8,128)(2,1)S(1)}, bf16[256,128]{1,0:T(8,128)(2,1)S(1)}, u32[]{:S(2)}, u32[]{:S(2)}) collective-permute-start(bf16[256,128]{1,0:T(8,128)(2,1)S(1)} %add_convert_fusion.7), channel_id=1, source_target_pairs={{0,65},{1,66},{2,67},{3,68},{4,69},{5,70},{6,71},{7,72},{8,73},{9,... | collective-permute-start | bytes 196616 | tf_op jit(solution)/shard_map/ppermute | solution.py:291
  42.0 1.8 %collective-permute-start.8 = (bf16[256,128]{1,0:T(8,128)(2,1)S(1)}, bf16[256,128]{1,0:T(8,128)(2,1)S(1)}, u32[]{:S(2)}, u32[]{:S(2)}) collective-permute-start(bf16[256,128]{1,0:T(8,128)(2,1)S(1)} %add_convert_fusion.7), channel_id=1, source_target_pairs={{0,64},{1,65},{2,66},{3,67},{4,68},{5,69},{6,70},{7,71},{8,72},{9,... | collective-permute-start | bytes 196616 | tf_op jit(solution)/shard_map/ppermute | solution.py:291
  44.1 4.7 %collective-permute-start.11 = (f32[256,128]{1,0:T(8,128)S(1)}, f32[256,128]{1,0:T(8,128)S(1)}, u32[]{:S(2)}, u32[]{:S(2)}) collective-permute-start(f32[256,128]{1,0:T(8,128)S(1)} %add.74), channel_id=1, source_target_pairs={{0,32},{1,33},{2,34},{3,35},{4,36},{5,37},{6,38},{7,39},{8,40},{9,... | collective-permute-start | bytes 393224 | tf_op jit(solution)/shard_map/ppermute | solution.py:291
  44.3 7.5 %collective-permute-start.15 = (bf16[896,128]{1,0:T(8,128)(2,1)S(1)}, bf16[896,128]{1,0:T(8,128)(2,1)S(1)}, u32[]{:S(2)}, u32[]{:S(2)}) collective-permute-start(bf16[896,128]{1,0:T(8,128)(2,1)S(1)} %get-tuple-element.104.own), channel_id=1, source_target_pairs={{0,1},{1,2},{2,3},{3,4},{4,5},{5,6},{6,7},{7,8},{8,9},{9,10},{10,1... | collective-permute-start | bytes 688136 | tf_op jit(solution)/shard_map/ppermute | solution.py:291
  48.8 2.1 %collective-permute-start.12 = (bf16[256,128]{1,0:T(8,128)(2,1)S(1)}, bf16[256,128]{1,0:T(8,128)(2,1)S(1)}, u32[]{:S(2)}, u32[]{:S(2)}) collective-permute-start(bf16[256,128]{1,0:T(8,128)(2,1)S(1)} %add_convert_fusion.6), channel_id=1, source_target_pairs={{64,130},{65,131},{66,132},{67,133},{68,134},{69,135},{70,136},{71... | collective-permute-start | bytes 196616 | tf_op jit(solution)/shard_map/ppermute | solution.py:291
  49.5 1.4 %collective-permute-start.13 = (bf16[256,128]{1,0:T(8,128)(2,1)S(1)}, bf16[256,128]{1,0:T(8,128)(2,1)S(1)}, u32[]{:S(2)}, u32[]{:S(2)}) collective-permute-start(bf16[256,128]{1,0:T(8,128)(2,1)S(1)} %add_convert_fusion.6), channel_id=1, source_target_pairs={{64,129},{65,130},{66,131},{67,132},{68,133},{69,134},{70,135},{71... | collective-permute-start | bytes 196616 | tf_op jit(solution)/shard_map/ppermute | solution.py:291
  50.2 0.7 collective-permute-start.14
  52.0 3.3 %collective-permute-start.16 = (f32[256,128]{1,0:T(8,128)S(1)}, f32[256,128]{1,0:T(8,128)S(1)}, u32[]{:S(2)}, u32[]{:S(2)}) collective-permute-start(f32[256,128]{1,0:T(8,128)S(1)} %add.76), channel_id=1, source_target_pairs={{0,32},{1,33},{2,34},{3,35},{4,36},{5,37},{6,38},{7,39},{8,40},{9,... | collective-permute-start | bytes 393224 | tf_op jit(solution)/shard_map/ppermute | solution.py:291
  54.4 5.1 %copy-start.2 = (bf16[256,384]{1,0:T(8,128)(2,1)}, bf16[256,384]{1,0:T(8,128)(2,1)S(1)}, u32[]{:S(2)}) copy-start(bf16[256,384]{1,0:T(8,128)(2,1)S(1)} %maximum_add_fusion) | copy-start | bytes 589828
  54.6 4.5 %collective-permute-start.22 = (f32[256,128]{1,0:T(8,128)S(1)}, f32[256,128]{1,0:T(8,128)S(1)}, u32[]{:S(2)}, u32[]{:S(2)}) collective-permute-start(f32[256,128]{1,0:T(8,128)S(1)} %fusion.54), channel_id=1, source_target_pairs={{0,32},{1,33},{2,34},{3,35},{4,36},{5,37},{6,38},{7,39},{8,40},{9,... | collective-permute-start | bytes 393224 | tf_op jit(solution)/shard_map/ppermute | solution.py:291
  54.7 2.6 %collective-permute-start.21 = (bf16[896,128]{1,0:T(8,128)(2,1)S(1)}, bf16[896,128]{1,0:T(8,128)(2,1)S(1)}, u32[]{:S(2)}, u32[]{:S(2)}) collective-permute-start(bf16[896,128]{1,0:T(8,128)(2,1)S(1)} %collective-permute-done.15.near), channel_id=1, source_target_pairs={{0,32},{1,33},{2,34},{3,35},{4,36},{5,37},{6,38},{7,39},{8,40},{9,... | collective-permute-start | bytes 688136 | tf_op jit(solution)/shard_map/ppermute | solution.py:291
  55.3 3.8 %collective-permute-start.17 = (bf16[256,128]{1,0:T(8,128)(2,1)S(1)}, bf16[256,128]{1,0:T(8,128)(2,1)S(1)}, u32[]{:S(2)}, u32[]{:S(2)}) collective-permute-start(bf16[256,128]{1,0:T(8,128)(2,1)S(1)} %add_convert_fusion.5), channel_id=1, source_target_pairs={{128,195},{129,196},{130,197},{131,198},{132,199},{133,200},{134,2... | collective-permute-start | bytes 196616 | tf_op jit(solution)/shard_map/ppermute | solution.py:291
  56.0 3.1 %collective-permute-start.18 = (bf16[256,128]{1,0:T(8,128)(2,1)S(1)}, bf16[256,128]{1,0:T(8,128)(2,1)S(1)}, u32[]{:S(2)}, u32[]{:S(2)}) collective-permute-start(bf16[256,128]{1,0:T(8,128)(2,1)S(1)} %add_convert_fusion.5), channel_id=1, source_target_pairs={{128,194},{129,195},{130,196},{131,197},{132,198},{133,199},{134,2... | collective-permute-start | bytes 196616 | tf_op jit(solution)/shard_map/ppermute | solution.py:291
  56.7 2.5 %collective-permute-start.19 = (bf16[256,128]{1,0:T(8,128)(2,1)S(1)}, bf16[256,128]{1,0:T(8,128)(2,1)S(1)}, u32[]{:S(2)}, u32[]{:S(2)}) collective-permute-start(bf16[256,128]{1,0:T(8,128)(2,1)S(1)} %add_convert_fusion.5), channel_id=1, source_target_pairs={{128,193},{129,194},{130,195},{131,196},{132,197},{133,198},{134,1... | collective-permute-start | bytes 196616 | tf_op jit(solution)/shard_map/ppermute | solution.py:291
  57.3 1.8 %collective-permute-start.20 = (bf16[256,128]{1,0:T(8,128)(2,1)S(1)}, bf16[256,128]{1,0:T(8,128)(2,1)S(1)}, u32[]{:S(2)}, u32[]{:S(2)}) collective-permute-start(bf16[256,128]{1,0:T(8,128)(2,1)S(1)} %add_convert_fusion.5), channel_id=1, source_target_pairs={{128,192},{129,193},{130,194},{131,195},{132,196},{133,197},{134,1... | collective-permute-start | bytes 196616 | tf_op jit(solution)/shard_map/ppermute | solution.py:291
  59.5 7.2 %slice-start = ((bf16[256,384]{1,0:T(8,128)(2,1)}), bf16[256,256]{1,0:T(8,128)(2,1)S(1)}, s32[]{:S(2)}) async-start(bf16[256,384]{1,0:T(8,128)(2,1)} %copy-done.2), calls=%async_computation | async-start | bytes 262144 | tf_op jit(solution)/shard_map/slice | solution.py:397
  59.5 16.3 %collective-permute-start.34 = (bf16[256,384]{1,0:T(8,128)(2,1)S(1)}, bf16[256,384]{1,0:T(8,128)(2,1)S(1)}, u32[]{:S(2)}, u32[]{:S(2)}) collective-permute-start(bf16[256,384]{1,0:T(8,128)(2,1)S(1)} %add.89.mine), channel_id=1, source_target_pairs={{0,32},{1,33},{2,34},{3,35},{4,36},{5,37},{6,38},{7,39},{8,40},{9,... | collective-permute-start | bytes 589832 | tf_op jit(solution)/shard_map/ppermute | solution.py:291
  60.0 1.3 %collective-permute-start.23 = (f32[256,128]{1,0:T(8,128)S(1)}, f32[256,128]{1,0:T(8,128)S(1)}, u32[]{:S(2)}, u32[]{:S(2)}) collective-permute-start(f32[256,128]{1,0:T(8,128)S(1)} %add.79), channel_id=1, source_target_pairs={{0,32},{1,33},{2,34},{3,35},{4,36},{5,37},{6,38},{7,39},{8,40},{9,... | collective-permute-start | bytes 393224 | tf_op jit(solution)/shard_map/ppermute | solution.py:291
  60.3 3.0 %collective-permute-start.27 = (f32[256,128]{1,0:T(8,128)S(1)}, f32[256,128]{1,0:T(8,128)S(1)}, u32[]{:S(2)}, u32[]{:S(2)}) collective-permute-start(f32[256,128]{1,0:T(8,128)S(1)} %fusion.52), channel_id=1, source_target_pairs={{0,32},{1,33},{2,34},{3,35},{4,36},{5,37},{6,38},{7,39},{8,40},{9,... | collective-permute-start | bytes 393224 | tf_op jit(solution)/shard_map/ppermute | solution.py:291
  61.4 6.7 %collective-permute-start.24 = (bf16[256,128]{1,0:T(8,128)(2,1)S(1)}, bf16[256,128]{1,0:T(8,128)(2,1)S(1)}, u32[]{:S(2)}, u32[]{:S(2)}) collective-permute-start(bf16[256,128]{1,0:T(8,128)(2,1)S(1)} %add_convert_fusion.4), channel_id=1, source_target_pairs={{192,130},{193,131},{194,132},{195,133},{196,134},{197,135},{198,1... | collective-permute-start | bytes 196616 | tf_op jit(solution)/shard_map/ppermute | solution.py:291
  62.0 6.0 %collective-permute-start.25 = (bf16[256,128]{1,0:T(8,128)(2,1)S(1)}, bf16[256,128]{1,0:T(8,128)(2,1)S(1)}, u32[]{:S(2)}, u32[]{:S(2)}) collective-permute-start(bf16[256,128]{1,0:T(8,128)(2,1)S(1)} %add_convert_fusion.4), channel_id=1, source_target_pairs={{192,129},{193,130},{194,131},{195,132},{196,133},{197,134},{198,1... | collective-permute-start | bytes 196616 | tf_op jit(solution)/shard_map/ppermute | solution.py:291
  62.7 5.4 %collective-permute-start.26 = (bf16[256,128]{1,0:T(8,128)(2,1)S(1)}, bf16[256,128]{1,0:T(8,128)(2,1)S(1)}, u32[]{:S(2)}, u32[]{:S(2)}) collective-permute-start(bf16[256,128]{1,0:T(8,128)(2,1)S(1)} %add_convert_fusion.4), channel_id=1, source_target_pairs={{192,128},{193,129},{194,130},{195,131},{196,132},{197,133},{198,1... | collective-permute-start | bytes 196616 | tf_op jit(solution)/shard_map/ppermute | solution.py:291
  63.4 4.6 %collective-permute-start.28 = (bf16[256,128]{1,0:T(8,128)(2,1)S(1)}, bf16[256,128]{1,0:T(8,128)(2,1)S(1)}, u32[]{:S(2)}, u32[]{:S(2)}) collective-permute-start(bf16[256,128]{1,0:T(8,128)(2,1)S(1)} %get-tuple-element.172), channel_id=1, source_target_pairs={{0,1},{1,2},{2,3},{3,4},{4,5},{5,6},{6,7},{7,8},{8,9},{9,10},{10,1... | collective-permute-start | bytes 196616 | tf_op jit(solution)/shard_map/ppermute | solution.py:291
  68.3 5.3 %collective-permute-start.29 = (f32[256,128]{1,0:T(8,128)S(1)}, f32[256,128]{1,0:T(8,128)S(1)}, u32[]{:S(2)}, u32[]{:S(2)}) collective-permute-start(f32[256,128]{1,0:T(8,128)S(1)} %add.84), channel_id=1, source_target_pairs={{0,32},{1,33},{2,34},{3,35},{4,36},{5,37},{6,38},{7,39},{8,40},{9,... | collective-permute-start | bytes 393224 | tf_op jit(solution)/shard_map/ppermute | solution.py:291
  71.8 5.0 %collective-permute-start.33 = (bf16[256,128]{1,0:T(8,128)(2,1)S(1)}, bf16[256,128]{1,0:T(8,128)(2,1)S(1)}, u32[]{:S(2)}, u32[]{:S(2)}) collective-permute-start(bf16[256,128]{1,0:T(8,128)(2,1)S(1)} %get-tuple-element.170), channel_id=1, source_target_pairs={{0,1},{1,2},{2,3},{3,4},{4,5},{5,6},{6,7},{7,8},{8,9},{9,10},{10,1... | collective-permute-start | bytes 196616 | tf_op jit(solution)/shard_map/ppermute | solution.py:291
  73.7 3.1 %collective-permute-start.30 = (bf16[256,128]{1,0:T(8,128)(2,1)S(1)}, bf16[256,128]{1,0:T(8,128)(2,1)S(1)}, u32[]{:S(2)}, u32[]{:S(2)}) collective-permute-start(bf16[256,128]{1,0:T(8,128)(2,1)S(1)} %add_convert_fusion.2), channel_id=1, source_target_pairs={{128,66},{129,67},{130,68},{131,69},{132,70},{133,71},{134,72},{13... | collective-permute-start | bytes 196616 | tf_op jit(solution)/shard_map/ppermute | solution.py:291
  74.4 2.4 %collective-permute-start.31 = (bf16[256,128]{1,0:T(8,128)(2,1)S(1)}, bf16[256,128]{1,0:T(8,128)(2,1)S(1)}, u32[]{:S(2)}, u32[]{:S(2)}) collective-permute-start(bf16[256,128]{1,0:T(8,128)(2,1)S(1)} %add_convert_fusion.2), channel_id=1, source_target_pairs={{128,65},{129,66},{130,67},{131,68},{132,69},{133,70},{134,71},{13... | collective-permute-start | bytes 196616 | tf_op jit(solution)/shard_map/ppermute | solution.py:291
  75.0 1.7 %collective-permute-start.32 = (bf16[256,128]{1,0:T(8,128)(2,1)S(1)}, bf16[256,128]{1,0:T(8,128)(2,1)S(1)}, u32[]{:S(2)}, u32[]{:S(2)}) collective-permute-start(bf16[256,128]{1,0:T(8,128)(2,1)S(1)} %add_convert_fusion.2), channel_id=1, source_target_pairs={{128,64},{129,65},{130,66},{131,67},{132,68},{133,69},{134,70},{13... | collective-permute-start | bytes 196616 | tf_op jit(solution)/shard_map/ppermute | solution.py:291
  77.0 27.3 %copy-start = (bf16[1,1,768,768]{3,2,1,0:T(8,128)(2,1)S(1)}, bf16[1,1,768,768]{3,2,1,0:T(8,128)(2,1)}, u32[]{:S(2)}) copy-start(bf16[1,1,768,768]{3,2,1,0:T(8,128)(2,1)} %param.6) | copy-start | bytes 3538948
  77.0 3.8 %collective-permute-start.35 = (f32[256,128]{1,0:T(8,128)S(1)}, f32[256,128]{1,0:T(8,128)S(1)}, u32[]{:S(2)}, u32[]{:S(2)}) collective-permute-start(f32[256,128]{1,0:T(8,128)S(1)} %add.90), channel_id=1, source_target_pairs={{0,32},{1,33},{2,34},{3,35},{4,36},{5,37},{6,38},{7,39},{8,40},{9,... | collective-permute-start | bytes 393224 | tf_op jit(solution)/shard_map/ppermute | solution.py:291
  79.8 4.3 %collective-permute-start.39 = (bf16[256,128]{1,0:T(8,128)(2,1)S(1)}, bf16[256,128]{1,0:T(8,128)(2,1)S(1)}, u32[]{:S(2)}, u32[]{:S(2)}) collective-permute-start(bf16[256,128]{1,0:T(8,128)(2,1)S(1)} %broadcast_select_fusion.3.near), channel_id=1, source_target_pairs={{0,32},{1,33},{2,34},{3,35},{4,36},{5,37},{6,38},{7,39},{8,40},{9,... | collective-permute-start | bytes 196616 | tf_op jit(solution)/shard_map/ppermute | solution.py:291
  80.8 15.9 %collective-permute-start.36 = (bf16[256,128]{1,0:T(8,128)(2,1)S(1)}, bf16[256,128]{1,0:T(8,128)(2,1)S(1)}, u32[]{:S(2)}, u32[]{:S(2)}) collective-permute-start(bf16[256,128]{1,0:T(8,128)(2,1)S(1)} %add_convert_fusion), channel_id=1, source_target_pairs={{64,2},{65,3},{66,4},{67,5},{68,6},{69,7},{70,8},{71,9},{72,10},{7... | collective-permute-start | bytes 196616 | tf_op jit(solution)/shard_map/ppermute | solution.py:291
  82.1 17.6 %collective-permute-start.37 = (bf16[256,128]{1,0:T(8,128)(2,1)S(1)}, bf16[256,128]{1,0:T(8,128)(2,1)S(1)}, u32[]{:S(2)}, u32[]{:S(2)}) collective-permute-start(bf16[256,128]{1,0:T(8,128)(2,1)S(1)} %add_convert_fusion), channel_id=1, source_target_pairs={{64,1},{65,2},{66,3},{67,4},{68,5},{69,6},{70,7},{71,8},{72,9},{73... | collective-permute-start | bytes 196616 | tf_op jit(solution)/shard_map/ppermute | solution.py:291
  83.4 16.3 %collective-permute-start.38 = (bf16[256,128]{1,0:T(8,128)(2,1)S(1)}, bf16[256,128]{1,0:T(8,128)(2,1)S(1)}, u32[]{:S(2)}, u32[]{:S(2)}) collective-permute-start(bf16[256,128]{1,0:T(8,128)(2,1)S(1)} %add_convert_fusion), channel_id=1, source_target_pairs={{64,0},{65,1},{66,2},{67,3},{68,4},{69,5},{70,6},{71,7},{72,8},{73... | collective-permute-start | bytes 196616 | tf_op jit(solution)/shard_map/ppermute | solution.py:291
  99.8 4.5 %collective-permute-start.40 = (bf16[256,384]{1,0:T(8,128)(2,1)S(1)}, bf16[256,384]{1,0:T(8,128)(2,1)S(1)}, u32[]{:S(2)}, u32[]{:S(2)}) collective-permute-start(bf16[256,384]{1,0:T(8,128)(2,1)S(1)} %maximum_add_fusion.2.mine), channel_id=1, source_target_pairs={{0,32},{1,33},{2,34},{3,35},{4,36},{5,37},{6,38},{7,39},{8,40},{9,... | collective-permute-start | bytes 589832 | tf_op jit(solution)/shard_map/ppermute | solution.py:291

commit v5 on v4

--- a/solution.py
+++ b/solution.py
@@ -244,37 +244,54 @@
     down[...] = jnp.where(scalars[0] == 0, faces[:, FACE : 4 * FACE], inside)
 
 
-def finish_kernel(
-    scalars, adjusted, near_basis, far_basis, down, mine, other, near, own, far, odd_rows, factor_ref, out
-):
+def settle_kernel(scalars, adjusted, near_basis, far_basis, down, near, own, far, odd_rows, factor_ref, out, operator):
     first = scalars[0] == 0
     factor = factor_ref[...]
-    faces = five(mine, other)
+    columns = out.shape[0]
     up3 = jnp.concatenate([near[...], own[...], far[...]], axis=1)
-    inside = between(up3, faces, odd_rows[...])
-    up = jnp.where(first, inside, faces[:, FACE : 4 * FACE])
+    up = jnp.where(first, up3, jnp.zeros_like(up3))
 
     def side(at, basis):
         part = slice(at * FACE, (at + 1) * FACE)
         return 0.5 * dot(jnp.concatenate([down[:, part], up[:, part]], axis=1), basis[...])
 
-    own = slice(FACE, 2 * FACE)
-    near, far = side(0, near_basis), side(2, far_basis)
-    low = adjusted[:, :KMAX] + jnp.where(first, near, far)
-    high = adjusted[:, M - KMAX :] + jnp.where(first, far, near)
+    middle = slice(FACE, 2 * FACE)
+    near_side, far_side = side(0, near_basis), side(2, far_basis)
+    low = adjusted[:, :KMAX] + jnp.where(first, near_side, far_side)
+    high = adjusted[:, M - KMAX :] + jnp.where(first, far_side, near_side)
     rows = jnp.concatenate(
         [
-            (low[:, :FACE] - down[:, own].astype(F32)).astype(BF),
+            (low[:, :FACE] - down[:, middle].astype(F32)).astype(BF),
             low[:, FACE:].astype(BF),
             adjusted[:, KMAX : M - KMAX].astype(BF),
             high[:, : KMAX - FACE].astype(BF),
-            (high[:, KMAX - FACE :] - up[:, own].astype(F32)).astype(BF),
+            (high[:, KMAX - FACE :] - up[:, middle].astype(F32)).astype(BF),
         ],
         axis=1,
     )
-    half = halves(rows, factor)
+
+    zero = jnp.zeros((FACE, FACE), BF)
+    one = jnp.where(
+        lax.broadcasted_iota(jnp.int32, (FACE, FACE), 0) == lax.broadcasted_iota(jnp.int32, (FACE, FACE), 1), 1.0, 0.0
+    ).astype(BF)
+    ends = [[], [], []]
+    for at in range(5):
+        for m in range(3):
+            inside = odd_rows[(m * 3 + at - m) * FACE : (m * 3 + at - m + 1) * FACE] if 0 <= at - m < 3 else zero
+            ends[m].append(jnp.where(first, inside, one if at == m + 1 else zero))
+    ends = [jnp.concatenate(blocks, axis=0) for blocks in ends]
+    near_end = 0.5 * dot(ends[0], near_basis[FACE:])
+    far_end = 0.5 * dot(ends[2], far_basis[FACE:])
+    low = jnp.where(first, near_end, far_end)
+    high = jnp.where(first, far_end, near_end)
+    high = high - jnp.concatenate([jnp.zeros_like(ends[1]), ends[1]], axis=1).astype(F32)
+    gap = jnp.zeros((5 * FACE, M - 2 * KMAX), BF)
+    change = jnp.concatenate([low.astype(BF), gap, high.astype(BF)], axis=1)
+    half = halves(jnp.concatenate([rows, change], axis=0), factor)
     for at in range(0, M, KMAX):
-        out[:, at : at + KMAX] = dot(half[:, at:], factor[at:, at : at + KMAX])
+        block_out = dot(half[:, at:], factor[at:, at : at + KMAX])
+        out[:, at : at + KMAX] = block_out[:columns]
+        operator[:, at : at + KMAX] = block_out[columns:].astype(BF)
 
 
 def on_device(right_side, inverse_factor, forward_trace, backward_trace, margin):
@@ -413,17 +430,16 @@
     pieces = hop(total, 1, -1, 2)
     seen = seen + new
     near, own = jnp.where(last_chip, near_last, near), jnp.where(last_chip, own_last, own)
-    pieces, seen, far = barrier((pieces, seen, swap(near)))
+    settled, operator = call(
+        settle_kernel,
+        [((columns, M), F32), ((five_, M), BF)],
+        scalars,
+        [adjusted, near_basis, far_basis, down, near, own, swap(near), odd_rows, factor],
+        (1 << 10, 1 << 10),
+    )
+    pieces, seen, operator = barrier((pieces, seen, operator))
     seen = seen + jnp.concatenate(pieces, axis=1)
-    out = call(
-        finish_kernel,
-        [((columns, M), F32)],
-        scalars,
-        [
-            adjusted, near_basis, far_basis, down, seen, swap(seen), near, own, far, odd_rows, factor,
-        ],
-        (1 << 29, 4 << 20),
-    )[0]
+    out = settled + dot(barrier(five(seen, swap(seen))), operator)
     return out[None, None]
 
 

time: 107 us -> 106 us (level)
  waiting for transfers between devices: 33.3 us -> 30.9 us
    ppermute x41, waiting for transfers between devices: 33.3 us -> 30.9 us  [send(): return lax.ppermute(value, AXES, pairs)]
    dot_general x10 -> x11, matrix products: 1.92 us -> 2.39 us  [dot(): lax.dot_general(a, b, (((1,), (0,)), ((), ())), preferred_element_type=F32)]
  transfers between devices with their start and end apart: 41 -> 41, of which waited for: 13 -> 13; matrix products, arithmetic and copies ran while one was open for 1% -> 1% of each run, Pallas kernels for 3% -> 5%
where the time goes in v5:
time: 106 us
  starting transfers between devices  59.3 us (56%)
  waiting for transfers between devices  30.9 us (29%)
  Pallas kernels  9.9 us (9%)
  matrix products  2.39 us (2%)
  other arithmetic  1.74 us (2%)
  between operations  1.36 us (1%)
    ppermute x41, starting transfers between devices, send(): return lax.ppermute(value, AXES, pairs)  59.3 us
    ppermute x41, waiting for transfers between devices, send(): return lax.ppermute(value, AXES, pairs)  30.9 us
    pallas_call x6, Pallas kernels, call(): pl.pallas_call(kernel, out_shape=[jax.ShapeDtypeStruct(shape, kind) for s...  9.9 us
    dot_general x11, matrix products, dot(): lax.dot_general(a, b, (((1,), (0,)), ((), ())), preferred_element_type=F32)  2.39 us
  transfers between devices with their start and end apart: 41, of which 13 were waited for; matrix products, arithmetic and copies ran while one was open for 1% of the time, Pallas kernels for 5%

profile of v5, /device:TPU:1, one launch (start us, length us, event | category | flops | bytes accessed | tf_op | source)
XLA Modules:
  0.0 105.7 jit_solution(12204220756415633005)
XLA Ops:
  0.7 3.7 %shard_map.55 = (bf16[512,256]{1,0:T(8,128)(2,1)S(1)}, bf16[512,256]{1,0:T(8,128)(2,1)S(1)}, bf16[256,768]{1,0:T(8,128)(2,1)S(1)}) custom-call(s32[3]{0:T(128)S(1)} %pad_add_fusion.scalars, f32[256,768]{1,0:T(8,128)} %bitcast.18, bf16[768,768]{1,0:T(8,128)(2,1)} %bitcast.16, bf16[128,768]{1,0:T(8,128)(2,1)} %bitcast.20, bf16[128,768]{1,0:T(8,128)(2,1)} %bitcast.21), custom_call_target="tpu_custom_call" | custom-call | flops 1073741824 | bytes 3145728 | tf_op jit(solution)/shard_map/pallas_call | solution.py:42
  4.4 8.9 %collective-permute-start = (bf16[512,256]{1,0:T(8,128)(2,1)S(1)}, bf16[512,256]{1,0:T(8,128)(2,1)S(1)}, u32[]{:S(2)}, u32[]{:S(2)}) collective-permute-start(bf16[512,256]{1,0:T(8,128)(2,1)S(1)} %get-tuple-element.89), channel_id=1, source_target_pairs={{0,1},{1,2},{2,3},{3,4},{4,5},{5,6},{6,7},{7,8},{8,9},{9,10},{10,1... | collective-permute-start | bytes 786440 | tf_op jit(solution)/shard_map/ppermute | solution.py:308
  13.3 4.9 %collective-permute-done.near = bf16[512,256]{1,0:T(8,128)(2,1)S(1)} collective-permute-done((bf16[512,256]{1,0:T(8,128)(2,1)S(1)}, bf16[512,256]{1,0:T(8,128)(2,1)S(1)}, u32[]{:S(2)}, u32[]{:S(2)}) %collective-permute-start) | collective-permute-done | bytes 262176 | tf_op jit(solution)/shard_map/ppermute | solution.py:308
  18.2 3.7 %collective-permute-done.1.far = bf16[512,256]{1,0:T(8,128)(2,1)S(1)} collective-permute-done((bf16[512,256]{1,0:T(8,128)(2,1)S(1)}, bf16[512,256]{1,0:T(8,128)(2,1)S(1)}, u32[]{:S(2)}, u32[]{:S(2)}) %collective-permute-start.1) | collective-permute-done | bytes 262176 | tf_op jit(solution)/shard_map/ppermute | solution.py:308
  21.9 1.0 shard_map.56
  23.5 0.9 collective-permute-done.2
  24.5 3.2 %collective-permute-start.3 = (bf16[1024,128]{1,0:T(8,128)(2,1)S(1)}, bf16[1024,128]{1,0:T(8,128)(2,1)S(1)}, u32[]{:S(2)}, u32[]{:S(2)}) collective-permute-start(bf16[1024,128]{1,0:T(8,128)(2,1)S(1)} %pad_maximum_fusion.1.own), channel_id=1, source_target_pairs={{0,1},{1,2},{2,3},{3,4},{4,5},{5,6},{6,7},{7,8},{8,9},{9,10},{10,1... | collective-permute-start | bytes 786440 | tf_op jit(solution)/shard_map/ppermute | solution.py:308
  27.7 3.3 %collective-permute-done.3.near = bf16[1024,128]{1,0:T(8,128)(2,1)S(1)} collective-permute-done((bf16[1024,128]{1,0:T(8,128)(2,1)S(1)}, bf16[1024,128]{1,0:T(8,128)(2,1)S(1)}, u32[]{:S(2)}, u32[]{:S(2)}) %collective-permute-start.3) | collective-permute-done | bytes 262176 | tf_op jit(solution)/shard_map/ppermute | solution.py:308
  31.2 3.5 %collective-permute-start.5 = (f32[256,128]{1,0:T(8,128)S(1)}, f32[256,128]{1,0:T(8,128)S(1)}, u32[]{:S(2)}, u32[]{:S(2)}) collective-permute-start(f32[256,128]{1,0:T(8,128)S(1)} %convolution_add_fusion), channel_id=1, source_target_pairs={{0,32},{1,33},{2,34},{3,35},{4,36},{5,37},{6,38},{7,39},{8,40},{9,... | collective-permute-start | bytes 393224 | tf_op jit(solution)/shard_map/ppermute | solution.py:308
  35.7 1.9 %collective-permute-start.6 = (bf16[256,128]{1,0:T(8,128)(2,1)S(1)}, bf16[256,128]{1,0:T(8,128)(2,1)S(1)}, u32[]{:S(2)}, u32[]{:S(2)}) collective-permute-start(bf16[256,128]{1,0:T(8,128)(2,1)S(1)} %add_convert_fusion.7), channel_id=1, source_target_pairs={{0,66},{1,67},{2,68},{3,69},{4,70},{5,71},{6,72},{7,73},{8,74},{9,... | collective-permute-start | bytes 196616 | tf_op jit(solution)/shard_map/ppermute | solution.py:308
  37.6 4.5 %collective-permute-start.7 = (bf16[256,128]{1,0:T(8,128)(2,1)S(1)}, bf16[256,128]{1,0:T(8,128)(2,1)S(1)}, u32[]{:S(2)}, u32[]{:S(2)}) collective-permute-start(bf16[256,128]{1,0:T(8,128)(2,1)S(1)} %add_convert_fusion.7), channel_id=1, source_target_pairs={{0,65},{1,66},{2,67},{3,68},{4,69},{5,70},{6,71},{7,72},{8,73},{9,... | collective-permute-start | bytes 196616 | tf_op jit(solution)/shard_map/ppermute | solution.py:308
  42.0 0.7 collective-permute-start.8
  42.7 1.1 %shard_map.57 = (bf16[640,128]{1,0:T(8,128)(2,1)S(1)}, bf16[640,128]{1,0:T(8,128)(2,1)S(1)}, bf16[896,128]{1,0:T(8,128)(2,1)S(1)}, f32[256,128]{1,0:T(8,128)S(1)...) custom-call(s32[3]{0:T(128)S(1)} %pad_add_fusion.scalars, ...), custom_call_target="tpu_custom_call" | custom-call | flops 1024 | bytes 1024 | tf_op jit(solution)/shard_map/pallas_call | solution.py:42
  44.3 4.5 %collective-permute-start.15 = (bf16[896,128]{1,0:T(8,128)(2,1)S(1)}, bf16[896,128]{1,0:T(8,128)(2,1)S(1)}, u32[]{:S(2)}, u32[]{:S(2)}) collective-permute-start(bf16[896,128]{1,0:T(8,128)(2,1)S(1)} %get-tuple-element.106.own), channel_id=1, source_target_pairs={{0,1},{1,2},{2,3},{3,4},{4,5},{5,6},{6,7},{7,8},{8,9},{9,10},{10,1... | collective-permute-start | bytes 688136 | tf_op jit(solution)/shard_map/ppermute | solution.py:308
  48.8 0.7 collective-permute-start.12
  49.5 0.7 collective-permute-start.13
  50.2 0.7 collective-permute-start.14
  50.9 0.8 collective-permute-done.15.near
  52.0 2.4 %collective-permute-start.16 = (f32[256,128]{1,0:T(8,128)S(1)}, f32[256,128]{1,0:T(8,128)S(1)}, u32[]{:S(2)}, u32[]{:S(2)}) collective-permute-start(f32[256,128]{1,0:T(8,128)S(1)} %add.82), channel_id=1, source_target_pairs={{0,32},{1,33},{2,34},{3,35},{4,36},{5,37},{6,38},{7,39},{8,40},{9,... | collective-permute-start | bytes 393224 | tf_op jit(solution)/shard_map/ppermute | solution.py:308
  54.7 0.5 collective-permute-start.21
  55.3 0.7 collective-permute-start.17
  56.0 0.7 collective-permute-start.18
  56.7 0.7 collective-permute-start.19
  57.3 0.8 collective-permute-start.20
  58.2 0.9 shard_map.58
  60.8 0.6 collective-permute-done.23
  61.4 0.7 collective-permute-start.24
  62.0 0.7 collective-permute-start.25
  62.7 0.7 collective-permute-start.26
  63.4 3.3 %collective-permute-start.28 = (bf16[256,128]{1,0:T(8,128)(2,1)S(1)}, bf16[256,128]{1,0:T(8,128)(2,1)S(1)}, u32[]{:S(2)}, u32[]{:S(2)}) collective-permute-start(bf16[256,128]{1,0:T(8,128)(2,1)S(1)} %get-tuple-element.176), channel_id=1, source_target_pairs={{0,1},{1,2},{2,3},{3,4},{4,5},{5,6},{6,7},{7,8},{8,9},{9,10},{10,1... | collective-permute-start | bytes 196616 | tf_op jit(solution)/shard_map/ppermute | solution.py:308
  66.9 1.1 %collective-permute-done.28 = bf16[256,128]{1,0:T(8,128)(2,1)S(1)} collective-permute-done((bf16[256,128]{1,0:T(8,128)(2,1)S(1)}, bf16[256,128]{1,0:T(8,128)(2,1)S(1)}, u32[]{:S(2)}, u32[]{:S(2)}) %collective-permute-start.28) | collective-permute-done | bytes 65568 | tf_op jit(solution)/shard_map/ppermute | solution.py:308
  68.3 3.4 %collective-permute-start.29 = (f32[256,128]{1,0:T(8,128)S(1)}, f32[256,128]{1,0:T(8,128)S(1)}, u32[]{:S(2)}, u32[]{:S(2)}) collective-permute-start(f32[256,128]{1,0:T(8,128)S(1)} %add.90), channel_id=1, source_target_pairs={{0,32},{1,33},{2,34},{3,35},{4,36},{5,37},{6,38},{7,39},{8,40},{9,... | collective-permute-start | bytes 393224 | tf_op jit(solution)/shard_map/ppermute | solution.py:308
  71.8 1.9 %collective-permute-start.33 = (bf16[256,128]{1,0:T(8,128)(2,1)S(1)}, bf16[256,128]{1,0:T(8,128)(2,1)S(1)}, u32[]{:S(2)}, u32[]{:S(2)}) collective-permute-start(bf16[256,128]{1,0:T(8,128)(2,1)S(1)} %get-tuple-element.174), channel_id=1, source_target_pairs={{0,1},{1,2},{2,3},{3,4},{4,5},{5,6},{6,7},{7,8},{8,9},{9,10},{10,1... | collective-permute-start | bytes 196616 | tf_op jit(solution)/shard_map/ppermute | solution.py:308
  73.7 0.7 collective-permute-start.30
  74.3 0.7 collective-permute-start.31
  75.0 0.7 collective-permute-start.32
  75.9 0.9 shard_map.59.down
  77.0 2.8 %collective-permute-start.36 = (f32[256,128]{1,0:T(8,128)S(1)}, f32[256,128]{1,0:T(8,128)S(1)}, u32[]{:S(2)}, u32[]{:S(2)}) collective-permute-start(f32[256,128]{1,0:T(8,128)S(1)} %add.96), channel_id=1, source_target_pairs={{0,32},{1,33},{2,34},{3,35},{4,36},{5,37},{6,38},{7,39},{8,40},{9,... | collective-permute-start | bytes 393224 | tf_op jit(solution)/shard_map/ppermute | solution.py:308
  79.9 0.9 collective-permute-done.36
  80.8 1.3 %collective-permute-start.37 = (bf16[256,128]{1,0:T(8,128)(2,1)S(1)}, bf16[256,128]{1,0:T(8,128)(2,1)S(1)}, u32[]{:S(2)}, u32[]{:S(2)}) collective-permute-start(bf16[256,128]{1,0:T(8,128)(2,1)S(1)} %add_convert_fusion), channel_id=1, source_target_pairs={{64,2},{65,3},{66,4},{67,5},{68,6},{69,7},{70,8},{71,9},{72,10},{7... | collective-permute-start | bytes 196616 | tf_op jit(solution)/shard_map/ppermute | solution.py:308
  82.1 1.3 %collective-permute-start.38 = (bf16[256,128]{1,0:T(8,128)(2,1)S(1)}, bf16[256,128]{1,0:T(8,128)(2,1)S(1)}, u32[]{:S(2)}, u32[]{:S(2)}) collective-permute-start(bf16[256,128]{1,0:T(8,128)(2,1)S(1)} %add_convert_fusion), channel_id=1, source_target_pairs={{64,1},{65,2},{66,3},{67,4},{68,5},{69,6},{70,7},{71,8},{72,9},{73... | collective-permute-start | bytes 196616 | tf_op jit(solution)/shard_map/ppermute | solution.py:308
  83.4 0.7 collective-permute-start.39
  84.1 2.4 %shard_map.60 = (f32[256,768]{1,0:T(8,128)S(1)}, bf16[640,768]{1,0:T(8,128)(2,1)S(1)}) custom-call(s32[3]{0:T(128)S(1)} %pad_add_fusion.scalars, f32[256,768]{1,0:T(8,128)S(1)} %get-tuple-element.92.adjusted, bf16[256,256]{1,0:T(8,128)(2,1)S(1)} %get-tuple-element.93.near_basis, bf16[256,256]{1,0:T(8,128)(2,1)S(1)} %get-tuple-element.94.far_basis, ...), custom_call_target="tpu_custom_call" | custom-call | flops 1024 | bytes 1024 | tf_op jit(solution)/shard_map/pallas_call | solution.py:42
  86.6 10.1 %collective-permute-done.37 = bf16[256,128]{1,0:T(8,128)(2,1)S(1)} collective-permute-done((bf16[256,128]{1,0:T(8,128)(2,1)S(1)}, bf16[256,128]{1,0:T(8,128)(2,1)S(1)}, u32[]{:S(2)}, u32[]{:S(2)}) %collective-permute-start.37) | collective-permute-done | bytes 65568 | tf_op jit(solution)/shard_map/ppermute | solution.py:308
  96.7 3.0 %collective-permute-done.38 = bf16[256,128]{1,0:T(8,128)(2,1)S(1)} collective-permute-done((bf16[256,128]{1,0:T(8,128)(2,1)S(1)}, bf16[256,128]{1,0:T(8,128)(2,1)S(1)}, u32[]{:S(2)}, u32[]{:S(2)}) %collective-permute-start.38) | collective-permute-done | bytes 65568 | tf_op jit(solution)/shard_map/ppermute | solution.py:308
  99.7 3.4 %collective-permute-start.40 = (bf16[256,384]{1,0:T(8,128)(2,1)S(1)}, bf16[256,384]{1,0:T(8,128)(2,1)S(1)}, u32[]{:S(2)}, u32[]{:S(2)}) collective-permute-start(bf16[256,384]{1,0:T(8,128)(2,1)S(1)} %maximum_add_fusion.2), channel_id=1, source_target_pairs={{0,32},{1,33},{2,34},{3,35},{4,36},{5,37},{6,38},{7,39},{8,40},{9,... | collective-permute-start | bytes 589832 | tf_op jit(solution)/shard_map/ppermute | solution.py:308
  103.1 1.1 %collective-permute-done.40 = bf16[256,384]{1,0:T(8,128)(2,1)S(1)} collective-permute-done((bf16[256,384]{1,0:T(8,128)(2,1)S(1)}, bf16[256,384]{1,0:T(8,128)(2,1)S(1)}, u32[]{:S(2)}, u32[]{:S(2)}) %collective-permute-start.40) | collective-permute-done | bytes 196640 | tf_op jit(solution)/shard_map/ppermute | solution.py:308
  104.7 1.0 add_bitcast_fusion
  (97 shorter events, 6.5 us)
Async XLA Ops:
  0.7 21.2 %copy-start.1 = (f32[1,1,256,768]{3,2,1,0:T(8,128)S(1)}, f32[1,1,256,768]{3,2,1,0:T(8,128)}, u32[]{:S(2)}) copy-start(f32[1,1,256,768]{3,2,1,0:T(8,128)} %param.5) | copy-start | bytes 2359300
  4.4 13.8 %collective-permute-start = (bf16[512,256]{1,0:T(8,128)(2,1)S(1)}, bf16[512,256]{1,0:T(8,128)(2,1)S(1)}, u32[]{:S(2)}, u32[]{:S(2)}) collective-permute-start(bf16[512,256]{1,0:T(8,128)(2,1)S(1)} %get-tuple-element.89), channel_id=1, source_target_pairs={{0,1},{1,2},{2,3},{3,4},{4,5},{5,6},{6,7},{7,8},{8,9},{9,10},{10,1... | collective-permute-start | bytes 786440 | tf_op jit(solution)/shard_map/ppermute | solution.py:308
  13.3 8.5 %collective-permute-start.1 = (bf16[512,256]{1,0:T(8,128)(2,1)S(1)}, bf16[512,256]{1,0:T(8,128)(2,1)S(1)}, u32[]{:S(2)}, u32[]{:S(2)}) collective-permute-start(bf16[512,256]{1,0:T(8,128)(2,1)S(1)} %get-tuple-element.90), channel_id=1, source_target_pairs={{0,31},{1,0},{2,1},{3,2},{4,3},{5,4},{6,5},{7,6},{8,7},{9,8},{10,9... | collective-permute-start | bytes 786440 | tf_op jit(solution)/shard_map/ppermute | solution.py:308
  22.9 1.5 %collective-permute-start.2 = (bf16[640,128]{1,0:T(8,128)(2,1)S(1)}, bf16[640,128]{1,0:T(8,128)(2,1)S(1)}, u32[]{:S(2)}, u32[]{:S(2)}) collective-permute-start(bf16[640,128]{1,0:T(8,128)(2,1)S(1)} %get-tuple-element.95), channel_id=1, source_target_pairs={{0,32},{1,33},{2,34},{3,35},{4,36},{5,37},{6,38},{7,39},{8,40},{9,... | collective-permute-start | bytes 491528 | tf_op jit(solution)/shard_map/ppermute | solution.py:308
  23.0 4.7 %collective-permute-start.4 = (bf16[640,128]{1,0:T(8,128)(2,1)S(1)}, bf16[640,128]{1,0:T(8,128)(2,1)S(1)}, u32[]{:S(2)}, u32[]{:S(2)}) collective-permute-start(bf16[640,128]{1,0:T(8,128)(2,1)S(1)} %get-tuple-element.96.outer), channel_id=1, source_target_pairs={{0,32},{1,33},{2,34},{3,35},{4,36},{5,37},{6,38},{7,39},{8,40},{9,... | collective-permute-start | bytes 491528 | tf_op jit(solution)/shard_map/ppermute | solution.py:308
  24.5 6.5 %collective-permute-start.3 = (bf16[1024,128]{1,0:T(8,128)(2,1)S(1)}, bf16[1024,128]{1,0:T(8,128)(2,1)S(1)}, u32[]{:S(2)}, u32[]{:S(2)}) collective-permute-start(bf16[1024,128]{1,0:T(8,128)(2,1)S(1)} %pad_maximum_fusion.1.own), channel_id=1, source_target_pairs={{0,1},{1,2},{2,3},{3,4},{4,5},{5,6},{6,7},{7,8},{8,9},{9,10},{10,1... | collective-permute-start | bytes 786440 | tf_op jit(solution)/shard_map/ppermute | solution.py:308
  31.2 4.5 %collective-permute-start.5 = (f32[256,128]{1,0:T(8,128)S(1)}, f32[256,128]{1,0:T(8,128)S(1)}, u32[]{:S(2)}, u32[]{:S(2)}) collective-permute-start(f32[256,128]{1,0:T(8,128)S(1)} %convolution_add_fusion), channel_id=1, source_target_pairs={{0,32},{1,33},{2,34},{3,35},{4,36},{5,37},{6,38},{7,39},{8,40},{9,... | collective-permute-start | bytes 393224 | tf_op jit(solution)/shard_map/ppermute | solution.py:308
  34.7 8.0 %collective-permute-start.10 = (bf16[640,128]{1,0:T(8,128)(2,1)S(1)}, bf16[640,128]{1,0:T(8,128)(2,1)S(1)}, u32[]{:S(2)}, u32[]{:S(2)}) collective-permute-start(bf16[640,128]{1,0:T(8,128)(2,1)S(1)} %get-tuple-element.97.extra), channel_id=1, source_target_pairs={{0,32},{1,33},{2,34},{3,35},{4,36},{5,37},{6,38},{7,39},{8,40},{9,... | collective-permute-start | bytes 491528 | tf_op jit(solution)/shard_map/ppermute | solution.py:308
  34.8 7.9 %collective-permute-start.9 = (bf16[1024,128]{1,0:T(8,128)(2,1)S(1)}, bf16[1024,128]{1,0:T(8,128)(2,1)S(1)}, u32[]{:S(2)}, u32[]{:S(2)}) collective-permute-start(bf16[1024,128]{1,0:T(8,128)(2,1)S(1)} %collective-permute-done.3.near), channel_id=1, source_target_pairs={{0,32},{1,33},{2,34},{3,35},{4,36},{5,37},{6,38},{7,39},{8,40},{9,... | collective-permute-start | bytes 786440 | tf_op jit(solution)/shard_map/ppermute | solution.py:308
  35.7 8.1 %collective-permute-start.6 = (bf16[256,128]{1,0:T(8,128)(2,1)S(1)}, bf16[256,128]{1,0:T(8,128)(2,1)S(1)}, u32[]{:S(2)}, u32[]{:S(2)}) collective-permute-start(bf16[256,128]{1,0:T(8,128)(2,1)S(1)} %add_convert_fusion.7), channel_id=1, source_target_pairs={{0,66},{1,67},{2,68},{3,69},{4,70},{5,71},{6,72},{7,73},{8,74},{9,... | collective-permute-start | bytes 196616 | tf_op jit(solution)/shard_map/ppermute | solution.py:308
  37.6 6.3 %collective-permute-start.7 = (bf16[256,128]{1,0:T(8,128)(2,1)S(1)}, bf16[256,128]{1,0:T(8,128)(2,1)S(1)}, u32[]{:S(2)}, u32[]{:S(2)}) collective-permute-start(bf16[256,128]{1,0:T(8,128)(2,1)S(1)} %add_convert_fusion.7), channel_id=1, source_target_pairs={{0,65},{1,66},{2,67},{3,68},{4,69},{5,70},{6,71},{7,72},{8,73},{9,... | collective-permute-start | bytes 196616 | tf_op jit(solution)/shard_map/ppermute | solution.py:308
  42.0 1.8 %collective-permute-start.8 = (bf16[256,128]{1,0:T(8,128)(2,1)S(1)}, bf16[256,128]{1,0:T(8,128)(2,1)S(1)}, u32[]{:S(2)}, u32[]{:S(2)}) collective-permute-start(bf16[256,128]{1,0:T(8,128)(2,1)S(1)} %add_convert_fusion.7), channel_id=1, source_target_pairs={{0,64},{1,65},{2,66},{3,67},{4,68},{5,69},{6,70},{7,71},{8,72},{9,... | collective-permute-start | bytes 196616 | tf_op jit(solution)/shard_map/ppermute | solution.py:308
  44.1 4.7 %collective-permute-start.11 = (f32[256,128]{1,0:T(8,128)S(1)}, f32[256,128]{1,0:T(8,128)S(1)}, u32[]{:S(2)}, u32[]{:S(2)}) collective-permute-start(f32[256,128]{1,0:T(8,128)S(1)} %add.80), channel_id=1, source_target_pairs={{0,32},{1,33},{2,34},{3,35},{4,36},{5,37},{6,38},{7,39},{8,40},{9,... | collective-permute-start | bytes 393224 | tf_op jit(solution)/shard_map/ppermute | solution.py:308
  44.3 7.5 %collective-permute-start.15 = (bf16[896,128]{1,0:T(8,128)(2,1)S(1)}, bf16[896,128]{1,0:T(8,128)(2,1)S(1)}, u32[]{:S(2)}, u32[]{:S(2)}) collective-permute-start(bf16[896,128]{1,0:T(8,128)(2,1)S(1)} %get-tuple-element.106.own), channel_id=1, source_target_pairs={{0,1},{1,2},{2,3},{3,4},{4,5},{5,6},{6,7},{7,8},{8,9},{9,10},{10,1... | collective-permute-start | bytes 688136 | tf_op jit(solution)/shard_map/ppermute | solution.py:308
  48.8 2.1 %collective-permute-start.12 = (bf16[256,128]{1,0:T(8,128)(2,1)S(1)}, bf16[256,128]{1,0:T(8,128)(2,1)S(1)}, u32[]{:S(2)}, u32[]{:S(2)}) collective-permute-start(bf16[256,128]{1,0:T(8,128)(2,1)S(1)} %add_convert_fusion.6), channel_id=1, source_target_pairs={{64,130},{65,131},{66,132},{67,133},{68,134},{69,135},{70,136},{71... | collective-permute-start | bytes 196616 | tf_op jit(solution)/shard_map/ppermute | solution.py:308
  49.5 1.4 %collective-permute-start.13 = (bf16[256,128]{1,0:T(8,128)(2,1)S(1)}, bf16[256,128]{1,0:T(8,128)(2,1)S(1)}, u32[]{:S(2)}, u32[]{:S(2)}) collective-permute-start(bf16[256,128]{1,0:T(8,128)(2,1)S(1)} %add_convert_fusion.6), channel_id=1, source_target_pairs={{64,129},{65,130},{66,131},{67,132},{68,133},{69,134},{70,135},{71... | collective-permute-start | bytes 196616 | tf_op jit(solution)/shard_map/ppermute | solution.py:308
  50.2 0.7 collective-permute-start.14
  52.0 3.3 %collective-permute-start.16 = (f32[256,128]{1,0:T(8,128)S(1)}, f32[256,128]{1,0:T(8,128)S(1)}, u32[]{:S(2)}, u32[]{:S(2)}) collective-permute-start(f32[256,128]{1,0:T(8,128)S(1)} %add.82), channel_id=1, source_target_pairs={{0,32},{1,33},{2,34},{3,35},{4,36},{5,37},{6,38},{7,39},{8,40},{9,... | collective-permute-start | bytes 393224 | tf_op jit(solution)/shard_map/ppermute | solution.py:308
  54.4 5.1 %copy-start.2 = (bf16[256,384]{1,0:T(8,128)(2,1)}, bf16[256,384]{1,0:T(8,128)(2,1)S(1)}, u32[]{:S(2)}) copy-start(bf16[256,384]{1,0:T(8,128)(2,1)S(1)} %maximum_add_fusion) | copy-start | bytes 589828
  54.6 4.5 %collective-permute-start.22 = (f32[256,128]{1,0:T(8,128)S(1)}, f32[256,128]{1,0:T(8,128)S(1)}, u32[]{:S(2)}, u32[]{:S(2)}) collective-permute-start(f32[256,128]{1,0:T(8,128)S(1)} %fusion.54), channel_id=1, source_target_pairs={{0,32},{1,33},{2,34},{3,35},{4,36},{5,37},{6,38},{7,39},{8,40},{9,... | collective-permute-start | bytes 393224 | tf_op jit(solution)/shard_map/ppermute | solution.py:308
  54.7 2.6 %collective-permute-start.21 = (bf16[896,128]{1,0:T(8,128)(2,1)S(1)}, bf16[896,128]{1,0:T(8,128)(2,1)S(1)}, u32[]{:S(2)}, u32[]{:S(2)}) collective-permute-start(bf16[896,128]{1,0:T(8,128)(2,1)S(1)} %collective-permute-done.15.near), channel_id=1, source_target_pairs={{0,32},{1,33},{2,34},{3,35},{4,36},{5,37},{6,38},{7,39},{8,40},{9,... | collective-permute-start | bytes 688136 | tf_op jit(solution)/shard_map/ppermute | solution.py:308
  55.3 3.8 %collective-permute-start.17 = (bf16[256,128]{1,0:T(8,128)(2,1)S(1)}, bf16[256,128]{1,0:T(8,128)(2,1)S(1)}, u32[]{:S(2)}, u32[]{:S(2)}) collective-permute-start(bf16[256,128]{1,0:T(8,128)(2,1)S(1)} %add_convert_fusion.5), channel_id=1, source_target_pairs={{128,195},{129,196},{130,197},{131,198},{132,199},{133,200},{134,2... | collective-permute-start | bytes 196616 | tf_op jit(solution)/shard_map/ppermute | solution.py:308
  56.0 3.1 %collective-permute-start.18 = (bf16[256,128]{1,0:T(8,128)(2,1)S(1)}, bf16[256,128]{1,0:T(8,128)(2,1)S(1)}, u32[]{:S(2)}, u32[]{:S(2)}) collective-permute-start(bf16[256,128]{1,0:T(8,128)(2,1)S(1)} %add_convert_fusion.5), channel_id=1, source_target_pairs={{128,194},{129,195},{130,196},{131,197},{132,198},{133,199},{134,2... | collective-permute-start | bytes 196616 | tf_op jit(solution)/shard_map/ppermute | solution.py:308
  56.7 2.5 %collective-permute-start.19 = (bf16[256,128]{1,0:T(8,128)(2,1)S(1)}, bf16[256,128]{1,0:T(8,128)(2,1)S(1)}, u32[]{:S(2)}, u32[]{:S(2)}) collective-permute-start(bf16[256,128]{1,0:T(8,128)(2,1)S(1)} %add_convert_fusion.5), channel_id=1, source_target_pairs={{128,193},{129,194},{130,195},{131,196},{132,197},{133,198},{134,1... | collective-permute-start | bytes 196616 | tf_op jit(solution)/shard_map/ppermute | solution.py:308
  57.3 1.8 %collective-permute-start.20 = (bf16[256,128]{1,0:T(8,128)(2,1)S(1)}, bf16[256,128]{1,0:T(8,128)(2,1)S(1)}, u32[]{:S(2)}, u32[]{:S(2)}) collective-permute-start(bf16[256,128]{1,0:T(8,128)(2,1)S(1)} %add_convert_fusion.5), channel_id=1, source_target_pairs={{128,192},{129,193},{130,194},{131,195},{132,196},{133,197},{134,1... | collective-permute-start | bytes 196616 | tf_op jit(solution)/shard_map/ppermute | solution.py:308
  59.5 7.2 %slice-start = ((bf16[256,384]{1,0:T(8,128)(2,1)}), bf16[256,256]{1,0:T(8,128)(2,1)S(1)}, s32[]{:S(2)}) async-start(bf16[256,384]{1,0:T(8,128)(2,1)} %copy-done.2), calls=%async_computation | async-start | bytes 262144 | tf_op jit(solution)/shard_map/slice | solution.py:414
  59.5 16.3 %collective-permute-start.34 = (bf16[256,384]{1,0:T(8,128)(2,1)S(1)}, bf16[256,384]{1,0:T(8,128)(2,1)S(1)}, u32[]{:S(2)}, u32[]{:S(2)}) collective-permute-start(bf16[256,384]{1,0:T(8,128)(2,1)S(1)} %add.95.mine), channel_id=1, source_target_pairs={{0,32},{1,33},{2,34},{3,35},{4,36},{5,37},{6,38},{7,39},{8,40},{9,... | collective-permute-start | bytes 589832 | tf_op jit(solution)/shard_map/ppermute | solution.py:308
  60.0 1.3 %collective-permute-start.23 = (f32[256,128]{1,0:T(8,128)S(1)}, f32[256,128]{1,0:T(8,128)S(1)}, u32[]{:S(2)}, u32[]{:S(2)}) collective-permute-start(f32[256,128]{1,0:T(8,128)S(1)} %add.85), channel_id=1, source_target_pairs={{0,32},{1,33},{2,34},{3,35},{4,36},{5,37},{6,38},{7,39},{8,40},{9,... | collective-permute-start | bytes 393224 | tf_op jit(solution)/shard_map/ppermute | solution.py:308
  60.3 3.0 %collective-permute-start.27 = (f32[256,128]{1,0:T(8,128)S(1)}, f32[256,128]{1,0:T(8,128)S(1)}, u32[]{:S(2)}, u32[]{:S(2)}) collective-permute-start(f32[256,128]{1,0:T(8,128)S(1)} %fusion.52), channel_id=1, source_target_pairs={{0,32},{1,33},{2,34},{3,35},{4,36},{5,37},{6,38},{7,39},{8,40},{9,... | collective-permute-start | bytes 393224 | tf_op jit(solution)/shard_map/ppermute | solution.py:308
  61.4 6.7 %collective-permute-start.24 = (bf16[256,128]{1,0:T(8,128)(2,1)S(1)}, bf16[256,128]{1,0:T(8,128)(2,1)S(1)}, u32[]{:S(2)}, u32[]{:S(2)}) collective-permute-start(bf16[256,128]{1,0:T(8,128)(2,1)S(1)} %add_convert_fusion.4), channel_id=1, source_target_pairs={{192,130},{193,131},{194,132},{195,133},{196,134},{197,135},{198,1... | collective-permute-start | bytes 196616 | tf_op jit(solution)/shard_map/ppermute | solution.py:308
  62.0 6.0 %collective-permute-start.25 = (bf16[256,128]{1,0:T(8,128)(2,1)S(1)}, bf16[256,128]{1,0:T(8,128)(2,1)S(1)}, u32[]{:S(2)}, u32[]{:S(2)}) collective-permute-start(bf16[256,128]{1,0:T(8,128)(2,1)S(1)} %add_convert_fusion.4), channel_id=1, source_target_pairs={{192,129},{193,130},{194,131},{195,132},{196,133},{197,134},{198,1... | collective-permute-start | bytes 196616 | tf_op jit(solution)/shard_map/ppermute | solution.py:308
  62.7 5.4 %collective-permute-start.26 = (bf16[256,128]{1,0:T(8,128)(2,1)S(1)}, bf16[256,128]{1,0:T(8,128)(2,1)S(1)}, u32[]{:S(2)}, u32[]{:S(2)}) collective-permute-start(bf16[256,128]{1,0:T(8,128)(2,1)S(1)} %add_convert_fusion.4), channel_id=1, source_target_pairs={{192,128},{193,129},{194,130},{195,131},{196,132},{197,133},{198,1... | collective-permute-start | bytes 196616 | tf_op jit(solution)/shard_map/ppermute | solution.py:308
  63.4 4.6 %collective-permute-start.28 = (bf16[256,128]{1,0:T(8,128)(2,1)S(1)}, bf16[256,128]{1,0:T(8,128)(2,1)S(1)}, u32[]{:S(2)}, u32[]{:S(2)}) collective-permute-start(bf16[256,128]{1,0:T(8,128)(2,1)S(1)} %get-tuple-element.176), channel_id=1, source_target_pairs={{0,1},{1,2},{2,3},{3,4},{4,5},{5,6},{6,7},{7,8},{8,9},{9,10},{10,1... | collective-permute-start | bytes 196616 | tf_op jit(solution)/shard_map/ppermute | solution.py:308
  68.3 5.3 %collective-permute-start.29 = (f32[256,128]{1,0:T(8,128)S(1)}, f32[256,128]{1,0:T(8,128)S(1)}, u32[]{:S(2)}, u32[]{:S(2)}) collective-permute-start(f32[256,128]{1,0:T(8,128)S(1)} %add.90), channel_id=1, source_target_pairs={{0,32},{1,33},{2,34},{3,35},{4,36},{5,37},{6,38},{7,39},{8,40},{9,... | collective-permute-start | bytes 393224 | tf_op jit(solution)/shard_map/ppermute | solution.py:308
  71.8 5.0 %collective-permute-start.33 = (bf16[256,128]{1,0:T(8,128)(2,1)S(1)}, bf16[256,128]{1,0:T(8,128)(2,1)S(1)}, u32[]{:S(2)}, u32[]{:S(2)}) collective-permute-start(bf16[256,128]{1,0:T(8,128)(2,1)S(1)} %get-tuple-element.174), channel_id=1, source_target_pairs={{0,1},{1,2},{2,3},{3,4},{4,5},{5,6},{6,7},{7,8},{8,9},{9,10},{10,1... | collective-permute-start | bytes 196616 | tf_op jit(solution)/shard_map/ppermute | solution.py:308
  73.7 3.1 %collective-permute-start.30 = (bf16[256,128]{1,0:T(8,128)(2,1)S(1)}, bf16[256,128]{1,0:T(8,128)(2,1)S(1)}, u32[]{:S(2)}, u32[]{:S(2)}) collective-permute-start(bf16[256,128]{1,0:T(8,128)(2,1)S(1)} %add_convert_fusion.2), channel_id=1, source_target_pairs={{128,66},{129,67},{130,68},{131,69},{132,70},{133,71},{134,72},{13... | collective-permute-start | bytes 196616 | tf_op jit(solution)/shard_map/ppermute | solution.py:308
  74.3 2.4 %collective-permute-start.31 = (bf16[256,128]{1,0:T(8,128)(2,1)S(1)}, bf16[256,128]{1,0:T(8,128)(2,1)S(1)}, u32[]{:S(2)}, u32[]{:S(2)}) collective-permute-start(bf16[256,128]{1,0:T(8,128)(2,1)S(1)} %add_convert_fusion.2), channel_id=1, source_target_pairs={{128,65},{129,66},{130,67},{131,68},{132,69},{133,70},{134,71},{13... | collective-permute-start | bytes 196616 | tf_op jit(solution)/shard_map/ppermute | solution.py:308
  75.0 1.7 %collective-permute-start.32 = (bf16[256,128]{1,0:T(8,128)(2,1)S(1)}, bf16[256,128]{1,0:T(8,128)(2,1)S(1)}, u32[]{:S(2)}, u32[]{:S(2)}) collective-permute-start(bf16[256,128]{1,0:T(8,128)(2,1)S(1)} %add_convert_fusion.2), channel_id=1, source_target_pairs={{128,64},{129,65},{130,66},{131,67},{132,68},{133,69},{134,70},{13... | collective-permute-start | bytes 196616 | tf_op jit(solution)/shard_map/ppermute | solution.py:308
  76.7 7.4 %copy-start = (bf16[1,1,768,768]{3,2,1,0:T(8,128)(2,1)S(1)}, bf16[1,1,768,768]{3,2,1,0:T(8,128)(2,1)}, u32[]{:S(2)}) copy-start(bf16[1,1,768,768]{3,2,1,0:T(8,128)(2,1)} %param.6) | copy-start | bytes 3538948
  77.0 3.7 %collective-permute-start.36 = (f32[256,128]{1,0:T(8,128)S(1)}, f32[256,128]{1,0:T(8,128)S(1)}, u32[]{:S(2)}, u32[]{:S(2)}) collective-permute-start(f32[256,128]{1,0:T(8,128)S(1)} %add.96), channel_id=1, source_target_pairs={{0,32},{1,33},{2,34},{3,35},{4,36},{5,37},{6,38},{7,39},{8,40},{9,... | collective-permute-start | bytes 393224 | tf_op jit(solution)/shard_map/ppermute | solution.py:308
  79.8 4.3 %collective-permute-start.35 = (bf16[256,128]{1,0:T(8,128)(2,1)S(1)}, bf16[256,128]{1,0:T(8,128)(2,1)S(1)}, u32[]{:S(2)}, u32[]{:S(2)}) collective-permute-start(bf16[256,128]{1,0:T(8,128)(2,1)S(1)} %broadcast_select_fusion.3.near), channel_id=1, source_target_pairs={{0,32},{1,33},{2,34},{3,35},{4,36},{5,37},{6,38},{7,39},{8,40},{9,... | collective-permute-start | bytes 196616 | tf_op jit(solution)/shard_map/ppermute | solution.py:308
  80.8 15.9 %collective-permute-start.37 = (bf16[256,128]{1,0:T(8,128)(2,1)S(1)}, bf16[256,128]{1,0:T(8,128)(2,1)S(1)}, u32[]{:S(2)}, u32[]{:S(2)}) collective-permute-start(bf16[256,128]{1,0:T(8,128)(2,1)S(1)} %add_convert_fusion), channel_id=1, source_target_pairs={{64,2},{65,3},{66,4},{67,5},{68,6},{69,7},{70,8},{71,9},{72,10},{7... | collective-permute-start | bytes 196616 | tf_op jit(solution)/shard_map/ppermute | solution.py:308
  82.1 17.6 %collective-permute-start.38 = (bf16[256,128]{1,0:T(8,128)(2,1)S(1)}, bf16[256,128]{1,0:T(8,128)(2,1)S(1)}, u32[]{:S(2)}, u32[]{:S(2)}) collective-permute-start(bf16[256,128]{1,0:T(8,128)(2,1)S(1)} %add_convert_fusion), channel_id=1, source_target_pairs={{64,1},{65,2},{66,3},{67,4},{68,5},{69,6},{70,7},{71,8},{72,9},{73... | collective-permute-start | bytes 196616 | tf_op jit(solution)/shard_map/ppermute | solution.py:308
  83.4 16.3 %collective-permute-start.39 = (bf16[256,128]{1,0:T(8,128)(2,1)S(1)}, bf16[256,128]{1,0:T(8,128)(2,1)S(1)}, u32[]{:S(2)}, u32[]{:S(2)}) collective-permute-start(bf16[256,128]{1,0:T(8,128)(2,1)S(1)} %add_convert_fusion), channel_id=1, source_target_pairs={{64,0},{65,1},{66,2},{67,3},{68,4},{69,5},{70,6},{71,7},{72,8},{73... | collective-permute-start | bytes 196616 | tf_op jit(solution)/shard_map/ppermute | solution.py:308
  99.7 4.5 %collective-permute-start.40 = (bf16[256,384]{1,0:T(8,128)(2,1)S(1)}, bf16[256,384]{1,0:T(8,128)(2,1)S(1)}, u32[]{:S(2)}, u32[]{:S(2)}) collective-permute-start(bf16[256,384]{1,0:T(8,128)(2,1)S(1)} %maximum_add_fusion.2), channel_id=1, source_target_pairs={{0,32},{1,33},{2,34},{3,35},{4,36},{5,37},{6,38},{7,39},{8,40},{9,... | collective-permute-start | bytes 589832 | tf_op jit(solution)/shard_map/ppermute | solution.py:308

commit v6 on v5

--- a/solution.py
+++ b/solution.py
@@ -54,53 +54,44 @@
     scalars, residual_in, factor_in, down_in, up_in, near, far, maps, residual, factor, down_map, up_map, sems
 ):
     last = M - KMAX
-    copies = [
-        pltpu.make_async_copy(source, target, sems.at[at])
-        for at, (source, target) in enumerate(
-            [
-                (residual_in, residual),
-                (down_in, down_map),
-                (up_in, up_map),
-                (factor_in.at[:KMAX, :KMAX], factor.at[:KMAX, :KMAX]),
-                (factor_in.at[KMAX:last, :last], factor.at[KMAX:last, :last]),
-                (factor_in.at[last:], factor.at[last:]),
-            ]
-        )
+    parts = [
+        (factor_in.at[:KMAX, :KMAX], factor.at[:KMAX, :KMAX]),
+        (factor_in.at[KMAX:last, :last], factor.at[KMAX:last, :last]),
+        (factor_in.at[last:], factor.at[last:]),
+        (down_in, down_map),
+        (up_in, up_map),
     ]
+    for at in range(0, M, KMAX):
+        parts.append((residual_in.at[:, at : at + KMAX], residual.at[:, at : at + KMAX]))
+    copies = [pltpu.make_async_copy(source, target, sems.at[at]) for at, (source, target) in enumerate(parts)]
     for copy in copies:
         copy.start()
     columns = residual.shape[0]
     first = scalars[0] == 0
-    for copy in copies[:4]:
+    for copy in copies[:3]:
         copy.wait()
-    rows = jnp.concatenate([residual[...].astype(BF), down_map[...], up_map[...]], axis=0)
-    half0 = dot_t(rows[:, :KMAX], factor[:KMAX, :KMAX]).astype(BF)
+    low = factor[:, :FACE].T
+    high = factor[M - FACE :, M - FACE :].T
+    low_head = dot(low, factor[:, :KMAX]).astype(BF)
+    high_head = dot(high, factor[M - FACE :, :KMAX]).astype(BF)
+    low_tail = dot(low[:, last:], factor[last:, last:]).astype(BF)
+    high_tail = dot(high, factor[M - FACE :, last:]).astype(BF)
+    copies[3].wait()
     copies[4].wait()
-    half1 = dot_t(rows[:, :last], factor[KMAX:last, :last]).astype(BF)
-    copies[5].wait()
-    half2 = dot_t(rows, factor[last:, :]).astype(BF)
-    half = jnp.concatenate([half0, half1, half2], axis=1)
+    rows, half = [], []
+    for at in range(3):
+        copies[5 + at].wait()
+        where = slice(at * KMAX, (at + 1) * KMAX)
+        rows.append(jnp.concatenate([residual[:, where].astype(BF), down_map[:, where], up_map[:, where]], axis=0))
+        known = jnp.concatenate(rows, axis=1)
+        half.append(dot_t(known, factor[where, : known.shape[1]]).astype(BF))
+    half2 = half[2]
+    half = jnp.concatenate(half, axis=1)
     first_block = dot(half, factor[:, :KMAX]).astype(BF)
     last_block = dot(half2, factor[last:, last:]).astype(BF)
     middle_block = dot(half[columns:, KMAX:], factor[KMAX:, KMAX:last]).astype(BF)
-    low = factor[:, :FACE].T
-    high = factor[M - FACE :, M - FACE :].T
-    head = jnp.concatenate(
-        [
-            first_block[:columns],
-            dot(low, factor[:, :KMAX]).astype(BF),
-            dot(high, factor[M - FACE :, :KMAX]).astype(BF),
-        ],
-        axis=0,
-    )
-    ends = jnp.concatenate(
-        [
-            last_block[:columns],
-            dot(low[:, last:], factor[last:, last:]).astype(BF),
-            dot(high, factor[M - FACE :, last:]).astype(BF),
-        ],
-        axis=0,
-    )
+    head = jnp.concatenate([first_block[:columns], low_head, high_head], axis=0)
+    ends = jnp.concatenate([last_block[:columns], low_tail, high_tail], axis=0)
     tail = dot(ends, placement(scalars[1])).astype(BF)
     near[...] = jnp.where(first, tail, head)
     far[...] = jnp.where(first, head, tail)
@@ -114,7 +105,7 @@
     reach = columns + 2 * FACE
     shapes = [((reach, KMAX), BF), ((reach, KMAX), BF), ((2 * FACE, M), BF)]
     arrays = [residual, factor, down_map, up_map]
-    scratch = [pltpu.VMEM(array.shape, array.dtype) for array in arrays] + [pltpu.SemaphoreType.DMA((6,))]
+    scratch = [pltpu.VMEM(array.shape, array.dtype) for array in arrays] + [pltpu.SemaphoreType.DMA((8,))]
     spaces = [pl.BlockSpec(memory_space=pltpu.HBM)] * 4
     arrays = [pltpu.with_memory_space_constraint(array, pltpu.HBM) for array in arrays]
     return call(prepare_kernel, shapes, scalars, arrays, (1 << 30, 3 << 20), spaces, scratch)

time: 106 us -> 106 us (level)
  no operation moved by 1% of the time
where the time goes in v6:
time: 106 us
  starting transfers between devices  59.3 us (56%)
  waiting for transfers between devices  30.9 us (29%)
  Pallas kernels  9.95 us (9%)
  matrix products  2.39 us (2%)
  other arithmetic  1.74 us (2%)
  between operations  1.36 us (1%)
    ppermute x41, starting transfers between devices, send(): return lax.ppermute(value, AXES, pairs)  59.3 us
    ppermute x41, waiting for transfers between devices, send(): return lax.ppermute(value, AXES, pairs)  30.9 us
    pallas_call x6, Pallas kernels, call(): pl.pallas_call(kernel, out_shape=[jax.ShapeDtypeStruct(shape, kind) for s...  9.95 us
    dot_general x11, matrix products, dot(): lax.dot_general(a, b, (((1,), (0,)), ((), ())), preferred_element_type=F32)  2.39 us
  transfers between devices with their start and end apart: 41, of which 13 were waited for; matrix products, arithmetic and copies ran while one was open for 1% of the time, Pallas kernels for 5%

profile of v6, /device:TPU:1, one launch (start us, length us, event | category | flops | bytes accessed | tf_op | source)
XLA Modules:
  0.0 105.8 jit_solution(5302165851836038694)
XLA Ops:
  0.7 3.7 %shard_map.55 = (bf16[512,256]{1,0:T(8,128)(2,1)S(1)}, bf16[512,256]{1,0:T(8,128)(2,1)S(1)}, bf16[256,768]{1,0:T(8,128)(2,1)S(1)}) custom-call(s32[3]{0:T(128)S(1)} %pad_add_fusion.scalars, f32[256,768]{1,0:T(8,128)} %bitcast.18, bf16[768,768]{1,0:T(8,128)(2,1)} %bitcast.16, bf16[128,768]{1,0:T(8,128)(2,1)} %bitcast.20, bf16[128,768]{1,0:T(8,128)(2,1)} %bitcast.21), custom_call_target="tpu_custom_call" | custom-call | flops 1073741824 | bytes 3145728 | tf_op jit(solution)/shard_map/pallas_call | solution.py:42
  4.5 8.9 %collective-permute-start = (bf16[512,256]{1,0:T(8,128)(2,1)S(1)}, bf16[512,256]{1,0:T(8,128)(2,1)S(1)}, u32[]{:S(2)}, u32[]{:S(2)}) collective-permute-start(bf16[512,256]{1,0:T(8,128)(2,1)S(1)} %get-tuple-element.89), channel_id=1, source_target_pairs={{0,1},{1,2},{2,3},{3,4},{4,5},{5,6},{6,7},{7,8},{8,9},{9,10},{10,1... | collective-permute-start | bytes 786440 | tf_op jit(solution)/shard_map/ppermute | solution.py:299
  13.4 4.9 %collective-permute-done.near = bf16[512,256]{1,0:T(8,128)(2,1)S(1)} collective-permute-done((bf16[512,256]{1,0:T(8,128)(2,1)S(1)}, bf16[512,256]{1,0:T(8,128)(2,1)S(1)}, u32[]{:S(2)}, u32[]{:S(2)}) %collective-permute-start) | collective-permute-done | bytes 262176 | tf_op jit(solution)/shard_map/ppermute | solution.py:299
  18.3 3.7 %collective-permute-done.1.far = bf16[512,256]{1,0:T(8,128)(2,1)S(1)} collective-permute-done((bf16[512,256]{1,0:T(8,128)(2,1)S(1)}, bf16[512,256]{1,0:T(8,128)(2,1)S(1)}, u32[]{:S(2)}, u32[]{:S(2)}) %collective-permute-start.1) | collective-permute-done | bytes 262176 | tf_op jit(solution)/shard_map/ppermute | solution.py:299
  21.9 1.0 shard_map.56
  23.6 0.9 collective-permute-done.2
  24.6 3.2 %collective-permute-start.3 = (bf16[1024,128]{1,0:T(8,128)(2,1)S(1)}, bf16[1024,128]{1,0:T(8,128)(2,1)S(1)}, u32[]{:S(2)}, u32[]{:S(2)}) collective-permute-start(bf16[1024,128]{1,0:T(8,128)(2,1)S(1)} %pad_maximum_fusion.1.own), channel_id=1, source_target_pairs={{0,1},{1,2},{2,3},{3,4},{4,5},{5,6},{6,7},{7,8},{8,9},{9,10},{10,1... | collective-permute-start | bytes 786440 | tf_op jit(solution)/shard_map/ppermute | solution.py:299
  27.8 3.3 %collective-permute-done.3.near = bf16[1024,128]{1,0:T(8,128)(2,1)S(1)} collective-permute-done((bf16[1024,128]{1,0:T(8,128)(2,1)S(1)}, bf16[1024,128]{1,0:T(8,128)(2,1)S(1)}, u32[]{:S(2)}, u32[]{:S(2)}) %collective-permute-start.3) | collective-permute-done | bytes 262176 | tf_op jit(solution)/shard_map/ppermute | solution.py:299
  31.3 3.5 %collective-permute-start.5 = (f32[256,128]{1,0:T(8,128)S(1)}, f32[256,128]{1,0:T(8,128)S(1)}, u32[]{:S(2)}, u32[]{:S(2)}) collective-permute-start(f32[256,128]{1,0:T(8,128)S(1)} %convolution_add_fusion), channel_id=1, source_target_pairs={{0,32},{1,33},{2,34},{3,35},{4,36},{5,37},{6,38},{7,39},{8,40},{9,... | collective-permute-start | bytes 393224 | tf_op jit(solution)/shard_map/ppermute | solution.py:299
  35.7 1.9 %collective-permute-start.6 = (bf16[256,128]{1,0:T(8,128)(2,1)S(1)}, bf16[256,128]{1,0:T(8,128)(2,1)S(1)}, u32[]{:S(2)}, u32[]{:S(2)}) collective-permute-start(bf16[256,128]{1,0:T(8,128)(2,1)S(1)} %add_convert_fusion.7), channel_id=1, source_target_pairs={{0,66},{1,67},{2,68},{3,69},{4,70},{5,71},{6,72},{7,73},{8,74},{9,... | collective-permute-start | bytes 196616 | tf_op jit(solution)/shard_map/ppermute | solution.py:299
  37.6 4.5 %collective-permute-start.7 = (bf16[256,128]{1,0:T(8,128)(2,1)S(1)}, bf16[256,128]{1,0:T(8,128)(2,1)S(1)}, u32[]{:S(2)}, u32[]{:S(2)}) collective-permute-start(bf16[256,128]{1,0:T(8,128)(2,1)S(1)} %add_convert_fusion.7), channel_id=1, source_target_pairs={{0,65},{1,66},{2,67},{3,68},{4,69},{5,70},{6,71},{7,72},{8,73},{9,... | collective-permute-start | bytes 196616 | tf_op jit(solution)/shard_map/ppermute | solution.py:299
  42.1 0.7 collective-permute-start.8
  42.8 1.1 %shard_map.57 = (bf16[640,128]{1,0:T(8,128)(2,1)S(1)}, bf16[640,128]{1,0:T(8,128)(2,1)S(1)}, bf16[896,128]{1,0:T(8,128)(2,1)S(1)}, f32[256,128]{1,0:T(8,128)S(1)...) custom-call(s32[3]{0:T(128)S(1)} %pad_add_fusion.scalars, ...), custom_call_target="tpu_custom_call" | custom-call | flops 1024 | bytes 1024 | tf_op jit(solution)/shard_map/pallas_call | solution.py:42
  44.3 4.5 %collective-permute-start.15 = (bf16[896,128]{1,0:T(8,128)(2,1)S(1)}, bf16[896,128]{1,0:T(8,128)(2,1)S(1)}, u32[]{:S(2)}, u32[]{:S(2)}) collective-permute-start(bf16[896,128]{1,0:T(8,128)(2,1)S(1)} %get-tuple-element.106.own), channel_id=1, source_target_pairs={{0,1},{1,2},{2,3},{3,4},{4,5},{5,6},{6,7},{7,8},{8,9},{9,10},{10,1... | collective-permute-start | bytes 688136 | tf_op jit(solution)/shard_map/ppermute | solution.py:299
  48.9 0.7 collective-permute-start.12
  49.6 0.7 collective-permute-start.13
  50.2 0.7 collective-permute-start.14
  51.0 0.8 collective-permute-done.15.near
  52.0 2.4 %collective-permute-start.16 = (f32[256,128]{1,0:T(8,128)S(1)}, f32[256,128]{1,0:T(8,128)S(1)}, u32[]{:S(2)}, u32[]{:S(2)}) collective-permute-start(f32[256,128]{1,0:T(8,128)S(1)} %add.82), channel_id=1, source_target_pairs={{0,32},{1,33},{2,34},{3,35},{4,36},{5,37},{6,38},{7,39},{8,40},{9,... | collective-permute-start | bytes 393224 | tf_op jit(solution)/shard_map/ppermute | solution.py:299
  54.8 0.5 collective-permute-start.21
  55.4 0.7 collective-permute-start.17
  56.0 0.7 collective-permute-start.18
  56.7 0.7 collective-permute-start.19
  57.4 0.8 collective-permute-start.20
  58.3 0.9 shard_map.58
  60.8 0.6 collective-permute-done.23
  61.4 0.7 collective-permute-start.24
  62.1 0.7 collective-permute-start.25
  62.8 0.7 collective-permute-start.26
  63.5 3.3 %collective-permute-start.28 = (bf16[256,128]{1,0:T(8,128)(2,1)S(1)}, bf16[256,128]{1,0:T(8,128)(2,1)S(1)}, u32[]{:S(2)}, u32[]{:S(2)}) collective-permute-start(bf16[256,128]{1,0:T(8,128)(2,1)S(1)} %get-tuple-element.176), channel_id=1, source_target_pairs={{0,1},{1,2},{2,3},{3,4},{4,5},{5,6},{6,7},{7,8},{8,9},{9,10},{10,1... | collective-permute-start | bytes 196616 | tf_op jit(solution)/shard_map/ppermute | solution.py:299
  67.0 1.1 %collective-permute-done.28 = bf16[256,128]{1,0:T(8,128)(2,1)S(1)} collective-permute-done((bf16[256,128]{1,0:T(8,128)(2,1)S(1)}, bf16[256,128]{1,0:T(8,128)(2,1)S(1)}, u32[]{:S(2)}, u32[]{:S(2)}) %collective-permute-start.28) | collective-permute-done | bytes 65568 | tf_op jit(solution)/shard_map/ppermute | solution.py:299
  68.4 3.4 %collective-permute-start.29 = (f32[256,128]{1,0:T(8,128)S(1)}, f32[256,128]{1,0:T(8,128)S(1)}, u32[]{:S(2)}, u32[]{:S(2)}) collective-permute-start(f32[256,128]{1,0:T(8,128)S(1)} %add.90), channel_id=1, source_target_pairs={{0,32},{1,33},{2,34},{3,35},{4,36},{5,37},{6,38},{7,39},{8,40},{9,... | collective-permute-start | bytes 393224 | tf_op jit(solution)/shard_map/ppermute | solution.py:299
  71.8 1.9 %collective-permute-start.33 = (bf16[256,128]{1,0:T(8,128)(2,1)S(1)}, bf16[256,128]{1,0:T(8,128)(2,1)S(1)}, u32[]{:S(2)}, u32[]{:S(2)}) collective-permute-start(bf16[256,128]{1,0:T(8,128)(2,1)S(1)} %get-tuple-element.174), channel_id=1, source_target_pairs={{0,1},{1,2},{2,3},{3,4},{4,5},{5,6},{6,7},{7,8},{8,9},{9,10},{10,1... | collective-permute-start | bytes 196616 | tf_op jit(solution)/shard_map/ppermute | solution.py:299
  73.7 0.7 collective-permute-start.30
  74.4 0.7 collective-permute-start.31
  75.1 0.7 collective-permute-start.32
  75.9 0.9 shard_map.59.down
  77.1 2.8 %collective-permute-start.36 = (f32[256,128]{1,0:T(8,128)S(1)}, f32[256,128]{1,0:T(8,128)S(1)}, u32[]{:S(2)}, u32[]{:S(2)}) collective-permute-start(f32[256,128]{1,0:T(8,128)S(1)} %add.96), channel_id=1, source_target_pairs={{0,32},{1,33},{2,34},{3,35},{4,36},{5,37},{6,38},{7,39},{8,40},{9,... | collective-permute-start | bytes 393224 | tf_op jit(solution)/shard_map/ppermute | solution.py:299
  79.9 0.9 collective-permute-done.36
  80.8 1.3 %collective-permute-start.37 = (bf16[256,128]{1,0:T(8,128)(2,1)S(1)}, bf16[256,128]{1,0:T(8,128)(2,1)S(1)}, u32[]{:S(2)}, u32[]{:S(2)}) collective-permute-start(bf16[256,128]{1,0:T(8,128)(2,1)S(1)} %add_convert_fusion), channel_id=1, source_target_pairs={{64,2},{65,3},{66,4},{67,5},{68,6},{69,7},{70,8},{71,9},{72,10},{7... | collective-permute-start | bytes 196616 | tf_op jit(solution)/shard_map/ppermute | solution.py:299
  82.1 1.3 %collective-permute-start.38 = (bf16[256,128]{1,0:T(8,128)(2,1)S(1)}, bf16[256,128]{1,0:T(8,128)(2,1)S(1)}, u32[]{:S(2)}, u32[]{:S(2)}) collective-permute-start(bf16[256,128]{1,0:T(8,128)(2,1)S(1)} %add_convert_fusion), channel_id=1, source_target_pairs={{64,1},{65,2},{66,3},{67,4},{68,5},{69,6},{70,7},{71,8},{72,9},{73... | collective-permute-start | bytes 196616 | tf_op jit(solution)/shard_map/ppermute | solution.py:299
  83.4 0.7 collective-permute-start.39
  84.2 2.4 %shard_map.60 = (f32[256,768]{1,0:T(8,128)S(1)}, bf16[640,768]{1,0:T(8,128)(2,1)S(1)}) custom-call(s32[3]{0:T(128)S(1)} %pad_add_fusion.scalars, f32[256,768]{1,0:T(8,128)S(1)} %get-tuple-element.92.adjusted, bf16[256,256]{1,0:T(8,128)(2,1)S(1)} %get-tuple-element.93.near_basis, bf16[256,256]{1,0:T(8,128)(2,1)S(1)} %get-tuple-element.94.far_basis, ...), custom_call_target="tpu_custom_call" | custom-call | flops 1024 | bytes 1024 | tf_op jit(solution)/shard_map/pallas_call | solution.py:42
  86.6 10.1 %collective-permute-done.37 = bf16[256,128]{1,0:T(8,128)(2,1)S(1)} collective-permute-done((bf16[256,128]{1,0:T(8,128)(2,1)S(1)}, bf16[256,128]{1,0:T(8,128)(2,1)S(1)}, u32[]{:S(2)}, u32[]{:S(2)}) %collective-permute-start.37) | collective-permute-done | bytes 65568 | tf_op jit(solution)/shard_map/ppermute | solution.py:299
  96.7 3.0 %collective-permute-done.38 = bf16[256,128]{1,0:T(8,128)(2,1)S(1)} collective-permute-done((bf16[256,128]{1,0:T(8,128)(2,1)S(1)}, bf16[256,128]{1,0:T(8,128)(2,1)S(1)}, u32[]{:S(2)}, u32[]{:S(2)}) %collective-permute-start.38) | collective-permute-done | bytes 65568 | tf_op jit(solution)/shard_map/ppermute | solution.py:299
  99.8 3.4 %collective-permute-start.40 = (bf16[256,384]{1,0:T(8,128)(2,1)S(1)}, bf16[256,384]{1,0:T(8,128)(2,1)S(1)}, u32[]{:S(2)}, u32[]{:S(2)}) collective-permute-start(bf16[256,384]{1,0:T(8,128)(2,1)S(1)} %maximum_add_fusion.2), channel_id=1, source_target_pairs={{0,32},{1,33},{2,34},{3,35},{4,36},{5,37},{6,38},{7,39},{8,40},{9,... | collective-permute-start | bytes 589832 | tf_op jit(solution)/shard_map/ppermute | solution.py:299
  103.2 1.1 %collective-permute-done.40 = bf16[256,384]{1,0:T(8,128)(2,1)S(1)} collective-permute-done((bf16[256,384]{1,0:T(8,128)(2,1)S(1)}, bf16[256,384]{1,0:T(8,128)(2,1)S(1)}, u32[]{:S(2)}, u32[]{:S(2)}) %collective-permute-start.40) | collective-permute-done | bytes 196640 | tf_op jit(solution)/shard_map/ppermute | solution.py:299
  104.8 1.0 add_bitcast_fusion
  (97 shorter events, 6.5 us)
Async XLA Ops:
  0.7 21.2 %copy-start.1 = (f32[1,1,256,768]{3,2,1,0:T(8,128)S(1)}, f32[1,1,256,768]{3,2,1,0:T(8,128)}, u32[]{:S(2)}) copy-start(f32[1,1,256,768]{3,2,1,0:T(8,128)} %param.5) | copy-start | bytes 2359300
  4.5 13.8 %collective-permute-start = (bf16[512,256]{1,0:T(8,128)(2,1)S(1)}, bf16[512,256]{1,0:T(8,128)(2,1)S(1)}, u32[]{:S(2)}, u32[]{:S(2)}) collective-permute-start(bf16[512,256]{1,0:T(8,128)(2,1)S(1)} %get-tuple-element.89), channel_id=1, source_target_pairs={{0,1},{1,2},{2,3},{3,4},{4,5},{5,6},{6,7},{7,8},{8,9},{9,10},{10,1... | collective-permute-start | bytes 786440 | tf_op jit(solution)/shard_map/ppermute | solution.py:299
  13.4 8.5 %collective-permute-start.1 = (bf16[512,256]{1,0:T(8,128)(2,1)S(1)}, bf16[512,256]{1,0:T(8,128)(2,1)S(1)}, u32[]{:S(2)}, u32[]{:S(2)}) collective-permute-start(bf16[512,256]{1,0:T(8,128)(2,1)S(1)} %get-tuple-element.90), channel_id=1, source_target_pairs={{0,31},{1,0},{2,1},{3,2},{4,3},{5,4},{6,5},{7,6},{8,7},{9,8},{10,9... | collective-permute-start | bytes 786440 | tf_op jit(solution)/shard_map/ppermute | solution.py:299
  23.0 1.5 %collective-permute-start.2 = (bf16[640,128]{1,0:T(8,128)(2,1)S(1)}, bf16[640,128]{1,0:T(8,128)(2,1)S(1)}, u32[]{:S(2)}, u32[]{:S(2)}) collective-permute-start(bf16[640,128]{1,0:T(8,128)(2,1)S(1)} %get-tuple-element.95), channel_id=1, source_target_pairs={{0,32},{1,33},{2,34},{3,35},{4,36},{5,37},{6,38},{7,39},{8,40},{9,... | collective-permute-start | bytes 491528 | tf_op jit(solution)/shard_map/ppermute | solution.py:299
  23.1 4.7 %collective-permute-start.4 = (bf16[640,128]{1,0:T(8,128)(2,1)S(1)}, bf16[640,128]{1,0:T(8,128)(2,1)S(1)}, u32[]{:S(2)}, u32[]{:S(2)}) collective-permute-start(bf16[640,128]{1,0:T(8,128)(2,1)S(1)} %get-tuple-element.96.outer), channel_id=1, source_target_pairs={{0,32},{1,33},{2,34},{3,35},{4,36},{5,37},{6,38},{7,39},{8,40},{9,... | collective-permute-start | bytes 491528 | tf_op jit(solution)/shard_map/ppermute | solution.py:299
  24.6 6.5 %collective-permute-start.3 = (bf16[1024,128]{1,0:T(8,128)(2,1)S(1)}, bf16[1024,128]{1,0:T(8,128)(2,1)S(1)}, u32[]{:S(2)}, u32[]{:S(2)}) collective-permute-start(bf16[1024,128]{1,0:T(8,128)(2,1)S(1)} %pad_maximum_fusion.1.own), channel_id=1, source_target_pairs={{0,1},{1,2},{2,3},{3,4},{4,5},{5,6},{6,7},{7,8},{8,9},{9,10},{10,1... | collective-permute-start | bytes 786440 | tf_op jit(solution)/shard_map/ppermute | solution.py:299
  31.3 4.5 %collective-permute-start.5 = (f32[256,128]{1,0:T(8,128)S(1)}, f32[256,128]{1,0:T(8,128)S(1)}, u32[]{:S(2)}, u32[]{:S(2)}) collective-permute-start(f32[256,128]{1,0:T(8,128)S(1)} %convolution_add_fusion), channel_id=1, source_target_pairs={{0,32},{1,33},{2,34},{3,35},{4,36},{5,37},{6,38},{7,39},{8,40},{9,... | collective-permute-start | bytes 393224 | tf_op jit(solution)/shard_map/ppermute | solution.py:299
  34.7 8.0 %collective-permute-start.10 = (bf16[640,128]{1,0:T(8,128)(2,1)S(1)}, bf16[640,128]{1,0:T(8,128)(2,1)S(1)}, u32[]{:S(2)}, u32[]{:S(2)}) collective-permute-start(bf16[640,128]{1,0:T(8,128)(2,1)S(1)} %get-tuple-element.97.extra), channel_id=1, source_target_pairs={{0,32},{1,33},{2,34},{3,35},{4,36},{5,37},{6,38},{7,39},{8,40},{9,... | collective-permute-start | bytes 491528 | tf_op jit(solution)/shard_map/ppermute | solution.py:299
  34.8 7.9 %collective-permute-start.9 = (bf16[1024,128]{1,0:T(8,128)(2,1)S(1)}, bf16[1024,128]{1,0:T(8,128)(2,1)S(1)}, u32[]{:S(2)}, u32[]{:S(2)}) collective-permute-start(bf16[1024,128]{1,0:T(8,128)(2,1)S(1)} %collective-permute-done.3.near), channel_id=1, source_target_pairs={{0,32},{1,33},{2,34},{3,35},{4,36},{5,37},{6,38},{7,39},{8,40},{9,... | collective-permute-start | bytes 786440 | tf_op jit(solution)/shard_map/ppermute | solution.py:299
  35.7 8.1 %collective-permute-start.6 = (bf16[256,128]{1,0:T(8,128)(2,1)S(1)}, bf16[256,128]{1,0:T(8,128)(2,1)S(1)}, u32[]{:S(2)}, u32[]{:S(2)}) collective-permute-start(bf16[256,128]{1,0:T(8,128)(2,1)S(1)} %add_convert_fusion.7), channel_id=1, source_target_pairs={{0,66},{1,67},{2,68},{3,69},{4,70},{5,71},{6,72},{7,73},{8,74},{9,... | collective-permute-start | bytes 196616 | tf_op jit(solution)/shard_map/ppermute | solution.py:299
  37.6 6.2 %collective-permute-start.7 = (bf16[256,128]{1,0:T(8,128)(2,1)S(1)}, bf16[256,128]{1,0:T(8,128)(2,1)S(1)}, u32[]{:S(2)}, u32[]{:S(2)}) collective-permute-start(bf16[256,128]{1,0:T(8,128)(2,1)S(1)} %add_convert_fusion.7), channel_id=1, source_target_pairs={{0,65},{1,66},{2,67},{3,68},{4,69},{5,70},{6,71},{7,72},{8,73},{9,... | collective-permute-start | bytes 196616 | tf_op jit(solution)/shard_map/ppermute | solution.py:299
  42.1 1.8 %collective-permute-start.8 = (bf16[256,128]{1,0:T(8,128)(2,1)S(1)}, bf16[256,128]{1,0:T(8,128)(2,1)S(1)}, u32[]{:S(2)}, u32[]{:S(2)}) collective-permute-start(bf16[256,128]{1,0:T(8,128)(2,1)S(1)} %add_convert_fusion.7), channel_id=1, source_target_pairs={{0,64},{1,65},{2,66},{3,67},{4,68},{5,69},{6,70},{7,71},{8,72},{9,... | collective-permute-start | bytes 196616 | tf_op jit(solution)/shard_map/ppermute | solution.py:299
  44.1 4.7 %collective-permute-start.11 = (f32[256,128]{1,0:T(8,128)S(1)}, f32[256,128]{1,0:T(8,128)S(1)}, u32[]{:S(2)}, u32[]{:S(2)}) collective-permute-start(f32[256,128]{1,0:T(8,128)S(1)} %add.80), channel_id=1, source_target_pairs={{0,32},{1,33},{2,34},{3,35},{4,36},{5,37},{6,38},{7,39},{8,40},{9,... | collective-permute-start | bytes 393224 | tf_op jit(solution)/shard_map/ppermute | solution.py:299
  44.3 7.5 %collective-permute-start.15 = (bf16[896,128]{1,0:T(8,128)(2,1)S(1)}, bf16[896,128]{1,0:T(8,128)(2,1)S(1)}, u32[]{:S(2)}, u32[]{:S(2)}) collective-permute-start(bf16[896,128]{1,0:T(8,128)(2,1)S(1)} %get-tuple-element.106.own), channel_id=1, source_target_pairs={{0,1},{1,2},{2,3},{3,4},{4,5},{5,6},{6,7},{7,8},{8,9},{9,10},{10,1... | collective-permute-start | bytes 688136 | tf_op jit(solution)/shard_map/ppermute | solution.py:299
  48.9 2.1 %collective-permute-start.12 = (bf16[256,128]{1,0:T(8,128)(2,1)S(1)}, bf16[256,128]{1,0:T(8,128)(2,1)S(1)}, u32[]{:S(2)}, u32[]{:S(2)}) collective-permute-start(bf16[256,128]{1,0:T(8,128)(2,1)S(1)} %add_convert_fusion.6), channel_id=1, source_target_pairs={{64,130},{65,131},{66,132},{67,133},{68,134},{69,135},{70,136},{71... | collective-permute-start | bytes 196616 | tf_op jit(solution)/shard_map/ppermute | solution.py:299
  49.6 1.4 %collective-permute-start.13 = (bf16[256,128]{1,0:T(8,128)(2,1)S(1)}, bf16[256,128]{1,0:T(8,128)(2,1)S(1)}, u32[]{:S(2)}, u32[]{:S(2)}) collective-permute-start(bf16[256,128]{1,0:T(8,128)(2,1)S(1)} %add_convert_fusion.6), channel_id=1, source_target_pairs={{64,129},{65,130},{66,131},{67,132},{68,133},{69,134},{70,135},{71... | collective-permute-start | bytes 196616 | tf_op jit(solution)/shard_map/ppermute | solution.py:299
  50.2 0.7 collective-permute-start.14
  52.0 3.3 %collective-permute-start.16 = (f32[256,128]{1,0:T(8,128)S(1)}, f32[256,128]{1,0:T(8,128)S(1)}, u32[]{:S(2)}, u32[]{:S(2)}) collective-permute-start(f32[256,128]{1,0:T(8,128)S(1)} %add.82), channel_id=1, source_target_pairs={{0,32},{1,33},{2,34},{3,35},{4,36},{5,37},{6,38},{7,39},{8,40},{9,... | collective-permute-start | bytes 393224 | tf_op jit(solution)/shard_map/ppermute | solution.py:299
  54.4 5.1 %copy-start.2 = (bf16[256,384]{1,0:T(8,128)(2,1)}, bf16[256,384]{1,0:T(8,128)(2,1)S(1)}, u32[]{:S(2)}) copy-start(bf16[256,384]{1,0:T(8,128)(2,1)S(1)} %maximum_add_fusion) | copy-start | bytes 589828
  54.6 4.5 %collective-permute-start.22 = (f32[256,128]{1,0:T(8,128)S(1)}, f32[256,128]{1,0:T(8,128)S(1)}, u32[]{:S(2)}, u32[]{:S(2)}) collective-permute-start(f32[256,128]{1,0:T(8,128)S(1)} %fusion.54), channel_id=1, source_target_pairs={{0,32},{1,33},{2,34},{3,35},{4,36},{5,37},{6,38},{7,39},{8,40},{9,... | collective-permute-start | bytes 393224 | tf_op jit(solution)/shard_map/ppermute | solution.py:299
  54.8 2.6 %collective-permute-start.21 = (bf16[896,128]{1,0:T(8,128)(2,1)S(1)}, bf16[896,128]{1,0:T(8,128)(2,1)S(1)}, u32[]{:S(2)}, u32[]{:S(2)}) collective-permute-start(bf16[896,128]{1,0:T(8,128)(2,1)S(1)} %collective-permute-done.15.near), channel_id=1, source_target_pairs={{0,32},{1,33},{2,34},{3,35},{4,36},{5,37},{6,38},{7,39},{8,40},{9,... | collective-permute-start | bytes 688136 | tf_op jit(solution)/shard_map/ppermute | solution.py:299
  55.4 3.8 %collective-permute-start.17 = (bf16[256,128]{1,0:T(8,128)(2,1)S(1)}, bf16[256,128]{1,0:T(8,128)(2,1)S(1)}, u32[]{:S(2)}, u32[]{:S(2)}) collective-permute-start(bf16[256,128]{1,0:T(8,128)(2,1)S(1)} %add_convert_fusion.5), channel_id=1, source_target_pairs={{128,195},{129,196},{130,197},{131,198},{132,199},{133,200},{134,2... | collective-permute-start | bytes 196616 | tf_op jit(solution)/shard_map/ppermute | solution.py:299
  56.0 3.1 %collective-permute-start.18 = (bf16[256,128]{1,0:T(8,128)(2,1)S(1)}, bf16[256,128]{1,0:T(8,128)(2,1)S(1)}, u32[]{:S(2)}, u32[]{:S(2)}) collective-permute-start(bf16[256,128]{1,0:T(8,128)(2,1)S(1)} %add_convert_fusion.5), channel_id=1, source_target_pairs={{128,194},{129,195},{130,196},{131,197},{132,198},{133,199},{134,2... | collective-permute-start | bytes 196616 | tf_op jit(solution)/shard_map/ppermute | solution.py:299
  56.7 2.5 %collective-permute-start.19 = (bf16[256,128]{1,0:T(8,128)(2,1)S(1)}, bf16[256,128]{1,0:T(8,128)(2,1)S(1)}, u32[]{:S(2)}, u32[]{:S(2)}) collective-permute-start(bf16[256,128]{1,0:T(8,128)(2,1)S(1)} %add_convert_fusion.5), channel_id=1, source_target_pairs={{128,193},{129,194},{130,195},{131,196},{132,197},{133,198},{134,1... | collective-permute-start | bytes 196616 | tf_op jit(solution)/shard_map/ppermute | solution.py:299
  57.4 1.8 %collective-permute-start.20 = (bf16[256,128]{1,0:T(8,128)(2,1)S(1)}, bf16[256,128]{1,0:T(8,128)(2,1)S(1)}, u32[]{:S(2)}, u32[]{:S(2)}) collective-permute-start(bf16[256,128]{1,0:T(8,128)(2,1)S(1)} %add_convert_fusion.5), channel_id=1, source_target_pairs={{128,192},{129,193},{130,194},{131,195},{132,196},{133,197},{134,1... | collective-permute-start | bytes 196616 | tf_op jit(solution)/shard_map/ppermute | solution.py:299
  59.6 7.2 %slice-start = ((bf16[256,384]{1,0:T(8,128)(2,1)}), bf16[256,256]{1,0:T(8,128)(2,1)S(1)}, s32[]{:S(2)}) async-start(bf16[256,384]{1,0:T(8,128)(2,1)} %copy-done.2), calls=%async_computation | async-start | bytes 262144 | tf_op jit(solution)/shard_map/slice | solution.py:405
  59.6 16.3 %collective-permute-start.34 = (bf16[256,384]{1,0:T(8,128)(2,1)S(1)}, bf16[256,384]{1,0:T(8,128)(2,1)S(1)}, u32[]{:S(2)}, u32[]{:S(2)}) collective-permute-start(bf16[256,384]{1,0:T(8,128)(2,1)S(1)} %add.95.mine), channel_id=1, source_target_pairs={{0,32},{1,33},{2,34},{3,35},{4,36},{5,37},{6,38},{7,39},{8,40},{9,... | collective-permute-start | bytes 589832 | tf_op jit(solution)/shard_map/ppermute | solution.py:299
  60.0 1.3 %collective-permute-start.23 = (f32[256,128]{1,0:T(8,128)S(1)}, f32[256,128]{1,0:T(8,128)S(1)}, u32[]{:S(2)}, u32[]{:S(2)}) collective-permute-start(f32[256,128]{1,0:T(8,128)S(1)} %add.85), channel_id=1, source_target_pairs={{0,32},{1,33},{2,34},{3,35},{4,36},{5,37},{6,38},{7,39},{8,40},{9,... | collective-permute-start | bytes 393224 | tf_op jit(solution)/shard_map/ppermute | solution.py:299
  60.4 3.0 %collective-permute-start.27 = (f32[256,128]{1,0:T(8,128)S(1)}, f32[256,128]{1,0:T(8,128)S(1)}, u32[]{:S(2)}, u32[]{:S(2)}) collective-permute-start(f32[256,128]{1,0:T(8,128)S(1)} %fusion.52), channel_id=1, source_target_pairs={{0,32},{1,33},{2,34},{3,35},{4,36},{5,37},{6,38},{7,39},{8,40},{9,... | collective-permute-start | bytes 393224 | tf_op jit(solution)/shard_map/ppermute | solution.py:299
  61.4 6.7 %collective-permute-start.24 = (bf16[256,128]{1,0:T(8,128)(2,1)S(1)}, bf16[256,128]{1,0:T(8,128)(2,1)S(1)}, u32[]{:S(2)}, u32[]{:S(2)}) collective-permute-start(bf16[256,128]{1,0:T(8,128)(2,1)S(1)} %add_convert_fusion.4), channel_id=1, source_target_pairs={{192,130},{193,131},{194,132},{195,133},{196,134},{197,135},{198,1... | collective-permute-start | bytes 196616 | tf_op jit(solution)/shard_map/ppermute | solution.py:299
  62.1 6.0 %collective-permute-start.25 = (bf16[256,128]{1,0:T(8,128)(2,1)S(1)}, bf16[256,128]{1,0:T(8,128)(2,1)S(1)}, u32[]{:S(2)}, u32[]{:S(2)}) collective-permute-start(bf16[256,128]{1,0:T(8,128)(2,1)S(1)} %add_convert_fusion.4), channel_id=1, source_target_pairs={{192,129},{193,130},{194,131},{195,132},{196,133},{197,134},{198,1... | collective-permute-start | bytes 196616 | tf_op jit(solution)/shard_map/ppermute | solution.py:299
  62.8 5.4 %collective-permute-start.26 = (bf16[256,128]{1,0:T(8,128)(2,1)S(1)}, bf16[256,128]{1,0:T(8,128)(2,1)S(1)}, u32[]{:S(2)}, u32[]{:S(2)}) collective-permute-start(bf16[256,128]{1,0:T(8,128)(2,1)S(1)} %add_convert_fusion.4), channel_id=1, source_target_pairs={{192,128},{193,129},{194,130},{195,131},{196,132},{197,133},{198,1... | collective-permute-start | bytes 196616 | tf_op jit(solution)/shard_map/ppermute | solution.py:299
  63.5 4.6 %collective-permute-start.28 = (bf16[256,128]{1,0:T(8,128)(2,1)S(1)}, bf16[256,128]{1,0:T(8,128)(2,1)S(1)}, u32[]{:S(2)}, u32[]{:S(2)}) collective-permute-start(bf16[256,128]{1,0:T(8,128)(2,1)S(1)} %get-tuple-element.176), channel_id=1, source_target_pairs={{0,1},{1,2},{2,3},{3,4},{4,5},{5,6},{6,7},{7,8},{8,9},{9,10},{10,1... | collective-permute-start | bytes 196616 | tf_op jit(solution)/shard_map/ppermute | solution.py:299
  68.4 5.3 %collective-permute-start.29 = (f32[256,128]{1,0:T(8,128)S(1)}, f32[256,128]{1,0:T(8,128)S(1)}, u32[]{:S(2)}, u32[]{:S(2)}) collective-permute-start(f32[256,128]{1,0:T(8,128)S(1)} %add.90), channel_id=1, source_target_pairs={{0,32},{1,33},{2,34},{3,35},{4,36},{5,37},{6,38},{7,39},{8,40},{9,... | collective-permute-start | bytes 393224 | tf_op jit(solution)/shard_map/ppermute | solution.py:299
  71.8 5.0 %collective-permute-start.33 = (bf16[256,128]{1,0:T(8,128)(2,1)S(1)}, bf16[256,128]{1,0:T(8,128)(2,1)S(1)}, u32[]{:S(2)}, u32[]{:S(2)}) collective-permute-start(bf16[256,128]{1,0:T(8,128)(2,1)S(1)} %get-tuple-element.174), channel_id=1, source_target_pairs={{0,1},{1,2},{2,3},{3,4},{4,5},{5,6},{6,7},{7,8},{8,9},{9,10},{10,1... | collective-permute-start | bytes 196616 | tf_op jit(solution)/shard_map/ppermute | solution.py:299
  73.7 3.1 %collective-permute-start.30 = (bf16[256,128]{1,0:T(8,128)(2,1)S(1)}, bf16[256,128]{1,0:T(8,128)(2,1)S(1)}, u32[]{:S(2)}, u32[]{:S(2)}) collective-permute-start(bf16[256,128]{1,0:T(8,128)(2,1)S(1)} %add_convert_fusion.2), channel_id=1, source_target_pairs={{128,66},{129,67},{130,68},{131,69},{132,70},{133,71},{134,72},{13... | collective-permute-start | bytes 196616 | tf_op jit(solution)/shard_map/ppermute | solution.py:299
  74.4 2.4 %collective-permute-start.31 = (bf16[256,128]{1,0:T(8,128)(2,1)S(1)}, bf16[256,128]{1,0:T(8,128)(2,1)S(1)}, u32[]{:S(2)}, u32[]{:S(2)}) collective-permute-start(bf16[256,128]{1,0:T(8,128)(2,1)S(1)} %add_convert_fusion.2), channel_id=1, source_target_pairs={{128,65},{129,66},{130,67},{131,68},{132,69},{133,70},{134,71},{13... | collective-permute-start | bytes 196616 | tf_op jit(solution)/shard_map/ppermute | solution.py:299
  75.1 1.7 %collective-permute-start.32 = (bf16[256,128]{1,0:T(8,128)(2,1)S(1)}, bf16[256,128]{1,0:T(8,128)(2,1)S(1)}, u32[]{:S(2)}, u32[]{:S(2)}) collective-permute-start(bf16[256,128]{1,0:T(8,128)(2,1)S(1)} %add_convert_fusion.2), channel_id=1, source_target_pairs={{128,64},{129,65},{130,66},{131,67},{132,68},{133,69},{134,70},{13... | collective-permute-start | bytes 196616 | tf_op jit(solution)/shard_map/ppermute | solution.py:299
  76.8 7.4 %copy-start = (bf16[1,1,768,768]{3,2,1,0:T(8,128)(2,1)S(1)}, bf16[1,1,768,768]{3,2,1,0:T(8,128)(2,1)}, u32[]{:S(2)}) copy-start(bf16[1,1,768,768]{3,2,1,0:T(8,128)(2,1)} %param.6) | copy-start | bytes 3538948
  77.1 3.7 %collective-permute-start.36 = (f32[256,128]{1,0:T(8,128)S(1)}, f32[256,128]{1,0:T(8,128)S(1)}, u32[]{:S(2)}, u32[]{:S(2)}) collective-permute-start(f32[256,128]{1,0:T(8,128)S(1)} %add.96), channel_id=1, source_target_pairs={{0,32},{1,33},{2,34},{3,35},{4,36},{5,37},{6,38},{7,39},{8,40},{9,... | collective-permute-start | bytes 393224 | tf_op jit(solution)/shard_map/ppermute | solution.py:299
  79.8 4.3 %collective-permute-start.35 = (bf16[256,128]{1,0:T(8,128)(2,1)S(1)}, bf16[256,128]{1,0:T(8,128)(2,1)S(1)}, u32[]{:S(2)}, u32[]{:S(2)}) collective-permute-start(bf16[256,128]{1,0:T(8,128)(2,1)S(1)} %broadcast_select_fusion.3.near), channel_id=1, source_target_pairs={{0,32},{1,33},{2,34},{3,35},{4,36},{5,37},{6,38},{7,39},{8,40},{9,... | collective-permute-start | bytes 196616 | tf_op jit(solution)/shard_map/ppermute | solution.py:299
  80.8 15.9 %collective-permute-start.37 = (bf16[256,128]{1,0:T(8,128)(2,1)S(1)}, bf16[256,128]{1,0:T(8,128)(2,1)S(1)}, u32[]{:S(2)}, u32[]{:S(2)}) collective-permute-start(bf16[256,128]{1,0:T(8,128)(2,1)S(1)} %add_convert_fusion), channel_id=1, source_target_pairs={{64,2},{65,3},{66,4},{67,5},{68,6},{69,7},{70,8},{71,9},{72,10},{7... | collective-permute-start | bytes 196616 | tf_op jit(solution)/shard_map/ppermute | solution.py:299
  82.1 17.6 %collective-permute-start.38 = (bf16[256,128]{1,0:T(8,128)(2,1)S(1)}, bf16[256,128]{1,0:T(8,128)(2,1)S(1)}, u32[]{:S(2)}, u32[]{:S(2)}) collective-permute-start(bf16[256,128]{1,0:T(8,128)(2,1)S(1)} %add_convert_fusion), channel_id=1, source_target_pairs={{64,1},{65,2},{66,3},{67,4},{68,5},{69,6},{70,7},{71,8},{72,9},{73... | collective-permute-start | bytes 196616 | tf_op jit(solution)/shard_map/ppermute | solution.py:299
  83.4 16.3 %collective-permute-start.39 = (bf16[256,128]{1,0:T(8,128)(2,1)S(1)}, bf16[256,128]{1,0:T(8,128)(2,1)S(1)}, u32[]{:S(2)}, u32[]{:S(2)}) collective-permute-start(bf16[256,128]{1,0:T(8,128)(2,1)S(1)} %add_convert_fusion), channel_id=1, source_target_pairs={{64,0},{65,1},{66,2},{67,3},{68,4},{69,5},{70,6},{71,7},{72,8},{73... | collective-permute-start | bytes 196616 | tf_op jit(solution)/shard_map/ppermute | solution.py:299
  99.8 4.5 %collective-permute-start.40 = (bf16[256,384]{1,0:T(8,128)(2,1)S(1)}, bf16[256,384]{1,0:T(8,128)(2,1)S(1)}, u32[]{:S(2)}, u32[]{:S(2)}) collective-permute-start(bf16[256,384]{1,0:T(8,128)(2,1)S(1)} %maximum_add_fusion.2), channel_id=1, source_target_pairs={{0,32},{1,33},{2,34},{3,35},{4,36},{5,37},{6,38},{7,39},{8,40},{9,... | collective-permute-start | bytes 589832 | tf_op jit(solution)/shard_map/ppermute | solution.py:299

commit v7 on v5

--- a/solution.py
+++ b/solution.py
@@ -354,7 +354,7 @@
     near = from_near(pack)
 
     def joined(part):
-        return (part + swap(part)).astype(BF)
+        return (part + swap(part.astype(BF)).astype(F32)).astype(BF)
 
     nothing = jnp.zeros(face, F32)
     odd_down = pick(turned(outer_other[columns:]), outer[columns:])

time: 106 us -> 105 us (level)
  transfers between devices with their start and end apart: 41 -> 41, of which waited for: 13 -> 11; matrix products, arithmetic and copies ran while one was open for 1% -> 1% of each run, Pallas kernels for 5% -> 5%
where the time goes in v7:
time: 105 us
  starting transfers between devices  59.4 us (57%)
  waiting for transfers between devices  30 us (29%)
  Pallas kernels  9.9 us (9%)
  matrix products  2.4 us (2%)
  other arithmetic  1.77 us (2%)
  between operations  1.38 us (1%)
    ppermute x41, starting transfers between devices, send(): return lax.ppermute(value, AXES, pairs)  59.4 us
    ppermute x41, waiting for transfers between devices, send(): return lax.ppermute(value, AXES, pairs)  30 us
    pallas_call x6, Pallas kernels, call(): pl.pallas_call(kernel, out_shape=[jax.ShapeDtypeStruct(shape, kind) for s...  9.9 us
    dot_general x11, matrix products, dot(): lax.dot_general(a, b, (((1,), (0,)), ((), ())), preferred_element_type=F32)  2.4 us
  transfers between devices with their start and end apart: 41, of which 11 were waited for; matrix products, arithmetic and copies ran while one was open for 1% of the time, Pallas kernels for 5%

profile of v7, /device:TPU:1, one launch (start us, length us, event | category | flops | bytes accessed | tf_op | source)
XLA Modules:
  0.0 105.1 jit_solution(6159302275656637122)
XLA Ops:
  0.7 3.7 %shard_map.55 = (bf16[512,256]{1,0:T(8,128)(2,1)S(1)}, bf16[512,256]{1,0:T(8,128)(2,1)S(1)}, bf16[256,768]{1,0:T(8,128)(2,1)S(1)}) custom-call(s32[3]{0:T(128)S(1)} %pad_add_fusion.scalars, f32[256,768]{1,0:T(8,128)} %bitcast.18, bf16[768,768]{1,0:T(8,128)(2,1)} %bitcast.16, bf16[128,768]{1,0:T(8,128)(2,1)} %bitcast.20, bf16[128,768]{1,0:T(8,128)(2,1)} %bitcast.21), custom_call_target="tpu_custom_call" | custom-call | flops 1073741824 | bytes 3145728 | tf_op jit(solution)/shard_map/pallas_call | solution.py:42
  4.4 8.9 %collective-permute-start = (bf16[512,256]{1,0:T(8,128)(2,1)S(1)}, bf16[512,256]{1,0:T(8,128)(2,1)S(1)}, u32[]{:S(2)}, u32[]{:S(2)}) collective-permute-start(bf16[512,256]{1,0:T(8,128)(2,1)S(1)} %get-tuple-element.89), channel_id=1, source_target_pairs={{0,1},{1,2},{2,3},{3,4},{4,5},{5,6},{6,7},{7,8},{8,9},{9,10},{10,1... | collective-permute-start | bytes 786440 | tf_op jit(solution)/shard_map/ppermute | solution.py:308
  13.3 4.9 %collective-permute-done.near = bf16[512,256]{1,0:T(8,128)(2,1)S(1)} collective-permute-done((bf16[512,256]{1,0:T(8,128)(2,1)S(1)}, bf16[512,256]{1,0:T(8,128)(2,1)S(1)}, u32[]{:S(2)}, u32[]{:S(2)}) %collective-permute-start) | collective-permute-done | bytes 262176 | tf_op jit(solution)/shard_map/ppermute | solution.py:308
  18.2 3.7 %collective-permute-done.1.far = bf16[512,256]{1,0:T(8,128)(2,1)S(1)} collective-permute-done((bf16[512,256]{1,0:T(8,128)(2,1)S(1)}, bf16[512,256]{1,0:T(8,128)(2,1)S(1)}, u32[]{:S(2)}, u32[]{:S(2)}) %collective-permute-start.1) | collective-permute-done | bytes 262176 | tf_op jit(solution)/shard_map/ppermute | solution.py:308
  21.9 1.0 shard_map.56
  23.0 0.5 collective-permute-start.4
  23.5 0.9 collective-permute-done.2
  24.5 3.2 %collective-permute-start.3 = (bf16[1024,128]{1,0:T(8,128)(2,1)S(1)}, bf16[1024,128]{1,0:T(8,128)(2,1)S(1)}, u32[]{:S(2)}, u32[]{:S(2)}) collective-permute-start(bf16[1024,128]{1,0:T(8,128)(2,1)S(1)} %pad_maximum_fusion.1.own), channel_id=1, source_target_pairs={{0,1},{1,2},{2,3},{3,4},{4,5},{5,6},{6,7},{7,8},{8,9},{9,10},{10,1... | collective-permute-start | bytes 786440 | tf_op jit(solution)/shard_map/ppermute | solution.py:308
  27.7 3.3 %collective-permute-done.3.near = bf16[1024,128]{1,0:T(8,128)(2,1)S(1)} collective-permute-done((bf16[1024,128]{1,0:T(8,128)(2,1)S(1)}, bf16[1024,128]{1,0:T(8,128)(2,1)S(1)}, u32[]{:S(2)}, u32[]{:S(2)}) %collective-permute-start.3) | collective-permute-done | bytes 262176 | tf_op jit(solution)/shard_map/ppermute | solution.py:308
  31.2 3.5 %collective-permute-start.5 = (bf16[256,128]{1,0:T(8,128)(2,1)S(1)}, bf16[256,128]{1,0:T(8,128)(2,1)S(1)}, u32[]{:S(2)}, u32[]{:S(2)}) collective-permute-start(bf16[256,128]{1,0:T(8,128)(2,1)S(1)} %get-tuple-element.192), channel_id=1, source_target_pairs={{0,32},{1,33},{2,34},{3,35},{4,36},{5,37},{6,38},{7,39},{8,40},{9,... | collective-permute-start | bytes 196616 | tf_op jit(solution)/shard_map/ppermute | solution.py:308
  35.6 1.9 %collective-permute-start.6 = (bf16[256,128]{1,0:T(8,128)(2,1)S(1)}, bf16[256,128]{1,0:T(8,128)(2,1)S(1)}, u32[]{:S(2)}, u32[]{:S(2)}) collective-permute-start(bf16[256,128]{1,0:T(8,128)(2,1)S(1)} %add_convert_fusion.7), channel_id=1, source_target_pairs={{0,66},{1,67},{2,68},{3,69},{4,70},{5,71},{6,72},{7,73},{8,74},{9,... | collective-permute-start | bytes 196616 | tf_op jit(solution)/shard_map/ppermute | solution.py:308
  37.5 4.5 %collective-permute-start.7 = (bf16[256,128]{1,0:T(8,128)(2,1)S(1)}, bf16[256,128]{1,0:T(8,128)(2,1)S(1)}, u32[]{:S(2)}, u32[]{:S(2)}) collective-permute-start(bf16[256,128]{1,0:T(8,128)(2,1)S(1)} %add_convert_fusion.7), channel_id=1, source_target_pairs={{0,65},{1,66},{2,67},{3,68},{4,69},{5,70},{6,71},{7,72},{8,73},{9,... | collective-permute-start | bytes 196616 | tf_op jit(solution)/shard_map/ppermute | solution.py:308
  41.9 0.7 collective-permute-start.8
  42.6 1.1 %shard_map.57 = (bf16[640,128]{1,0:T(8,128)(2,1)S(1)}, bf16[640,128]{1,0:T(8,128)(2,1)S(1)}, bf16[896,128]{1,0:T(8,128)(2,1)S(1)}, f32[256,128]{1,0:T(8,128)S(1)...) custom-call(s32[3]{0:T(128)S(1)} %pad_add_fusion.scalars, ...), custom_call_target="tpu_custom_call" | custom-call | flops 1024 | bytes 1024 | tf_op jit(solution)/shard_map/pallas_call | solution.py:42
  44.2 4.6 %collective-permute-start.15 = (bf16[896,128]{1,0:T(8,128)(2,1)S(1)}, bf16[896,128]{1,0:T(8,128)(2,1)S(1)}, u32[]{:S(2)}, u32[]{:S(2)}) collective-permute-start(bf16[896,128]{1,0:T(8,128)(2,1)S(1)} %get-tuple-element.106.own), channel_id=1, source_target_pairs={{0,1},{1,2},{2,3},{3,4},{4,5},{5,6},{6,7},{7,8},{8,9},{9,10},{10,1... | collective-permute-start | bytes 688136 | tf_op jit(solution)/shard_map/ppermute | solution.py:308
  48.8 0.7 collective-permute-start.12
  49.5 0.7 collective-permute-start.13
  50.2 0.7 collective-permute-start.14
  50.9 0.8 collective-permute-done.15.near
  52.0 2.4 %collective-permute-start.16 = (bf16[256,128]{1,0:T(8,128)(2,1)S(1)}, bf16[256,128]{1,0:T(8,128)(2,1)S(1)}, u32[]{:S(2)}, u32[]{:S(2)}) collective-permute-start(bf16[256,128]{1,0:T(8,128)(2,1)S(1)} %convert_element_type.71), channel_id=1, source_target_pairs={{0,32},{1,33},{2,34},{3,35},{4,36},{5,37},{6,38},{7,39},{8,40},{9,... | collective-permute-start | bytes 196616 | tf_op jit(solution)/shard_map/ppermute | solution.py:308
  54.7 0.5 collective-permute-start.21
  55.3 0.7 collective-permute-start.17
  55.9 0.7 collective-permute-start.18
  56.6 0.7 collective-permute-start.19
  57.3 0.8 collective-permute-start.20
  58.2 0.9 shard_map.58
  60.8 0.7 collective-permute-start.24
  61.4 0.7 collective-permute-start.25
  62.1 0.7 collective-permute-start.26
  62.8 3.4 %collective-permute-start.28 = (bf16[256,128]{1,0:T(8,128)(2,1)S(1)}, bf16[256,128]{1,0:T(8,128)(2,1)S(1)}, u32[]{:S(2)}, u32[]{:S(2)}) collective-permute-start(bf16[256,128]{1,0:T(8,128)(2,1)S(1)} %get-tuple-element.176), channel_id=1, source_target_pairs={{0,1},{1,2},{2,3},{3,4},{4,5},{5,6},{6,7},{7,8},{8,9},{9,10},{10,1... | collective-permute-start | bytes 196616 | tf_op jit(solution)/shard_map/ppermute | solution.py:308
  66.5 1.1 %collective-permute-done.28 = bf16[256,128]{1,0:T(8,128)(2,1)S(1)} collective-permute-done((bf16[256,128]{1,0:T(8,128)(2,1)S(1)}, bf16[256,128]{1,0:T(8,128)(2,1)S(1)}, u32[]{:S(2)}, u32[]{:S(2)}) %collective-permute-start.28) | collective-permute-done | bytes 65568 | tf_op jit(solution)/shard_map/ppermute | solution.py:308
  67.8 3.4 %collective-permute-start.29 = (bf16[256,128]{1,0:T(8,128)(2,1)S(1)}, bf16[256,128]{1,0:T(8,128)(2,1)S(1)}, u32[]{:S(2)}, u32[]{:S(2)}) collective-permute-start(bf16[256,128]{1,0:T(8,128)(2,1)S(1)} %convert_element_type.78), channel_id=1, source_target_pairs={{0,32},{1,33},{2,34},{3,35},{4,36},{5,37},{6,38},{7,39},{8,40},{9,... | collective-permute-start | bytes 196616 | tf_op jit(solution)/shard_map/ppermute | solution.py:308
  71.2 1.9 %collective-permute-start.33 = (bf16[256,128]{1,0:T(8,128)(2,1)S(1)}, bf16[256,128]{1,0:T(8,128)(2,1)S(1)}, u32[]{:S(2)}, u32[]{:S(2)}) collective-permute-start(bf16[256,128]{1,0:T(8,128)(2,1)S(1)} %get-tuple-element.174), channel_id=1, source_target_pairs={{0,1},{1,2},{2,3},{3,4},{4,5},{5,6},{6,7},{7,8},{8,9},{9,10},{10,1... | collective-permute-start | bytes 196616 | tf_op jit(solution)/shard_map/ppermute | solution.py:308
  73.2 0.7 collective-permute-start.30
  73.8 0.7 collective-permute-start.31
  74.5 0.7 collective-permute-start.32
  75.3 0.9 shard_map.59.down
  76.5 2.8 %collective-permute-start.36 = (bf16[256,128]{1,0:T(8,128)(2,1)S(1)}, bf16[256,128]{1,0:T(8,128)(2,1)S(1)}, u32[]{:S(2)}, u32[]{:S(2)}) collective-permute-start(bf16[256,128]{1,0:T(8,128)(2,1)S(1)} %convert_element_type.82), channel_id=1, source_target_pairs={{0,32},{1,33},{2,34},{3,35},{4,36},{5,37},{6,38},{7,39},{8,40},{9,... | collective-permute-start | bytes 196616 | tf_op jit(solution)/shard_map/ppermute | solution.py:308
  79.4 0.8 collective-permute-done.36
  80.2 1.3 %collective-permute-start.37 = (bf16[256,128]{1,0:T(8,128)(2,1)S(1)}, bf16[256,128]{1,0:T(8,128)(2,1)S(1)}, u32[]{:S(2)}, u32[]{:S(2)}) collective-permute-start(bf16[256,128]{1,0:T(8,128)(2,1)S(1)} %add_convert_fusion), channel_id=1, source_target_pairs={{64,2},{65,3},{66,4},{67,5},{68,6},{69,7},{70,8},{71,9},{72,10},{7... | collective-permute-start | bytes 196616 | tf_op jit(solution)/shard_map/ppermute | solution.py:308
  81.5 1.3 %collective-permute-start.38 = (bf16[256,128]{1,0:T(8,128)(2,1)S(1)}, bf16[256,128]{1,0:T(8,128)(2,1)S(1)}, u32[]{:S(2)}, u32[]{:S(2)}) collective-permute-start(bf16[256,128]{1,0:T(8,128)(2,1)S(1)} %add_convert_fusion), channel_id=1, source_target_pairs={{64,1},{65,2},{66,3},{67,4},{68,5},{69,6},{70,7},{71,8},{72,9},{73... | collective-permute-start | bytes 196616 | tf_op jit(solution)/shard_map/ppermute | solution.py:308
  82.8 0.7 collective-permute-start.39
  83.5 2.4 %shard_map.60 = (f32[256,768]{1,0:T(8,128)S(1)}, bf16[640,768]{1,0:T(8,128)(2,1)S(1)}) custom-call(s32[3]{0:T(128)S(1)} %pad_add_fusion.scalars, f32[256,768]{1,0:T(8,128)S(1)} %get-tuple-element.92.adjusted, bf16[256,256]{1,0:T(8,128)(2,1)S(1)} %get-tuple-element.93.near_basis, bf16[256,256]{1,0:T(8,128)(2,1)S(1)} %get-tuple-element.94.far_basis, ...), custom_call_target="tpu_custom_call" | custom-call | flops 1024 | bytes 1024 | tf_op jit(solution)/shard_map/pallas_call | solution.py:42
  86.0 10.0 %collective-permute-done.37 = bf16[256,128]{1,0:T(8,128)(2,1)S(1)} collective-permute-done((bf16[256,128]{1,0:T(8,128)(2,1)S(1)}, bf16[256,128]{1,0:T(8,128)(2,1)S(1)}, u32[]{:S(2)}, u32[]{:S(2)}) %collective-permute-start.37) | collective-permute-done | bytes 65568 | tf_op jit(solution)/shard_map/ppermute | solution.py:308
  95.9 3.1 %collective-permute-done.38 = bf16[256,128]{1,0:T(8,128)(2,1)S(1)} collective-permute-done((bf16[256,128]{1,0:T(8,128)(2,1)S(1)}, bf16[256,128]{1,0:T(8,128)(2,1)S(1)}, u32[]{:S(2)}, u32[]{:S(2)}) %collective-permute-start.38) | collective-permute-done | bytes 65568 | tf_op jit(solution)/shard_map/ppermute | solution.py:308
  99.1 3.4 %collective-permute-start.40 = (bf16[256,384]{1,0:T(8,128)(2,1)S(1)}, bf16[256,384]{1,0:T(8,128)(2,1)S(1)}, u32[]{:S(2)}, u32[]{:S(2)}) collective-permute-start(bf16[256,384]{1,0:T(8,128)(2,1)S(1)} %maximum_add_fusion.2), channel_id=1, source_target_pairs={{0,32},{1,33},{2,34},{3,35},{4,36},{5,37},{6,38},{7,39},{8,40},{9,... | collective-permute-start | bytes 589832 | tf_op jit(solution)/shard_map/ppermute | solution.py:308
  102.5 1.1 %collective-permute-done.40 = bf16[256,384]{1,0:T(8,128)(2,1)S(1)} collective-permute-done((bf16[256,384]{1,0:T(8,128)(2,1)S(1)}, bf16[256,384]{1,0:T(8,128)(2,1)S(1)}, u32[]{:S(2)}, u32[]{:S(2)}) %collective-permute-start.40) | collective-permute-done | bytes 196640 | tf_op jit(solution)/shard_map/ppermute | solution.py:308
  104.1 1.0 add_bitcast_fusion
  (99 shorter events, 5.9 us)
Async XLA Ops:
  0.7 21.2 %copy-start.1 = (f32[1,1,256,768]{3,2,1,0:T(8,128)S(1)}, f32[1,1,256,768]{3,2,1,0:T(8,128)}, u32[]{:S(2)}) copy-start(f32[1,1,256,768]{3,2,1,0:T(8,128)} %param.5) | copy-start | bytes 2359300
  4.4 13.8 %collective-permute-start = (bf16[512,256]{1,0:T(8,128)(2,1)S(1)}, bf16[512,256]{1,0:T(8,128)(2,1)S(1)}, u32[]{:S(2)}, u32[]{:S(2)}) collective-permute-start(bf16[512,256]{1,0:T(8,128)(2,1)S(1)} %get-tuple-element.89), channel_id=1, source_target_pairs={{0,1},{1,2},{2,3},{3,4},{4,5},{5,6},{6,7},{7,8},{8,9},{9,10},{10,1... | collective-permute-start | bytes 786440 | tf_op jit(solution)/shard_map/ppermute | solution.py:308
  13.3 8.5 %collective-permute-start.1 = (bf16[512,256]{1,0:T(8,128)(2,1)S(1)}, bf16[512,256]{1,0:T(8,128)(2,1)S(1)}, u32[]{:S(2)}, u32[]{:S(2)}) collective-permute-start(bf16[512,256]{1,0:T(8,128)(2,1)S(1)} %get-tuple-element.90), channel_id=1, source_target_pairs={{0,31},{1,0},{2,1},{3,2},{4,3},{5,4},{6,5},{7,6},{8,7},{9,8},{10,9... | collective-permute-start | bytes 786440 | tf_op jit(solution)/shard_map/ppermute | solution.py:308
  22.9 1.5 %collective-permute-start.2 = (bf16[640,128]{1,0:T(8,128)(2,1)S(1)}, bf16[640,128]{1,0:T(8,128)(2,1)S(1)}, u32[]{:S(2)}, u32[]{:S(2)}) collective-permute-start(bf16[640,128]{1,0:T(8,128)(2,1)S(1)} %get-tuple-element.95), channel_id=1, source_target_pairs={{0,32},{1,33},{2,34},{3,35},{4,36},{5,37},{6,38},{7,39},{8,40},{9,... | collective-permute-start | bytes 491528 | tf_op jit(solution)/shard_map/ppermute | solution.py:308
  23.0 4.7 %collective-permute-start.4 = (bf16[640,128]{1,0:T(8,128)(2,1)S(1)}, bf16[640,128]{1,0:T(8,128)(2,1)S(1)}, u32[]{:S(2)}, u32[]{:S(2)}) collective-permute-start(bf16[640,128]{1,0:T(8,128)(2,1)S(1)} %get-tuple-element.96.outer), channel_id=1, source_target_pairs={{0,32},{1,33},{2,34},{3,35},{4,36},{5,37},{6,38},{7,39},{8,40},{9,... | collective-permute-start | bytes 491528 | tf_op jit(solution)/shard_map/ppermute | solution.py:308
  24.5 6.5 %collective-permute-start.3 = (bf16[1024,128]{1,0:T(8,128)(2,1)S(1)}, bf16[1024,128]{1,0:T(8,128)(2,1)S(1)}, u32[]{:S(2)}, u32[]{:S(2)}) collective-permute-start(bf16[1024,128]{1,0:T(8,128)(2,1)S(1)} %pad_maximum_fusion.1.own), channel_id=1, source_target_pairs={{0,1},{1,2},{2,3},{3,4},{4,5},{5,6},{6,7},{7,8},{8,9},{9,10},{10,1... | collective-permute-start | bytes 786440 | tf_op jit(solution)/shard_map/ppermute | solution.py:308
  31.2 4.4 %collective-permute-start.5 = (bf16[256,128]{1,0:T(8,128)(2,1)S(1)}, bf16[256,128]{1,0:T(8,128)(2,1)S(1)}, u32[]{:S(2)}, u32[]{:S(2)}) collective-permute-start(bf16[256,128]{1,0:T(8,128)(2,1)S(1)} %get-tuple-element.192), channel_id=1, source_target_pairs={{0,32},{1,33},{2,34},{3,35},{4,36},{5,37},{6,38},{7,39},{8,40},{9,... | collective-permute-start | bytes 196616 | tf_op jit(solution)/shard_map/ppermute | solution.py:308
  34.7 7.9 %collective-permute-start.10 = (bf16[640,128]{1,0:T(8,128)(2,1)S(1)}, bf16[640,128]{1,0:T(8,128)(2,1)S(1)}, u32[]{:S(2)}, u32[]{:S(2)}) collective-permute-start(bf16[640,128]{1,0:T(8,128)(2,1)S(1)} %get-tuple-element.97.extra), channel_id=1, source_target_pairs={{0,32},{1,33},{2,34},{3,35},{4,36},{5,37},{6,38},{7,39},{8,40},{9,... | collective-permute-start | bytes 491528 | tf_op jit(solution)/shard_map/ppermute | solution.py:308
  34.8 7.8 %collective-permute-start.9 = (bf16[1024,128]{1,0:T(8,128)(2,1)S(1)}, bf16[1024,128]{1,0:T(8,128)(2,1)S(1)}, u32[]{:S(2)}, u32[]{:S(2)}) collective-permute-start(bf16[1024,128]{1,0:T(8,128)(2,1)S(1)} %collective-permute-done.3.near), channel_id=1, source_target_pairs={{0,32},{1,33},{2,34},{3,35},{4,36},{5,37},{6,38},{7,39},{8,40},{9,... | collective-permute-start | bytes 786440 | tf_op jit(solution)/shard_map/ppermute | solution.py:308
  35.6 8.1 %collective-permute-start.6 = (bf16[256,128]{1,0:T(8,128)(2,1)S(1)}, bf16[256,128]{1,0:T(8,128)(2,1)S(1)}, u32[]{:S(2)}, u32[]{:S(2)}) collective-permute-start(bf16[256,128]{1,0:T(8,128)(2,1)S(1)} %add_convert_fusion.7), channel_id=1, source_target_pairs={{0,66},{1,67},{2,68},{3,69},{4,70},{5,71},{6,72},{7,73},{8,74},{9,... | collective-permute-start | bytes 196616 | tf_op jit(solution)/shard_map/ppermute | solution.py:308
  37.5 6.2 %collective-permute-start.7 = (bf16[256,128]{1,0:T(8,128)(2,1)S(1)}, bf16[256,128]{1,0:T(8,128)(2,1)S(1)}, u32[]{:S(2)}, u32[]{:S(2)}) collective-permute-start(bf16[256,128]{1,0:T(8,128)(2,1)S(1)} %add_convert_fusion.7), channel_id=1, source_target_pairs={{0,65},{1,66},{2,67},{3,68},{4,69},{5,70},{6,71},{7,72},{8,73},{9,... | collective-permute-start | bytes 196616 | tf_op jit(solution)/shard_map/ppermute | solution.py:308
  41.9 1.8 %collective-permute-start.8 = (bf16[256,128]{1,0:T(8,128)(2,1)S(1)}, bf16[256,128]{1,0:T(8,128)(2,1)S(1)}, u32[]{:S(2)}, u32[]{:S(2)}) collective-permute-start(bf16[256,128]{1,0:T(8,128)(2,1)S(1)} %add_convert_fusion.7), channel_id=1, source_target_pairs={{0,64},{1,65},{2,66},{3,67},{4,68},{5,69},{6,70},{7,71},{8,72},{9,... | collective-permute-start | bytes 196616 | tf_op jit(solution)/shard_map/ppermute | solution.py:308
  44.0 4.8 %collective-permute-start.11 = (bf16[256,128]{1,0:T(8,128)(2,1)S(1)}, bf16[256,128]{1,0:T(8,128)(2,1)S(1)}, u32[]{:S(2)}, u32[]{:S(2)}) collective-permute-start(bf16[256,128]{1,0:T(8,128)(2,1)S(1)} %convert_element_type.68), channel_id=1, source_target_pairs={{0,32},{1,33},{2,34},{3,35},{4,36},{5,37},{6,38},{7,39},{8,40},{9,... | collective-permute-start | bytes 196616 | tf_op jit(solution)/shard_map/ppermute | solution.py:308
  44.2 7.5 %collective-permute-start.15 = (bf16[896,128]{1,0:T(8,128)(2,1)S(1)}, bf16[896,128]{1,0:T(8,128)(2,1)S(1)}, u32[]{:S(2)}, u32[]{:S(2)}) collective-permute-start(bf16[896,128]{1,0:T(8,128)(2,1)S(1)} %get-tuple-element.106.own), channel_id=1, source_target_pairs={{0,1},{1,2},{2,3},{3,4},{4,5},{5,6},{6,7},{7,8},{8,9},{9,10},{10,1... | collective-permute-start | bytes 688136 | tf_op jit(solution)/shard_map/ppermute | solution.py:308
  48.8 2.1 %collective-permute-start.12 = (bf16[256,128]{1,0:T(8,128)(2,1)S(1)}, bf16[256,128]{1,0:T(8,128)(2,1)S(1)}, u32[]{:S(2)}, u32[]{:S(2)}) collective-permute-start(bf16[256,128]{1,0:T(8,128)(2,1)S(1)} %add_convert_fusion.6), channel_id=1, source_target_pairs={{64,130},{65,131},{66,132},{67,133},{68,134},{69,135},{70,136},{71... | collective-permute-start | bytes 196616 | tf_op jit(solution)/shard_map/ppermute | solution.py:308
  49.5 1.4 %collective-permute-start.13 = (bf16[256,128]{1,0:T(8,128)(2,1)S(1)}, bf16[256,128]{1,0:T(8,128)(2,1)S(1)}, u32[]{:S(2)}, u32[]{:S(2)}) collective-permute-start(bf16[256,128]{1,0:T(8,128)(2,1)S(1)} %add_convert_fusion.6), channel_id=1, source_target_pairs={{64,129},{65,130},{66,131},{67,132},{68,133},{69,134},{70,135},{71... | collective-permute-start | bytes 196616 | tf_op jit(solution)/shard_map/ppermute | solution.py:308
  50.2 0.7 collective-permute-start.14
  52.0 3.3 %collective-permute-start.16 = (bf16[256,128]{1,0:T(8,128)(2,1)S(1)}, bf16[256,128]{1,0:T(8,128)(2,1)S(1)}, u32[]{:S(2)}, u32[]{:S(2)}) collective-permute-start(bf16[256,128]{1,0:T(8,128)(2,1)S(1)} %convert_element_type.71), channel_id=1, source_target_pairs={{0,32},{1,33},{2,34},{3,35},{4,36},{5,37},{6,38},{7,39},{8,40},{9,... | collective-permute-start | bytes 196616 | tf_op jit(solution)/shard_map/ppermute | solution.py:308
  54.6 4.4 %collective-permute-start.22 = (f32[256,128]{1,0:T(8,128)S(1)}, f32[256,128]{1,0:T(8,128)S(1)}, u32[]{:S(2)}, u32[]{:S(2)}) collective-permute-start(f32[256,128]{1,0:T(8,128)S(1)} %fusion.54), channel_id=1, source_target_pairs={{0,32},{1,33},{2,34},{3,35},{4,36},{5,37},{6,38},{7,39},{8,40},{9,... | collective-permute-start | bytes 393224 | tf_op jit(solution)/shard_map/ppermute | solution.py:308
  54.7 2.6 %collective-permute-start.21 = (bf16[896,128]{1,0:T(8,128)(2,1)S(1)}, bf16[896,128]{1,0:T(8,128)(2,1)S(1)}, u32[]{:S(2)}, u32[]{:S(2)}) collective-permute-start(bf16[896,128]{1,0:T(8,128)(2,1)S(1)} %collective-permute-done.15.near), channel_id=1, source_target_pairs={{0,32},{1,33},{2,34},{3,35},{4,36},{5,37},{6,38},{7,39},{8,40},{9,... | collective-permute-start | bytes 688136 | tf_op jit(solution)/shard_map/ppermute | solution.py:308
  55.3 3.8 %collective-permute-start.17 = (bf16[256,128]{1,0:T(8,128)(2,1)S(1)}, bf16[256,128]{1,0:T(8,128)(2,1)S(1)}, u32[]{:S(2)}, u32[]{:S(2)}) collective-permute-start(bf16[256,128]{1,0:T(8,128)(2,1)S(1)} %add_convert_fusion.5), channel_id=1, source_target_pairs={{128,195},{129,196},{130,197},{131,198},{132,199},{133,200},{134,2... | collective-permute-start | bytes 196616 | tf_op jit(solution)/shard_map/ppermute | solution.py:308
  55.9 3.1 %collective-permute-start.18 = (bf16[256,128]{1,0:T(8,128)(2,1)S(1)}, bf16[256,128]{1,0:T(8,128)(2,1)S(1)}, u32[]{:S(2)}, u32[]{:S(2)}) collective-permute-start(bf16[256,128]{1,0:T(8,128)(2,1)S(1)} %add_convert_fusion.5), channel_id=1, source_target_pairs={{128,194},{129,195},{130,196},{131,197},{132,198},{133,199},{134,2... | collective-permute-start | bytes 196616 | tf_op jit(solution)/shard_map/ppermute | solution.py:308
  56.6 2.5 %collective-permute-start.19 = (bf16[256,128]{1,0:T(8,128)(2,1)S(1)}, bf16[256,128]{1,0:T(8,128)(2,1)S(1)}, u32[]{:S(2)}, u32[]{:S(2)}) collective-permute-start(bf16[256,128]{1,0:T(8,128)(2,1)S(1)} %add_convert_fusion.5), channel_id=1, source_target_pairs={{128,193},{129,194},{130,195},{131,196},{132,197},{133,198},{134,1... | collective-permute-start | bytes 196616 | tf_op jit(solution)/shard_map/ppermute | solution.py:308
  57.3 1.8 %collective-permute-start.20 = (bf16[256,128]{1,0:T(8,128)(2,1)S(1)}, bf16[256,128]{1,0:T(8,128)(2,1)S(1)}, u32[]{:S(2)}, u32[]{:S(2)}) collective-permute-start(bf16[256,128]{1,0:T(8,128)(2,1)S(1)} %add_convert_fusion.5), channel_id=1, source_target_pairs={{128,192},{129,193},{130,194},{131,195},{132,196},{133,197},{134,1... | collective-permute-start | bytes 196616 | tf_op jit(solution)/shard_map/ppermute | solution.py:308
  59.4 1.3 %collective-permute-start.23 = (bf16[256,128]{1,0:T(8,128)(2,1)S(1)}, bf16[256,128]{1,0:T(8,128)(2,1)S(1)}, u32[]{:S(2)}, u32[]{:S(2)}) collective-permute-start(bf16[256,128]{1,0:T(8,128)(2,1)S(1)} %convert_element_type.74), channel_id=1, source_target_pairs={{0,32},{1,33},{2,34},{3,35},{4,36},{5,37},{6,38},{7,39},{8,40},{9,... | collective-permute-start | bytes 196616 | tf_op jit(solution)/shard_map/ppermute | solution.py:308
  60.1 15.2 %collective-permute-start.34 = (bf16[256,384]{1,0:T(8,128)(2,1)S(1)}, bf16[256,384]{1,0:T(8,128)(2,1)S(1)}, u32[]{:S(2)}, u32[]{:S(2)}) collective-permute-start(bf16[256,384]{1,0:T(8,128)(2,1)S(1)} %add.95.mine), channel_id=1, source_target_pairs={{0,32},{1,33},{2,34},{3,35},{4,36},{5,37},{6,38},{7,39},{8,40},{9,... | collective-permute-start | bytes 589832 | tf_op jit(solution)/shard_map/ppermute | solution.py:308
  60.4 2.4 %collective-permute-start.27 = (f32[256,128]{1,0:T(8,128)S(1)}, f32[256,128]{1,0:T(8,128)S(1)}, u32[]{:S(2)}, u32[]{:S(2)}) collective-permute-start(f32[256,128]{1,0:T(8,128)S(1)} %fusion.52), channel_id=1, source_target_pairs={{0,32},{1,33},{2,34},{3,35},{4,36},{5,37},{6,38},{7,39},{8,40},{9,... | collective-permute-start | bytes 393224 | tf_op jit(solution)/shard_map/ppermute | solution.py:308
  60.8 5.7 %collective-permute-start.24 = (bf16[256,128]{1,0:T(8,128)(2,1)S(1)}, bf16[256,128]{1,0:T(8,128)(2,1)S(1)}, u32[]{:S(2)}, u32[]{:S(2)}) collective-permute-start(bf16[256,128]{1,0:T(8,128)(2,1)S(1)} %add_convert_fusion.4), channel_id=1, source_target_pairs={{192,130},{193,131},{194,132},{195,133},{196,134},{197,135},{198,1... | collective-permute-start | bytes 196616 | tf_op jit(solution)/shard_map/ppermute | solution.py:308
  61.4 5.0 %collective-permute-start.25 = (bf16[256,128]{1,0:T(8,128)(2,1)S(1)}, bf16[256,128]{1,0:T(8,128)(2,1)S(1)}, u32[]{:S(2)}, u32[]{:S(2)}) collective-permute-start(bf16[256,128]{1,0:T(8,128)(2,1)S(1)} %add_convert_fusion.4), channel_id=1, source_target_pairs={{192,129},{193,130},{194,131},{195,132},{196,133},{197,134},{198,1... | collective-permute-start | bytes 196616 | tf_op jit(solution)/shard_map/ppermute | solution.py:308
  62.1 4.3 %collective-permute-start.26 = (bf16[256,128]{1,0:T(8,128)(2,1)S(1)}, bf16[256,128]{1,0:T(8,128)(2,1)S(1)}, u32[]{:S(2)}, u32[]{:S(2)}) collective-permute-start(bf16[256,128]{1,0:T(8,128)(2,1)S(1)} %add_convert_fusion.4), channel_id=1, source_target_pairs={{192,128},{193,129},{194,130},{195,131},{196,132},{197,133},{198,1... | collective-permute-start | bytes 196616 | tf_op jit(solution)/shard_map/ppermute | solution.py:308
  62.8 4.7 %collective-permute-start.28 = (bf16[256,128]{1,0:T(8,128)(2,1)S(1)}, bf16[256,128]{1,0:T(8,128)(2,1)S(1)}, u32[]{:S(2)}, u32[]{:S(2)}) collective-permute-start(bf16[256,128]{1,0:T(8,128)(2,1)S(1)} %get-tuple-element.176), channel_id=1, source_target_pairs={{0,1},{1,2},{2,3},{3,4},{4,5},{5,6},{6,7},{7,8},{8,9},{9,10},{10,1... | collective-permute-start | bytes 196616 | tf_op jit(solution)/shard_map/ppermute | solution.py:308
  67.8 5.3 %collective-permute-start.29 = (bf16[256,128]{1,0:T(8,128)(2,1)S(1)}, bf16[256,128]{1,0:T(8,128)(2,1)S(1)}, u32[]{:S(2)}, u32[]{:S(2)}) collective-permute-start(bf16[256,128]{1,0:T(8,128)(2,1)S(1)} %convert_element_type.78), channel_id=1, source_target_pairs={{0,32},{1,33},{2,34},{3,35},{4,36},{5,37},{6,38},{7,39},{8,40},{9,... | collective-permute-start | bytes 196616 | tf_op jit(solution)/shard_map/ppermute | solution.py:308
  71.2 5.0 %collective-permute-start.33 = (bf16[256,128]{1,0:T(8,128)(2,1)S(1)}, bf16[256,128]{1,0:T(8,128)(2,1)S(1)}, u32[]{:S(2)}, u32[]{:S(2)}) collective-permute-start(bf16[256,128]{1,0:T(8,128)(2,1)S(1)} %get-tuple-element.174), channel_id=1, source_target_pairs={{0,1},{1,2},{2,3},{3,4},{4,5},{5,6},{6,7},{7,8},{8,9},{9,10},{10,1... | collective-permute-start | bytes 196616 | tf_op jit(solution)/shard_map/ppermute | solution.py:308
  73.2 3.1 %collective-permute-start.30 = (bf16[256,128]{1,0:T(8,128)(2,1)S(1)}, bf16[256,128]{1,0:T(8,128)(2,1)S(1)}, u32[]{:S(2)}, u32[]{:S(2)}) collective-permute-start(bf16[256,128]{1,0:T(8,128)(2,1)S(1)} %add_convert_fusion.2), channel_id=1, source_target_pairs={{128,66},{129,67},{130,68},{131,69},{132,70},{133,71},{134,72},{13... | collective-permute-start | bytes 196616 | tf_op jit(solution)/shard_map/ppermute | solution.py:308
  73.8 2.4 %collective-permute-start.31 = (bf16[256,128]{1,0:T(8,128)(2,1)S(1)}, bf16[256,128]{1,0:T(8,128)(2,1)S(1)}, u32[]{:S(2)}, u32[]{:S(2)}) collective-permute-start(bf16[256,128]{1,0:T(8,128)(2,1)S(1)} %add_convert_fusion.2), channel_id=1, source_target_pairs={{128,65},{129,66},{130,67},{131,68},{132,69},{133,70},{134,71},{13... | collective-permute-start | bytes 196616 | tf_op jit(solution)/shard_map/ppermute | solution.py:308
  74.5 1.7 %collective-permute-start.32 = (bf16[256,128]{1,0:T(8,128)(2,1)S(1)}, bf16[256,128]{1,0:T(8,128)(2,1)S(1)}, u32[]{:S(2)}, u32[]{:S(2)}) collective-permute-start(bf16[256,128]{1,0:T(8,128)(2,1)S(1)} %add_convert_fusion.2), channel_id=1, source_target_pairs={{128,64},{129,65},{130,66},{131,67},{132,68},{133,69},{134,70},{13... | collective-permute-start | bytes 196616 | tf_op jit(solution)/shard_map/ppermute | solution.py:308
  76.2 7.3 %copy-start = (bf16[1,1,768,768]{3,2,1,0:T(8,128)(2,1)S(1)}, bf16[1,1,768,768]{3,2,1,0:T(8,128)(2,1)}, u32[]{:S(2)}) copy-start(bf16[1,1,768,768]{3,2,1,0:T(8,128)(2,1)} %param.6) | copy-start | bytes 3538948
  76.5 3.7 %collective-permute-start.36 = (bf16[256,128]{1,0:T(8,128)(2,1)S(1)}, bf16[256,128]{1,0:T(8,128)(2,1)S(1)}, u32[]{:S(2)}, u32[]{:S(2)}) collective-permute-start(bf16[256,128]{1,0:T(8,128)(2,1)S(1)} %convert_element_type.82), channel_id=1, source_target_pairs={{0,32},{1,33},{2,34},{3,35},{4,36},{5,37},{6,38},{7,39},{8,40},{9,... | collective-permute-start | bytes 196616 | tf_op jit(solution)/shard_map/ppermute | solution.py:308
  79.3 4.3 %collective-permute-start.35 = (bf16[256,128]{1,0:T(8,128)(2,1)S(1)}, bf16[256,128]{1,0:T(8,128)(2,1)S(1)}, u32[]{:S(2)}, u32[]{:S(2)}) collective-permute-start(bf16[256,128]{1,0:T(8,128)(2,1)S(1)} %broadcast_select_fusion.3.near), channel_id=1, source_target_pairs={{0,32},{1,33},{2,34},{3,35},{4,36},{5,37},{6,38},{7,39},{8,40},{9,... | collective-permute-start | bytes 196616 | tf_op jit(solution)/shard_map/ppermute | solution.py:308
  80.2 15.8 %collective-permute-start.37 = (bf16[256,128]{1,0:T(8,128)(2,1)S(1)}, bf16[256,128]{1,0:T(8,128)(2,1)S(1)}, u32[]{:S(2)}, u32[]{:S(2)}) collective-permute-start(bf16[256,128]{1,0:T(8,128)(2,1)S(1)} %add_convert_fusion), channel_id=1, source_target_pairs={{64,2},{65,3},{66,4},{67,5},{68,6},{69,7},{70,8},{71,9},{72,10},{7... | collective-permute-start | bytes 196616 | tf_op jit(solution)/shard_map/ppermute | solution.py:308
  81.5 17.5 %collective-permute-start.38 = (bf16[256,128]{1,0:T(8,128)(2,1)S(1)}, bf16[256,128]{1,0:T(8,128)(2,1)S(1)}, u32[]{:S(2)}, u32[]{:S(2)}) collective-permute-start(bf16[256,128]{1,0:T(8,128)(2,1)S(1)} %add_convert_fusion), channel_id=1, source_target_pairs={{64,1},{65,2},{66,3},{67,4},{68,5},{69,6},{70,7},{71,8},{72,9},{73... | collective-permute-start | bytes 196616 | tf_op jit(solution)/shard_map/ppermute | solution.py:308
  82.8 16.2 %collective-permute-start.39 = (bf16[256,128]{1,0:T(8,128)(2,1)S(1)}, bf16[256,128]{1,0:T(8,128)(2,1)S(1)}, u32[]{:S(2)}, u32[]{:S(2)}) collective-permute-start(bf16[256,128]{1,0:T(8,128)(2,1)S(1)} %add_convert_fusion), channel_id=1, source_target_pairs={{64,0},{65,1},{66,2},{67,3},{68,4},{69,5},{70,6},{71,7},{72,8},{73... | collective-permute-start | bytes 196616 | tf_op jit(solution)/shard_map/ppermute | solution.py:308
  99.1 4.5 %collective-permute-start.40 = (bf16[256,384]{1,0:T(8,128)(2,1)S(1)}, bf16[256,384]{1,0:T(8,128)(2,1)S(1)}, u32[]{:S(2)}, u32[]{:S(2)}) collective-permute-start(bf16[256,384]{1,0:T(8,128)(2,1)S(1)} %maximum_add_fusion.2), channel_id=1, source_target_pairs={{0,32},{1,33},{2,34},{3,35},{4,36},{5,37},{6,38},{7,39},{8,40},{9,... | collective-permute-start | bytes 589832 | tf_op jit(solution)/shard_map/ppermute | solution.py:308
